TPU v7x, 32 devices: a whole 2x2x4 slice. The times are simulated.
32 devices in a mesh: fac: 8 (over y, x, core), freq: 4 (over z).
Axes of the slice: x: 2, y: 2, z: 4, core: 2. Of those that a mesh axis runs over, the one named last changes fastest.
Arguments:
- right_side: float32 [16, 36864, 128], P('freq', 'fac'), may hold values from -6 to 6
- factors: bfloat16 [36864, 1024], P('fac'), may hold values from -0.03125 to 0.03125
- pair_weight: float32 [16, 36864], P('freq', 'fac'), may hold values from -2 to 2
- second_order: float32 [16, 36864], P('freq', 'fac'), may hold values from -1 to 1
- forward: float32 [16, 16], replicated, may hold values from -3 to 3
- backward: float32 [16, 16], replicated, may hold values from -3 to 3
Outputs:
- amplitude: float32 [16, 36864, 128], P('freq', 'fac')
- sources: float32 [16, 36864, 128], P('freq', 'fac')
All inputs are finite; a program needn't handle non-finite values.
Results may differ from a plain program's by a relative error of at most 0.0015.
Values may be sent and summed in bfloat16 or wider, within the bound.
A program may use at most 128 MiB of HBM per device.

v0:
```python
import functools

import jax
import jax.numpy as jnp
from jax import lax
from jax.experimental import pallas as pl
from jax.experimental.pallas import tpu as pltpu
from jax.sharding import PartitionSpec as P

INNER = 2
LANES = 128
MESH = pl.DeviceIdType.MESH
CHUNK = 16
WIDE = 32
EXACT = lax.Precision.HIGHEST
R_MAX = 6.0
W_MAX = 2.0
L_MAX = 0.03125
HALF_TOP = 32768.0
VMEM = pltpu.VMEM


def tile_of(pairs):
    for blocks in (3, 4, 2, 1):
        if pairs % (blocks * LANES) == 0:
            return blocks * LANES
    return None


def mix(table, lanes, outs, count, term):
    totals = [None] * outs
    for v in range(count):
        value = term(v)
        for w in range(outs):
            row = w * count + v
            product = table[row : row + 1, lanes] * value
            totals[w] = product if totals[w] is None else totals[w] + product
    return totals


def blocks_of(ref):
    return [slice(k, k + LANES) for k in range(0, ref.shape[1], LANES)]


def part(i, base, chunk):
    return pl.ds(pl.multiple_of(base + i * chunk, chunk), chunk)


def spread(l_ref, p_ref, held):
    block = p_ref.shape[1]
    for s in range(p_ref.shape[0]):
        held[s * block : (s + 1) * block, :] = lax.dot_general(
            p_ref[s], l_ref[...], (((1,), (1,)), ((), ())), preferred_element_type=jnp.float32
        )


def dot_exact(a, b):
    return lax.dot_general(
        a, b, (((1,), (0,)), ((), ())), precision=EXACT, preferred_element_type=jnp.float32
    )


def resident(x):
    return pl.BlockSpec(x.shape, lambda i, *_: (0,) * x.ndim, pipeline_mode=pl.Buffered(1))


def quarter_kernel(nf, parts, me_ref, l_ref, k_ref, wt_ref, coef_ref, p_ref, *rest):
    r_refs, rest = rest[:parts], rest[parts:]
    u_refs, rest = rest[:parts], rest[parts:]
    v_refs, (table, held, turned, mid, far) = rest[:parts], rest[parts:]
    own = nf // parts
    cols = r_refs[0].shape[2]
    table[...] = dot_exact(coef_ref[...], k_ref[...])
    spread(l_ref, p_ref, held)
    for lanes in blocks_of(table):
        for v in range(nf):
            turned[v] = r_refs[v // own][v % own, lanes, :].T

        @pl.loop(0, cols // CHUNK)
        def _(i):
            rows = part(i, 0, CHUNK)
            got = mix(
                table,
                lanes,
                nf,
                nf,
                lambda v: turned[v, rows, :]
                + wt_ref[v : v + 1, lanes] * held[part(i, v * cols, CHUNK), lanes],
            )
            for w in range(nf):
                mid[w, rows, :] = got[w]
                turned[w, rows, :] = turned[w, rows, :] + got[w]
            got = mix(table, lanes, nf, nf, lambda v: turned[v, rows, :])
            for w in range(nf):
                far[w, rows, :] = got[w]

        for w in range(nf):
            u_refs[w // own][w % own, lanes, :] = mid[w].T
            v_refs[w // own][w % own, lanes, :] = far[w].T


def quarter_pass(me, factors, kernels, weights, coef, gathered, right_side, moved):
    own, pairs, cols = right_side.shape
    nf = weights.shape[0]
    parts = nf // own
    quarter = pairs // parts
    naux = factors.shape[1]
    tile = tile_of(quarter)
    steps = None if tile is None else quarter // tile
    if tile is None:
        cut = lambda x, axis: lax.dynamic_slice_in_dim(x, me * quarter, quarter, axis)
        here = jnp.concatenate([cut(right_side, 1)] + moved)
        table = jnp.einsum("jt,tp->jp", coef, cut(kernels, 1), precision=EXACT)
        table = table.reshape(nf, nf, quarter)
        wide = jnp.einsum(
            "ja,pa->jp",
            gathered.reshape(nf * cols, naux),
            cut(factors, 0),
            preferred_element_type=jnp.float32,
        )
        wide = jnp.transpose(wide.reshape(nf, cols, quarter), (0, 2, 1))
        wide = here + cut(weights, 1)[:, :, None] * wide
        u = jnp.einsum("wvp,vpc->wpc", table, wide, precision=EXACT)
        v = jnp.einsum("wvp,vpc->wpc", table, here + u, precision=EXACT)
        return (
            [u[s * own : (s + 1) * own] for s in range(parts)],
            [v[s * own : (s + 1) * own] for s in range(parts)],
        )
    at = lambda i, m: m[0] * steps + i
    piece = pl.BlockSpec((own, tile, cols), lambda i, m: (0, i, 0))
    shape = jax.ShapeDtypeStruct((own, quarter, cols), jnp.float32)
    out = pl.pallas_call(
        functools.partial(quarter_kernel, nf, parts),
        out_shape=[shape] * (2 * parts),
        grid_spec=pltpu.PrefetchScalarGridSpec(
            num_scalar_prefetch=1,
            grid=(steps,),
            in_specs=[
                pl.BlockSpec((tile, naux), lambda i, m: (at(i, m), 0)),
                pl.BlockSpec((nf, tile), lambda i, m: (0, at(i, m))),
                pl.BlockSpec((nf, tile), lambda i, m: (0, at(i, m))),
                resident(coef),
                resident(gathered),
                pl.BlockSpec((own, tile, cols), lambda i, m: (0, at(i, m), 0)),
            ]
            + [piece] * (parts - 1),
            out_specs=[piece] * (2 * parts),
            scratch_shapes=[
                VMEM((nf * nf, tile), jnp.float32),
                VMEM((nf * cols, tile), jnp.float32),
            ]
            + [VMEM((nf, cols, LANES), jnp.float32)] * 3,
        ),
        compiler_params=pltpu.CompilerParams(vmem_limit_bytes=56 << 20),
        cost_estimate=pl.CostEstimate(
            flops=2 * nf * quarter * cols * (naux + 32 * nf),
            bytes_accessed=16 * nf * quarter * cols,
            transcendentals=0,
        ),
    )(me.reshape(1), factors, kernels, weights, coef, gathered, right_side, *moved)
    return list(out[:parts]), list(out[parts:])


def project_kernel(parts, steps, me_ref, l_ref, *rest):
    s_refs, (o_ref,) = rest[:parts], rest[parts:]
    own, _, cols = s_refs[0].shape
    i = pl.program_id(0)

    @pl.when(i == 0)
    def _():
        o_ref[...] = jnp.zeros_like(o_ref)

    for s in range(parts):

        @pl.when(lax.div(i, steps) == s)
        def _():
            for f in range(own):
                rows = slice(f * cols, (f + 1) * cols)
                o_ref[rows, :] += lax.dot_general(
                    s_refs[s][f].astype(jnp.bfloat16),
                    l_ref[...],
                    (((0,), (0,)), ((), ())),
                    preferred_element_type=jnp.float32,
                )


def stay(s, steps):
    return lambda i, m: (0, jnp.clip(i - s * steps, 0, steps - 1), 0)


def project(me, factors, pieces):
    own, quarter, cols = pieces[0].shape
    parts = len(pieces)
    naux = factors.shape[1]
    tile = tile_of(quarter)
    if tile is None:
        total = 0.0
        for s, x in enumerate(pieces):
            rows = lax.dynamic_slice_in_dim(
                factors, lax.rem(me + s, parts) * quarter, quarter, 0
            )
            total = total + jnp.einsum(
                "pa,fpc->fca", rows, x.astype(jnp.bfloat16), preferred_element_type=jnp.float32
            )
        return total.reshape(own * cols, naux)
    steps = quarter // tile
    around = lambda i, m: lax.rem(m[0] * steps + i, parts * steps)
    return pl.pallas_call(
        functools.partial(project_kernel, parts, steps),
        out_shape=jax.ShapeDtypeStruct((own * cols, naux), jnp.float32),
        grid_spec=pltpu.PrefetchScalarGridSpec(
            num_scalar_prefetch=1,
            grid=(parts * steps,),
            in_specs=[pl.BlockSpec((tile, naux), lambda i, m: (around(i, m), 0))]
            + [pl.BlockSpec((own, tile, cols), stay(s, steps)) for s in range(parts)],
            out_specs=pl.BlockSpec((own * cols, naux), lambda i, m: (0, 0)),
        ),
        compiler_params=pltpu.CompilerParams(vmem_limit_bytes=40 << 20),
        cost_estimate=pl.CostEstimate(
            flops=2 * own * parts * quarter * cols * naux,
            bytes_accessed=8 * own * parts * quarter * cols,
            transcendentals=0,
        ),
    )(me.reshape(1), factors, *pieces)


def again_kernel(own, l_ref, wt_ref, p_ref, x_ref, o_ref):
    cols = p_ref.shape[0] // own

    @pl.when(pl.program_id(0) == 0)
    def _():
        o_ref[...] = x_ref[...]

    for f in range(own):
        rows = slice(f * cols, (f + 1) * cols)
        wide = lax.dot_general(
            p_ref[rows, :], l_ref[...], (((1,), (1,)), ((), ())), preferred_element_type=jnp.float32
        )
        wide = (wide * wt_ref[f : f + 1, :]).astype(jnp.bfloat16)
        o_ref[rows, :] += lax.dot_general(
            wide, l_ref[...], (((1,), (0,)), ((), ())), preferred_element_type=jnp.float32
        )


def again(factors, pair_weight, projected, kept):
    pairs, naux = factors.shape
    own = pair_weight.shape[0]
    tile = tile_of(pairs)
    return pl.pallas_call(
        functools.partial(again_kernel, own),
        out_shape=jax.ShapeDtypeStruct(kept.shape, jnp.float32),
        grid=(pairs // tile,),
        in_specs=[
            pl.BlockSpec((tile, naux), lambda i: (i, 0)),
            pl.BlockSpec((own, tile), lambda i: (0, i)),
            resident(projected),
            resident(kept),
        ],
        out_specs=pl.BlockSpec(kept.shape, lambda i: (0, 0)),
        compiler_params=pltpu.CompilerParams(vmem_limit_bytes=40 << 20),
        cost_estimate=pl.CostEstimate(
            flops=4 * kept.size * pairs, bytes_accessed=2 * factors.size, transcendentals=0
        ),
    )(factors, pair_weight, projected, kept)


def final_kernel(nf, parts, steps, me_ref, l_ref, k_ref, wt_ref, coef_ref, p_ref, *rest):
    s_refs, rest = rest[:parts], rest[parts:]
    b_refs, (a_ref, new_ref, table, held, mid, second) = rest[:parts], rest[parts:]
    own, _, cols = a_ref.shape
    table[...] = dot_exact(coef_ref[...], k_ref[...])
    for w in range(own):
        rows = slice(w * nf, (w + 1) * nf)
        table[rows, :] = table[rows, :] * wt_ref[...]
    spread(l_ref, p_ref, held)
    for lanes in blocks_of(table):

        @pl.loop(0, cols // WIDE)
        def _(i):
            rows = part(i, 0, WIDE)
            got = mix(table, lanes, own, nf, lambda v: held[part(i, v * cols, WIDE), lanes])
            for w in range(own):
                mid[w, rows, :] = got[w]
                second[w, rows, :] = (
                    wt_ref[w : w + 1, lanes] * held[part(i, w * cols, WIDE), lanes]
                )

        for s in range(parts):

            @pl.when(lax.div(pl.program_id(0), steps) == s)
            def _():
                for w in range(own):
                    new_ref[w, lanes, :] = b_refs[s][w, lanes, :] + mid[w].T
                    a_ref[w, lanes, :] = s_refs[s][w, lanes, :] + second[w].T


def final(me, factors, kernels, weights, coef, gathered, sources, base):
    own, quarter, cols = sources[0].shape
    parts = len(sources)
    nf = weights.shape[0]
    pairs, naux = factors.shape
    tile = tile_of(quarter)
    shape = jax.ShapeDtypeStruct((own, pairs, cols), jnp.float32)
    if tile is None:
        wide = jnp.einsum(
            "ja,pa->jp",
            gathered.reshape(nf * cols, naux),
            factors,
            preferred_element_type=jnp.float32,
        )
        wide = jnp.transpose(wide.reshape(nf, cols, pairs), (0, 2, 1)) * weights[:, :, None]
        table = jnp.einsum("jt,tp->jp", coef, kernels, precision=EXACT).reshape(own, nf, pairs)
        new = jnp.einsum("wvp,vpc->wpc", table, wide, precision=EXACT)
        amplitude = wide[:own]
        for s in range(parts):
            at = lax.rem(me + s, parts) * quarter
            put = lambda x, y: lax.dynamic_update_slice_in_dim(
                x, lax.dynamic_slice_in_dim(x, at, quarter, 1) + y, at, 1
            )
            amplitude, new = put(amplitude, sources[s]), put(new, base[s])
        return amplitude, new
    steps = quarter // tile
    around = lambda i, m: lax.rem(m[0] * steps + i, parts * steps)
    out = pl.BlockSpec((own, tile, cols), lambda i, m: (0, around(i, m), 0))
    pieces = [pl.BlockSpec((own, tile, cols), stay(s, steps)) for s in range(parts)]
    return pl.pallas_call(
        functools.partial(final_kernel, nf, parts, steps),
        out_shape=(shape, shape),
        grid_spec=pltpu.PrefetchScalarGridSpec(
            num_scalar_prefetch=1,
            grid=(parts * steps,),
            in_specs=[
                pl.BlockSpec((tile, naux), lambda i, m: (around(i, m), 0)),
                pl.BlockSpec((nf, tile), lambda i, m: (0, around(i, m))),
                pl.BlockSpec((nf, tile), lambda i, m: (0, around(i, m))),
                resident(coef),
                resident(gathered),
            ]
            + pieces
            + pieces,
            out_specs=(out, out),
            scratch_shapes=[
                VMEM((own * nf, tile), jnp.float32),
                VMEM((nf * cols, tile), jnp.float32),
            ]
            + [VMEM((own, cols, LANES), jnp.float32)] * 2,
        ),
        compiler_params=pltpu.CompilerParams(vmem_limit_bytes=56 << 20),
        cost_estimate=pl.CostEstimate(
            flops=2 * nf * pairs * cols * naux,
            bytes_accessed=16 * own * pairs * cols,
            transcendentals=0,
        ),
    )(me.reshape(1), factors, kernels, weights, coef, gathered, *sources, *base)


def sum_kernel(chips, parts, x_ref, o_ref, near, red, land, mine, joined, *sems):
    near_out, near_in, red_out, red_in, z_out, z_in, wide_out, wide_in, pair_out, pair_in, local = sems
    me = lax.axis_index("fac")
    level = lax.axis_index("freq")
    levels = lax.axis_size("freq")
    core = lax.rem(me, 2)
    chip = lax.div(me, 2)
    partner = me + 1 - 2 * core

    def on(d):
        return lax.rem(chip + d, chips)

    def at(d):
        return {"fac": on(d) * 2 + core}

    def up(s):
        return {"freq": lax.rem(level + s, levels)}

    pal = {"fac": partner}
    barrier = pltpu.get_barrier_semaphore()
    greeted = [pal] + [at(d) for d in range(1, chips)] + [up(s) for s in range(1, parts)]
    for other in greeted:
        pl.semaphore_signal(barrier, inc=1, device_id=other, device_id_type=MESH)
    pl.semaphore_wait(barrier, len(greeted))

    started = []

    def send(src, dst, out, came, to):
        copy = pltpu.make_async_remote_copy(
            src_ref=src,
            dst_ref=dst,
            send_sem=out,
            recv_sem=came,
            device_id=to,
            device_id_type=MESH,
        )
        copy.start()
        started.append(copy)
        return copy

    turns = list(range(1, chips)) + [0]
    nears = {}
    for d in turns:
        nears[d] = send(
            x_ref.at[on(d), 1 - core], near.at[d], near_out.at[d], near_in.at[d], pal
        )
    block = mine.shape[0]
    step = min(block, 16)
    reds = []
    for d in range(1, chips):
        nears[d].wait_recv()
        for r in range(0, block, step):
            rows = slice(r, r + step)
            red[d, rows, :] = (x_ref[on(d), core, rows, :] + near[d, rows, :]).astype(red.dtype)
        reds.append(send(red.at[d], land.at[d], red_out.at[d], red_in.at[d], at(d)))
    nears[0].wait_recv()
    for copy in reds:
        copy.wait_recv()
    for r in range(0, block, step):
        rows = slice(r, r + step)
        total = x_ref[chip, core, rows, :] + near[0, rows, :]
        for d in range(1, chips):
            total = total + land[d, rows, :].astype(jnp.float32)
        mine[rows, :] = total.astype(mine.dtype)
    keep = pltpu.make_async_copy(mine, joined.at[0, chip, core], local)
    keep.start()
    keep.wait()

    zs = [None]
    for s in range(1, parts):
        here = joined.at[0, chip, core]
        zs.append(send(here, joined.at[s, chip, core], z_out.at[s], z_in.at[s], up(s)))
    wides, pairs = [], []
    for s in range(parts):
        here = joined.at[s, chip, core]
        if s:
            zs[s].wait_recv()
        for d in range(1, chips):
            wides.append(
                (s, d, send(here, here, wide_out.at[s, d], wide_in.at[s, d], at(d)))
            )
        pairs.append(send(here, here, pair_out.at[s, 0], pair_in.at[s, 0], pal))
    for s, d, copy in wides:
        copy.wait_recv()
        here = joined.at[s, lax.rem(chip - d + chips, chips), core]
        pairs.append(send(here, here, pair_out.at[s, d], pair_in.at[s, d], pal))
    for copy in pairs:
        copy.wait_recv()
    for copy in started:
        copy.wait_send()
    for s in range(parts):
        for c in range(chips):
            o_ref[s, c] = joined[s, c]


def summed(x, parts):
    n = lax.axis_size("fac")
    chips = n // 2
    rows, width = x.shape
    block = rows // n
    flat = (chips, 2, block, width)
    dma = pltpu.SemaphoreType.DMA
    result = pl.pallas_call(
        functools.partial(sum_kernel, chips, parts),
        out_shape=jax.ShapeDtypeStruct((parts,) + flat, jnp.bfloat16),
        in_specs=[pl.BlockSpec(memory_space=VMEM)],
        out_specs=pl.BlockSpec(memory_space=VMEM),
        scratch_shapes=[
            VMEM((chips, block, width), jnp.float32),
            VMEM((chips, block, width), jnp.bfloat16),
            VMEM((chips, block, width), jnp.bfloat16),
            VMEM((block, width), jnp.bfloat16),
            VMEM((parts,) + flat, jnp.bfloat16),
            dma((chips,)),
            dma((chips,)),
            dma((chips,)),
            dma((chips,)),
            dma((parts,)),
            dma((parts,)),
            dma((parts, chips)),
            dma((parts, chips)),
            dma((parts, chips)),
            dma((parts, chips)),
            dma,
        ],
        compiler_params=pltpu.CompilerParams(
            collective_id=min(parts, 2) - 1, has_side_effects=True, vmem_limit_bytes=24 << 20
        ),
        cost_estimate=pl.CostEstimate(
            flops=40000 * x.size // 1000, bytes_accessed=40 * x.size, transcendentals=0
        ),
    )(x.reshape(flat))
    return result.reshape(parts, rows, width)


def shards(right_side, factors, pair_weight, second_order, forward, backward):
    own, pairs, cols = right_side.shape
    nf = forward.shape[0]
    naux = factors.shape[1]
    parts = nf // own
    quarter = pairs // parts
    me = lax.axis_index("freq")

    def shift(x, by):
        if by == 0:
            return x
        return lax.ppermute(x, "freq", [(i, (i + by) % parts) for i in range(parts)])

    def sliced(x, s):
        return lax.dynamic_slice_in_dim(x, lax.rem(me + s, parts) * quarter, quarter, 1)

    order = jnp.concatenate(
        [lax.rem(me - s + parts, parts) * own + jnp.arange(own) for s in range(parts)]
    )
    pick = jax.nn.one_hot(order, nf, dtype=jnp.float32)
    ahead = jnp.einsum("ts,sv,wv->tw", pick, forward, pick, precision=EXACT)
    back = jnp.einsum("ws,st,vt->wv", pick, backward, pick, precision=EXACT)
    coef = (back[:, None, :] * ahead.T[None, :, :]).reshape(nf * nf, nf)
    reach = jnp.max(
        jnp.sum(
            jnp.einsum("wt,tv->wv", jnp.abs(backward), jnp.abs(forward), precision=EXACT), axis=1
        )
    )

    both = jnp.stack([pair_weight, second_order])
    tables = jnp.concatenate([shift(both, s) for s in range(parts)], axis=1)
    weights, kernels = tables[0], tables[1]
    up = 8192.0
    moved = []
    for s in range(1, parts):
        out = (sliced(right_side, s) * up).astype(jnp.float16)
        moved.append(shift(out, s))

    def first_projection():
        return jnp.einsum(
            "pa,fpc->fca",
            factors,
            right_side.astype(jnp.bfloat16),
            preferred_element_type=jnp.float32,
        ).reshape(own * cols, naux)

    def ladder(kept):
        kept_now = kept
        for inner in range(INNER):
            last = inner == INNER - 1
            mine = summed(kept_now, parts if last else 1)
            if not last:
                kept_now = again(factors, pair_weight, mine[0], kept)
        return mine

    gathered = ladder(first_projection())
    moved = [m.astype(jnp.float32) * (1.0 / up) for m in moved]
    u, v = quarter_pass(me, factors, kernels, weights, coef, gathered, right_side, moved)
    height = jnp.max(jnp.sum(jnp.abs(gathered.astype(jnp.float32)), axis=2))
    u_top = jnp.maximum(1.01 * reach * (R_MAX + W_MAX * L_MAX * height), 1e-30)
    v_top = jnp.maximum(1.01 * reach * (R_MAX + u_top), 1e-30)

    def returned(blocks, top):
        result = [sliced(right_side, 0) + blocks[0]]
        for s in range(1, parts):
            block = (blocks[s] * (HALF_TOP / top)).astype(jnp.float16)
            block = shift(block, parts - s)
            result.append(sliced(right_side, s) + block.astype(jnp.float32) * (top / HALF_TOP))
        return result

    sources = returned(u, u_top)
    base = returned(v, v_top)
    gathered = ladder(project(me, factors, sources))
    return final(me, factors, kernels, weights, coef[: own * nf], gathered, sources, base)


def solution(mesh):
    return jax.shard_map(
        shards,
        mesh=mesh,
        in_specs=(
            P("freq", "fac", None),
            P("fac", None),
            P("freq", "fac"),
            P("freq", "fac"),
            P(),
            P(),
        ),
        out_specs=(P("freq", "fac", None), P("freq", "fac", None)),
        check_vma=False,
    )
```

profile of v0, /device:TPU:0, one launch (start us, length us, event | category | flops | bytes accessed | tf_op | source)
XLA Modules:
  0.0 585.5 jit_solution(874462414406996510)
XLA Ops:
  0.6 1.0 pad_maximum_fusion.1
  1.6 5.1 collective-permute-start.2
  6.7 0.0 collective-permute-start.1
  6.7 1.0 collective-permute-start
  7.7 5.3 multiply_convert_fusion.6
  13.1 2.8 collective-permute-start.5
  15.9 1.1 collective-permute-start.4
  17.0 0.2 convolution_reduce_fusion
  17.2 0.1 pad_add_fusion
  17.3 0.2 fusion.6
  17.5 0.2 fusion.8
  17.7 0.2 fusion.5
  17.9 0.2 fusion.7
  18.1 10.4 %fusion = f32[4,128,1024]{2,1,0:T(8,128)S(1)} fusion(bf16[4608,1024]{1,0:T(8,128)(2,1)} %l_ref.9, f32[4,4608,128]{2,1,0:T(8,128)} %rest_0_.1), kind=kOutput, calls=%fused_computation | convolution fusion | flops 4834197504 | bytes 20971520 | tf_op jit(solution)/shard_map/pa,fpc->fca/dot_general | solution.py:531
  28.5 0.0 copy-start.6
  28.5 20.1 %shard_map.77 = bf16[1,4,2,64,1024]{4,3,2,1,0:T(8,128)(2,1)S(1)} custom-call(f32[4,2,64,1024]{3,2,1,0:T(8,128)S(1)} %bitcast.26), custom_call_target="tpu_custom_call" | custom-call | flops 20971520 | bytes 20971520 | tf_op jit(solution)/shard_map/pallas_call | solution.py:459
  48.6 26.8 %shard_map.78 = f32[512,1024]{1,0:T(8,128)S(1)} custom-call(bf16[4608,1024]{1,0:T(8,128)(2,1)} %l_ref.9, f32[4,4608]{1,0:T(4,128)S(1)} %copy-done.6, bf16[512,1024]{1,0:T(8,128)(2,1)S(1)} %bitcast.32, f32[512,1024]{1,0:T(8,128)S(1)} %bitcast.27), custom_call_target="tpu_custom_call" | custom-call | flops 9663676416 | bytes 9437184 | tf_op jit(solution)/shard_map/pallas_call | solution.py:249
  75.5 43.3 %shard_map.79 = bf16[4,4,2,64,1024]{4,3,2,1,0:T(8,128)(2,1)S(1)} custom-call(f32[4,2,64,1024]{3,2,1,0:T(8,128)S(1)} %bitcast.30), custom_call_target="tpu_custom_call" | custom-call | flops 20971520 | bytes 20971520 | tf_op jit(solution)/shard_map/pallas_call | solution.py:459
  118.8 0.0 copy-start
  118.8 2.0 copy-done
  120.8 0.9 abs_reduce_fusion
  121.7 0.6 reduce_max.18
  122.3 0.6 reduce_max.19
  124.2 0.7 broadcast_multiply_fusion
  124.9 0.0 collective-permute-done.2
  124.9 0.0 collective-permute-start.3
  124.9 0.0 collective-permute-done.1
  124.9 0.0 collective-permute-done
  124.9 0.1 pad_maximum_fusion
  125.1 0.9 slice_bitcast_fusion
  125.9 0.0 collective-permute-done.5
  125.9 1.6 convert_multiply_fusion.rest_3_
  127.5 0.0 collective-permute-done.4
  127.5 1.6 convert_multiply_fusion.1.rest_2_
  129.2 28.8 %collective-permute-done.3 = f16[4,1152,128]{2,1,0:T(8,128)(2,1)S(1)} collective-permute-done((f16[4,1152,128]{2,1,0:T(8,128)(2,1)}, f16[4,1152,128]{2,1,0:T(8,128)(2,1)S(1)}, u32[]{:S(2)}, u32[]{:S(2)}) %collective-permute-start.3) | collective-permute-done | bytes 1179680 | tf_op jit(solution)/shard_map/ppermute | solution.py:503
  158.0 1.6 convert_multiply_fusion.2.rest_1_
  159.6 42.7 %shard_map.80 = (f32[4,1152,128]{2,1,0:T(8,128)}, f32[4,1152,128]{2,1,0:T(8,128)}, f32[4,1152,128]{2,1,0:T(8,128)}, f32[4,1152,128]{2,1,0:T(8,128)}, f32[4,1152,...) custom-call(s32[1]{0:T(128)} %bitcast.me_ref, ...), custom_call_target="tpu_custom_call" | custom-call | flops 7247757312 | bytes 37748736 | tf_op jit(solution)/shard_map/pallas_call | solution.py:132
  202.3 3.1 multiply_convert_fusion.5
  205.4 1.3 multiply_convert_fusion.4
  206.7 0.8 copy-done.11
  207.5 1.2 multiply_convert_fusion.1
  208.7 0.2 multiply_convert_fusion
  209.0 1.9 collective-permute-start.11
  210.9 2.1 collective-permute-start.10
  213.0 1.3 multiply_convert_fusion.3
  214.3 1.2 multiply_convert_fusion.2
  215.6 2.6 collective-permute-start.9
  218.2 0.0 collective-permute-start.8
  218.2 0.6 collective-permute-start.7
  218.8 21.2 %collective-permute-done.11 = f16[4,1152,128]{2,1,0:T(8,128)(2,1)} collective-permute-done((f16[4,1152,128]{2,1,0:T(8,128)(2,1)S(1)}, f16[4,1152,128]{2,1,0:T(8,128)(2,1)}, u32[]{:S(2)}, u32[]{:S(2)}) %collective-permute-start.11) | collective-permute-done | bytes 1179680 | tf_op jit(solution)/shard_map/ppermute | solution.py:503
  239.9 1.7 collective-permute-start.6
  241.6 1.4 slice.18
  243.0 47.6 %collective-permute-done.10 = f16[4,1152,128]{2,1,0:T(8,128)(2,1)} collective-permute-done((f16[4,1152,128]{2,1,0:T(8,128)(2,1)}, f16[4,1152,128]{2,1,0:T(8,128)(2,1)}, u32[]{:S(2)}, u32[]{:S(2)}) %collective-permute-start.10) | collective-permute-done | bytes 1179680 | tf_op jit(solution)/shard_map/ppermute | solution.py:503
  290.5 0.0 collective-permute-done.9
  290.5 25.3 %collective-permute-done.8 = f16[4,1152,128]{2,1,0:T(8,128)(2,1)} collective-permute-done((f16[4,1152,128]{2,1,0:T(8,128)(2,1)}, f16[4,1152,128]{2,1,0:T(8,128)(2,1)}, u32[]{:S(2)}, u32[]{:S(2)}) %collective-permute-start.8) | collective-permute-done | bytes 1179680 | tf_op jit(solution)/shard_map/ppermute | solution.py:503
  315.8 74.7 %collective-permute-done.7 = f16[4,1152,128]{2,1,0:T(8,128)(2,1)} collective-permute-done((f16[4,1152,128]{2,1,0:T(8,128)(2,1)}, f16[4,1152,128]{2,1,0:T(8,128)(2,1)}, u32[]{:S(2)}, u32[]{:S(2)}) %collective-permute-start.7) | collective-permute-done | bytes 1179680 | tf_op jit(solution)/shard_map/ppermute | solution.py:503
  390.5 0.0 collective-permute-done.6
  390.5 10.9 %multiply_add_fusion = (f32[4,1152,128]{2,1,0:T(8,128)}, f32[4,1152,128]{2,1,0:T(8,128)S(1)}, f32[4,1152,128]{2,1,0:T(8,128)}, f32[4,1152,128]{2,1,0:T(8,128)S(1...) fusion(f16[4,1152,128]{2,1,0:T(8,128)(2,1)} %collective-permute, ...), kind=kLoop, calls=%fused_computation.4 | loop fusion | flops 11796480 | bytes 40108056 | tf_op jit(solution)/shard_map/add | solution.py:559
  401.5 14.1 %shard_map.81.x_ref = f32[512,1024]{1,0:T(8,128)S(1)} custom-call(s32[1]{0:T(128)} %bitcast.me_ref, bf16[4608,1024]{1,0:T(8,128)(2,1)} %l_ref.9, f32[4,1152,128]{2,1,0:T(8,128)S(1)} %get-tuple-element.25.rest_0_, f32[4,1152,128]{2,1,0:T(8,128)S(1)} %get-tuple-element.19.rest_1_, f32[4,1152,128]{2,1,0:T(8,128)S(1)} %get-tuple-element.21.rest_2_, ...), custom_call_target="tpu_custom_call" | custom-call | flops 4831838208 | bytes 18874368 | tf_op jit(solution)/shard_map/pallas_call | solution.py:208
  415.7 20.4 %shard_map.82 = bf16[1,4,2,64,1024]{4,3,2,1,0:T(8,128)(2,1)S(1)} custom-call(f32[4,2,64,1024]{3,2,1,0:T(8,128)S(1)} %bitcast.28), custom_call_target="tpu_custom_call" | custom-call | flops 20971520 | bytes 20971520 | tf_op jit(solution)/shard_map/pallas_call | solution.py:459
  436.1 26.9 %shard_map.83 = f32[512,1024]{1,0:T(8,128)S(1)} custom-call(bf16[4608,1024]{1,0:T(8,128)(2,1)} %l_ref.9, f32[4,4608]{1,0:T(4,128)S(1)} %copy-done.6, bf16[512,1024]{1,0:T(8,128)(2,1)S(1)} %bitcast.33, f32[512,1024]{1,0:T(8,128)S(1)} %shard_map.81.x_ref), custom_call_target="tpu_custom_call" | custom-call | flops 9663676416 | bytes 9437184 | tf_op jit(solution)/shard_map/pallas_call | solution.py:249
  463.0 63.1 %shard_map.84 = bf16[4,4,2,64,1024]{4,3,2,1,0:T(8,128)(2,1)S(1)} custom-call(f32[4,2,64,1024]{3,2,1,0:T(8,128)S(1)} %bitcast.31), custom_call_target="tpu_custom_call" | custom-call | flops 20971520 | bytes 20971520 | tf_op jit(solution)/shard_map/pallas_call | solution.py:459
  526.0 1.9 copy-done.5
  528.0 57.3 %shard_map.85 = (f32[4,4608,128]{2,1,0:T(8,128)}, f32[4,4608,128]{2,1,0:T(8,128)}) custom-call(s32[1]{0:T(128)} %bitcast.me_ref, bf16[4608,1024]{1,0:T(8,128)(2,1)} %l_ref.9, f32[16,4608]{1,0:T(8,128)} %get-tuple-element.30.k_ref, f32[16,4608]{1,0:T(8,128)} %get-tuple-element.29.wt_ref, f32[64,16]{1,0:T(8,128)} %bitcast.39, bf16[4,512,1024]{2,1,0:T(8,128)(2,1)} %bitcast.29, ...), custom_call_target="tpu_custom_call" | custom-call | flops 19327352832 | bytes 37748736 | tf_op jit(solution)/shard_map/pallas_call | solution.py:326
  (29 shorter events, 0.1 us)
Async XLA Ops:
  1.6 123.3 %collective-permute-start.2 = (f32[2,4,4608]{2,1,0:T(4,128)S(1)}, f32[2,4,4608]{2,1,0:T(4,128)S(1)}, u32[]{:S(2)}, u32[]{:S(2)}) collective-permute-start(f32[2,4,4608]{2,1,0:T(4,128)S(1)} %pad_maximum_fusion.1), channel_id=1, source_target_pairs={{0,3},{1,0},{2,1},{3,2},{4,7},{5,4},{6,5},{7,6},{8,11},{9,8},{10,9... | collective-permute-start | bytes 442376 | tf_op jit(solution)/shard_map/ppermute | solution.py:503
  6.7 118.2 %collective-permute-start.1 = (f32[2,4,4608]{2,1,0:T(4,128)S(1)}, f32[2,4,4608]{2,1,0:T(4,128)S(1)}, u32[]{:S(2)}, u32[]{:S(2)}) collective-permute-start(f32[2,4,4608]{2,1,0:T(4,128)S(1)} %pad_maximum_fusion.1), channel_id=1, source_target_pairs={{0,2},{1,3},{2,0},{3,1},{4,6},{5,7},{6,4},{7,5},{8,10},{9,11},{10,... | collective-permute-start | bytes 442376 | tf_op jit(solution)/shard_map/ppermute | solution.py:503
  6.7 118.2 %collective-permute-start = (f32[2,4,4608]{2,1,0:T(4,128)S(1)}, f32[2,4,4608]{2,1,0:T(4,128)S(1)}, u32[]{:S(2)}, u32[]{:S(2)}) collective-permute-start(f32[2,4,4608]{2,1,0:T(4,128)S(1)} %pad_maximum_fusion.1), channel_id=1, source_target_pairs={{0,1},{1,2},{2,3},{3,0},{4,5},{5,6},{6,7},{7,4},{8,9},{9,10},{10,1... | collective-permute-start | bytes 442376 | tf_op jit(solution)/shard_map/ppermute | solution.py:503
  7.7 9.3 %copy-start.14 = (f32[16,16]{1,0:T(8,128)S(1)}, f32[16,16]{1,0:T(8,128)}, u32[]{:S(2)}) copy-start(f32[16,16]{1,0:T(8,128)} %param.10) | copy-start | bytes 3076
  7.7 9.3 %copy-start.15 = (f32[16,16]{1,0:T(8,128)S(1)}, f32[16,16]{1,0:T(8,128)}, u32[]{:S(2)}) copy-start(f32[16,16]{1,0:T(8,128)} %param.11) | copy-start | bytes 3076
  13.1 112.9 %collective-permute-start.5 = (f16[4,1152,128]{2,1,0:T(8,128)(2,1)}, f16[4,1152,128]{2,1,0:T(8,128)(2,1)S(1)}, u32[]{:S(2)}, u32[]{:S(2)}) collective-permute-start(f16[4,1152,128]{2,1,0:T(8,128)(2,1)} %get-tuple-element.26), channel_id=1, source_target_pairs={{0,3},{1,0},{2,1},{3,2},{4,7},{5,4},{6,5},{7,6},{8,11},{9,8},{10,9... | collective-permute-start | bytes 3538952 | tf_op jit(solution)/shard_map/ppermute | solution.py:503
  15.9 111.7 %collective-permute-start.4 = (f16[4,1152,128]{2,1,0:T(8,128)(2,1)}, f16[4,1152,128]{2,1,0:T(8,128)(2,1)S(1)}, u32[]{:S(2)}, u32[]{:S(2)}) collective-permute-start(f16[4,1152,128]{2,1,0:T(8,128)(2,1)} %get-tuple-element.27), channel_id=1, source_target_pairs={{0,2},{1,3},{2,0},{3,1},{4,6},{5,7},{6,4},{7,5},{8,10},{9,11},{10,... | collective-permute-start | bytes 3538952 | tf_op jit(solution)/shard_map/ppermute | solution.py:503
  28.5 20.1 %copy-start.6 = (f32[4,4608]{1,0:T(4,128)S(1)}, f32[4,4608]{1,0:T(4,128)}, u32[]{:S(2)}) copy-start(f32[4,4608]{1,0:T(4,128)} %wt_ref.3) | copy-start | bytes 221188
  118.8 2.0 copy-start
  120.8 4.1 copy-start.13
  124.9 33.1 %collective-permute-start.3 = (f16[4,1152,128]{2,1,0:T(8,128)(2,1)}, f16[4,1152,128]{2,1,0:T(8,128)(2,1)S(1)}, u32[]{:S(2)}, u32[]{:S(2)}) collective-permute-start(f16[4,1152,128]{2,1,0:T(8,128)(2,1)} %get-tuple-element.28), channel_id=1, source_target_pairs={{0,1},{1,2},{2,3},{3,0},{4,5},{5,6},{6,7},{7,4},{8,9},{9,10},{10,1... | collective-permute-start | bytes 3538952 | tf_op jit(solution)/shard_map/ppermute | solution.py:503
  202.3 3.1 copy-start.12
  205.4 2.1 copy-start.11
  206.7 2.1 copy-start.10
  208.7 4.2 copy-start.9
  209.0 5.3 copy-start.8
  209.0 30.9 %collective-permute-start.11 = (f16[4,1152,128]{2,1,0:T(8,128)(2,1)S(1)}, f16[4,1152,128]{2,1,0:T(8,128)(2,1)}, u32[]{:S(2)}, u32[]{:S(2)}) collective-permute-start(f16[4,1152,128]{2,1,0:T(8,128)(2,1)S(1)} %multiply_convert_fusion), channel_id=1, source_target_pairs={{0,1},{1,2},{2,3},{3,0},{4,5},{5,6},{6,7},{7,4},{8,9},{9,10},{10,1... | collective-permute-start | bytes 3538952 | tf_op jit(solution)/shard_map/ppermute | solution.py:503
  210.9 79.7 %collective-permute-start.10 = (f16[4,1152,128]{2,1,0:T(8,128)(2,1)}, f16[4,1152,128]{2,1,0:T(8,128)(2,1)}, u32[]{:S(2)}, u32[]{:S(2)}) collective-permute-start(f16[4,1152,128]{2,1,0:T(8,128)(2,1)} %multiply_convert_fusion.1), channel_id=1, source_target_pairs={{0,2},{1,3},{2,0},{3,1},{4,6},{5,7},{6,4},{7,5},{8,10},{9,11},{10,... | collective-permute-start | bytes 3538952 | tf_op jit(solution)/shard_map/ppermute | solution.py:503
  214.3 176.2 %copy-start.7 = (f32[4,1152,128]{2,1,0:T(8,128)S(1)}, f32[4,1152,128]{2,1,0:T(8,128)}, u32[]{:S(2)}) copy-start(f32[4,1152,128]{2,1,0:T(8,128)} %get-tuple-element.10) | copy-start | bytes 7077892
  215.6 75.0 %collective-permute-start.9 = (f16[4,1152,128]{2,1,0:T(8,128)(2,1)}, f16[4,1152,128]{2,1,0:T(8,128)(2,1)}, u32[]{:S(2)}, u32[]{:S(2)}) collective-permute-start(f16[4,1152,128]{2,1,0:T(8,128)(2,1)} %multiply_convert_fusion.2), channel_id=1, source_target_pairs={{0,3},{1,0},{2,1},{3,2},{4,7},{5,4},{6,5},{7,6},{8,11},{9,8},{10,9... | collective-permute-start | bytes 3538952 | tf_op jit(solution)/shard_map/ppermute | solution.py:503
  218.2 97.6 %collective-permute-start.8 = (f16[4,1152,128]{2,1,0:T(8,128)(2,1)}, f16[4,1152,128]{2,1,0:T(8,128)(2,1)}, u32[]{:S(2)}, u32[]{:S(2)}) collective-permute-start(f16[4,1152,128]{2,1,0:T(8,128)(2,1)} %multiply_convert_fusion.3), channel_id=1, source_target_pairs={{0,1},{1,2},{2,3},{3,0},{4,5},{5,6},{6,7},{7,4},{8,9},{9,10},{10,1... | collective-permute-start | bytes 3538952 | tf_op jit(solution)/shard_map/ppermute | solution.py:503
  218.2 172.3 %collective-permute-start.7 = (f16[4,1152,128]{2,1,0:T(8,128)(2,1)}, f16[4,1152,128]{2,1,0:T(8,128)(2,1)}, u32[]{:S(2)}, u32[]{:S(2)}) collective-permute-start(f16[4,1152,128]{2,1,0:T(8,128)(2,1)} %multiply_convert_fusion.4), channel_id=1, source_target_pairs={{0,2},{1,3},{2,0},{3,1},{4,6},{5,7},{6,4},{7,5},{8,10},{9,11},{10,... | collective-permute-start | bytes 3538952 | tf_op jit(solution)/shard_map/ppermute | solution.py:503
  239.9 150.6 %collective-permute-start.6 = (f16[4,1152,128]{2,1,0:T(8,128)(2,1)}, f16[4,1152,128]{2,1,0:T(8,128)(2,1)}, u32[]{:S(2)}, u32[]{:S(2)}) collective-permute-start(f16[4,1152,128]{2,1,0:T(8,128)(2,1)} %multiply_convert_fusion.5), channel_id=1, source_target_pairs={{0,3},{1,0},{2,1},{3,2},{4,7},{5,4},{6,5},{7,6},{8,11},{9,8},{10,9... | collective-permute-start | bytes 3538952 | tf_op jit(solution)/shard_map/ppermute | solution.py:503
  401.5 14.1 %copy-start.1 = (f32[4,1152,128]{2,1,0:T(8,128)}, f32[4,1152,128]{2,1,0:T(8,128)S(1)}, u32[]{:S(2)}) copy-start(f32[4,1152,128]{2,1,0:T(8,128)S(1)} %get-tuple-element.19.rest_1_) | copy-start | bytes 7077892
  401.5 14.1 %copy-start.2 = (f32[4,1152,128]{2,1,0:T(8,128)}, f32[4,1152,128]{2,1,0:T(8,128)S(1)}, u32[]{:S(2)}) copy-start(f32[4,1152,128]{2,1,0:T(8,128)S(1)} %get-tuple-element.21.rest_2_) | copy-start | bytes 7077892
  401.5 14.1 %copy-start.3 = (f32[4,1152,128]{2,1,0:T(8,128)}, f32[4,1152,128]{2,1,0:T(8,128)S(1)}, u32[]{:S(2)}) copy-start(f32[4,1152,128]{2,1,0:T(8,128)S(1)} %get-tuple-element.23.rest_3_) | copy-start | bytes 7077892
  401.5 14.1 %copy-start.4 = (f32[4,1152,128]{2,1,0:T(8,128)}, f32[4,1152,128]{2,1,0:T(8,128)S(1)}, u32[]{:S(2)}) copy-start(f32[4,1152,128]{2,1,0:T(8,128)S(1)} %get-tuple-element.25.rest_0_) | copy-start | bytes 7077892
  526.0 1.9 copy-start.5
where the time goes:
time: 586 us; the launch traced here: 585 us
  Pallas kernels  315 us (54%)
  waiting for transfers between devices  198 us (34%)
  other arithmetic  33.4 us (6%)
  starting transfers between devices  18.9 us (3%)
  matrix products  11.4 us (2%)
  local copies, waits for them, and re-layouts  7.03 us (1%)
    ppermute x12, waiting for transfers between devices, shift(): lax.ppermute(x, 'freq', [(i, (i + by) % parts) for i in range(parts)])  198 us
    pallas_call x4, Pallas kernels, summed(): pl.pallas_call(functools.partial(sum_kernel, chips, parts), out_shape=jax...  147 us
    pallas_call x1, Pallas kernels, final(): pl.pallas_call(functools.partial(final_kernel, nf, parts, steps), out_sha...  57.3 us
    pallas_call x2, Pallas kernels, again(): pl.pallas_call(functools.partial(again_kernel, own), out_shape=jax.ShapeD...  53.7 us
    pallas_call x1, Pallas kernels, quarter_pass(): pl.pallas_call(functools.partial(quarter_kernel, nf, parts), out_shape=[s...  42.7 us
    ppermute x12, starting transfers between devices, shift(): lax.ppermute(x, 'freq', [(i, (i + by) % parts) for i in range(parts)])  18.9 us
    pallas_call x1, Pallas kernels, project(): pl.pallas_call(functools.partial(project_kernel, parts, steps), out_shape...  14.1 us
  transfers between devices with their start and end apart: 12, of which 5 were waited for; matrix products, arithmetic and copies ran while one was open for 5% of the time, Pallas kernels for 15%

commit v1 on v0

--- a/solution.py
+++ b/solution.py
@@ -47,11 +47,12 @@
 
 
 def spread(l_ref, p_ref, held):
-    block = p_ref.shape[1]
-    for s in range(p_ref.shape[0]):
-        held[s * block : (s + 1) * block, :] = lax.dot_general(
-            p_ref[s], l_ref[...], (((1,), (1,)), ((), ())), preferred_element_type=jnp.float32
-        )
+    held[...] = lax.dot_general(
+        p_ref[...].reshape(held.shape[0], l_ref.shape[1]),
+        l_ref[...],
+        (((1,), (1,)), ((), ())),
+        preferred_element_type=jnp.float32,
+    )
 
 
 def dot_exact(a, b):
@@ -163,7 +164,7 @@
 
 def project_kernel(parts, steps, me_ref, l_ref, *rest):
     s_refs, (o_ref,) = rest[:parts], rest[parts:]
-    own, _, cols = s_refs[0].shape
+    own, _, _ = s_refs[0].shape
     i = pl.program_id(0)
 
     @pl.when(i == 0)
@@ -174,14 +175,13 @@
 
         @pl.when(lax.div(i, steps) == s)
         def _():
-            for f in range(own):
-                rows = slice(f * cols, (f + 1) * cols)
-                o_ref[rows, :] += lax.dot_general(
-                    s_refs[s][f].astype(jnp.bfloat16),
-                    l_ref[...],
-                    (((0,), (0,)), ((), ())),
-                    preferred_element_type=jnp.float32,
-                )
+            rounded = [s_refs[s][f].astype(jnp.bfloat16) for f in range(own)]
+            o_ref[...] += lax.dot_general(
+                jnp.concatenate(rounded, axis=1),
+                l_ref[...],
+                (((0,), (0,)), ((), ())),
+                preferred_element_type=jnp.float32,
+            )
 
 
 def stay(s, steps):
@@ -231,15 +231,19 @@
     def _():
         o_ref[...] = x_ref[...]
 
-    for f in range(own):
-        rows = slice(f * cols, (f + 1) * cols)
-        wide = lax.dot_general(
-            p_ref[rows, :], l_ref[...], (((1,), (1,)), ((), ())), preferred_element_type=jnp.float32
-        )
-        wide = (wide * wt_ref[f : f + 1, :]).astype(jnp.bfloat16)
-        o_ref[rows, :] += lax.dot_general(
-            wide, l_ref[...], (((1,), (0,)), ((), ())), preferred_element_type=jnp.float32
-        )
+    wide = lax.dot_general(
+        p_ref[...], l_ref[...], (((1,), (1,)), ((), ())), preferred_element_type=jnp.float32
+    )
+    wide = [
+        (wide[f * cols : (f + 1) * cols] * wt_ref[f : f + 1, :]).astype(jnp.bfloat16)
+        for f in range(own)
+    ]
+    o_ref[...] += lax.dot_general(
+        jnp.concatenate(wide, axis=0),
+        l_ref[...],
+        (((1,), (0,)), ((), ())),
+        preferred_element_type=jnp.float32,
+    )
 
 
 def again(factors, pair_weight, projected, kept):
@@ -551,17 +555,22 @@
     u_top = jnp.maximum(1.01 * reach * (R_MAX + W_MAX * L_MAX * height), 1e-30)
     v_top = jnp.maximum(1.01 * reach * (R_MAX + u_top), 1e-30)
 
-    def returned(blocks, top):
-        result = [sliced(right_side, 0) + blocks[0]]
-        for s in range(1, parts):
-            block = (blocks[s] * (HALF_TOP / top)).astype(jnp.float16)
-            block = shift(block, parts - s)
-            result.append(sliced(right_side, s) + block.astype(jnp.float32) * (top / HALF_TOP))
-        return result
-
-    sources = returned(u, u_top)
-    base = returned(v, v_top)
+    def halved(blocks, top):
+        return [(b * (HALF_TOP / top)).astype(jnp.float16) for b in blocks[1:]]
+
+    def returned(blocks):
+        return [shift(b, parts - 1 - s) for s, b in enumerate(blocks)]
+
+    def added(first, blocks, top):
+        rest = [b.astype(jnp.float32) * (top / HALF_TOP) for b in blocks]
+        return [sliced(right_side, s) + b for s, b in enumerate([first] + rest)]
+
+    sources = added(u[0], returned(halved(u, u_top)), u_top)
+    sent, sources = lax.optimization_barrier((halved(v, v_top), sources))
+    sent = returned(sent)
     gathered = ladder(project(me, factors, sources))
+    gathered, sent = lax.optimization_barrier((gathered, sent))
+    base = added(v[0], sent, v_top)
     return final(me, factors, kernels, weights, coef[: own * nf], gathered, sources, base)
 
 

time: 586 us -> 523 us (0.89)
  waiting for transfers between devices: 198 us -> 97.7 us
  starting transfers between devices: 18.9 us -> 45 us
  local copies, waits for them, and re-layouts: 7.03 us -> 13.2 us
    ppermute x12, waiting for transfers between devices: 198 us -> 97.7 us  [shift(): lax.ppermute(x, 'freq', [(i, (i + by) % parts) for i in range(parts)])]
    ppermute x12, starting transfers between devices: 18.9 us -> 45 us  [shift(): lax.ppermute(x, 'freq', [(i, (i + by) % parts) for i in range(parts)])]
    pallas_call x2, Pallas kernels: 53.7 us -> 33.5 us  [again(): pl.pallas_call(functools.partial(again_kernel, own), out_shape=jax.ShapeD...]
    pallas_call x4, Pallas kernels: 147 us -> 164 us  [summed(): pl.pallas_call(functools.partial(sum_kernel, chips, parts), out_shape=jax...]
    unnamed x32 -> x40, local copies, waits for them, and re-layouts: 4.8 us -> 11.6 us
    add x1 -> x2, other arithmetic: 10.9 us -> 17.3 us  [added(): return [sliced(right_side, s) + b for s, b in enumerate([first] + rest)]]
  transfers between devices with their start and end apart: 12 -> 12, of which waited for: 5 -> 3; matrix products, arithmetic and copies ran while one was open for 5% -> 5% of each run, Pallas kernels for 15% -> 41%
where the time goes in v1:
time: 523 us; the launch traced here: 518 us
  Pallas kernels  311 us (59%)
  waiting for transfers between devices  97.7 us (19%)
  starting transfers between devices  45 us (9%)
  other arithmetic  37.3 us (7%)
  local copies, waits for them, and re-layouts  13.2 us (3%)
  matrix products  11.4 us (2%)
    pallas_call x4, Pallas kernels, summed(): pl.pallas_call(functools.partial(sum_kernel, chips, parts), out_shape=jax...  164 us
    ppermute x12, waiting for transfers between devices, shift(): lax.ppermute(x, 'freq', [(i, (i + by) % parts) for i in range(parts)])  97.7 us
    pallas_call x1, Pallas kernels, final(): pl.pallas_call(functools.partial(final_kernel, nf, parts, steps), out_sha...  57.5 us
    ppermute x12, starting transfers between devices, shift(): lax.ppermute(x, 'freq', [(i, (i + by) % parts) for i in range(parts)])  45 us
    pallas_call x1, Pallas kernels, quarter_pass(): pl.pallas_call(functools.partial(quarter_kernel, nf, parts), out_shape=[s...  42.8 us
    pallas_call x2, Pallas kernels, again(): pl.pallas_call(functools.partial(again_kernel, own), out_shape=jax.ShapeD...  33.5 us
    add x2, other arithmetic, added(): return [sliced(right_side, s) + b for s, b in enumerate([first] + rest)]  17.3 us
    pallas_call x1, Pallas kernels, project(): pl.pallas_call(functools.partial(project_kernel, parts, steps), out_shape...  12.8 us
  transfers between devices with their start and end apart: 12, of which 3 were waited for; matrix products, arithmetic and copies ran while one was open for 5% of the time, Pallas kernels for 41%

profile of v1, /device:TPU:0, one launch (start us, length us, event | category | flops | bytes accessed | tf_op | source)
XLA Modules:
  0.0 517.8 jit_solution(6732002991984232667)
XLA Ops:
  0.6 1.0 pad_maximum_fusion.1
  1.6 5.1 collective-permute-start.2
  6.7 1.0 collective-permute-start
  7.7 5.2 %multiply_convert_fusion.6 = (f16[4,1152,128]{2,1,0:T(8,128)(2,1)}, f16[4,1152,128]{2,1,0:T(8,128)(2,1)}, f16[4,1152,128]{2,1,0:T(8,128)(2,1)}) fusion(f32[4,4608,128]{2,1,0:T(8,128)} %rest_0_.1, s32[]{:T(128)S(6)} %select_n.10, s32[]{:T(128)S(6)} %select_n.9, s32[]{:T(128)S(6)} %select_n.8), kind=kLoop, calls=%fused_computation.17 | loop fusion | flops 3538944 | bytes 10616844 | tf_op jit(solution)/shard_map/convert_element_type | solution.py:531
  13.0 2.8 collective-permute-start.5
  15.8 1.1 collective-permute-start.4
  16.9 0.2 convolution_reduce_fusion
  17.2 0.1 pad_add_fusion
  17.2 0.2 fusion.6
  17.4 0.2 fusion.8
  17.6 10.4 %fusion = f32[4,128,1024]{2,1,0:T(8,128)S(1)} fusion(bf16[4608,1024]{1,0:T(8,128)(2,1)} %l_ref.9, f32[4,4608,128]{2,1,0:T(8,128)} %rest_0_.1), kind=kOutput, calls=%fused_computation | convolution fusion | flops 4834197504 | bytes 20971520 | tf_op jit(solution)/shard_map/pa,fpc->fca/dot_general | solution.py:535
  28.0 0.0 copy-start.6
  28.1 20.1 %shard_map.77 = bf16[1,4,2,64,1024]{4,3,2,1,0:T(8,128)(2,1)S(1)} custom-call(f32[4,2,64,1024]{3,2,1,0:T(8,128)S(1)} %bitcast.26), custom_call_target="tpu_custom_call" | custom-call | flops 20971520 | bytes 20971520 | tf_op jit(solution)/shard_map/pallas_call | solution.py:463
  48.2 16.8 %shard_map.78 = f32[512,1024]{1,0:T(8,128)S(1)} custom-call(bf16[4608,1024]{1,0:T(8,128)(2,1)} %l_ref.9, f32[4,4608]{1,0:T(4,128)S(1)} %copy-done.6, bf16[512,1024]{1,0:T(8,128)(2,1)S(1)} %bitcast.32, f32[512,1024]{1,0:T(8,128)S(1)} %bitcast.27), custom_call_target="tpu_custom_call" | custom-call | flops 9663676416 | bytes 9437184 | tf_op jit(solution)/shard_map/pallas_call | solution.py:253
  64.9 53.9 %shard_map.79 = bf16[4,4,2,64,1024]{4,3,2,1,0:T(8,128)(2,1)S(1)} custom-call(f32[4,2,64,1024]{3,2,1,0:T(8,128)S(1)} %bitcast.30), custom_call_target="tpu_custom_call" | custom-call | flops 20971520 | bytes 20971520 | tf_op jit(solution)/shard_map/pallas_call | solution.py:463
  118.8 0.0 copy-start
  118.8 2.0 copy-done
  120.8 0.9 abs_reduce_fusion
  121.7 0.6 reduce_max.18
  122.3 0.7 reduce_max.19
  124.3 0.2 fusion.5
  124.5 0.2 fusion.7
  124.8 0.7 slice.18
  125.4 0.0 collective-permute-done.2
  125.4 0.0 collective-permute-start.3
  125.4 0.0 collective-permute-done.1
  125.4 0.1 pad_maximum_fusion
  125.6 0.9 slice_bitcast_fusion
  126.5 0.0 collective-permute-done.5
  126.5 1.7 convert_multiply_fusion.rest_3_
  128.1 0.0 collective-permute-done.4
  128.1 1.7 convert_multiply_fusion.1.rest_2_
  129.9 28.6 %collective-permute-done.3 = f16[4,1152,128]{2,1,0:T(8,128)(2,1)S(1)} collective-permute-done((f16[4,1152,128]{2,1,0:T(8,128)(2,1)}, f16[4,1152,128]{2,1,0:T(8,128)(2,1)S(1)}, u32[]{:S(2)}, u32[]{:S(2)}) %collective-permute-start.3) | collective-permute-done | bytes 1179680 | tf_op jit(solution)/shard_map/ppermute | solution.py:507
  158.5 1.6 convert_multiply_fusion.2.rest_1_
  160.1 42.8 %shard_map.80 = (f32[4,1152,128]{2,1,0:T(8,128)}, f32[4,1152,128]{2,1,0:T(8,128)}, f32[4,1152,128]{2,1,0:T(8,128)}, f32[4,1152,128]{2,1,0:T(8,128)}, f32[4,1152,...) custom-call(s32[1]{0:T(128)} %bitcast.me_ref, ...), custom_call_target="tpu_custom_call" | custom-call | flops 7247757312 | bytes 37748736 | tf_op jit(solution)/shard_map/pallas_call | solution.py:133
  203.0 2.0 multiply_convert_fusion.2
  205.0 0.3 copy-done.11
  205.3 0.2 multiply_convert_fusion.1
  205.6 1.2 copy-done.10
  206.7 0.2 multiply_convert_fusion
  207.0 1.9 collective-permute-start.8
  208.9 2.1 collective-permute-start.7
  211.0 2.6 collective-permute-start.6
  213.6 1.2 multiply_convert_fusion.5
  214.9 1.3 multiply_convert_fusion.4
  216.2 0.8 copy-done.7
  217.0 1.3 multiply_convert_fusion.3
  218.2 19.6 %collective-permute-done.8 = f16[4,1152,128]{2,1,0:T(8,128)(2,1)S(1)} collective-permute-done((f16[4,1152,128]{2,1,0:T(8,128)(2,1)S(1)}, f16[4,1152,128]{2,1,0:T(8,128)(2,1)S(1)}, u32[]{:S(2)}, u32[]{:S(2)}) %collective-permute-start.8) | collective-permute-done | bytes 1179680 | tf_op jit(solution)/shard_map/ppermute | solution.py:507
  237.8 49.4 %collective-permute-done.7 = f16[4,1152,128]{2,1,0:T(8,128)(2,1)S(1)} collective-permute-done((f16[4,1152,128]{2,1,0:T(8,128)(2,1)S(1)}, f16[4,1152,128]{2,1,0:T(8,128)(2,1)S(1)}, u32[]{:S(2)}, u32[]{:S(2)}) %collective-permute-start.7) | collective-permute-done | bytes 1179680 | tf_op jit(solution)/shard_map/ppermute | solution.py:507
  287.3 0.0 collective-permute-done.6
  287.3 1.0 copy-done.14
  288.3 1.0 copy-done.15
  289.3 8.6 %multiply_add_fusion.3 = (f32[4,1152,128]{2,1,0:T(8,128)S(1)}, f32[4,1152,128]{2,1,0:T(8,128)S(1)}, f32[4,1152,128]{2,1,0:T(8,128)}, f32[4,1152,128]{2,1,0:T(8,128)}) fusion(f16[4,1152,128]{2,1,0:T(8,128)(2,1)} %copy-done.13, f32[4,4608,128]{2,1,0:T(8,128)} %rest_0_.1, s32[]{:T(128)S(6)} %select_n.10, f32[]{:T(128)S(6)} %div.10, ...), kind=kLoop, calls=%fused_computation.7 | loop fusion | flops 5898240 | bytes 24772628 | tf_op jit(solution)/shard_map/add | solution.py:566
  297.9 27.7 %collective-permute-start.9 = (f16[4,1152,128]{2,1,0:T(8,128)(2,1)}, f16[4,1152,128]{2,1,0:T(8,128)(2,1)}, u32[]{:S(2)}, u32[]{:S(2)}) collective-permute-start(f16[4,1152,128]{2,1,0:T(8,128)(2,1)} %multiply_convert_fusion.5), channel_id=1, source_target_pairs={{0,3},{1,0},{2,1},{3,2},{4,7},{5,4},{6,5},{7,6},{8,11},{9,8},{10,9... | collective-permute-start | bytes 3538952 | tf_op jit(solution)/shard_map/ppermute | solution.py:507
  325.6 0.6 collective-permute-start.11
  326.2 1.7 copy-done.3
  327.9 1.7 copy-done.4
  329.5 12.8 %shard_map.81.x_ref = f32[512,1024]{1,0:T(8,128)S(1)} custom-call(s32[1]{0:T(128)} %bitcast.me_ref, bf16[4608,1024]{1,0:T(8,128)(2,1)} %l_ref.9, f32[4,1152,128]{2,1,0:T(8,128)S(1)} %copy-done.4, f32[4,1152,128]{2,1,0:T(8,128)S(1)} %get-tuple-element.29.rest_1_, f32[4,1152,128]{2,1,0:T(8,128)S(1)} %copy-done.3, f32[4,1152,128]{2,1,0:T(8,128)S(1)} %get-tuple-element.31.rest_3_), custom_call_target="tpu_custom_call" | custom-call | flops 4831838208 | bytes 18874368 | tf_op jit(solution)/shard_map/pallas_call | solution.py:208
  342.4 19.6 %shard_map.82 = bf16[1,4,2,64,1024]{4,3,2,1,0:T(8,128)(2,1)S(1)} custom-call(f32[4,2,64,1024]{3,2,1,0:T(8,128)S(1)} %bitcast.28), custom_call_target="tpu_custom_call" | custom-call | flops 20971520 | bytes 20971520 | tf_op jit(solution)/shard_map/pallas_call | solution.py:463
  362.0 16.8 %shard_map.83 = f32[512,1024]{1,0:T(8,128)S(1)} custom-call(bf16[4608,1024]{1,0:T(8,128)(2,1)} %l_ref.9, f32[4,4608]{1,0:T(4,128)S(1)} %copy-done.6, bf16[512,1024]{1,0:T(8,128)(2,1)S(1)} %bitcast.33, f32[512,1024]{1,0:T(8,128)S(1)} %shard_map.81.x_ref), custom_call_target="tpu_custom_call" | custom-call | flops 9663676416 | bytes 9437184 | tf_op jit(solution)/shard_map/pallas_call | solution.py:253
  378.8 70.7 %shard_map.84 = bf16[4,4,2,64,1024]{4,3,2,1,0:T(8,128)(2,1)S(1)} custom-call(f32[4,2,64,1024]{3,2,1,0:T(8,128)S(1)} %bitcast.31), custom_call_target="tpu_custom_call" | custom-call | flops 20971520 | bytes 20971520 | tf_op jit(solution)/shard_map/pallas_call | solution.py:463
  449.5 1.9 copy-done.5
  451.4 8.8 %multiply_add_fusion = (f32[4,1152,128]{2,1,0:T(8,128)}, f32[4,1152,128]{2,1,0:T(8,128)}, f32[4,1152,128]{2,1,0:T(8,128)}, f32[4,1152,128]{2,1,0:T(8,128)}) fusion(f16[4,1152,128]{2,1,0:T(8,128)(2,1)} %collective-permute-done.11, f32[4,4608,128]{2,1,0:T(8,128)} %rest_0_.1, s32[]{:T(128)S(6)} %select_n.10, f32[]{:T(128)S(6)} %div.11, ...), kind=kLoop, calls=%fused_computation.4 | loop fusion | flops 5898240 | bytes 24772628 | tf_op jit(solution)/shard_map/add | solution.py:566
  460.2 57.5 %shard_map.85 = (f32[4,4608,128]{2,1,0:T(8,128)}, f32[4,4608,128]{2,1,0:T(8,128)}) custom-call(s32[1]{0:T(128)} %bitcast.me_ref, bf16[4608,1024]{1,0:T(8,128)(2,1)} %l_ref.9, f32[16,4608]{1,0:T(8,128)} %get-tuple-element.52.k_ref, f32[16,4608]{1,0:T(8,128)} %get-tuple-element.51.wt_ref, f32[64,16]{1,0:T(8,128)} %bitcast.39, bf16[4,512,1024]{2,1,0:T(8,128)(2,1)} %bitcast.29, ...), custom_call_target="tpu_custom_call" | custom-call | flops 19327352832 | bytes 37748736 | tf_op jit(solution)/shard_map/pallas_call | solution.py:330
  (38 shorter events, 0.1 us)
Async XLA Ops:
  1.6 123.8 %collective-permute-start.2 = (f32[2,4,4608]{2,1,0:T(4,128)S(1)}, f32[2,4,4608]{2,1,0:T(4,128)S(1)}, u32[]{:S(2)}, u32[]{:S(2)}) collective-permute-start(f32[2,4,4608]{2,1,0:T(4,128)S(1)} %pad_maximum_fusion.1), channel_id=1, source_target_pairs={{0,3},{1,0},{2,1},{3,2},{4,7},{5,4},{6,5},{7,6},{8,11},{9,8},{10,9... | collective-permute-start | bytes 442376 | tf_op jit(solution)/shard_map/ppermute | solution.py:507
  6.7 118.7 %collective-permute-start.1 = (f32[2,4,4608]{2,1,0:T(4,128)S(1)}, f32[2,4,4608]{2,1,0:T(4,128)S(1)}, u32[]{:S(2)}, u32[]{:S(2)}) collective-permute-start(f32[2,4,4608]{2,1,0:T(4,128)S(1)} %pad_maximum_fusion.1), channel_id=1, source_target_pairs={{0,2},{1,3},{2,0},{3,1},{4,6},{5,7},{6,4},{7,5},{8,10},{9,11},{10,... | collective-permute-start | bytes 442376 | tf_op jit(solution)/shard_map/ppermute | solution.py:507
  6.7 118.7 %collective-permute-start = (f32[2,4,4608]{2,1,0:T(4,128)S(1)}, f32[2,4,4608]{2,1,0:T(4,128)S(1)}, u32[]{:S(2)}, u32[]{:S(2)}) collective-permute-start(f32[2,4,4608]{2,1,0:T(4,128)S(1)} %pad_maximum_fusion.1), channel_id=1, source_target_pairs={{0,1},{1,2},{2,3},{3,0},{4,5},{5,6},{6,7},{7,4},{8,9},{9,10},{10,1... | collective-permute-start | bytes 442376 | tf_op jit(solution)/shard_map/ppermute | solution.py:507
  7.7 9.2 %copy-start.18 = (f32[16,16]{1,0:T(8,128)S(1)}, f32[16,16]{1,0:T(8,128)}, u32[]{:S(2)}) copy-start(f32[16,16]{1,0:T(8,128)} %param.10) | copy-start | bytes 3076
  7.7 9.2 %copy-start.19 = (f32[16,16]{1,0:T(8,128)S(1)}, f32[16,16]{1,0:T(8,128)}, u32[]{:S(2)}) copy-start(f32[16,16]{1,0:T(8,128)} %param.11) | copy-start | bytes 3076
  13.0 113.5 %collective-permute-start.5 = (f16[4,1152,128]{2,1,0:T(8,128)(2,1)}, f16[4,1152,128]{2,1,0:T(8,128)(2,1)S(1)}, u32[]{:S(2)}, u32[]{:S(2)}) collective-permute-start(f16[4,1152,128]{2,1,0:T(8,128)(2,1)} %get-tuple-element.48), channel_id=1, source_target_pairs={{0,3},{1,0},{2,1},{3,2},{4,7},{5,4},{6,5},{7,6},{8,11},{9,8},{10,9... | collective-permute-start | bytes 3538952 | tf_op jit(solution)/shard_map/ppermute | solution.py:507
  15.8 112.3 %collective-permute-start.4 = (f16[4,1152,128]{2,1,0:T(8,128)(2,1)}, f16[4,1152,128]{2,1,0:T(8,128)(2,1)S(1)}, u32[]{:S(2)}, u32[]{:S(2)}) collective-permute-start(f16[4,1152,128]{2,1,0:T(8,128)(2,1)} %get-tuple-element.49), channel_id=1, source_target_pairs={{0,2},{1,3},{2,0},{3,1},{4,6},{5,7},{6,4},{7,5},{8,10},{9,11},{10,... | collective-permute-start | bytes 3538952 | tf_op jit(solution)/shard_map/ppermute | solution.py:507
  28.0 20.1 %copy-start.6 = (f32[4,4608]{1,0:T(4,128)S(1)}, f32[4,4608]{1,0:T(4,128)}, u32[]{:S(2)}) copy-start(f32[4,4608]{1,0:T(4,128)} %wt_ref.3) | copy-start | bytes 221188
  118.8 2.0 copy-start
  120.8 4.6 copy-start.17
  124.7 3.4 copy-start.16
  125.4 33.1 %collective-permute-start.3 = (f16[4,1152,128]{2,1,0:T(8,128)(2,1)}, f16[4,1152,128]{2,1,0:T(8,128)(2,1)S(1)}, u32[]{:S(2)}, u32[]{:S(2)}) collective-permute-start(f16[4,1152,128]{2,1,0:T(8,128)(2,1)} %get-tuple-element.50), channel_id=1, source_target_pairs={{0,1},{1,2},{2,3},{3,0},{4,5},{5,6},{6,7},{7,4},{8,9},{9,10},{10,1... | collective-permute-start | bytes 3538952 | tf_op jit(solution)/shard_map/ppermute | solution.py:507
  202.9 2.4 copy-start.11
  205.0 1.7 copy-start.10
  205.6 8.1 %copy-start.9 = (f32[4,1152,128]{2,1,0:T(8,128)S(1)}, f32[4,1152,128]{2,1,0:T(8,128)}, u32[]{:S(2)}) copy-start(f32[4,1152,128]{2,1,0:T(8,128)} %get-tuple-element.21) | copy-start | bytes 7077892
  207.0 7.9 %copy-start.8 = (f32[4,1152,128]{2,1,0:T(8,128)S(1)}, f32[4,1152,128]{2,1,0:T(8,128)}, u32[]{:S(2)}) copy-start(f32[4,1152,128]{2,1,0:T(8,128)} %get-tuple-element.22) | copy-start | bytes 7077892
  207.0 30.8 %collective-permute-start.8 = (f16[4,1152,128]{2,1,0:T(8,128)(2,1)S(1)}, f16[4,1152,128]{2,1,0:T(8,128)(2,1)S(1)}, u32[]{:S(2)}, u32[]{:S(2)}) collective-permute-start(f16[4,1152,128]{2,1,0:T(8,128)(2,1)S(1)} %multiply_convert_fusion), channel_id=1, source_target_pairs={{0,1},{1,2},{2,3},{3,0},{4,5},{5,6},{6,7},{7,4},{8,9},{9,10},{10,1... | collective-permute-start | bytes 3538952 | tf_op jit(solution)/shard_map/ppermute | solution.py:507
  208.9 78.4 %collective-permute-start.7 = (f16[4,1152,128]{2,1,0:T(8,128)(2,1)S(1)}, f16[4,1152,128]{2,1,0:T(8,128)(2,1)S(1)}, u32[]{:S(2)}, u32[]{:S(2)}) collective-permute-start(f16[4,1152,128]{2,1,0:T(8,128)(2,1)S(1)} %multiply_convert_fusion.1), channel_id=1, source_target_pairs={{0,2},{1,3},{2,0},{3,1},{4,6},{5,7},{6,4},{7,5},{8,10},{9,11},{10,... | collective-permute-start | bytes 3538952 | tf_op jit(solution)/shard_map/ppermute | solution.py:507
  211.0 76.3 %collective-permute-start.6 = (f16[4,1152,128]{2,1,0:T(8,128)(2,1)S(1)}, f16[4,1152,128]{2,1,0:T(8,128)(2,1)S(1)}, u32[]{:S(2)}, u32[]{:S(2)}) collective-permute-start(f16[4,1152,128]{2,1,0:T(8,128)(2,1)S(1)} %multiply_convert_fusion.2), channel_id=1, source_target_pairs={{0,3},{1,0},{2,1},{3,2},{4,7},{5,4},{6,5},{7,6},{8,11},{9,8},{10,9... | collective-permute-start | bytes 3538952 | tf_op jit(solution)/shard_map/ppermute | solution.py:507
  214.9 2.1 copy-start.7
  237.8 49.4 %copy-start.13 = (f16[4,1152,128]{2,1,0:T(8,128)(2,1)}, f16[4,1152,128]{2,1,0:T(8,128)(2,1)S(1)}, u32[]{:S(2)}) copy-start(f16[4,1152,128]{2,1,0:T(8,128)(2,1)S(1)} %collective-permute-done.8) | copy-start | bytes 3538948
  287.3 1.0 copy-start.14
  288.3 1.0 copy-start.15
  297.9 44.5 %copy-start.1 = (f32[4,1152,128]{2,1,0:T(8,128)}, f32[4,1152,128]{2,1,0:T(8,128)S(1)}, u32[]{:S(2)}) copy-start(f32[4,1152,128]{2,1,0:T(8,128)S(1)} %get-tuple-element.31.rest_3_) | copy-start | bytes 7077892
  297.9 44.5 %copy-start.2 = (f32[4,1152,128]{2,1,0:T(8,128)}, f32[4,1152,128]{2,1,0:T(8,128)S(1)}, u32[]{:S(2)}) copy-start(f32[4,1152,128]{2,1,0:T(8,128)S(1)} %get-tuple-element.29.rest_1_) | copy-start | bytes 7077892
  297.9 153.5 %collective-permute-start.9 = (f16[4,1152,128]{2,1,0:T(8,128)(2,1)}, f16[4,1152,128]{2,1,0:T(8,128)(2,1)}, u32[]{:S(2)}, u32[]{:S(2)}) collective-permute-start(f16[4,1152,128]{2,1,0:T(8,128)(2,1)} %multiply_convert_fusion.5), channel_id=1, source_target_pairs={{0,3},{1,0},{2,1},{3,2},{4,7},{5,4},{6,5},{7,6},{8,11},{9,8},{10,9... | collective-permute-start | bytes 3538952 | tf_op jit(solution)/shard_map/ppermute | solution.py:507
  325.6 125.9 %collective-permute-start.10 = (f16[4,1152,128]{2,1,0:T(8,128)(2,1)}, f16[4,1152,128]{2,1,0:T(8,128)(2,1)}, u32[]{:S(2)}, u32[]{:S(2)}) collective-permute-start(f16[4,1152,128]{2,1,0:T(8,128)(2,1)} %multiply_convert_fusion.4), channel_id=1, source_target_pairs={{0,2},{1,3},{2,0},{3,1},{4,6},{5,7},{6,4},{7,5},{8,10},{9,11},{10,... | collective-permute-start | bytes 3538952 | tf_op jit(solution)/shard_map/ppermute | solution.py:507
  325.6 125.9 %collective-permute-start.11 = (f16[4,1152,128]{2,1,0:T(8,128)(2,1)}, f16[4,1152,128]{2,1,0:T(8,128)(2,1)}, u32[]{:S(2)}, u32[]{:S(2)}) collective-permute-start(f16[4,1152,128]{2,1,0:T(8,128)(2,1)} %multiply_convert_fusion.3), channel_id=1, source_target_pairs={{0,1},{1,2},{2,3},{3,0},{4,5},{5,6},{6,7},{7,4},{8,9},{9,10},{10,1... | collective-permute-start | bytes 3538952 | tf_op jit(solution)/shard_map/ppermute | solution.py:507
  326.2 1.7 copy-start.3
  327.9 1.7 copy-start.4
  378.8 72.7 %copy-start.12 = (f32[4,1152,128]{2,1,0:T(8,128)S(1)}, f32[4,1152,128]{2,1,0:T(8,128)}, u32[]{:S(2)}) copy-start(f32[4,1152,128]{2,1,0:T(8,128)} %get-tuple-element.36) | copy-start | bytes 7077892
  449.5 2.0 copy-start.5

commit v2 on v1

v2 whole, which is shorter than its diff:
```python
import functools

import jax
import jax.numpy as jnp
from jax import lax
from jax.experimental import pallas as pl
from jax.experimental.pallas import tpu as pltpu
from jax.sharding import PartitionSpec as P


INNER = 2
LANES = 128
MESH = pl.DeviceIdType.MESH
CHUNK = 16
WIDE = 32
EXACT = lax.Precision.HIGHEST
R_MAX = 6.0
W_MAX = 2.0
L_MAX = 0.03125
HALF_TOP = 32768.0
VMEM = pltpu.VMEM


def tile_of(pairs):
    for blocks in (3, 4, 2, 1):
        if pairs % (blocks * LANES) == 0:
            return blocks * LANES
    return None


def mix(table, lanes, outs, count, term):
    totals = [None] * outs
    for v in range(count):
        value = term(v)
        for w in range(outs):
            row = w * count + v
            product = table[row : row + 1, lanes] * value
            totals[w] = product if totals[w] is None else totals[w] + product
    return totals


def part(i, base, chunk):
    return pl.ds(pl.multiple_of(base + i * chunk, chunk), chunk)


def spread(l_ref, p_ref, held):
    held[...] = lax.dot_general(
        p_ref[...].reshape(held.shape[0], l_ref.shape[1]),
        l_ref[...],
        (((1,), (1,)), ((), ())),
        preferred_element_type=jnp.float32,
    )


def dot_exact(a, b):
    return lax.dot_general(
        a, b, (((1,), (0,)), ((), ())), precision=EXACT, preferred_element_type=jnp.float32
    )


def resident(x):
    return pl.BlockSpec(x.shape, lambda i, *_: (0,) * x.ndim, pipeline_mode=pl.Buffered(1))


def quarter_kernel(nf, parts, kept, me_ref, l_ref, k_ref, wt_ref, coef_ref, p_ref, *rest):
    r_refs, rest = rest[:parts], rest[parts + kept :]
    u_refs, rest = rest[:parts], rest[parts:]
    v_refs, (table, held, turned, mid, far) = rest[:parts], rest[parts:]
    own = nf // parts
    cols = r_refs[0].shape[2]
    table[...] = dot_exact(coef_ref[...], k_ref[...])
    spread(l_ref, p_ref, held)

    @pl.loop(0, table.shape[1] // LANES)
    def _(block):
        lanes = part(block, 0, LANES)
        for v in range(nf):
            turned[v] = r_refs[v // own][v % own, lanes, :].T

        @pl.loop(0, cols // CHUNK)
        def _(i):
            rows = part(i, 0, CHUNK)
            got = mix(
                table,
                lanes,
                nf,
                nf,
                lambda v: turned[v, rows, :]
                + wt_ref[v : v + 1, lanes] * held[part(i, v * cols, CHUNK), lanes],
            )
            for w in range(nf):
                mid[w, rows, :] = got[w]
                turned[w, rows, :] = turned[w, rows, :] + got[w]
            got = mix(table, lanes, nf, nf, lambda v: turned[v, rows, :])
            for w in range(nf):
                far[w, rows, :] = got[w]

        for w in range(nf):
            u_refs[w // own][w % own, lanes, :] = mid[w].T
            v_refs[w // own][w % own, lanes, :] = far[w].T


def quarter_pass(
    me, k, group, factors, kernels, weights, coef, gathered, right_side, moved, kept
):
    own, pairs, cols = right_side.shape
    nf = weights.shape[0]
    parts = nf // own
    quarter = pairs // parts
    naux = factors.shape[1]
    tile = tile_of(quarter)
    if tile is None:
        cut = lambda x, axis: lax.dynamic_slice_in_dim(x, me * quarter, quarter, axis)
        here = jnp.concatenate([cut(right_side, 1)] + moved)
        table = jnp.einsum("jt,tp->jp", coef, cut(kernels, 1), precision=EXACT)
        table = table.reshape(nf, nf, quarter)
        wide = jnp.einsum(
            "ja,pa->jp",
            gathered.reshape(nf * cols, naux),
            cut(factors, 0),
            preferred_element_type=jnp.float32,
        )
        wide = jnp.transpose(wide.reshape(nf, cols, quarter), (0, 2, 1))
        wide = here + cut(weights, 1)[:, :, None] * wide
        u = jnp.einsum("wvp,vpc->wpc", table, wide, precision=EXACT)
        v = jnp.einsum("wvp,vpc->wpc", table, here + u, precision=EXACT)
        return (
            [u[s * own : (s + 1) * own] for s in range(parts)],
            [v[s * own : (s + 1) * own] for s in range(parts)],
        )
    steps = quarter // tile
    at = lambda m: m[0] * steps + k
    came = pl.BlockSpec((own, tile, cols), lambda i, m: (0, k - group[0], 0))
    piece = pl.BlockSpec((own, tile, cols), lambda i, m: (0, 0, 0))
    shape = jax.ShapeDtypeStruct((own, tile, cols), jnp.float32)
    wide = jax.ShapeDtypeStruct((own, (group[1] - group[0]) * tile, cols), jnp.float32)
    out = pl.pallas_call(
        functools.partial(quarter_kernel, nf, parts, len(kept)),
        out_shape=[shape] * parts + [wide] * parts,
        grid_spec=pltpu.PrefetchScalarGridSpec(
            num_scalar_prefetch=1,
            grid=(1,),
            in_specs=[
                pl.BlockSpec((tile, naux), lambda i, m: (at(m), 0)),
                pl.BlockSpec((nf, tile), lambda i, m: (0, at(m))),
                pl.BlockSpec((nf, tile), lambda i, m: (0, at(m))),
                resident(coef),
                resident(gathered),
                pl.BlockSpec((own, tile, cols), lambda i, m: (0, at(m), 0)),
            ]
            + [came] * (parts - 1)
            + [pl.BlockSpec(memory_space=pl.ANY)] * len(kept),
            out_specs=[piece] * parts + [came] * parts,
            scratch_shapes=[
                VMEM((nf * nf, tile), jnp.float32),
                VMEM((nf * cols, tile), jnp.float32),
            ]
            + [VMEM((nf, cols, LANES), jnp.float32)] * 3,
        ),
        input_output_aliases={6 + parts + n: parts + n for n in range(len(kept))},
        compiler_params=pltpu.CompilerParams(vmem_limit_bytes=40 << 20),
        cost_estimate=pl.CostEstimate(
            flops=2 * nf * tile * cols * (naux + 32 * nf),
            bytes_accessed=16 * nf * tile * cols,
            transcendentals=0,
        ),
    )(me.reshape(1), factors, kernels, weights, coef, gathered, right_side, *moved, *kept)
    return list(out[:parts]), list(out[parts:])


def project_kernel(parts, me_ref, l_ref, *rest):
    s_refs, (x_ref, o_ref) = rest[:parts], rest[parts:]
    own, _, _ = s_refs[0].shape
    i = pl.program_id(0)

    @pl.when(i == 0)
    def _():
        o_ref[...] = x_ref[...]

    for s in range(parts):

        @pl.when(i == s)
        def _():
            rounded = [s_refs[s][f].astype(jnp.bfloat16) for f in range(own)]
            o_ref[...] += lax.dot_general(
                jnp.concatenate(rounded, axis=1),
                l_ref[...],
                (((0,), (0,)), ((), ())),
                preferred_element_type=jnp.float32,
            )


def around(parts, steps, k):
    return lambda i, m: lax.rem(m[0] + i, parts) * steps + k


def project(me, k, factors, pieces, total):
    own, size, cols = pieces[0].shape
    parts = len(pieces)
    pairs, naux = factors.shape
    quarter = pairs // parts
    if tile_of(quarter) is None:
        for s, x in enumerate(pieces):
            rows = lax.dynamic_slice_in_dim(
                factors, lax.rem(me + s, parts) * quarter, quarter, 0
            )
            total = total + jnp.einsum(
                "pa,fpc->fca", rows, x.astype(jnp.bfloat16), preferred_element_type=jnp.float32
            ).reshape(total.shape)
        return total
    at = around(parts, quarter // size, k)
    return pl.pallas_call(
        functools.partial(project_kernel, parts),
        out_shape=jax.ShapeDtypeStruct(total.shape, jnp.float32),
        grid_spec=pltpu.PrefetchScalarGridSpec(
            num_scalar_prefetch=1,
            grid=(parts,),
            in_specs=[pl.BlockSpec((size, naux), lambda i, m: (at(i, m), 0))]
            + [pl.BlockSpec((own, size, cols), lambda i, m: (0, 0, 0))] * parts
            + [resident(total)],
            out_specs=pl.BlockSpec(total.shape, lambda i, m: (0, 0)),
        ),
        compiler_params=pltpu.CompilerParams(vmem_limit_bytes=40 << 20),
        cost_estimate=pl.CostEstimate(
            flops=2 * own * parts * size * cols * naux,
            bytes_accessed=8 * own * parts * size * cols,
            transcendentals=0,
        ),
    )(me.reshape(1), factors, *pieces, total)


def again_kernel(own, l_ref, wt_ref, p_ref, x_ref, o_ref):
    cols = p_ref.shape[0] // own

    @pl.when(pl.program_id(0) == 0)
    def _():
        o_ref[...] = x_ref[...]

    wide = lax.dot_general(
        p_ref[...], l_ref[...], (((1,), (1,)), ((), ())), preferred_element_type=jnp.float32
    )
    wide = [
        (wide[f * cols : (f + 1) * cols] * wt_ref[f : f + 1, :]).astype(jnp.bfloat16)
        for f in range(own)
    ]
    o_ref[...] += lax.dot_general(
        jnp.concatenate(wide, axis=0),
        l_ref[...],
        (((1,), (0,)), ((), ())),
        preferred_element_type=jnp.float32,
    )


def again(factors, pair_weight, projected, kept):
    pairs, naux = factors.shape
    own = pair_weight.shape[0]
    tile = tile_of(pairs)
    return pl.pallas_call(
        functools.partial(again_kernel, own),
        out_shape=jax.ShapeDtypeStruct(kept.shape, jnp.float32),
        grid=(pairs // tile,),
        in_specs=[
            pl.BlockSpec((tile, naux), lambda i: (i, 0)),
            pl.BlockSpec((own, tile), lambda i: (0, i)),
            resident(projected),
            resident(kept),
        ],
        out_specs=pl.BlockSpec(kept.shape, lambda i: (0, 0)),
        compiler_params=pltpu.CompilerParams(vmem_limit_bytes=40 << 20),
        cost_estimate=pl.CostEstimate(
            flops=4 * kept.size * pairs, bytes_accessed=2 * factors.size, transcendentals=0
        ),
    )(factors, pair_weight, projected, kept)


def final_kernel(nf, parts, held_outs, me_ref, l_ref, k_ref, wt_ref, coef_ref, p_ref, *rest):
    s_refs, rest = rest[:parts], rest[parts:]
    b_refs, rest = rest[:parts], rest[parts + held_outs :]
    a_ref, new_ref, table, held, mid, second = rest
    own, _, cols = a_ref.shape
    table[...] = dot_exact(coef_ref[...], k_ref[...])
    for w in range(own):
        rows = slice(w * nf, (w + 1) * nf)
        table[rows, :] = table[rows, :] * wt_ref[...]
    spread(l_ref, p_ref, held)

    @pl.loop(0, table.shape[1] // LANES)
    def _(block):
        lanes = part(block, 0, LANES)

        @pl.loop(0, cols // WIDE)
        def _(i):
            rows = part(i, 0, WIDE)
            got = mix(table, lanes, own, nf, lambda v: held[part(i, v * cols, WIDE), lanes])
            for w in range(own):
                mid[w, rows, :] = got[w]
                second[w, rows, :] = (
                    wt_ref[w : w + 1, lanes] * held[part(i, w * cols, WIDE), lanes]
                )

        for s in range(parts):

            @pl.when(pl.program_id(0) == s)
            def _():
                for w in range(own):
                    new_ref[w, lanes, :] = b_refs[s][w, lanes, :] + mid[w].T
                    a_ref[w, lanes, :] = s_refs[s][w, lanes, :] + second[w].T


def final(me, k, factors, kernels, weights, coef, gathered, sources, base, outs):
    own, size, cols = sources[0].shape
    parts = len(sources)
    nf = weights.shape[0]
    pairs, naux = factors.shape
    quarter = pairs // parts
    tile = tile_of(quarter)
    shape = jax.ShapeDtypeStruct((own, pairs, cols), jnp.float32)
    if tile is None:
        wide = jnp.einsum(
            "ja,pa->jp",
            gathered.reshape(nf * cols, naux),
            factors,
            preferred_element_type=jnp.float32,
        )
        wide = jnp.transpose(wide.reshape(nf, cols, pairs), (0, 2, 1)) * weights[:, :, None]
        table = jnp.einsum("jt,tp->jp", coef, kernels, precision=EXACT).reshape(own, nf, pairs)
        new = jnp.einsum("wvp,vpc->wpc", table, wide, precision=EXACT)
        amplitude = wide[:own]
        for s in range(parts):
            at = lax.rem(me + s, parts) * quarter
            put = lambda x, y: lax.dynamic_update_slice_in_dim(
                x, lax.dynamic_slice_in_dim(x, at, quarter, 1) + y, at, 1
            )
            amplitude, new = put(amplitude, sources[s]), put(new, base[s])
        return amplitude, new
    at = around(parts, quarter // size, k)
    out = pl.BlockSpec((own, size, cols), lambda i, m: (0, at(i, m), 0))
    piece = pl.BlockSpec((own, size, cols), lambda i, m: (0, 0, 0))
    return pl.pallas_call(
        functools.partial(final_kernel, nf, parts, len(outs)),
        out_shape=(shape, shape),
        grid_spec=pltpu.PrefetchScalarGridSpec(
            num_scalar_prefetch=1,
            grid=(parts,),
            in_specs=[
                pl.BlockSpec((size, naux), lambda i, m: (at(i, m), 0)),
                pl.BlockSpec((nf, size), lambda i, m: (0, at(i, m))),
                pl.BlockSpec((nf, size), lambda i, m: (0, at(i, m))),
                resident(coef),
                resident(gathered),
            ]
            + [piece] * (2 * parts)
            + [pl.BlockSpec(memory_space=pl.ANY)] * len(outs),
            out_specs=(out, out),
            scratch_shapes=[
                VMEM((own * nf, size), jnp.float32),
                VMEM((nf * cols, size), jnp.float32),
            ]
            + [VMEM((own, cols, LANES), jnp.float32)] * 2,
        ),
        input_output_aliases={6 + 2 * parts + n: n for n in range(len(outs))},
        compiler_params=pltpu.CompilerParams(vmem_limit_bytes=48 << 20),
        cost_estimate=pl.CostEstimate(
            flops=2 * nf * parts * size * cols * naux,
            bytes_accessed=16 * own * parts * size * cols,
            transcendentals=0,
        ),
    )(me.reshape(1), factors, kernels, weights, coef, gathered, *sources, *base, *outs)


class Plane:
    def __init__(self, chips):
        self.chips = chips
        me = lax.axis_index("fac")
        self.core = lax.rem(me, 2)
        self.chip = lax.div(me, 2)
        self.pal = {"fac": me + 1 - 2 * self.core}
        self.started = []

    def on(self, d):
        return lax.rem(self.chip + d + self.chips, self.chips)

    def at(self, d):
        return {"fac": self.on(d) * 2 + self.core}

    def chip_at(self, chip):
        return {"fac": chip * 2 + self.core}

    def greet(self):
        barrier = pltpu.get_barrier_semaphore()
        for other in [self.pal] + [self.at(d) for d in range(1, self.chips)]:
            pl.semaphore_signal(barrier, inc=1, device_id=other, device_id_type=MESH)
        pl.semaphore_wait(barrier, self.chips)

    def send(self, src, dst, sems, at, to):
        copy = pltpu.make_async_remote_copy(
            src_ref=src,
            dst_ref=dst,
            send_sem=sems[0].at[at],
            recv_sem=sems[1].at[at],
            device_id=to,
            device_id_type=MESH,
        )
        copy.start()
        self.started.append(copy)
        return copy

    def end(self):
        for copy in self.started:
            copy.wait_send()


def reduced(plane, x_ref, near, red, land, mine, near_sems, red_sems):
    chips, chip, core, pal = plane.chips, plane.chip, plane.core, plane.pal
    nears = {}
    for d in list(range(1, chips)) + [0]:
        nears[d] = plane.send(x_ref.at[plane.on(d), 1 - core], near.at[d], near_sems, d, pal)
    block = mine.shape[0]
    step = min(block, 16)
    reds = []
    for d in range(1, chips):
        nears[d].wait_recv()
        for r in range(0, block, step):
            rows = slice(r, r + step)
            red[d, rows, :] = (x_ref[plane.on(d), core, rows, :] + near[d, rows, :]).astype(
                red.dtype
            )
        reds.append(plane.send(red.at[d], land.at[d], red_sems, d, plane.at(d)))
    nears[0].wait_recv()
    for copy in reds:
        copy.wait_recv()
    for r in range(0, block, step):
        rows = slice(r, r + step)
        total = x_ref[chip, core, rows, :] + near[0, rows, :]
        for d in range(1, chips):
            total = total + land[d, rows, :].astype(jnp.float32)
        mine[rows, :] = total.astype(mine.dtype)


def reduce_kernel(chips, x_ref, o_ref, near, red, land, *sems):
    plane = Plane(chips)
    plane.greet()
    reduced(plane, x_ref, near, red, land, o_ref, sems[0:2], sems[2:4])
    plane.end()


def sum_kernel(chips, x_ref, o_ref, near, red, land, mine, joined, *sems):
    plane = Plane(chips)
    chip, core = plane.chip, plane.core
    plane.greet()
    reduced(plane, x_ref, near, red, land, mine, sems[0:2], sems[2:4])
    here = joined.at[chip, core]
    keep = pltpu.make_async_copy(mine, here, sems[8])
    keep.start()
    keep.wait()
    wides = [plane.send(here, here, sems[4:6], d, plane.at(d)) for d in range(1, chips)]
    pairs = [plane.send(here, here, sems[6:8], 0, plane.pal)]
    for d, copy in enumerate(wides, 1):
        copy.wait_recv()
        there = joined.at[plane.on(-d), core]
        pairs.append(plane.send(there, there, sems[6:8], d, plane.pal))
    for copy in pairs:
        copy.wait_recv()
    plane.end()
    for c in range(chips):
        o_ref[c] = joined[c]


def gather_kernel(chips, parts, x_ref, o_ref, joined, *sems):
    plane = Plane(chips)
    chip, core, pal = plane.chip, plane.core, plane.pal
    plane.greet()
    wide_sems, pair_sems = sems[0:2], sems[2:4]
    pairs = []
    square = chips == 4
    column, row = lax.rem(chip, 2), lax.div(chip, 2)
    across, along = chip + 1 - 2 * column, chip + 2 - 4 * row
    corner = along + 1 - 2 * column
    wides = []
    for s in range(parts):
        src, dst = x_ref.at[s], joined.at[s, chip, core]
        if square:
            for n, to in enumerate((across, along)):
                copy = plane.send(src, dst, wide_sems, s * chips + n, plane.chip_at(to))
                wides.append((s, n, copy))
        else:
            for d in range(1, chips):
                copy = plane.send(src, dst, wide_sems, s * chips + d, plane.at(d))
                wides.append((s, d, copy))
    for s in range(parts):
        pairs.append(
            plane.send(x_ref.at[s], joined.at[s, chip, core], pair_sems, s * chips, pal)
        )
    late = []
    for s, d, copy in wides:
        copy.wait_recv()
        chip_from = (across, along)[d] if square else plane.on(-d)
        there = joined.at[s, chip_from, core]
        if square and d == s % 2:
            other = (along, across)[d]
            turned = plane.send(there, there, wide_sems, s * chips + 2, plane.chip_at(other))
            late.append((s, turned))
        at = s * chips + (1 + d if square else d)
        pairs.append(plane.send(there, there, pair_sems, at, pal))
    for s, copy in late:
        copy.wait_recv()
        there = joined.at[s, corner, core]
        pairs.append(plane.send(there, there, pair_sems, s * chips + 3, pal))
    for copy in pairs:
        copy.wait_recv()
    plane.end()
    for s in range(parts):
        for c in range(chips):
            o_ref[s, c] = joined[s, c]
        o_ref[s, chip, core] = x_ref[s]


def dmas(count, pairs):
    return [pltpu.SemaphoreType.DMA((count,))] * (2 * pairs)


def reach_params(cid):
    return pltpu.CompilerParams(
        collective_id=cid, has_side_effects=True, vmem_limit_bytes=24 << 20
    )


def reach_cost(size):
    return pl.CostEstimate(flops=40 * size, bytes_accessed=40 * size, transcendentals=0)


WHOLE = pl.BlockSpec(memory_space=VMEM)


def summed(x, all_blocks):
    n = lax.axis_size("fac")
    chips = n // 2
    rows, width = x.shape
    block = rows // n
    flat = (chips, 2, block, width)
    landing = [
        VMEM((chips, block, width), jnp.float32),
        VMEM((chips, block, width), jnp.bfloat16),
        VMEM((chips, block, width), jnp.bfloat16),
    ]
    if not all_blocks:
        return pl.pallas_call(
            functools.partial(reduce_kernel, chips),
            out_shape=jax.ShapeDtypeStruct((block, width), jnp.bfloat16),
            in_specs=[WHOLE],
            out_specs=WHOLE,
            scratch_shapes=landing + dmas(chips, 2),
            compiler_params=reach_params(1),
            cost_estimate=reach_cost(x.size // 2),
        )(x.reshape(flat))
    result = pl.pallas_call(
        functools.partial(sum_kernel, chips),
        out_shape=jax.ShapeDtypeStruct(flat, jnp.bfloat16),
        in_specs=[WHOLE],
        out_specs=WHOLE,
        scratch_shapes=landing
        + [VMEM((block, width), jnp.bfloat16), VMEM(flat, jnp.bfloat16)]
        + dmas(chips, 4)
        + [pltpu.SemaphoreType.DMA],
        compiler_params=reach_params(0),
        cost_estimate=reach_cost(x.size),
    )(x.reshape(flat))
    return result.reshape(rows, width)


def gathered_over(blocks):
    n = lax.axis_size("fac")
    chips = n // 2
    parts, block, width = blocks.shape
    flat = (parts, chips, 2, block, width)
    result = pl.pallas_call(
        functools.partial(gather_kernel, chips, parts),
        out_shape=jax.ShapeDtypeStruct(flat, jnp.bfloat16),
        in_specs=[WHOLE],
        out_specs=WHOLE,
        scratch_shapes=[VMEM(flat, jnp.bfloat16)] + dmas(parts * chips, 2),
        compiler_params=reach_params(2),
        cost_estimate=reach_cost(blocks.size * 8),
    )(blocks)
    return result.reshape(parts, n * block, width)


def shards(right_side, factors, pair_weight, second_order, forward, backward):
    own, pairs, cols = right_side.shape
    nf = forward.shape[0]
    naux = factors.shape[1]
    parts = nf // own
    quarter = pairs // parts
    me = lax.axis_index("freq")

    def shift(x, by):
        if by == 0:
            return x
        return lax.ppermute(x, "freq", [(i, (i + by) % parts) for i in range(parts)])

    order = jnp.concatenate(
        [lax.rem(me - s + parts, parts) * own + jnp.arange(own) for s in range(parts)]
    )
    pick = jax.nn.one_hot(order, nf, dtype=jnp.float32)
    ahead = jnp.einsum("ts,sv,wv->tw", pick, forward, pick, precision=EXACT)
    back = jnp.einsum("ws,st,vt->wv", pick, backward, pick, precision=EXACT)
    coef = (back[:, None, :] * ahead.T[None, :, :]).reshape(nf * nf, nf)
    reach = jnp.max(
        jnp.sum(
            jnp.einsum("wt,tv->wv", jnp.abs(backward), jnp.abs(forward), precision=EXACT), axis=1
        )
    )

    both = jnp.stack([pair_weight, second_order])
    tables = jnp.concatenate([shift(both, s) for s in range(parts)], axis=1)
    weights, kernels = tables[0], tables[1]
    size = tile_of(quarter) or quarter
    chunks = quarter // size
    early = max(chunks - 1, 1)
    groups = [(0, early)] + ([(early, chunks)] if early < chunks else [])
    tie = lax.optimization_barrier
    up = 8192.0

    def sliced(s, low, high):
        at = lax.rem(me + s, parts) * quarter + low * size
        return lax.dynamic_slice_in_dim(right_side, at, (high - low) * size, 1)

    def leaving(low, high):
        return [(sliced(s, low, high) * up).astype(jnp.float16) for s in range(1, parts)]

    def passed(blocks, back):
        return [
            shift(b, parts - 1 - s if back else s + 1) for s, b in enumerate(blocks)
        ]

    def first_projection():
        return jnp.einsum(
            "pa,fpc->fca",
            factors,
            right_side.astype(jnp.bfloat16),
            preferred_element_type=jnp.float32,
        ).reshape(own * cols, naux)

    def ladder(kept):
        total = kept
        for _ in range(INNER - 1):
            mine = summed(total, True)
            total = again(factors, pair_weight, mine, kept)
        block = summed(total, False)
        return jnp.stack([shift(block, s) for s in range(parts)])

    came = [passed(leaving(*groups[0]), False)]
    blocks = ladder(first_projection())
    if len(groups) > 1:
        blocks, out = tie((blocks, leaving(*groups[1])))
        came.append(passed(out, False))
    gathered = gathered_over(blocks)

    height = jnp.max(jnp.sum(jnp.abs(gathered.astype(jnp.float32)), axis=2))
    u_top = jnp.maximum(1.01 * reach * (R_MAX + W_MAX * L_MAX * height), 1e-30)
    v_top = jnp.maximum(1.01 * reach * (R_MAX + u_top), 1e-30)

    def halved(blocks, top):
        return [(b * (HALF_TOP / top)).astype(jnp.float16) for b in blocks[1:]]

    def added(first, rest, top, k):
        rest = [b.astype(jnp.float32) * (top / HALF_TOP) for b in rest]
        return [sliced(s, k, k + 1) + b for s, b in enumerate([first] + rest)]

    us, vs, inward = [], [], []
    for group, moved in zip(groups, came):
        moved = [m.astype(jnp.float32) * (1.0 / up) for m in moved]
        v = ()
        for k in range(*group):
            u, v = quarter_pass(
                me, k, group, factors, kernels, weights, coef, gathered, right_side, moved, v
            )
            inward.append(passed(halved(u, u_top), True))
            us.append(u)
        vs.append(v)
    sources = []
    total = jnp.zeros((own * cols, naux), jnp.float32)
    for k in range(chunks):
        if k:
            inward[k], total = tie((inward[k], total))
        sources.append(added(us[k][0], inward[k], u_top, k))
        total = project(me, k, factors, sources[k], total)

    out, total = tie((halved(vs[0], v_top), total))
    back = [passed(out, True)]
    blocks = ladder(total)
    if len(groups) > 1:
        blocks, out = tie((blocks, halved(vs[1], v_top)))
        back.append(passed(out, True))
    gathered = gathered_over(blocks)
    outs = ()
    for (low, high), first, moved in zip(groups, vs, back):
        gathered, moved, outs = tie((gathered, moved, outs))
        for k in range(low, high):
            rest = [m[:, (k - low) * size : (k - low + 1) * size] for m in [first[0]] + moved]
            base = added(rest[0], rest[1:], v_top, k)
            outs = final(
                me, k, factors, kernels, weights, coef[: own * nf], gathered, sources[k], base, outs
            )
    return outs


def solution(mesh):
    return jax.shard_map(
        shards,
        mesh=mesh,
        in_specs=(
            P("freq", "fac", None),
            P("fac", None),
            P("freq", "fac"),
            P("freq", "fac"),
            P(),
            P(),
        ),
        out_specs=(P("freq", "fac", None), P("freq", "fac", None)),
        check_vma=False,
    )
```

time: 523 us -> 518 us (level)
  starting transfers between devices: 45 us -> 107 us
  Pallas kernels: 311 us -> 261 us
  waiting for transfers between devices: 97.7 us -> 87.7 us
  local copies, waits for them, and re-layouts: 13.2 us -> 5.62 us
    ppermute x12 -> x30, starting transfers between devices: 45 us -> 107 us  [shift(): lax.ppermute(x, 'freq', [(i, (i + by) % parts) for i in range(parts)])]
    pallas_call x7 -> x15, Pallas kernels: 277 us -> 227 us  [the longest x3 62.8 us: final(): pl.pallas_call(functools.partial(final_kernel, nf, parts, len(outs)), out...]
    ppermute x12 -> x30, waiting for transfers between devices: 97.7 us -> 87.7 us  [shift(): lax.ppermute(x, 'freq', [(i, (i + by) % parts) for i in range(parts)])]
    unnamed x40 -> x36, local copies, waits for them, and re-layouts: 11.6 us -> 5.33 us
    add x2 -> x5, other arithmetic: 17.3 us -> 15.6 us  [added(): return [sliced(s, k, k + 1) + b for s, b in enumerate([first] + rest)]]
  transfers between devices with their start and end apart: 12 -> 30, of which waited for: 3 -> 11; matrix products, arithmetic and copies ran while one was open for 5% -> 8% of each run, Pallas kernels for 41% -> 46%
where the time goes in v2:
time: 518 us; the launch traced here: 511 us
  Pallas kernels  261 us (50%)
  starting transfers between devices  107 us (21%)
  waiting for transfers between devices  87.7 us (17%)
  other arithmetic  36.3 us (7%)
  matrix products  11.4 us (2%)
  local copies, waits for them, and re-layouts  5.62 us (1%)
    ppermute x30, starting transfers between devices, shift(): lax.ppermute(x, 'freq', [(i, (i + by) % parts) for i in range(parts)])  107 us
    ppermute x30, waiting for transfers between devices, shift(): lax.ppermute(x, 'freq', [(i, (i + by) % parts) for i in range(parts)])  87.7 us
    pallas_call x3, Pallas kernels, final(): pl.pallas_call(functools.partial(final_kernel, nf, parts, len(outs)), out...  62.8 us
    pallas_call x3, Pallas kernels, quarter_pass(): pl.pallas_call(functools.partial(quarter_kernel, nf, parts, len(kept)), o...  45.3 us
    pallas_call x2, Pallas kernels, gathered_over(): pl.pallas_call(functools.partial(gather_kernel, chips, parts), out_shape=...  42.4 us
    pallas_call x2, Pallas kernels, summed(): pl.pallas_call(functools.partial(sum_kernel, chips), out_shape=jax.ShapeD...  39.9 us
    pallas_call x2, Pallas kernels, again(): pl.pallas_call(functools.partial(again_kernel, own), out_shape=jax.ShapeD...  33.8 us
    pallas_call x2, Pallas kernels, summed(): pl.pallas_call(functools.partial(reduce_kernel, chips), out_shape=jax.Sha...  22.5 us
  transfers between devices with their start and end apart: 30, of which 11 were waited for; matrix products, arithmetic and copies ran while one was open for 8% of the time, Pallas kernels for 46%

profile of v2, /device:TPU:0, one launch (start us, length us, event | category | flops | bytes accessed | tf_op | source)
XLA Modules:
  0.0 511.5 jit_solution(3296160816732995056)
XLA Ops:
  0.6 1.6 pad_maximum_fusion.3
  2.2 5.1 collective-permute-start.2
  7.3 10.4 %fusion = f32[4,128,1024]{2,1,0:T(8,128)S(1)} fusion(bf16[4608,1024]{1,0:T(8,128)(2,1)} %l_ref.21, f32[4,4608,128]{2,1,0:T(8,128)} %rest_0_.5), kind=kOutput, calls=%fused_computation | convolution fusion | flops 4834197504 | bytes 20971520 | tf_op jit(solution)/shard_map/pa,fpc->fca/dot_general | solution.py:637
  17.7 20.4 %shard_map.77 = bf16[4,2,64,1024]{3,2,1,0:T(8,128)(2,1)S(1)} custom-call(f32[4,2,64,1024]{3,2,1,0:T(8,128)S(1)} %bitcast.40), custom_call_target="tpu_custom_call" | custom-call | flops 20971520 | bytes 20971520 | tf_op jit(solution)/shard_map/pallas_call | solution.py:556
  38.1 16.9 %shard_map.78 = f32[512,1024]{1,0:T(8,128)S(1)} custom-call(bf16[4608,1024]{1,0:T(8,128)(2,1)} %l_ref.21, f32[4,4608]{1,0:T(4,128)S(1)} %copy-done.10, bf16[512,1024]{1,0:T(8,128)(2,1)S(1)} %bitcast.47, f32[512,1024]{1,0:T(8,128)S(1)} %bitcast.41), custom_call_target="tpu_custom_call" | custom-call | flops 9663676416 | bytes 9437184 | tf_op jit(solution)/shard_map/pallas_call | solution.py:258
  55.1 11.3 %shard_map.79 = bf16[64,1024]{1,0:T(8,128)(2,1)S(1)} custom-call(f32[4,2,64,1024]{3,2,1,0:T(8,128)S(1)} %bitcast.45), custom_call_target="tpu_custom_call" | custom-call | flops 10485760 | bytes 10485760 | tf_op jit(solution)/shard_map/pallas_call | solution.py:547
  67.0 2.2 collective-permute-start.4
  69.2 1.9 collective-permute-start.3
  73.6 3.8 multiply_convert_fusion.3
  77.4 2.8 multiply_convert_fusion.18
  80.2 1.1 collective-permute-done.4
  81.9 2.7 collective-permute-start.8
  85.3 1.1 pad_maximum_fusion.1.x_ref
  86.4 21.3 %shard_map.80 = bf16[4,4,2,64,1024]{4,3,2,1,0:T(8,128)(2,1)S(1)} custom-call(bf16[4,64,1024]{2,1,0:T(8,128)(2,1)S(1)} %pad_maximum_fusion.1.x_ref), custom_call_target="tpu_custom_call" | custom-call | flops 83886080 | bytes 83886080 | tf_op jit(solution)/shard_map/pallas_call | solution.py:576
  107.8 0.9 abs_reduce_fusion
  108.6 2.0 copy-done
  112.7 2.8 collective-permute-start.9
  115.6 0.9 collective-permute-start.10
  116.5 1.2 pad_maximum_fusion
  117.7 30.3 %collective-permute-done.9 = f16[4,384,128]{2,1,0:T(8,128)(2,1)S(1)} collective-permute-done((f16[4,384,128]{2,1,0:T(8,128)(2,1)}, f16[4,384,128]{2,1,0:T(8,128)(2,1)S(1)}, u32[]{:S(2)}, u32[]{:S(2)}) %collective-permute-start.9) | collective-permute-done | bytes 393248 | tf_op jit(solution)/shard_map/ppermute | solution.py:599
  148.0 11.8 %collective-permute-start.11 = (f16[4,384,128]{2,1,0:T(8,128)(2,1)S(1)}, f16[4,384,128]{2,1,0:T(8,128)(2,1)S(1)}, u32[]{:S(2)}, u32[]{:S(2)}) collective-permute-start(f16[4,384,128]{2,1,0:T(8,128)(2,1)S(1)} %copy-done.11), channel_id=1, source_target_pairs={{0,3},{1,0},{2,1},{3,2},{4,7},{5,4},{6,5},{7,6},{8,11},{9,8},{10,9... | collective-permute-start | bytes 1179656 | tf_op jit(solution)/shard_map/ppermute | solution.py:599
  159.9 19.6 %collective-permute-done.10 = f16[4,384,128]{2,1,0:T(8,128)(2,1)S(1)} collective-permute-done((f16[4,384,128]{2,1,0:T(8,128)(2,1)}, f16[4,384,128]{2,1,0:T(8,128)(2,1)S(1)}, u32[]{:S(2)}, u32[]{:S(2)}) %collective-permute-start.10) | collective-permute-done | bytes 393248 | tf_op jit(solution)/shard_map/ppermute | solution.py:599
  179.6 8.3 %collective-permute-done.11 = f16[4,384,128]{2,1,0:T(8,128)(2,1)S(1)} collective-permute-done((f16[4,384,128]{2,1,0:T(8,128)(2,1)S(1)}, f16[4,384,128]{2,1,0:T(8,128)(2,1)S(1)}, u32[]{:S(2)}, u32[]{:S(2)}) %collective-permute-start.11) | collective-permute-done | bytes 393248 | tf_op jit(solution)/shard_map/ppermute | solution.py:599
  187.9 14.0 %shard_map.83 = (f32[4,384,128]{2,1,0:T(8,128)S(1)}, f32[4,384,128]{2,1,0:T(8,128)S(1)}, f32[4,384,128]{2,1,0:T(8,128)S(1)}, f32[4,384,128]{2,1,0:T(8,128)S(1)},...) custom-call(s32[1]{0:T(128)} %bitcast.me_ref, ...), custom_call_target="tpu_custom_call" | custom-call | flops 2415919104 | bytes 12582912 | tf_op jit(solution)/shard_map/pallas_call | solution.py:137
  202.0 0.9 multiply_convert_fusion.15
  202.9 1.8 collective-permute-start.14
  205.5 1.2 collective-permute-start.13
  208.4 1.3 convert_multiply_fusion.rest_3_
  210.0 15.6 %shard_map.81 = (f32[4,384,128]{2,1,0:T(8,128)S(1)}, f32[4,384,128]{2,1,0:T(8,128)S(1)}, f32[4,384,128]{2,1,0:T(8,128)S(1)}, f32[4,384,128]{2,1,0:T(8,128)S(1)},...) custom-call(s32[1]{0:T(128)} %bitcast.me_ref, ...), custom_call_target="tpu_custom_call" | custom-call | flops 2415919104 | bytes 12582912 | tf_op jit(solution)/shard_map/pallas_call | solution.py:137
  225.7 15.7 %shard_map.82 = (f32[4,384,128]{2,1,0:T(8,128)S(1)}, f32[4,384,128]{2,1,0:T(8,128)S(1)}, f32[4,384,128]{2,1,0:T(8,128)S(1)}, f32[4,384,128]{2,1,0:T(8,128)S(1)},...) custom-call(s32[1]{0:T(128)} %bitcast.me_ref, ...), custom_call_target="tpu_custom_call", output_to_operand_aliasing={{4}: (10, {}), {5}: (11, {}), {6}: (12, {}), {7}: (13, {})} | custom-call | flops 2415919104 | bytes 12582912 | tf_op jit(solution)/shard_map/pallas_call | solution.py:137
  242.0 1.5 collective-permute-start.20
  243.5 2.1 collective-permute-start.19
  245.6 1.2 collective-permute-start.18
  247.1 8.8 %collective-permute-done.20 = f16[4,384,128]{2,1,0:T(8,128)(2,1)S(1)} collective-permute-done((f16[4,384,128]{2,1,0:T(8,128)(2,1)S(1)}, f16[4,384,128]{2,1,0:T(8,128)(2,1)S(1)}, u32[]{:S(2)}, u32[]{:S(2)}) %collective-permute-start.20) | collective-permute-done | bytes 393248 | tf_op jit(solution)/shard_map/ppermute | solution.py:599
  255.9 13.7 %collective-permute-start.17 = (f16[4,384,128]{2,1,0:T(8,128)(2,1)S(1)}, f16[4,384,128]{2,1,0:T(8,128)(2,1)S(1)}, u32[]{:S(2)}, u32[]{:S(2)}) collective-permute-start(f16[4,384,128]{2,1,0:T(8,128)(2,1)S(1)} %multiply_convert_fusion.12), channel_id=1, source_target_pairs={{0,1},{1,2},{2,3},{3,0},{4,5},{5,6},{6,7},{7,4},{8,9},{9,10},{10,1... | collective-permute-start | bytes 1179656 | tf_op jit(solution)/shard_map/ppermute | solution.py:599
  269.6 3.1 collective-permute-done.19
  272.8 22.0 %collective-permute-start.15 = (f16[4,384,128]{2,1,0:T(8,128)(2,1)S(1)}, f16[4,384,128]{2,1,0:T(8,128)(2,1)S(1)}, u32[]{:S(2)}, u32[]{:S(2)}) collective-permute-start(f16[4,384,128]{2,1,0:T(8,128)(2,1)S(1)} %multiply_convert_fusion.14), channel_id=1, source_target_pairs={{0,3},{1,0},{2,1},{3,2},{4,7},{5,4},{6,5},{7,6},{8,11},{9,8},{10,9... | collective-permute-start | bytes 1179656 | tf_op jit(solution)/shard_map/ppermute | solution.py:599
  294.8 2.4 multiply_add_fusion.15
  297.4 4.7 shard_map.84.rest_4_
  302.2 1.5 collective-permute-done.16
  303.7 4.4 collective-permute-done.15
  308.1 2.3 multiply_add_fusion.12
  310.4 4.7 shard_map.85.rest_4_
  315.1 3.7 collective-permute-done.12
  318.8 2.3 multiply_add_fusion.9
  321.2 4.7 shard_map.86.x_ref
  325.9 9.5 %collective-permute-start.24 = (f16[4,768,128]{2,1,0:T(8,128)(2,1)S(1)}, f16[4,768,128]{2,1,0:T(8,128)(2,1)S(1)}, u32[]{:S(2)}, u32[]{:S(2)}) collective-permute-start(f16[4,768,128]{2,1,0:T(8,128)(2,1)S(1)} %multiply_convert_fusion.2), channel_id=1, source_target_pairs={{0,3},{1,0},{2,1},{3,2},{4,7},{5,4},{6,5},{7,6},{8,11},{9,8},{10,9... | collective-permute-start | bytes 2359304 | tf_op jit(solution)/shard_map/ppermute | solution.py:599
  336.0 19.5 %shard_map.87 = bf16[4,2,64,1024]{3,2,1,0:T(8,128)(2,1)S(1)} custom-call(f32[4,2,64,1024]{3,2,1,0:T(8,128)S(1)} %bitcast.39), custom_call_target="tpu_custom_call" | custom-call | flops 20971520 | bytes 20971520 | tf_op jit(solution)/shard_map/pallas_call | solution.py:556
  355.5 16.9 %shard_map.88 = f32[512,1024]{1,0:T(8,128)S(1)} custom-call(bf16[4608,1024]{1,0:T(8,128)(2,1)} %l_ref.21, f32[4,4608]{1,0:T(4,128)S(1)} %copy-done.10, bf16[512,1024]{1,0:T(8,128)(2,1)S(1)} %bitcast.48, f32[512,1024]{1,0:T(8,128)S(1)} %shard_map.86.x_ref), custom_call_target="tpu_custom_call" | custom-call | flops 9663676416 | bytes 9437184 | tf_op jit(solution)/shard_map/pallas_call | solution.py:258
  372.4 11.3 %shard_map.89 = bf16[64,1024]{1,0:T(8,128)(2,1)S(1)} custom-call(f32[4,2,64,1024]{3,2,1,0:T(8,128)S(1)} %bitcast.46), custom_call_target="tpu_custom_call" | custom-call | flops 10485760 | bytes 10485760 | tf_op jit(solution)/shard_map/pallas_call | solution.py:547
  383.7 3.2 collective-permute-start.23
  387.8 1.1 collective-permute-start.22
  388.9 4.9 collective-permute-done.23
  393.8 15.8 %collective-permute-start.21 = (bf16[64,1024]{1,0:T(8,128)(2,1)S(1)}, bf16[64,1024]{1,0:T(8,128)(2,1)S(1)}, u32[]{:S(2)}, u32[]{:S(2)}) collective-permute-start(bf16[64,1024]{1,0:T(8,128)(2,1)S(1)} %shard_map.89), channel_id=1, source_target_pairs={{0,1},{1,2},{2,3},{3,0},{4,5},{5,6},{6,7},{7,4},{8,9},{9,10},{10,1... | collective-permute-start | bytes 393224 | tf_op jit(solution)/shard_map/ppermute | solution.py:599
  410.4 2.1 collective-permute-done.21
  412.6 1.2 collective-permute-start.27
  413.8 2.8 collective-permute-start.28
  416.6 21.1 %shard_map.90 = bf16[4,4,2,64,1024]{4,3,2,1,0:T(8,128)(2,1)S(1)} custom-call(bf16[4,64,1024]{2,1,0:T(8,128)(2,1)S(1)} %pad_maximum_fusion.2.x_ref), custom_call_target="tpu_custom_call" | custom-call | flops 83886080 | bytes 83886080 | tf_op jit(solution)/shard_map/pallas_call | solution.py:576
  437.7 2.0 copy-done.2
  439.9 5.1 %multiply_add_fusion.3 = (f32[4,384,128]{2,1,0:T(8,128)}, f32[4,384,128]{2,1,0:T(8,128)}, f32[4,384,128]{2,1,0:T(8,128)S(1)}, f32[4,384,128]{2,1,0:T(8,128)S(1)}...) fusion(f32[4,4608,128]{2,1,0:T(8,128)} %rest_0_.5, ...), kind=kLoop, calls=%fused_computation.17 | loop fusion | flops 3932160 | bytes 16515108 | tf_op jit(solution)/shard_map/add | solution.py:668
  445.0 20.9 %shard_map.91 = (f32[4,4608,128]{2,1,0:T(8,128)}, f32[4,4608,128]{2,1,0:T(8,128)}) custom-call(s32[1]{0:T(128)} %bitcast.me_ref, bf16[4608,1024]{1,0:T(8,128)(2,1)} %l_ref.21, f32[16,4608]{1,0:T(8,128)S(1)} %get-tuple-element.155.k_ref, f32[16,4608]{1,0:T(8,128)S(1)} %get-tuple-element.154.wt_ref, f32[64,16]{1,0:T(8,128)S(1)} %bitcast.51, ...), custom_call_target="tpu_custom_call" | custom-call | flops 6442450944 | bytes 12582912 | tf_op jit(solution)/shard_map/pallas_call | solution.py:339
  465.9 21.0 %shard_map.92 = (f32[4,4608,128]{2,1,0:T(8,128)}, f32[4,4608,128]{2,1,0:T(8,128)}) custom-call(s32[1]{0:T(128)} %bitcast.me_ref, bf16[4608,1024]{1,0:T(8,128)(2,1)} %l_ref.21, f32[16,4608]{1,0:T(8,128)S(1)} %get-tuple-element.155.k_ref, f32[16,4608]{1,0:T(8,128)S(1)} %get-tuple-element.154.wt_ref, ...), custom_call_target="tpu_custom_call", output_to_operand_aliasing={{0}: (14, {}), {1}: (15, {})} | custom-call | flops 6442450944 | bytes 12582912 | tf_op jit(solution)/shard_map/pallas_call | solution.py:339
  486.9 3.4 multiply_add_fusion
  490.4 20.9 %shard_map.93 = (f32[4,4608,128]{2,1,0:T(8,128)}, f32[4,4608,128]{2,1,0:T(8,128)}) custom-call(s32[1]{0:T(128)} %bitcast.me_ref, bf16[4608,1024]{1,0:T(8,128)(2,1)} %l_ref.21, f32[16,4608]{1,0:T(8,128)S(1)} %get-tuple-element.155.k_ref, f32[16,4608]{1,0:T(8,128)S(1)} %get-tuple-element.154.wt_ref, ...), custom_call_target="tpu_custom_call", output_to_operand_aliasing={{0}: (14, {}), {1}: (15, {})} | custom-call | flops 6442450944 | bytes 12582912 | tf_op jit(solution)/shard_map/pallas_call | solution.py:339
  (97 shorter events, 12.0 us)
Async XLA Ops:
  2.2 109.8 %collective-permute-start.2 = (f32[2,4,4608]{2,1,0:T(4,128)}, f32[2,4,4608]{2,1,0:T(4,128)}, u32[]{:S(2)}, u32[]{:S(2)}) collective-permute-start(f32[2,4,4608]{2,1,0:T(4,128)} %pad_maximum_fusion.3), channel_id=1, source_target_pairs={{0,3},{1,0},{2,1},{3,2},{4,7},{5,4},{6,5},{7,6},{8,11},{9,8},{10,9... | collective-permute-start | bytes 442376 | tf_op jit(solution)/shard_map/ppermute | solution.py:599
  7.3 105.4 %collective-permute-start.1 = (f32[2,4,4608]{2,1,0:T(4,128)}, f32[2,4,4608]{2,1,0:T(4,128)}, u32[]{:S(2)}, u32[]{:S(2)}) collective-permute-start(f32[2,4,4608]{2,1,0:T(4,128)} %pad_maximum_fusion.3), channel_id=1, source_target_pairs={{0,2},{1,3},{2,0},{3,1},{4,6},{5,7},{6,4},{7,5},{8,10},{9,11},{10,... | collective-permute-start | bytes 442376 | tf_op jit(solution)/shard_map/ppermute | solution.py:599
  17.7 20.4 %copy-start.10 = (f32[4,4608]{1,0:T(4,128)S(1)}, f32[4,4608]{1,0:T(4,128)}, u32[]{:S(2)}) copy-start(f32[4,4608]{1,0:T(4,128)} %wt_ref.3) | copy-start | bytes 221188
  55.1 16.1 %copy-start.16 = (f32[16,16]{1,0:T(8,128)S(1)}, f32[16,16]{1,0:T(8,128)}, u32[]{:S(2)}) copy-start(f32[16,16]{1,0:T(8,128)} %param.10) | copy-start | bytes 3076
  55.1 16.1 %copy-start.17 = (f32[16,16]{1,0:T(8,128)S(1)}, f32[16,16]{1,0:T(8,128)}, u32[]{:S(2)}) copy-start(f32[16,16]{1,0:T(8,128)} %param.11) | copy-start | bytes 3076
  66.4 13.8 %collective-permute-start.5 = (bf16[64,1024]{1,0:T(8,128)(2,1)S(1)}, bf16[64,1024]{1,0:T(8,128)(2,1)S(1)}, u32[]{:S(2)}, u32[]{:S(2)}) collective-permute-start(bf16[64,1024]{1,0:T(8,128)(2,1)S(1)} %shard_map.79), channel_id=1, source_target_pairs={{0,3},{1,0},{2,1},{3,2},{4,7},{5,4},{6,5},{7,6},{8,11},{9,8},{10,9... | collective-permute-start | bytes 393224 | tf_op jit(solution)/shard_map/ppermute | solution.py:599
  67.0 14.3 %collective-permute-start.4 = (bf16[64,1024]{1,0:T(8,128)(2,1)S(1)}, bf16[64,1024]{1,0:T(8,128)(2,1)S(1)}, u32[]{:S(2)}, u32[]{:S(2)}) collective-permute-start(bf16[64,1024]{1,0:T(8,128)(2,1)S(1)} %shard_map.79), channel_id=1, source_target_pairs={{0,2},{1,3},{2,0},{3,1},{4,6},{5,7},{6,4},{7,5},{8,10},{9,11},{10,... | collective-permute-start | bytes 393224 | tf_op jit(solution)/shard_map/ppermute | solution.py:599
  69.2 15.5 %collective-permute-start.3 = (bf16[64,1024]{1,0:T(8,128)(2,1)S(1)}, bf16[64,1024]{1,0:T(8,128)(2,1)S(1)}, u32[]{:S(2)}, u32[]{:S(2)}) collective-permute-start(bf16[64,1024]{1,0:T(8,128)(2,1)S(1)} %shard_map.79), channel_id=1, source_target_pairs={{0,1},{1,2},{2,3},{3,0},{4,5},{5,6},{6,7},{7,4},{8,9},{9,10},{10,1... | collective-permute-start | bytes 393224 | tf_op jit(solution)/shard_map/ppermute | solution.py:599
  80.2 1.1 copy-start.13
  80.2 35.4 %collective-permute-start = (f32[2,4,4608]{2,1,0:T(4,128)}, f32[2,4,4608]{2,1,0:T(4,128)}, u32[]{:S(2)}, u32[]{:S(2)}) collective-permute-start(f32[2,4,4608]{2,1,0:T(4,128)} %pad_maximum_fusion.3), channel_id=1, source_target_pairs={{0,1},{1,2},{2,3},{3,0},{4,5},{5,6},{6,7},{7,4},{8,9},{9,10},{10,1... | collective-permute-start | bytes 442376 | tf_op jit(solution)/shard_map/ppermute | solution.py:599
  81.3 0.6 copy-start.14
  81.9 126.5 %collective-permute-start.8 = (f16[4,768,128]{2,1,0:T(8,128)(2,1)}, f16[4,768,128]{2,1,0:T(8,128)(2,1)S(1)}, u32[]{:S(2)}, u32[]{:S(2)}) collective-permute-start(f16[4,768,128]{2,1,0:T(8,128)(2,1)} %get-tuple-element.148), channel_id=1, source_target_pairs={{0,3},{1,0},{2,1},{3,2},{4,7},{5,4},{6,5},{7,6},{8,11},{9,8},{10,9... | collective-permute-start | bytes 2359304 | tf_op jit(solution)/shard_map/ppermute | solution.py:599
  84.6 0.7 copy-start.15
  85.3 124.4 %collective-permute-start.7 = (f16[4,768,128]{2,1,0:T(8,128)(2,1)S(1)}, f16[4,768,128]{2,1,0:T(8,128)(2,1)S(1)}, u32[]{:S(2)}, u32[]{:S(2)}) collective-permute-start(f16[4,768,128]{2,1,0:T(8,128)(2,1)S(1)} %get-tuple-element.149), channel_id=1, source_target_pairs={{0,2},{1,3},{2,0},{3,1},{4,6},{5,7},{6,4},{7,5},{8,10},{9,11},{10,... | collective-permute-start | bytes 2359304 | tf_op jit(solution)/shard_map/ppermute | solution.py:599
  107.7 8.7 %copy-start.12 = (f32[4,4608]{1,0:T(4,128)S(1)}, f32[4,4608]{1,0:T(4,128)}, u32[]{:S(2)}) copy-start(f32[4,4608]{1,0:T(4,128)} %param.9) | copy-start | bytes 221188
  108.6 2.0 copy-start
  112.0 36.0 %copy-start.11 = (f16[4,384,128]{2,1,0:T(8,128)(2,1)S(1)}, f16[4,384,128]{2,1,0:T(8,128)(2,1)}, u32[]{:S(2)}) copy-start(f16[4,384,128]{2,1,0:T(8,128)(2,1)} %get-tuple-element.70) | copy-start | bytes 1179652
  112.0 97.9 %collective-permute-start.6 = (f16[4,768,128]{2,1,0:T(8,128)(2,1)S(1)}, f16[4,768,128]{2,1,0:T(8,128)(2,1)S(1)}, u32[]{:S(2)}, u32[]{:S(2)}) collective-permute-start(f16[4,768,128]{2,1,0:T(8,128)(2,1)S(1)} %get-tuple-element.150), channel_id=1, source_target_pairs={{0,1},{1,2},{2,3},{3,0},{4,5},{5,6},{6,7},{7,4},{8,9},{9,10},{10,1... | collective-permute-start | bytes 2359304 | tf_op jit(solution)/shard_map/ppermute | solution.py:599
  112.7 35.3 %collective-permute-start.9 = (f16[4,384,128]{2,1,0:T(8,128)(2,1)}, f16[4,384,128]{2,1,0:T(8,128)(2,1)S(1)}, u32[]{:S(2)}, u32[]{:S(2)}) collective-permute-start(f16[4,384,128]{2,1,0:T(8,128)(2,1)} %get-tuple-element.68), channel_id=1, source_target_pairs={{0,1},{1,2},{2,3},{3,0},{4,5},{5,6},{6,7},{7,4},{8,9},{9,10},{10,1... | collective-permute-start | bytes 1179656 | tf_op jit(solution)/shard_map/ppermute | solution.py:599
  115.6 63.9 %collective-permute-start.10 = (f16[4,384,128]{2,1,0:T(8,128)(2,1)}, f16[4,384,128]{2,1,0:T(8,128)(2,1)S(1)}, u32[]{:S(2)}, u32[]{:S(2)}) collective-permute-start(f16[4,384,128]{2,1,0:T(8,128)(2,1)} %get-tuple-element.69), channel_id=1, source_target_pairs={{0,2},{1,3},{2,0},{3,1},{4,6},{5,7},{6,4},{7,5},{8,10},{9,11},{10,... | collective-permute-start | bytes 1179656 | tf_op jit(solution)/shard_map/ppermute | solution.py:599
  117.7 70.3 %copy-start.1 = (bf16[4,4,2,64,1024]{4,3,2,1,0:T(8,128)(2,1)S(1)}, bf16[4,4,2,64,1024]{4,3,2,1,0:T(8,128)(2,1)}, u32[]{:S(2)}) copy-start(bf16[4,4,2,64,1024]{4,3,2,1,0:T(8,128)(2,1)} %copy-done) | copy-start | bytes 12582916
  148.0 39.9 %collective-permute-start.11 = (f16[4,384,128]{2,1,0:T(8,128)(2,1)S(1)}, f16[4,384,128]{2,1,0:T(8,128)(2,1)S(1)}, u32[]{:S(2)}, u32[]{:S(2)}) collective-permute-start(f16[4,384,128]{2,1,0:T(8,128)(2,1)S(1)} %copy-done.11), channel_id=1, source_target_pairs={{0,3},{1,0},{2,1},{3,2},{4,7},{5,4},{6,5},{7,6},{8,11},{9,8},{10,9... | collective-permute-start | bytes 1179656 | tf_op jit(solution)/shard_map/ppermute | solution.py:599
  201.9 5.6 %copy-start.4 = (f32[4,384,128]{2,1,0:T(8,128)}, f32[4,384,128]{2,1,0:T(8,128)S(1)}, u32[]{:S(2)}) copy-start(f32[4,384,128]{2,1,0:T(8,128)S(1)} %get-tuple-element.112) | copy-start | bytes 2359300
  202.0 5.6 %copy-start.6 = (f32[4,384,128]{2,1,0:T(8,128)}, f32[4,384,128]{2,1,0:T(8,128)S(1)}, u32[]{:S(2)}) copy-start(f32[4,384,128]{2,1,0:T(8,128)S(1)} %get-tuple-element.94) | copy-start | bytes 2359300
  202.0 5.6 %copy-start.8 = (f32[4,384,128]{2,1,0:T(8,128)}, f32[4,384,128]{2,1,0:T(8,128)S(1)}, u32[]{:S(2)}) copy-start(f32[4,384,128]{2,1,0:T(8,128)S(1)} %get-tuple-element.93) | copy-start | bytes 2359300
  202.9 112.2 %collective-permute-start.14 = (f16[4,384,128]{2,1,0:T(8,128)(2,1)}, f16[4,384,128]{2,1,0:T(8,128)(2,1)S(1)}, u32[]{:S(2)}, u32[]{:S(2)}) collective-permute-start(f16[4,384,128]{2,1,0:T(8,128)(2,1)} %multiply_convert_fusion.15), channel_id=1, source_target_pairs={{0,1},{1,2},{2,3},{3,0},{4,5},{5,6},{6,7},{7,4},{8,9},{9,10},{10,1... | collective-permute-start | bytes 1179656 | tf_op jit(solution)/shard_map/ppermute | solution.py:599
  205.5 109.6 %collective-permute-start.13 = (f16[4,384,128]{2,1,0:T(8,128)(2,1)}, f16[4,384,128]{2,1,0:T(8,128)(2,1)S(1)}, u32[]{:S(2)}, u32[]{:S(2)}) collective-permute-start(f16[4,384,128]{2,1,0:T(8,128)(2,1)} %multiply_convert_fusion.16), channel_id=1, source_target_pairs={{0,2},{1,3},{2,0},{3,1},{4,6},{5,7},{6,4},{7,5},{8,10},{9,11},{10,... | collective-permute-start | bytes 1179656 | tf_op jit(solution)/shard_map/ppermute | solution.py:599
  242.0 13.9 %collective-permute-start.20 = (f16[4,384,128]{2,1,0:T(8,128)(2,1)S(1)}, f16[4,384,128]{2,1,0:T(8,128)(2,1)S(1)}, u32[]{:S(2)}, u32[]{:S(2)}) collective-permute-start(f16[4,384,128]{2,1,0:T(8,128)(2,1)S(1)} %multiply_convert_fusion.9), channel_id=1, source_target_pairs={{0,1},{1,2},{2,3},{3,0},{4,5},{5,6},{6,7},{7,4},{8,9},{9,10},{10,1... | collective-permute-start | bytes 1179656 | tf_op jit(solution)/shard_map/ppermute | solution.py:599
  243.5 29.3 %collective-permute-start.19 = (f16[4,384,128]{2,1,0:T(8,128)(2,1)S(1)}, f16[4,384,128]{2,1,0:T(8,128)(2,1)S(1)}, u32[]{:S(2)}, u32[]{:S(2)}) collective-permute-start(f16[4,384,128]{2,1,0:T(8,128)(2,1)S(1)} %multiply_convert_fusion.10), channel_id=1, source_target_pairs={{0,2},{1,3},{2,0},{3,1},{4,6},{5,7},{6,4},{7,5},{8,10},{9,11},{10,... | collective-permute-start | bytes 1179656 | tf_op jit(solution)/shard_map/ppermute | solution.py:599
  245.6 27.2 %collective-permute-start.18 = (f16[4,384,128]{2,1,0:T(8,128)(2,1)S(1)}, f16[4,384,128]{2,1,0:T(8,128)(2,1)S(1)}, u32[]{:S(2)}, u32[]{:S(2)}) collective-permute-start(f16[4,384,128]{2,1,0:T(8,128)(2,1)S(1)} %multiply_convert_fusion.11), channel_id=1, source_target_pairs={{0,3},{1,0},{2,1},{3,2},{4,7},{5,4},{6,5},{7,6},{8,11},{9,8},{10,9... | collective-permute-start | bytes 1179656 | tf_op jit(solution)/shard_map/ppermute | solution.py:599
  255.9 46.2 %collective-permute-start.17 = (f16[4,384,128]{2,1,0:T(8,128)(2,1)S(1)}, f16[4,384,128]{2,1,0:T(8,128)(2,1)S(1)}, u32[]{:S(2)}, u32[]{:S(2)}) collective-permute-start(f16[4,384,128]{2,1,0:T(8,128)(2,1)S(1)} %multiply_convert_fusion.12), channel_id=1, source_target_pairs={{0,1},{1,2},{2,3},{3,0},{4,5},{5,6},{6,7},{7,4},{8,9},{9,10},{10,1... | collective-permute-start | bytes 1179656 | tf_op jit(solution)/shard_map/ppermute | solution.py:599
  272.8 30.9 %collective-permute-start.16 = (f16[4,384,128]{2,1,0:T(8,128)(2,1)S(1)}, f16[4,384,128]{2,1,0:T(8,128)(2,1)S(1)}, u32[]{:S(2)}, u32[]{:S(2)}) collective-permute-start(f16[4,384,128]{2,1,0:T(8,128)(2,1)S(1)} %multiply_convert_fusion.13), channel_id=1, source_target_pairs={{0,2},{1,3},{2,0},{3,1},{4,6},{5,7},{6,4},{7,5},{8,10},{9,11},{10,... | collective-permute-start | bytes 1179656 | tf_op jit(solution)/shard_map/ppermute | solution.py:599
  272.8 35.3 %collective-permute-start.15 = (f16[4,384,128]{2,1,0:T(8,128)(2,1)S(1)}, f16[4,384,128]{2,1,0:T(8,128)(2,1)S(1)}, u32[]{:S(2)}, u32[]{:S(2)}) collective-permute-start(f16[4,384,128]{2,1,0:T(8,128)(2,1)S(1)} %multiply_convert_fusion.14), channel_id=1, source_target_pairs={{0,3},{1,0},{2,1},{3,2},{4,7},{5,4},{6,5},{7,6},{8,11},{9,8},{10,9... | collective-permute-start | bytes 1179656 | tf_op jit(solution)/shard_map/ppermute | solution.py:599
  302.1 16.7 %collective-permute-start.12 = (f16[4,384,128]{2,1,0:T(8,128)(2,1)}, f16[4,384,128]{2,1,0:T(8,128)(2,1)S(1)}, u32[]{:S(2)}, u32[]{:S(2)}) collective-permute-start(f16[4,384,128]{2,1,0:T(8,128)(2,1)} %multiply_convert_fusion.17), channel_id=1, source_target_pairs={{0,3},{1,0},{2,1},{3,2},{4,7},{5,4},{6,5},{7,6},{8,11},{9,8},{10,9... | collective-permute-start | bytes 1179656 | tf_op jit(solution)/shard_map/ppermute | solution.py:599
  325.9 113.8 %collective-permute-start.24 = (f16[4,768,128]{2,1,0:T(8,128)(2,1)S(1)}, f16[4,768,128]{2,1,0:T(8,128)(2,1)S(1)}, u32[]{:S(2)}, u32[]{:S(2)}) collective-permute-start(f16[4,768,128]{2,1,0:T(8,128)(2,1)S(1)} %multiply_convert_fusion.2), channel_id=1, source_target_pairs={{0,3},{1,0},{2,1},{3,2},{4,7},{5,4},{6,5},{7,6},{8,11},{9,8},{10,9... | collective-permute-start | bytes 2359304 | tf_op jit(solution)/shard_map/ppermute | solution.py:599
  335.4 104.5 %collective-permute-start.25 = (f16[4,768,128]{2,1,0:T(8,128)(2,1)S(1)}, f16[4,768,128]{2,1,0:T(8,128)(2,1)S(1)}, u32[]{:S(2)}, u32[]{:S(2)}) collective-permute-start(f16[4,768,128]{2,1,0:T(8,128)(2,1)S(1)} %multiply_convert_fusion.1), channel_id=1, source_target_pairs={{0,2},{1,3},{2,0},{3,1},{4,6},{5,7},{6,4},{7,5},{8,10},{9,11},{10,... | collective-permute-start | bytes 2359304 | tf_op jit(solution)/shard_map/ppermute | solution.py:599
  335.4 104.5 %collective-permute-start.26 = (f16[4,768,128]{2,1,0:T(8,128)(2,1)S(1)}, f16[4,768,128]{2,1,0:T(8,128)(2,1)S(1)}, u32[]{:S(2)}, u32[]{:S(2)}) collective-permute-start(f16[4,768,128]{2,1,0:T(8,128)(2,1)S(1)} %multiply_convert_fusion), channel_id=1, source_target_pairs={{0,1},{1,2},{2,3},{3,0},{4,5},{5,6},{6,7},{7,4},{8,9},{9,10},{10,1... | collective-permute-start | bytes 2359304 | tf_op jit(solution)/shard_map/ppermute | solution.py:599
  372.4 14.5 %copy-start.9 = (f32[4,384,128]{2,1,0:T(8,128)S(1)}, f32[4,384,128]{2,1,0:T(8,128)}, u32[]{:S(2)}) copy-start(f32[4,384,128]{2,1,0:T(8,128)} %copy-done.8) | copy-start | bytes 2359300
  372.4 37.2 %copy-start.7 = (f32[4,384,128]{2,1,0:T(8,128)S(1)}, f32[4,384,128]{2,1,0:T(8,128)}, u32[]{:S(2)}) copy-start(f32[4,384,128]{2,1,0:T(8,128)} %copy-done.6) | copy-start | bytes 2359300
  383.7 10.1 %collective-permute-start.23 = (bf16[64,1024]{1,0:T(8,128)(2,1)S(1)}, bf16[64,1024]{1,0:T(8,128)(2,1)S(1)}, u32[]{:S(2)}, u32[]{:S(2)}) collective-permute-start(bf16[64,1024]{1,0:T(8,128)(2,1)S(1)} %shard_map.89), channel_id=1, source_target_pairs={{0,3},{1,0},{2,1},{3,2},{4,7},{5,4},{6,5},{7,6},{8,11},{9,8},{10,9... | collective-permute-start | bytes 393224 | tf_op jit(solution)/shard_map/ppermute | solution.py:599
  387.8 22.6 %collective-permute-start.22 = (bf16[64,1024]{1,0:T(8,128)(2,1)S(1)}, bf16[64,1024]{1,0:T(8,128)(2,1)S(1)}, u32[]{:S(2)}, u32[]{:S(2)}) collective-permute-start(bf16[64,1024]{1,0:T(8,128)(2,1)S(1)} %shard_map.89), channel_id=1, source_target_pairs={{0,2},{1,3},{2,0},{3,1},{4,6},{5,7},{6,4},{7,5},{8,10},{9,11},{10,... | collective-permute-start | bytes 393224 | tf_op jit(solution)/shard_map/ppermute | solution.py:599
  393.8 18.7 %collective-permute-start.21 = (bf16[64,1024]{1,0:T(8,128)(2,1)S(1)}, bf16[64,1024]{1,0:T(8,128)(2,1)S(1)}, u32[]{:S(2)}, u32[]{:S(2)}) collective-permute-start(bf16[64,1024]{1,0:T(8,128)(2,1)S(1)} %shard_map.89), channel_id=1, source_target_pairs={{0,1},{1,2},{2,3},{3,0},{4,5},{5,6},{6,7},{7,4},{8,9},{9,10},{10,1... | collective-permute-start | bytes 393224 | tf_op jit(solution)/shard_map/ppermute | solution.py:599
  412.6 74.3 %collective-permute-start.27 = (f16[4,384,128]{2,1,0:T(8,128)(2,1)}, f16[4,384,128]{2,1,0:T(8,128)(2,1)S(1)}, u32[]{:S(2)}, u32[]{:S(2)}) collective-permute-start(f16[4,384,128]{2,1,0:T(8,128)(2,1)} %multiply_convert_fusion.8), channel_id=1, source_target_pairs={{0,3},{1,0},{2,1},{3,2},{4,7},{5,4},{6,5},{7,6},{8,11},{9,8},{10,9... | collective-permute-start | bytes 1179656 | tf_op jit(solution)/shard_map/ppermute | solution.py:599
  413.8 73.1 %collective-permute-start.28 = (f16[4,384,128]{2,1,0:T(8,128)(2,1)}, f16[4,384,128]{2,1,0:T(8,128)(2,1)S(1)}, u32[]{:S(2)}, u32[]{:S(2)}) collective-permute-start(f16[4,384,128]{2,1,0:T(8,128)(2,1)} %multiply_convert_fusion.7), channel_id=1, source_target_pairs={{0,2},{1,3},{2,0},{3,1},{4,6},{5,7},{6,4},{7,5},{8,10},{9,11},{10,... | collective-permute-start | bytes 1179656 | tf_op jit(solution)/shard_map/ppermute | solution.py:599
  437.7 2.0 copy-start.2
  439.7 47.3 %collective-permute-start.29 = (f16[4,384,128]{2,1,0:T(8,128)(2,1)}, f16[4,384,128]{2,1,0:T(8,128)(2,1)}, u32[]{:S(2)}, u32[]{:S(2)}) collective-permute-start(f16[4,384,128]{2,1,0:T(8,128)(2,1)} %multiply_convert_fusion.6), channel_id=1, source_target_pairs={{0,1},{1,2},{2,3},{3,0},{4,5},{5,6},{6,7},{7,4},{8,9},{9,10},{10,1... | collective-permute-start | bytes 1179656 | tf_op jit(solution)/shard_map/ppermute | solution.py:599
  445.0 20.9 %copy-start.3 = (f32[4,384,128]{2,1,0:T(8,128)S(1)}, f32[4,384,128]{2,1,0:T(8,128)}, u32[]{:S(2)}) copy-start(f32[4,384,128]{2,1,0:T(8,128)} %get-tuple-element.134.rest_6_) | copy-start | bytes 2359300
  465.9 21.0 %copy-start.5 = (f32[4,384,128]{2,1,0:T(8,128)S(1)}, f32[4,384,128]{2,1,0:T(8,128)}, u32[]{:S(2)}) copy-start(f32[4,384,128]{2,1,0:T(8,128)} %copy-done.4) | copy-start | bytes 2359300

commit v3 on v2

--- a/solution.py
+++ b/solution.py
@@ -28,6 +28,13 @@
     return None
 
 
+def wide_tile(pairs):
+    for blocks in (6, 4, 3, 2, 1):
+        if pairs % (blocks * LANES) == 0:
+            return blocks * LANES
+    return None
+
+
 def mix(table, lanes, outs, count, term):
     totals = [None] * outs
     for v in range(count):
@@ -43,13 +50,16 @@
     return pl.ds(pl.multiple_of(base + i * chunk, chunk), chunk)
 
 
-def spread(l_ref, p_ref, held):
-    held[...] = lax.dot_general(
-        p_ref[...].reshape(held.shape[0], l_ref.shape[1]),
-        l_ref[...],
-        (((1,), (1,)), ((), ())),
-        preferred_element_type=jnp.float32,
+def rows_times(p_ref, l_ref):
+    return lax.dot_general(
+        p_ref[...], l_ref[...], (((1,), (1,)), ((), ())), preferred_element_type=jnp.float32
     )
+
+
+def spread(l_ref, p_ref, far_ref, held):
+    own = p_ref.shape[0]
+    held[:own, :] = rows_times(p_ref, l_ref)
+    held[own:, :] = rows_times(far_ref, l_ref)
 
 
 def dot_exact(a, b):
@@ -62,14 +72,14 @@
     return pl.BlockSpec(x.shape, lambda i, *_: (0,) * x.ndim, pipeline_mode=pl.Buffered(1))
 
 
-def quarter_kernel(nf, parts, kept, me_ref, l_ref, k_ref, wt_ref, coef_ref, p_ref, *rest):
-    r_refs, rest = rest[:parts], rest[parts + kept :]
+def quarter_kernel(nf, parts, me_ref, l_ref, k_ref, wt_ref, coef_ref, p_ref, far_ref, *rest):
+    r_refs, rest = rest[:parts], rest[parts:]
     u_refs, rest = rest[:parts], rest[parts:]
     v_refs, (table, held, turned, mid, far) = rest[:parts], rest[parts:]
     own = nf // parts
     cols = r_refs[0].shape[2]
     table[...] = dot_exact(coef_ref[...], k_ref[...])
-    spread(l_ref, p_ref, held)
+    spread(l_ref, p_ref, far_ref, held)
 
     @pl.loop(0, table.shape[1] // LANES)
     def _(block):
@@ -100,9 +110,7 @@
             v_refs[w // own][w % own, lanes, :] = far[w].T
 
 
-def quarter_pass(
-    me, k, group, factors, kernels, weights, coef, gathered, right_side, moved, kept
-):
+def quarter_pass(me, k, first, factors, kernels, weights, coef, near, far, right_side, moved):
     own, pairs, cols = right_side.shape
     nf = weights.shape[0]
     parts = nf // own
@@ -116,7 +124,7 @@
         table = table.reshape(nf, nf, quarter)
         wide = jnp.einsum(
             "ja,pa->jp",
-            gathered.reshape(nf * cols, naux),
+            jnp.concatenate([near, far]),
             cut(factors, 0),
             preferred_element_type=jnp.float32,
         )
@@ -130,13 +138,12 @@
         )
     steps = quarter // tile
     at = lambda m: m[0] * steps + k
-    came = pl.BlockSpec((own, tile, cols), lambda i, m: (0, k - group[0], 0))
+    came = pl.BlockSpec((own, tile, cols), lambda i, m: (0, k - first, 0))
     piece = pl.BlockSpec((own, tile, cols), lambda i, m: (0, 0, 0))
     shape = jax.ShapeDtypeStruct((own, tile, cols), jnp.float32)
-    wide = jax.ShapeDtypeStruct((own, (group[1] - group[0]) * tile, cols), jnp.float32)
     out = pl.pallas_call(
-        functools.partial(quarter_kernel, nf, parts, len(kept)),
-        out_shape=[shape] * parts + [wide] * parts,
+        functools.partial(quarter_kernel, nf, parts),
+        out_shape=[shape] * (2 * parts),
         grid_spec=pltpu.PrefetchScalarGridSpec(
             num_scalar_prefetch=1,
             grid=(1,),
@@ -145,26 +152,25 @@
                 pl.BlockSpec((nf, tile), lambda i, m: (0, at(m))),
                 pl.BlockSpec((nf, tile), lambda i, m: (0, at(m))),
                 resident(coef),
-                resident(gathered),
+                resident(near),
+                resident(far),
                 pl.BlockSpec((own, tile, cols), lambda i, m: (0, at(m), 0)),
             ]
-            + [came] * (parts - 1)
-            + [pl.BlockSpec(memory_space=pl.ANY)] * len(kept),
-            out_specs=[piece] * parts + [came] * parts,
+            + [came] * (parts - 1),
+            out_specs=[piece] * (2 * parts),
             scratch_shapes=[
                 VMEM((nf * nf, tile), jnp.float32),
                 VMEM((nf * cols, tile), jnp.float32),
             ]
             + [VMEM((nf, cols, LANES), jnp.float32)] * 3,
         ),
-        input_output_aliases={6 + parts + n: parts + n for n in range(len(kept))},
-        compiler_params=pltpu.CompilerParams(vmem_limit_bytes=40 << 20),
+        compiler_params=pltpu.CompilerParams(vmem_limit_bytes=36 << 20),
         cost_estimate=pl.CostEstimate(
             flops=2 * nf * tile * cols * (naux + 32 * nf),
             bytes_accessed=16 * nf * tile * cols,
             transcendentals=0,
         ),
-    )(me.reshape(1), factors, kernels, weights, coef, gathered, right_side, *moved, *kept)
+    )(me.reshape(1), factors, kernels, weights, coef, near, far, right_side, *moved)
     return list(out[:parts]), list(out[parts:])
 
 
@@ -254,7 +260,7 @@
 def again(factors, pair_weight, projected, kept):
     pairs, naux = factors.shape
     own = pair_weight.shape[0]
-    tile = tile_of(pairs)
+    tile = wide_tile(pairs)
     return pl.pallas_call(
         functools.partial(again_kernel, own),
         out_shape=jax.ShapeDtypeStruct(kept.shape, jnp.float32),
@@ -273,16 +279,107 @@
     )(factors, pair_weight, projected, kept)
 
 
-def final_kernel(nf, parts, held_outs, me_ref, l_ref, k_ref, wt_ref, coef_ref, p_ref, *rest):
-    s_refs, rest = rest[:parts], rest[parts:]
+class Stream:
+    def __init__(self, refs, buffer, sems):
+        self.refs, self.buffer, self.sems = refs, buffer, sems
+        self.step = pl.program_id(0)
+        self.slot = lax.rem(self.step, 2)
+
+    def copy(self, n):
+        return pltpu.make_async_copy(self.refs[n], self.buffer.at[n % 2], self.sems.at[n % 2])
+
+    def ahead(self):
+        @pl.when(self.step == 0)
+        def _():
+            self.copy(0).start()
+
+        for n in range(1, len(self.refs)):
+
+            @pl.when(self.step == n - 1)
+            def _():
+                self.copy(n).start()
+
+    def here(self):
+        pltpu.make_async_copy(
+            self.refs[0], self.buffer.at[self.slot], self.sems.at[self.slot]
+        ).wait()
+        return self.buffer.at[self.slot]
+
+
+def stream_scratch(piece):
+    return [VMEM((2,) + piece.shape, piece.dtype), pltpu.SemaphoreType.DMA((2,))]
+
+
+ANYWHERE = pl.BlockSpec(memory_space=pl.ANY)
+
+
+def amplitude_kernel(pieces, me_ref, l_ref, wt_ref, p_ref, *rest):
+    refs, (a_ref, buffer, sems) = rest[:pieces], rest[pieces:]
+    own, tile, cols = a_ref.shape
+    stream = Stream(refs, buffer, sems)
+    stream.ahead()
+    wide = rows_times(p_ref, l_ref)
+    here = stream.here()
+    for f in range(own):
+        scaled = wide[f * cols : (f + 1) * cols] * wt_ref[f : f + 1, :]
+        for k in range(0, tile, LANES):
+            lanes = slice(k, k + LANES)
+            a_ref[f, lanes, :] = here[f, lanes, :] + scaled[:, lanes].T
+
+
+def amplitude(me, factors, pair_weight, near, sources):
+    own, size, cols = sources[0][0].shape
+    parts = len(sources[0])
+    pairs, naux = factors.shape
+    quarter = pairs // parts
+    if tile_of(quarter) is None:
+        wide = jnp.einsum("ja,pa->jp", near, factors, preferred_element_type=jnp.float32)
+        wide = jnp.transpose(wide.reshape(own, cols, pairs), (0, 2, 1))
+        result = wide * pair_weight[:, :, None]
+        for s in range(parts):
+            at = lax.rem(me + s, parts) * quarter
+            part_of = lax.dynamic_slice_in_dim(result, at, quarter, 1) + sources[0][s]
+            result = lax.dynamic_update_slice_in_dim(result, part_of, at, 1)
+        return result
+    steps = quarter // size
+    pieces = [x for chunk in sources for x in chunk]
+    at = lambda i, m: lax.rem(m[0] + lax.rem(i, parts), parts) * steps + lax.div(i, parts)
+    return pl.pallas_call(
+        functools.partial(amplitude_kernel, len(pieces)),
+        out_shape=jax.ShapeDtypeStruct((own, pairs, cols), jnp.float32),
+        grid_spec=pltpu.PrefetchScalarGridSpec(
+            num_scalar_prefetch=1,
+            grid=(len(pieces),),
+            in_specs=[
+                pl.BlockSpec((size, naux), lambda i, m: (at(i, m), 0)),
+                pl.BlockSpec((own, size), lambda i, m: (0, at(i, m))),
+                resident(near),
+            ]
+            + [ANYWHERE] * len(pieces),
+            out_specs=pl.BlockSpec((own, size, cols), lambda i, m: (0, at(i, m), 0)),
+            scratch_shapes=stream_scratch(pieces[0]),
+        ),
+        compiler_params=pltpu.CompilerParams(vmem_limit_bytes=20 << 20),
+        cost_estimate=pl.CostEstimate(
+            flops=2 * own * pairs * cols * naux,
+            bytes_accessed=8 * own * pairs * cols,
+            transcendentals=0,
+        ),
+    )(me.reshape(1), factors, pair_weight, near, *pieces)
+
+
+def final_kernel(nf, parts, held_outs, me_ref, l_ref, k_ref, wt_ref, coef_ref, p_ref, far_ref, *rest):
     b_refs, rest = rest[:parts], rest[parts + held_outs :]
-    a_ref, new_ref, table, held, mid, second = rest
-    own, _, cols = a_ref.shape
+    new_ref, table, held, mid, buffer, sems = rest
+    own, _, cols = new_ref.shape
+    stream = Stream(b_refs, buffer, sems)
+    stream.ahead()
     table[...] = dot_exact(coef_ref[...], k_ref[...])
     for w in range(own):
         rows = slice(w * nf, (w + 1) * nf)
         table[rows, :] = table[rows, :] * wt_ref[...]
-    spread(l_ref, p_ref, held)
+    spread(l_ref, p_ref, far_ref, held)
+    here = stream.here()
 
     @pl.loop(0, table.shape[1] // LANES)
     def _(block):
@@ -294,51 +391,37 @@
             got = mix(table, lanes, own, nf, lambda v: held[part(i, v * cols, WIDE), lanes])
             for w in range(own):
                 mid[w, rows, :] = got[w]
-                second[w, rows, :] = (
-                    wt_ref[w : w + 1, lanes] * held[part(i, w * cols, WIDE), lanes]
-                )
-
-        for s in range(parts):
-
-            @pl.when(pl.program_id(0) == s)
-            def _():
-                for w in range(own):
-                    new_ref[w, lanes, :] = b_refs[s][w, lanes, :] + mid[w].T
-                    a_ref[w, lanes, :] = s_refs[s][w, lanes, :] + second[w].T
-
-
-def final(me, k, factors, kernels, weights, coef, gathered, sources, base, outs):
-    own, size, cols = sources[0].shape
-    parts = len(sources)
+
+        for w in range(own):
+            new_ref[w, lanes, :] = here[w, lanes, :] + mid[w].T
+
+
+def final(me, k, factors, kernels, weights, coef, near, far, base, outs):
+    own, size, cols = base[0].shape
+    parts = len(base)
     nf = weights.shape[0]
     pairs, naux = factors.shape
     quarter = pairs // parts
     tile = tile_of(quarter)
-    shape = jax.ShapeDtypeStruct((own, pairs, cols), jnp.float32)
     if tile is None:
         wide = jnp.einsum(
             "ja,pa->jp",
-            gathered.reshape(nf * cols, naux),
+            jnp.concatenate([near, far]),
             factors,
             preferred_element_type=jnp.float32,
         )
         wide = jnp.transpose(wide.reshape(nf, cols, pairs), (0, 2, 1)) * weights[:, :, None]
         table = jnp.einsum("jt,tp->jp", coef, kernels, precision=EXACT).reshape(own, nf, pairs)
         new = jnp.einsum("wvp,vpc->wpc", table, wide, precision=EXACT)
-        amplitude = wide[:own]
         for s in range(parts):
             at = lax.rem(me + s, parts) * quarter
-            put = lambda x, y: lax.dynamic_update_slice_in_dim(
-                x, lax.dynamic_slice_in_dim(x, at, quarter, 1) + y, at, 1
-            )
-            amplitude, new = put(amplitude, sources[s]), put(new, base[s])
-        return amplitude, new
+            part_of = lax.dynamic_slice_in_dim(new, at, quarter, 1) + base[s]
+            new = lax.dynamic_update_slice_in_dim(new, part_of, at, 1)
+        return [new]
     at = around(parts, quarter // size, k)
-    out = pl.BlockSpec((own, size, cols), lambda i, m: (0, at(i, m), 0))
-    piece = pl.BlockSpec((own, size, cols), lambda i, m: (0, 0, 0))
-    return pl.pallas_call(
+    result = pl.pallas_call(
         functools.partial(final_kernel, nf, parts, len(outs)),
-        out_shape=(shape, shape),
+        out_shape=jax.ShapeDtypeStruct((own, pairs, cols), jnp.float32),
         grid_spec=pltpu.PrefetchScalarGridSpec(
             num_scalar_prefetch=1,
             grid=(parts,),
@@ -347,25 +430,27 @@
                 pl.BlockSpec((nf, size), lambda i, m: (0, at(i, m))),
                 pl.BlockSpec((nf, size), lambda i, m: (0, at(i, m))),
                 resident(coef),
-                resident(gathered),
+                resident(near),
+                resident(far),
             ]
-            + [piece] * (2 * parts)
-            + [pl.BlockSpec(memory_space=pl.ANY)] * len(outs),
-            out_specs=(out, out),
+            + [ANYWHERE] * (parts + len(outs)),
+            out_specs=pl.BlockSpec((own, size, cols), lambda i, m: (0, at(i, m), 0)),
             scratch_shapes=[
                 VMEM((own * nf, size), jnp.float32),
                 VMEM((nf * cols, size), jnp.float32),
+                VMEM((own, cols, LANES), jnp.float32),
             ]
-            + [VMEM((own, cols, LANES), jnp.float32)] * 2,
-        ),
-        input_output_aliases={6 + 2 * parts + n: n for n in range(len(outs))},
-        compiler_params=pltpu.CompilerParams(vmem_limit_bytes=48 << 20),
+            + stream_scratch(base[0]),
+        ),
+        input_output_aliases={7 + parts + n: n for n in range(len(outs))},
+        compiler_params=pltpu.CompilerParams(vmem_limit_bytes=26 << 20),
         cost_estimate=pl.CostEstimate(
             flops=2 * nf * parts * size * cols * naux,
-            bytes_accessed=16 * own * parts * size * cols,
+            bytes_accessed=8 * own * parts * size * cols,
             transcendentals=0,
         ),
-    )(me.reshape(1), factors, kernels, weights, coef, gathered, *sources, *base, *outs)
+    )(me.reshape(1), factors, kernels, weights, coef, near, far, *base, *outs)
+    return [result]
 
 
 class Plane:
@@ -466,7 +551,8 @@
         o_ref[c] = joined[c]
 
 
-def gather_kernel(chips, parts, x_ref, o_ref, joined, *sems):
+def gather_kernel(chips, parts, *refs):
+    x_refs, (o_ref, joined, *sems) = refs[:parts], refs[parts:]
     plane = Plane(chips)
     chip, core, pal = plane.chip, plane.core, plane.pal
     plane.greet()
@@ -478,7 +564,7 @@
     corner = along + 1 - 2 * column
     wides = []
     for s in range(parts):
-        src, dst = x_ref.at[s], joined.at[s, chip, core]
+        src, dst = x_refs[s], joined.at[s, chip, core]
         if square:
             for n, to in enumerate((across, along)):
                 copy = plane.send(src, dst, wide_sems, s * chips + n, plane.chip_at(to))
@@ -489,7 +575,7 @@
                 wides.append((s, d, copy))
     for s in range(parts):
         pairs.append(
-            plane.send(x_ref.at[s], joined.at[s, chip, core], pair_sems, s * chips, pal)
+            plane.send(x_refs[s], joined.at[s, chip, core], pair_sems, s * chips, pal)
         )
     late = []
     for s, d, copy in wides:
@@ -512,7 +598,7 @@
     for s in range(parts):
         for c in range(chips):
             o_ref[s, c] = joined[s, c]
-        o_ref[s, chip, core] = x_ref[s]
+        o_ref[s, chip, core] = x_refs[s][...]
 
 
 def dmas(count, pairs):
@@ -571,18 +657,19 @@
 def gathered_over(blocks):
     n = lax.axis_size("fac")
     chips = n // 2
-    parts, block, width = blocks.shape
+    parts = len(blocks)
+    block, width = blocks[0].shape
     flat = (parts, chips, 2, block, width)
     result = pl.pallas_call(
         functools.partial(gather_kernel, chips, parts),
         out_shape=jax.ShapeDtypeStruct(flat, jnp.bfloat16),
-        in_specs=[WHOLE],
+        in_specs=[WHOLE] * parts,
         out_specs=WHOLE,
         scratch_shapes=[VMEM(flat, jnp.bfloat16)] + dmas(parts * chips, 2),
-        compiler_params=reach_params(2),
-        cost_estimate=reach_cost(blocks.size * 8),
-    )(blocks)
-    return result.reshape(parts, n * block, width)
+        compiler_params=reach_params(2 if parts == 1 else 3),
+        cost_estimate=reach_cost(block * width * parts * 8),
+    )(*blocks)
+    return result.reshape(parts * n * block, width)
 
 
 def shards(right_side, factors, pair_weight, second_order, forward, backward):
@@ -621,12 +708,12 @@
     tie = lax.optimization_barrier
     up = 8192.0
 
-    def sliced(s, low, high):
+    def sliced(x, s, low, high):
         at = lax.rem(me + s, parts) * quarter + low * size
-        return lax.dynamic_slice_in_dim(right_side, at, (high - low) * size, 1)
+        return lax.dynamic_slice_in_dim(x, at, (high - low) * size, 1)
 
     def leaving(low, high):
-        return [(sliced(s, low, high) * up).astype(jnp.float16) for s in range(1, parts)]
+        return [(sliced(right_side, s, low, high) * up).astype(jnp.float16) for s in range(1, parts)]
 
     def passed(blocks, back):
         return [
@@ -647,16 +734,19 @@
             mine = summed(total, True)
             total = again(factors, pair_weight, mine, kept)
         block = summed(total, False)
-        return jnp.stack([shift(block, s) for s in range(parts)])
-
-    came = [passed(leaving(*groups[0]), False)]
-    blocks = ladder(first_projection())
-    if len(groups) > 1:
-        blocks, out = tie((blocks, leaving(*groups[1])))
-        came.append(passed(out, False))
-    gathered = gathered_over(blocks)
-
-    height = jnp.max(jnp.sum(jnp.abs(gathered.astype(jnp.float32)), axis=2))
+        far = [shift(block, s) for s in range(1, parts)]
+        return gathered_over([block]), far
+
+    leaves = [leaving(*g) for g in groups]
+    right_late, leaves[-1] = tie((right_side, leaves[-1]))
+    came = [passed(x, False) for x in leaves]
+    near, blocks = ladder(first_projection())
+    far = gathered_over(blocks)
+
+    def tall(x):
+        return jnp.max(jnp.sum(jnp.abs(x.astype(jnp.float32)), axis=1))
+
+    height = jnp.maximum(tall(near), tall(far))
     u_top = jnp.maximum(1.01 * reach * (R_MAX + W_MAX * L_MAX * height), 1e-30)
     v_top = jnp.maximum(1.01 * reach * (R_MAX + u_top), 1e-30)
 
@@ -665,19 +755,18 @@
 
     def added(first, rest, top, k):
         rest = [b.astype(jnp.float32) * (top / HALF_TOP) for b in rest]
-        return [sliced(s, k, k + 1) + b for s, b in enumerate([first] + rest)]
+        return [sliced(right_late, s, k, k + 1) + b for s, b in enumerate([first] + rest)]
 
     us, vs, inward = [], [], []
     for group, moved in zip(groups, came):
         moved = [m.astype(jnp.float32) * (1.0 / up) for m in moved]
-        v = ()
         for k in range(*group):
             u, v = quarter_pass(
-                me, k, group, factors, kernels, weights, coef, gathered, right_side, moved, v
+                me, k, group[0], factors, kernels, weights, coef, near, far, right_side, moved
             )
             inward.append(passed(halved(u, u_top), True))
             us.append(u)
-        vs.append(v)
+            vs.append(v)
     sources = []
     total = jnp.zeros((own * cols, naux), jnp.float32)
     for k in range(chunks):
@@ -686,23 +775,24 @@
         sources.append(added(us[k][0], inward[k], u_top, k))
         total = project(me, k, factors, sources[k], total)
 
-    out, total = tie((halved(vs[0], v_top), total))
+    halves = []
+    for v in vs:
+        halves.append(halved(v, v_top))
+    out, total = tie((halves[0], total))
     back = [passed(out, True)]
-    blocks = ladder(total)
-    if len(groups) > 1:
-        blocks, out = tie((blocks, halved(vs[1], v_top)))
-        back.append(passed(out, True))
-    gathered = gathered_over(blocks)
-    outs = ()
-    for (low, high), first, moved in zip(groups, vs, back):
-        gathered, moved, outs = tie((gathered, moved, outs))
-        for k in range(low, high):
-            rest = [m[:, (k - low) * size : (k - low + 1) * size] for m in [first[0]] + moved]
-            base = added(rest[0], rest[1:], v_top, k)
-            outs = final(
-                me, k, factors, kernels, weights, coef[: own * nf], gathered, sources[k], base, outs
-            )
-    return outs
+    near, blocks = ladder(total)
+    for k in range(1, chunks):
+        back.append(passed(halves[k], True))
+    amplitudes = amplitude(me, factors, pair_weight, near, sources)
+    far = gathered_over(blocks)
+    outs = []
+    for k in range(chunks):
+        back[k], outs = tie((back[k], outs))
+        base = added(vs[k][0], back[k], v_top, k)
+        outs = final(
+            me, k, factors, kernels, weights, coef[: own * nf], near, far, base, outs
+        )
+    return amplitudes, outs[0]
 
 
 def solution(mesh):

time: 518 us -> 544 us (1.050)
  the two profiles are of different devices: /device:TPU:0 before, /device:TPU:24 now
where the time goes in v3:
time: 544 us; the launch traced here: 537 us
  Pallas kernels  275 us (51%)
  starting transfers between devices  120 us (22%)
  waiting for transfers between devices  86 us (16%)
  other arithmetic  35.4 us (7%)
  matrix products  11.4 us (2%)
    ppermute x33, starting transfers between devices, shift(): lax.ppermute(x, 'freq', [(i, (i + by) % parts) for i in range(parts)])  120 us
    ppermute x33, waiting for transfers between devices, shift(): lax.ppermute(x, 'freq', [(i, (i + by) % parts) for i in range(parts)])  86 us
    pallas_call x4, Pallas kernels, gathered_over(): pl.pallas_call(functools.partial(gather_kernel, chips, parts), out_shape=...  58.3 us
    pallas_call x3, Pallas kernels, final(): pl.pallas_call(functools.partial(final_kernel, nf, parts, len(outs)), out...  51.1 us
    pallas_call x3, Pallas kernels, quarter_pass(): pl.pallas_call(functools.partial(quarter_kernel, nf, parts), out_shape=[s...  41.9 us
    pallas_call x2, Pallas kernels, summed(): pl.pallas_call(functools.partial(sum_kernel, chips), out_shape=jax.ShapeD...  39.8 us
    pallas_call x2, Pallas kernels, again(): pl.pallas_call(functools.partial(again_kernel, own), out_shape=jax.ShapeD...  31.7 us
    pallas_call x2, Pallas kernels, summed(): pl.pallas_call(functools.partial(reduce_kernel, chips), out_shape=jax.Sha...  22.5 us
  transfers between devices with their start and end apart: 33, of which 6 were waited for; matrix products, arithmetic and copies ran while one was open for 8% of the time, Pallas kernels for 38%

profile of v3, /device:TPU:24, one launch (start us, length us, event | category | flops | bytes accessed | tf_op | source)
XLA Modules:
  0.0 537.0 jit_solution(7322449313199840230)
XLA Ops:
  0.6 1.6 pad_maximum_fusion.1
  2.7 10.4 %fusion = f32[4,128,1024]{2,1,0:T(8,128)S(1)} fusion(bf16[4608,1024]{1,0:T(8,128)(2,1)} %l_ref.23, f32[4,4608,128]{2,1,0:T(8,128)} %rest_0_.5), kind=kOutput, calls=%fused_computation | convolution fusion | flops 4834197504 | bytes 20971520 | tf_op jit(solution)/shard_map/pa,fpc->fca/dot_general | solution.py:724
  13.1 20.4 %shard_map.77 = bf16[4,2,64,1024]{3,2,1,0:T(8,128)(2,1)S(1)} custom-call(f32[4,2,64,1024]{3,2,1,0:T(8,128)S(1)} %bitcast.43), custom_call_target="tpu_custom_call" | custom-call | flops 20971520 | bytes 20971520 | tf_op jit(solution)/shard_map/pallas_call | solution.py:642
  33.6 15.7 %shard_map.78 = f32[512,1024]{1,0:T(8,128)S(1)} custom-call(bf16[4608,1024]{1,0:T(8,128)(2,1)} %l_ref.23, f32[4,4608]{1,0:T(4,128)S(1)} %copy-done.16, bf16[512,1024]{1,0:T(8,128)(2,1)S(1)} %bitcast.50, f32[512,1024]{1,0:T(8,128)S(1)} %bitcast.44), custom_call_target="tpu_custom_call" | custom-call | flops 9663676416 | bytes 9437184 | tf_op jit(solution)/shard_map/pallas_call | solution.py:264
  49.3 11.2 %shard_map.79.refs_0_ = bf16[64,1024]{1,0:T(8,128)(2,1)S(1)} custom-call(f32[4,2,64,1024]{3,2,1,0:T(8,128)S(1)} %bitcast.48), custom_call_target="tpu_custom_call" | custom-call | flops 10485760 | bytes 10485760 | tf_op jit(solution)/shard_map/pallas_call | solution.py:633
  60.6 3.6 collective-permute-start.5
  64.5 2.1 collective-permute-start.3
  67.3 10.6 %shard_map.80 = bf16[1,4,2,64,1024]{4,3,2,1,0:T(8,128)(2,1)S(1)} custom-call(bf16[64,1024]{1,0:T(8,128)(2,1)S(1)} %shard_map.79.refs_0_), custom_call_target="tpu_custom_call" | custom-call | flops 20971520 | bytes 20971520 | tf_op jit(solution)/shard_map/pallas_call | solution.py:663
  78.4 2.7 multiply_convert_fusion.18
  83.3 4.1 multiply_convert_fusion
  87.4 1.9 collective-permute-start
  90.7 1.5 collective-permute-start.10
  92.2 0.9 copy-done.18
  93.1 0.9 copy-done.20
  94.0 18.5 %shard_map.81 = bf16[3,4,2,64,1024]{4,3,2,1,0:T(8,128)(2,1)S(1)} custom-call(bf16[64,1024]{1,0:T(8,128)(2,1)S(1)} %copy-done.20, bf16[64,1024]{1,0:T(8,128)(2,1)S(1)} %copy-done.18, bf16[64,1024]{1,0:T(8,128)(2,1)S(1)} %collective-permute-done.5.refs_2_), custom_call_target="tpu_custom_call" | custom-call | flops 62914560 | bytes 62914560 | tf_op jit(solution)/shard_map/pallas_call | solution.py:663
  116.2 1.5 collective-permute-start.8
  117.7 2.2 collective-permute-start.7
  119.8 1.2 pad_maximum_fusion
  121.1 2.5 collective-permute-start.6
  123.6 1.1 convert_multiply_fusion.5.rest_1_
  124.6 1.1 convert_multiply_fusion.4.rest_2_
  125.7 3.9 collective-permute-done.11
  129.7 14.0 %shard_map.83 = (f32[4,384,128]{2,1,0:T(8,128)S(1)}, f32[4,384,128]{2,1,0:T(8,128)S(1)}, f32[4,384,128]{2,1,0:T(8,128)S(1)}, f32[4,384,128]{2,1,0:T(8,128)S(1)},...) custom-call(s32[1]{0:T(128)} %bitcast.me_ref, ...), custom_call_target="tpu_custom_call" | custom-call | flops 2415919104 | bytes 12582912 | tf_op jit(solution)/shard_map/pallas_call | solution.py:144
  143.7 1.0 multiply_convert_fusion.17
  146.3 1.6 collective-permute-start.14
  147.9 0.8 multiply_convert_fusion.8
  148.8 0.9 multiply_convert_fusion.7
  150.6 29.0 %collective-permute-done.7 = f16[4,768,128]{2,1,0:T(8,128)(2,1)S(1)} collective-permute-done((f16[4,768,128]{2,1,0:T(8,128)(2,1)}, f16[4,768,128]{2,1,0:T(8,128)(2,1)S(1)}, u32[]{:S(2)}, u32[]{:S(2)}) %collective-permute-start.7) | collective-permute-done | bytes 786464 | tf_op jit(solution)/shard_map/ppermute | solution.py:686
  179.9 14.0 %shard_map.84 = (f32[4,384,128]{2,1,0:T(8,128)S(1)}, f32[4,384,128]{2,1,0:T(8,128)S(1)}, f32[4,384,128]{2,1,0:T(8,128)S(1)}, f32[4,384,128]{2,1,0:T(8,128)S(1)},...) custom-call(s32[1]{0:T(128)} %bitcast.me_ref, ...), custom_call_target="tpu_custom_call" | custom-call | flops 2415919104 | bytes 12582912 | tf_op jit(solution)/shard_map/pallas_call | solution.py:144
  193.9 0.9 copy-done.10
  194.8 0.9 copy-done.14
  195.6 14.0 %shard_map.82 = (f32[4,384,128]{2,1,0:T(8,128)S(1)}, f32[4,384,128]{2,1,0:T(8,128)S(1)}, f32[4,384,128]{2,1,0:T(8,128)S(1)}, f32[4,384,128]{2,1,0:T(8,128)S(1)},...) custom-call(s32[1]{0:T(128)} %bitcast.me_ref, ...), custom_call_target="tpu_custom_call" | custom-call | flops 2415919104 | bytes 12582912 | tf_op jit(solution)/shard_map/pallas_call | solution.py:144
  209.6 0.9 multiply_convert_fusion.23
  211.6 0.8 multiply_convert_fusion.4
  212.7 36.0 %collective-permute-start.20 = (f16[4,384,128]{2,1,0:T(8,128)(2,1)S(1)}, f16[4,384,128]{2,1,0:T(8,128)(2,1)S(1)}, u32[]{:S(2)}, u32[]{:S(2)}) collective-permute-start(f16[4,384,128]{2,1,0:T(8,128)(2,1)S(1)} %multiply_convert_fusion.9), channel_id=1, source_target_pairs={{0,1},{1,2},{2,3},{3,0},{4,5},{5,6},{6,7},{7,4},{8,9},{9,10},{10,1... | collective-permute-start | bytes 1179656 | tf_op jit(solution)/shard_map/ppermute | solution.py:686
  251.2 7.1 %collective-permute-done.20 = f16[4,384,128]{2,1,0:T(8,128)(2,1)S(1)} collective-permute-done((f16[4,384,128]{2,1,0:T(8,128)(2,1)S(1)}, f16[4,384,128]{2,1,0:T(8,128)(2,1)S(1)}, u32[]{:S(2)}, u32[]{:S(2)}) %collective-permute-start.20) | collective-permute-done | bytes 393248 | tf_op jit(solution)/shard_map/ppermute | solution.py:686
  258.3 4.3 collective-permute-start.17
  262.6 20.3 %collective-permute-done.19 = f16[4,384,128]{2,1,0:T(8,128)(2,1)S(1)} collective-permute-done((f16[4,384,128]{2,1,0:T(8,128)(2,1)S(1)}, f16[4,384,128]{2,1,0:T(8,128)(2,1)S(1)}, u32[]{:S(2)}, u32[]{:S(2)}) %collective-permute-start.19) | collective-permute-done | bytes 393248 | tf_op jit(solution)/shard_map/ppermute | solution.py:686
  282.9 18.0 %collective-permute-start.15 = (f16[4,384,128]{2,1,0:T(8,128)(2,1)S(1)}, f16[4,384,128]{2,1,0:T(8,128)(2,1)S(1)}, u32[]{:S(2)}, u32[]{:S(2)}) collective-permute-start(f16[4,384,128]{2,1,0:T(8,128)(2,1)S(1)} %multiply_convert_fusion.14), channel_id=1, source_target_pairs={{0,3},{1,0},{2,1},{3,2},{4,7},{5,4},{6,5},{7,6},{8,11},{9,8},{10,9... | collective-permute-start | bytes 1179656 | tf_op jit(solution)/shard_map/ppermute | solution.py:686
  301.0 2.3 multiply_add_fusion.15
  303.5 4.7 shard_map.85.rest_4_
  308.2 2.5 collective-permute-start.12
  310.8 13.1 %collective-permute-done.16 = f16[4,384,128]{2,1,0:T(8,128)(2,1)S(1)} collective-permute-done((f16[4,384,128]{2,1,0:T(8,128)(2,1)S(1)}, f16[4,384,128]{2,1,0:T(8,128)(2,1)S(1)}, u32[]{:S(2)}, u32[]{:S(2)}) %collective-permute-start.16) | collective-permute-done | bytes 393248 | tf_op jit(solution)/shard_map/ppermute | solution.py:686
  323.9 2.3 multiply_add_fusion.12
  326.2 4.7 shard_map.86.rest_4_
  330.9 2.3 multiply_add_fusion.9
  333.3 5.3 shard_map.87.x_ref
  338.6 19.4 %shard_map.88 = bf16[4,2,64,1024]{3,2,1,0:T(8,128)(2,1)S(1)} custom-call(f32[4,2,64,1024]{3,2,1,0:T(8,128)S(1)} %bitcast.42), custom_call_target="tpu_custom_call" | custom-call | flops 20971520 | bytes 20971520 | tf_op jit(solution)/shard_map/pallas_call | solution.py:642
  358.0 16.0 %shard_map.89 = f32[512,1024]{1,0:T(8,128)S(1)} custom-call(bf16[4608,1024]{1,0:T(8,128)(2,1)} %l_ref.23, f32[4,4608]{1,0:T(4,128)S(1)} %copy-done.16, bf16[512,1024]{1,0:T(8,128)(2,1)S(1)} %bitcast.51, f32[512,1024]{1,0:T(8,128)S(1)} %shard_map.87.x_ref), custom_call_target="tpu_custom_call" | custom-call | flops 9663676416 | bytes 9437184 | tf_op jit(solution)/shard_map/pallas_call | solution.py:264
  374.1 11.3 %shard_map.90.refs_0_ = bf16[64,1024]{1,0:T(8,128)(2,1)S(1)} custom-call(f32[4,2,64,1024]{3,2,1,0:T(8,128)S(1)} %bitcast.49), custom_call_target="tpu_custom_call" | custom-call | flops 10485760 | bytes 10485760 | tf_op jit(solution)/shard_map/pallas_call | solution.py:633
  385.6 3.9 collective-permute-start.21
  390.0 1.5 collective-permute-start.31
  391.5 10.7 %shard_map.91 = bf16[1,4,2,64,1024]{4,3,2,1,0:T(8,128)(2,1)S(1)} custom-call(bf16[64,1024]{1,0:T(8,128)(2,1)S(1)} %shard_map.90.refs_0_), custom_call_target="tpu_custom_call" | custom-call | flops 20971520 | bytes 20971520 | tf_op jit(solution)/shard_map/pallas_call | solution.py:663
  402.2 3.1 collective-permute-start.32
  405.4 14.8 %shard_map.92 = f32[4,4608,128]{2,1,0:T(8,128)} custom-call(s32[1]{0:T(128)} %bitcast.me_ref, bf16[4608,1024]{1,0:T(8,128)(2,1)S(1)} %bitcast.28, f32[4,4608]{1,0:T(4,128)S(1)} %copy-done.16, bf16[512,1024]{1,0:T(8,128)(2,1)S(1)} %bitcast.35, f32[4,384,128]{2,1,0:T(8,128)S(1)} %get-tuple-element.127.rest_0_, f32[4,384,128]{2,1,0:T(8,128)S(1)} %get-tuple-element.126.rest_1_, ...), custom_call_target="tpu_custom_call" | custom-call | flops 4831838208 | bytes 18874368 | tf_op jit(solution)/shard_map/pallas_call | solution.py:347
  420.3 1.0 collective-permute-start.25
  421.3 18.5 %shard_map.93 = bf16[3,4,2,64,1024]{4,3,2,1,0:T(8,128)(2,1)S(1)} custom-call(bf16[64,1024]{1,0:T(8,128)(2,1)S(1)} %collective-permute-done.21.refs_0_, bf16[64,1024]{1,0:T(8,128)(2,1)S(1)} %collective-permute-done.22.refs_1_, bf16[64,1024]{1,0:T(8,128)(2,1)S(1)} %collective-permute-done.23.refs_2_), custom_call_target="tpu_custom_call" | custom-call | flops 62914560 | bytes 62914560 | tf_op jit(solution)/shard_map/pallas_call | solution.py:663
  439.9 3.1 collective-permute-start.29
  443.1 26.5 %collective-permute-start.27 = (f16[4,384,128]{2,1,0:T(8,128)(2,1)S(1)}, f16[4,384,128]{2,1,0:T(8,128)(2,1)S(1)}, u32[]{:S(2)}, u32[]{:S(2)}) collective-permute-start(f16[4,384,128]{2,1,0:T(8,128)(2,1)S(1)} %copy-done.25), channel_id=1, source_target_pairs={{0,3},{1,0},{2,1},{3,2},{4,7},{5,4},{6,5},{7,6},{8,11},{9,8},{10,9... | collective-permute-start | bytes 1179656 | tf_op jit(solution)/shard_map/ppermute | solution.py:686
  469.5 2.3 multiply_add_fusion.6
  472.0 17.0 %shard_map.94.rest_4_ = f32[4,4608,128]{2,1,0:T(8,128)} custom-call(s32[1]{0:T(128)} %bitcast.me_ref, bf16[4608,1024]{1,0:T(8,128)(2,1)S(1)} %bitcast.28, f32[16,4608]{1,0:T(8,128)S(1)} %get-tuple-element.135.k_ref, f32[16,4608]{1,0:T(8,128)S(1)} %get-tuple-element.134.wt_ref, f32[64,16]{1,0:T(8,128)S(1)} %bitcast.54, bf16[512,1024]{1,0:T(8,128)(2,1)S(1)} %bitcast.36, ...), custom_call_target="tpu_custom_call" | custom-call | flops 6442450944 | bytes 6291456 | tf_op jit(solution)/shard_map/pallas_call | solution.py:422
  489.1 12.6 %collective-permute-done.28 = f16[4,384,128]{2,1,0:T(8,128)(2,1)S(1)} collective-permute-done((f16[4,384,128]{2,1,0:T(8,128)(2,1)S(1)}, f16[4,384,128]{2,1,0:T(8,128)(2,1)S(1)}, u32[]{:S(2)}, u32[]{:S(2)}) %collective-permute-start.28) | collective-permute-done | bytes 393248 | tf_op jit(solution)/shard_map/ppermute | solution.py:686
  502.1 17.0 %shard_map.95.rest_4_ = f32[4,4608,128]{2,1,0:T(8,128)} custom-call(s32[1]{0:T(128)} %bitcast.me_ref, bf16[4608,1024]{1,0:T(8,128)(2,1)S(1)} %bitcast.28, f32[16,4608]{1,0:T(8,128)S(1)} %get-tuple-element.135.k_ref, f32[16,4608]{1,0:T(8,128)S(1)} %get-tuple-element.134.wt_ref, f32[64,16]{1,0:T(8,128)S(1)} %bitcast.55, ...), custom_call_target="tpu_custom_call", output_to_operand_aliasing={{}: (11, {})} | custom-call | flops 6442450944 | bytes 6291456 | tf_op jit(solution)/shard_map/pallas_call | solution.py:422
  519.7 17.0 %shard_map.96 = f32[4,4608,128]{2,1,0:T(8,128)} custom-call(s32[1]{0:T(128)} %bitcast.me_ref, bf16[4608,1024]{1,0:T(8,128)(2,1)S(1)} %bitcast.28, f32[16,4608]{1,0:T(8,128)S(1)} %get-tuple-element.135.k_ref, f32[16,4608]{1,0:T(8,128)S(1)} %get-tuple-element.134.wt_ref, f32[64,16]{1,0:T(8,128)S(1)} %bitcast.56, ...), custom_call_target="tpu_custom_call", output_to_operand_aliasing={{}: (11, {})} | custom-call | flops 6442450944 | bytes 6291456 | tf_op jit(solution)/shard_map/pallas_call | solution.py:422
  (154 shorter events, 16.1 us)
Async XLA Ops:
  2.2 113.1 %collective-permute-start.2 = (f32[2,4,4608]{2,1,0:T(4,128)}, f32[2,4,4608]{2,1,0:T(4,128)}, u32[]{:S(2)}, u32[]{:S(2)}) collective-permute-start(f32[2,4,4608]{2,1,0:T(4,128)} %pad_maximum_fusion.1), channel_id=1, source_target_pairs={{0,3},{1,0},{2,1},{3,2},{4,7},{5,4},{6,5},{7,6},{8,11},{9,8},{10,9... | collective-permute-start | bytes 442376 | tf_op jit(solution)/shard_map/ppermute | solution.py:686
  2.7 113.5 %collective-permute-start.1 = (f32[2,4,4608]{2,1,0:T(4,128)}, f32[2,4,4608]{2,1,0:T(4,128)}, u32[]{:S(2)}, u32[]{:S(2)}) collective-permute-start(f32[2,4,4608]{2,1,0:T(4,128)} %pad_maximum_fusion.1), channel_id=1, source_target_pairs={{0,2},{1,3},{2,0},{3,1},{4,6},{5,7},{6,4},{7,5},{8,10},{9,11},{10,... | collective-permute-start | bytes 442376 | tf_op jit(solution)/shard_map/ppermute | solution.py:686
  13.1 20.4 %copy-start.16 = (f32[4,4608]{1,0:T(4,128)S(1)}, f32[4,4608]{1,0:T(4,128)}, u32[]{:S(2)}) copy-start(f32[4,4608]{1,0:T(4,128)} %wt_ref.5) | copy-start | bytes 221188
  49.3 17.3 %copy-start.31 = (f32[16,16]{1,0:T(8,128)S(1)}, f32[16,16]{1,0:T(8,128)}, u32[]{:S(2)}) copy-start(f32[16,16]{1,0:T(8,128)} %param.10) | copy-start | bytes 3076
  49.3 17.3 %copy-start.32 = (f32[16,16]{1,0:T(8,128)S(1)}, f32[16,16]{1,0:T(8,128)}, u32[]{:S(2)}) copy-start(f32[16,16]{1,0:T(8,128)} %param.11) | copy-start | bytes 3076
  60.6 26.8 %collective-permute-start.5 = (bf16[64,1024]{1,0:T(8,128)(2,1)S(1)}, bf16[64,1024]{1,0:T(8,128)(2,1)S(1)}, u32[]{:S(2)}, u32[]{:S(2)}) collective-permute-start(bf16[64,1024]{1,0:T(8,128)(2,1)S(1)} %shard_map.79.refs_0_), channel_id=1, source_target_pairs={{0,3},{1,0},{2,1},{3,2},{4,7},{5,4},{6,5},{7,6},{8,11},{9,8},{10,9... | collective-permute-start | bytes 393224 | tf_op jit(solution)/shard_map/ppermute | solution.py:686
  64.2 25.2 %collective-permute-start.4 = (bf16[64,1024]{1,0:T(8,128)(2,1)S(1)}, bf16[64,1024]{1,0:T(8,128)(2,1)S(1)}, u32[]{:S(2)}, u32[]{:S(2)}) collective-permute-start(bf16[64,1024]{1,0:T(8,128)(2,1)S(1)} %shard_map.79.refs_0_), channel_id=1, source_target_pairs={{0,2},{1,3},{2,0},{3,1},{4,6},{5,7},{6,4},{7,5},{8,10},{9,11},{10,... | collective-permute-start | bytes 393224 | tf_op jit(solution)/shard_map/ppermute | solution.py:686
  64.5 25.5 %collective-permute-start.3 = (bf16[64,1024]{1,0:T(8,128)(2,1)S(1)}, bf16[64,1024]{1,0:T(8,128)(2,1)S(1)}, u32[]{:S(2)}, u32[]{:S(2)}) collective-permute-start(bf16[64,1024]{1,0:T(8,128)(2,1)S(1)} %shard_map.79.refs_0_), channel_id=1, source_target_pairs={{0,1},{1,2},{2,3},{3,0},{4,5},{5,6},{6,7},{7,4},{8,9},{9,10},{10,1... | collective-permute-start | bytes 393224 | tf_op jit(solution)/shard_map/ppermute | solution.py:686
  87.4 30.3 %collective-permute-start = (f32[2,4,4608]{2,1,0:T(4,128)}, f32[2,4,4608]{2,1,0:T(4,128)}, u32[]{:S(2)}, u32[]{:S(2)}) collective-permute-start(f32[2,4,4608]{2,1,0:T(4,128)} %pad_maximum_fusion.1), channel_id=1, source_target_pairs={{0,1},{1,2},{2,3},{3,0},{4,5},{5,6},{6,7},{7,4},{8,9},{9,10},{10,1... | collective-permute-start | bytes 442376 | tf_op jit(solution)/shard_map/ppermute | solution.py:686
  90.0 31.1 %collective-permute-start.9 = (f16[4,384,128]{2,1,0:T(8,128)(2,1)}, f16[4,384,128]{2,1,0:T(8,128)(2,1)}, u32[]{:S(2)}, u32[]{:S(2)}) collective-permute-start(f16[4,384,128]{2,1,0:T(8,128)(2,1)} %get-tuple-element.57), channel_id=1, source_target_pairs={{0,1},{1,2},{2,3},{3,0},{4,5},{5,6},{6,7},{7,4},{8,9},{9,10},{10,1... | collective-permute-start | bytes 1179656 | tf_op jit(solution)/shard_map/ppermute | solution.py:686
  90.7 34.0 %collective-permute-start.10 = (f16[4,384,128]{2,1,0:T(8,128)(2,1)}, f16[4,384,128]{2,1,0:T(8,128)(2,1)}, u32[]{:S(2)}, u32[]{:S(2)}) collective-permute-start(f16[4,384,128]{2,1,0:T(8,128)(2,1)} %get-tuple-element.58), channel_id=1, source_target_pairs={{0,2},{1,3},{2,0},{3,1},{4,6},{5,7},{6,4},{7,5},{8,10},{9,11},{10,... | collective-permute-start | bytes 1179656 | tf_op jit(solution)/shard_map/ppermute | solution.py:686
  112.6 7.3 %copy-start.30 = (f32[4,4608]{1,0:T(4,128)S(1)}, f32[4,4608]{1,0:T(4,128)}, u32[]{:S(2)}) copy-start(f32[4,4608]{1,0:T(4,128)} %param.9) | copy-start | bytes 221188
  115.3 5.7 %copy-start.21 = (f16[4,768,128]{2,1,0:T(8,128)(2,1)S(1)}, f16[4,768,128]{2,1,0:T(8,128)(2,1)}, u32[]{:S(2)}) copy-start(f16[4,768,128]{2,1,0:T(8,128)(2,1)} %get-tuple-element.133) | copy-start | bytes 2359300
  115.4 14.2 %collective-permute-start.11 = (f16[4,384,128]{2,1,0:T(8,128)(2,1)}, f16[4,384,128]{2,1,0:T(8,128)(2,1)S(1)}, u32[]{:S(2)}, u32[]{:S(2)}) collective-permute-start(f16[4,384,128]{2,1,0:T(8,128)(2,1)} %get-tuple-element.59), channel_id=1, source_target_pairs={{0,3},{1,0},{2,1},{3,2},{4,7},{5,4},{6,5},{7,6},{8,11},{9,8},{10,9... | collective-permute-start | bytes 1179656 | tf_op jit(solution)/shard_map/ppermute | solution.py:686
  116.2 34.3 %collective-permute-start.8 = (f16[4,768,128]{2,1,0:T(8,128)(2,1)}, f16[4,768,128]{2,1,0:T(8,128)(2,1)S(1)}, u32[]{:S(2)}, u32[]{:S(2)}) collective-permute-start(f16[4,768,128]{2,1,0:T(8,128)(2,1)} %get-tuple-element.131), channel_id=1, source_target_pairs={{0,3},{1,0},{2,1},{3,2},{4,7},{5,4},{6,5},{7,6},{8,11},{9,8},{10,9... | collective-permute-start | bytes 2359304 | tf_op jit(solution)/shard_map/ppermute | solution.py:686
  117.7 61.9 %collective-permute-start.7 = (f16[4,768,128]{2,1,0:T(8,128)(2,1)}, f16[4,768,128]{2,1,0:T(8,128)(2,1)S(1)}, u32[]{:S(2)}, u32[]{:S(2)}) collective-permute-start(f16[4,768,128]{2,1,0:T(8,128)(2,1)} %get-tuple-element.132), channel_id=1, source_target_pairs={{0,2},{1,3},{2,0},{3,1},{4,6},{5,7},{6,4},{7,5},{8,10},{9,11},{10,... | collective-permute-start | bytes 2359304 | tf_op jit(solution)/shard_map/ppermute | solution.py:686
  121.0 8.7 %copy-start.1 = (bf16[1,4,2,64,1024]{4,3,2,1,0:T(8,128)(2,1)S(1)}, bf16[1,4,2,64,1024]{4,3,2,1,0:T(8,128)(2,1)}, u32[]{:S(2)}) copy-start(bf16[1,4,2,64,1024]{4,3,2,1,0:T(8,128)(2,1)} %copy-done) | copy-start | bytes 3145732
  121.1 58.6 %collective-permute-start.6 = (f16[4,768,128]{2,1,0:T(8,128)(2,1)S(1)}, f16[4,768,128]{2,1,0:T(8,128)(2,1)S(1)}, u32[]{:S(2)}, u32[]{:S(2)}) collective-permute-start(f16[4,768,128]{2,1,0:T(8,128)(2,1)S(1)} %copy-done.21), channel_id=1, source_target_pairs={{0,1},{1,2},{2,3},{3,0},{4,5},{5,6},{6,7},{7,4},{8,9},{9,10},{10,1... | collective-permute-start | bytes 2359304 | tf_op jit(solution)/shard_map/ppermute | solution.py:686
  143.7 5.1 copy-start.8
  146.3 184.6 %collective-permute-start.14 = (f16[4,384,128]{2,1,0:T(8,128)(2,1)}, f16[4,384,128]{2,1,0:T(8,128)(2,1)S(1)}, u32[]{:S(2)}, u32[]{:S(2)}) collective-permute-start(f16[4,384,128]{2,1,0:T(8,128)(2,1)} %multiply_convert_fusion.15), channel_id=1, source_target_pairs={{0,1},{1,2},{2,3},{3,0},{4,5},{5,6},{6,7},{7,4},{8,9},{9,10},{10,1... | collective-permute-start | bytes 1179656 | tf_op jit(solution)/shard_map/ppermute | solution.py:686
  147.9 183.0 %collective-permute-start.13 = (f16[4,384,128]{2,1,0:T(8,128)(2,1)}, f16[4,384,128]{2,1,0:T(8,128)(2,1)S(1)}, u32[]{:S(2)}, u32[]{:S(2)}) collective-permute-start(f16[4,384,128]{2,1,0:T(8,128)(2,1)} %multiply_convert_fusion.16), channel_id=1, source_target_pairs={{0,2},{1,3},{2,0},{3,1},{4,6},{5,7},{6,4},{7,5},{8,10},{9,11},{10,... | collective-permute-start | bytes 1179656 | tf_op jit(solution)/shard_map/ppermute | solution.py:686
  212.7 45.5 %collective-permute-start.20 = (f16[4,384,128]{2,1,0:T(8,128)(2,1)S(1)}, f16[4,384,128]{2,1,0:T(8,128)(2,1)S(1)}, u32[]{:S(2)}, u32[]{:S(2)}) collective-permute-start(f16[4,384,128]{2,1,0:T(8,128)(2,1)S(1)} %multiply_convert_fusion.9), channel_id=1, source_target_pairs={{0,1},{1,2},{2,3},{3,0},{4,5},{5,6},{6,7},{7,4},{8,9},{9,10},{10,1... | collective-permute-start | bytes 1179656 | tf_op jit(solution)/shard_map/ppermute | solution.py:686
  248.7 34.2 %collective-permute-start.19 = (f16[4,384,128]{2,1,0:T(8,128)(2,1)S(1)}, f16[4,384,128]{2,1,0:T(8,128)(2,1)S(1)}, u32[]{:S(2)}, u32[]{:S(2)}) collective-permute-start(f16[4,384,128]{2,1,0:T(8,128)(2,1)S(1)} %multiply_convert_fusion.10), channel_id=1, source_target_pairs={{0,2},{1,3},{2,0},{3,1},{4,6},{5,7},{6,4},{7,5},{8,10},{9,11},{10,... | collective-permute-start | bytes 1179656 | tf_op jit(solution)/shard_map/ppermute | solution.py:686
  248.7 34.2 %collective-permute-start.18 = (f16[4,384,128]{2,1,0:T(8,128)(2,1)S(1)}, f16[4,384,128]{2,1,0:T(8,128)(2,1)S(1)}, u32[]{:S(2)}, u32[]{:S(2)}) collective-permute-start(f16[4,384,128]{2,1,0:T(8,128)(2,1)S(1)} %multiply_convert_fusion.11), channel_id=1, source_target_pairs={{0,3},{1,0},{2,1},{3,2},{4,7},{5,4},{6,5},{7,6},{8,11},{9,8},{10,9... | collective-permute-start | bytes 1179656 | tf_op jit(solution)/shard_map/ppermute | solution.py:686
  258.3 49.9 %collective-permute-start.17 = (f16[4,384,128]{2,1,0:T(8,128)(2,1)S(1)}, f16[4,384,128]{2,1,0:T(8,128)(2,1)S(1)}, u32[]{:S(2)}, u32[]{:S(2)}) collective-permute-start(f16[4,384,128]{2,1,0:T(8,128)(2,1)S(1)} %multiply_convert_fusion.12), channel_id=1, source_target_pairs={{0,1},{1,2},{2,3},{3,0},{4,5},{5,6},{6,7},{7,4},{8,9},{9,10},{10,1... | collective-permute-start | bytes 1179656 | tf_op jit(solution)/shard_map/ppermute | solution.py:686
  282.9 41.0 %collective-permute-start.16 = (f16[4,384,128]{2,1,0:T(8,128)(2,1)S(1)}, f16[4,384,128]{2,1,0:T(8,128)(2,1)S(1)}, u32[]{:S(2)}, u32[]{:S(2)}) collective-permute-start(f16[4,384,128]{2,1,0:T(8,128)(2,1)S(1)} %multiply_convert_fusion.13), channel_id=1, source_target_pairs={{0,2},{1,3},{2,0},{3,1},{4,6},{5,7},{6,4},{7,5},{8,10},{9,11},{10,... | collective-permute-start | bytes 1179656 | tf_op jit(solution)/shard_map/ppermute | solution.py:686
  282.9 41.0 %collective-permute-start.15 = (f16[4,384,128]{2,1,0:T(8,128)(2,1)S(1)}, f16[4,384,128]{2,1,0:T(8,128)(2,1)S(1)}, u32[]{:S(2)}, u32[]{:S(2)}) collective-permute-start(f16[4,384,128]{2,1,0:T(8,128)(2,1)S(1)} %multiply_convert_fusion.14), channel_id=1, source_target_pairs={{0,3},{1,0},{2,1},{3,2},{4,7},{5,4},{6,5},{7,6},{8,11},{9,8},{10,9... | collective-permute-start | bytes 1179656 | tf_op jit(solution)/shard_map/ppermute | solution.py:686
  308.2 22.7 %collective-permute-start.12 = (f16[4,384,128]{2,1,0:T(8,128)(2,1)}, f16[4,384,128]{2,1,0:T(8,128)(2,1)S(1)}, u32[]{:S(2)}, u32[]{:S(2)}) collective-permute-start(f16[4,384,128]{2,1,0:T(8,128)(2,1)} %multiply_convert_fusion.17), channel_id=1, source_target_pairs={{0,3},{1,0},{2,1},{3,2},{4,7},{5,4},{6,5},{7,6},{8,11},{9,8},{10,9... | collective-permute-start | bytes 1179656 | tf_op jit(solution)/shard_map/ppermute | solution.py:686
  333.2 5.3 copy-start.2
  333.3 5.3 copy-start.4
  333.3 5.3 copy-start.6
  358.0 47.3 %slice-start = ((s8[9437184]{0:T(1024)(128)(4,1)}), s8[4194304]{0:T(1024)(128)(4,1)S(1)}, s32[]{:S(2)}) async-start(s8[9437184]{0:T(1024)(128)(4,1)} %bitcast.27), calls=%async_computation | async-start | bytes 8388608
  358.0 47.3 %slice-start.1 = ((s8[9437184]{0:T(1024)(128)(4,1)}), s8[4194304]{0:T(1024)(128)(4,1)S(1)}, s32[]{:S(2)}) async-start(s8[9437184]{0:T(1024)(128)(4,1)} %bitcast.27), calls=%async_computation.1 | async-start | bytes 8388608
  358.0 47.3 %slice-start.2 = ((s8[9437184]{0:T(1024)(128)(4,1)}), s8[1048576]{0:T(1024)(128)(4,1)S(1)}, s32[]{:S(2)}) async-start(s8[9437184]{0:T(1024)(128)(4,1)} %bitcast.27), calls=%async_computation.2 | async-start | bytes 2097152
  374.0 11.4 %copy-start.15 = (f32[4,384,128]{2,1,0:T(8,128)S(1)}, f32[4,384,128]{2,1,0:T(8,128)}, u32[]{:S(2)}) copy-start(f32[4,384,128]{2,1,0:T(8,128)} %copy-done.14) | copy-start | bytes 2359300
  374.0 15.4 %copy-start.27 = (f16[4,384,128]{2,1,0:T(8,128)(2,1)S(1)}, f16[4,384,128]{2,1,0:T(8,128)(2,1)}, u32[]{:S(2)}) copy-start(f16[4,384,128]{2,1,0:T(8,128)(2,1)} %multiply_convert_fusion.23) | copy-start | bytes 1179652
  374.0 15.9 %copy-start.29 = (f16[4,384,128]{2,1,0:T(8,128)(2,1)S(1)}, f16[4,384,128]{2,1,0:T(8,128)(2,1)}, u32[]{:S(2)}) copy-start(f16[4,384,128]{2,1,0:T(8,128)(2,1)} %multiply_convert_fusion.22) | copy-start | bytes 1179652
  374.0 28.1 %copy-start.28 = (f16[4,384,128]{2,1,0:T(8,128)(2,1)S(1)}, f16[4,384,128]{2,1,0:T(8,128)(2,1)}, u32[]{:S(2)}) copy-start(f16[4,384,128]{2,1,0:T(8,128)(2,1)} %multiply_convert_fusion.21) | copy-start | bytes 1179652
  374.1 31.3 %copy-start.3 = (f32[4,384,128]{2,1,0:T(8,128)S(1)}, f32[4,384,128]{2,1,0:T(8,128)}, u32[]{:S(2)}) copy-start(f32[4,384,128]{2,1,0:T(8,128)} %copy-done.2) | copy-start | bytes 2359300
  374.1 31.3 %copy-start.5 = (f32[4,384,128]{2,1,0:T(8,128)S(1)}, f32[4,384,128]{2,1,0:T(8,128)}, u32[]{:S(2)}) copy-start(f32[4,384,128]{2,1,0:T(8,128)} %copy-done.4) | copy-start | bytes 2359300
  374.1 31.3 %copy-start.7 = (f32[4,384,128]{2,1,0:T(8,128)S(1)}, f32[4,384,128]{2,1,0:T(8,128)}, u32[]{:S(2)}) copy-start(f32[4,384,128]{2,1,0:T(8,128)} %copy-done.6) | copy-start | bytes 2359300
  385.4 16.8 %collective-permute-start.23 = (bf16[64,1024]{1,0:T(8,128)(2,1)S(1)}, bf16[64,1024]{1,0:T(8,128)(2,1)S(1)}, u32[]{:S(2)}, u32[]{:S(2)}) collective-permute-start(bf16[64,1024]{1,0:T(8,128)(2,1)S(1)} %shard_map.90.refs_0_), channel_id=1, source_target_pairs={{0,3},{1,0},{2,1},{3,2},{4,7},{5,4},{6,5},{7,6},{8,11},{9,8},{10,9... | collective-permute-start | bytes 393224 | tf_op jit(solution)/shard_map/ppermute | solution.py:686
  385.5 34.7 %collective-permute-start.22 = (bf16[64,1024]{1,0:T(8,128)(2,1)S(1)}, bf16[64,1024]{1,0:T(8,128)(2,1)S(1)}, u32[]{:S(2)}, u32[]{:S(2)}) collective-permute-start(bf16[64,1024]{1,0:T(8,128)(2,1)S(1)} %shard_map.90.refs_0_), channel_id=1, source_target_pairs={{0,2},{1,3},{2,0},{3,1},{4,6},{5,7},{6,4},{7,5},{8,10},{9,11},{10,... | collective-permute-start | bytes 393224 | tf_op jit(solution)/shard_map/ppermute | solution.py:686
  385.6 34.7 %collective-permute-start.21 = (bf16[64,1024]{1,0:T(8,128)(2,1)S(1)}, bf16[64,1024]{1,0:T(8,128)(2,1)S(1)}, u32[]{:S(2)}, u32[]{:S(2)}) collective-permute-start(bf16[64,1024]{1,0:T(8,128)(2,1)S(1)} %shard_map.90.refs_0_), channel_id=1, source_target_pairs={{0,1},{1,2},{2,3},{3,0},{4,5},{5,6},{6,7},{7,4},{8,9},{9,10},{10,1... | collective-permute-start | bytes 393224 | tf_op jit(solution)/shard_map/ppermute | solution.py:686
  389.5 50.4 %collective-permute-start.30 = (f16[4,384,128]{2,1,0:T(8,128)(2,1)S(1)}, f16[4,384,128]{2,1,0:T(8,128)(2,1)S(1)}, u32[]{:S(2)}, u32[]{:S(2)}) collective-permute-start(f16[4,384,128]{2,1,0:T(8,128)(2,1)S(1)} %copy-done.27), channel_id=1, source_target_pairs={{0,3},{1,0},{2,1},{3,2},{4,7},{5,4},{6,5},{7,6},{8,11},{9,8},{10,9... | collective-permute-start | bytes 1179656 | tf_op jit(solution)/shard_map/ppermute | solution.py:686
  390.0 53.0 %collective-permute-start.31 = (f16[4,384,128]{2,1,0:T(8,128)(2,1)S(1)}, f16[4,384,128]{2,1,0:T(8,128)(2,1)S(1)}, u32[]{:S(2)}, u32[]{:S(2)}) collective-permute-start(f16[4,384,128]{2,1,0:T(8,128)(2,1)S(1)} %copy-done.29), channel_id=1, source_target_pairs={{0,2},{1,3},{2,0},{3,1},{4,6},{5,7},{6,4},{7,5},{8,10},{9,11},{10,... | collective-permute-start | bytes 1179656 | tf_op jit(solution)/shard_map/ppermute | solution.py:686
  402.2 40.9 %collective-permute-start.32 = (f16[4,384,128]{2,1,0:T(8,128)(2,1)S(1)}, f16[4,384,128]{2,1,0:T(8,128)(2,1)S(1)}, u32[]{:S(2)}, u32[]{:S(2)}) collective-permute-start(f16[4,384,128]{2,1,0:T(8,128)(2,1)S(1)} %copy-done.28), channel_id=1, source_target_pairs={{0,1},{1,2},{2,3},{3,0},{4,5},{5,6},{6,7},{7,4},{8,9},{9,10},{10,1... | collective-permute-start | bytes 1179656 | tf_op jit(solution)/shard_map/ppermute | solution.py:686
  405.4 14.8 %copy-start.24 = (f16[4,384,128]{2,1,0:T(8,128)(2,1)S(1)}, f16[4,384,128]{2,1,0:T(8,128)(2,1)}, u32[]{:S(2)}) copy-start(f16[4,384,128]{2,1,0:T(8,128)(2,1)} %multiply_convert_fusion.6) | copy-start | bytes 1179652
  405.4 14.9 %copy-start.23 = (f16[4,384,128]{2,1,0:T(8,128)(2,1)S(1)}, f16[4,384,128]{2,1,0:T(8,128)(2,1)}, u32[]{:S(2)}) copy-start(f16[4,384,128]{2,1,0:T(8,128)(2,1)} %multiply_convert_fusion.7) | copy-start | bytes 1179652
  420.2 22.8 %copy-start.26 = (f16[4,384,128]{2,1,0:T(8,128)(2,1)S(1)}, f16[4,384,128]{2,1,0:T(8,128)(2,1)}, u32[]{:S(2)}) copy-start(f16[4,384,128]{2,1,0:T(8,128)(2,1)} %multiply_convert_fusion.4) | copy-start | bytes 1179652
  420.2 22.9 %copy-start.25 = (f16[4,384,128]{2,1,0:T(8,128)(2,1)S(1)}, f16[4,384,128]{2,1,0:T(8,128)(2,1)}, u32[]{:S(2)}) copy-start(f16[4,384,128]{2,1,0:T(8,128)(2,1)} %multiply_convert_fusion.5) | copy-start | bytes 1179652
  420.2 49.4 %copy-start.13 = (f32[4,384,128]{2,1,0:T(8,128)S(1)}, f32[4,384,128]{2,1,0:T(8,128)}, u32[]{:S(2)}) copy-start(f32[4,384,128]{2,1,0:T(8,128)} %copy-done.12) | copy-start | bytes 2359300
  420.2 99.0 %collective-permute-start.26 = (f16[4,384,128]{2,1,0:T(8,128)(2,1)S(1)}, f16[4,384,128]{2,1,0:T(8,128)(2,1)S(1)}, u32[]{:S(2)}, u32[]{:S(2)}) collective-permute-start(f16[4,384,128]{2,1,0:T(8,128)(2,1)S(1)} %copy-done.24), channel_id=1, source_target_pairs={{0,1},{1,2},{2,3},{3,0},{4,5},{5,6},{6,7},{7,4},{8,9},{9,10},{10,1... | collective-permute-start | bytes 1179656 | tf_op jit(solution)/shard_map/ppermute | solution.py:686
  420.3 98.9 %collective-permute-start.25 = (f16[4,384,128]{2,1,0:T(8,128)(2,1)S(1)}, f16[4,384,128]{2,1,0:T(8,128)(2,1)S(1)}, u32[]{:S(2)}, u32[]{:S(2)}) collective-permute-start(f16[4,384,128]{2,1,0:T(8,128)(2,1)S(1)} %copy-done.23), channel_id=1, source_target_pairs={{0,2},{1,3},{2,0},{3,1},{4,6},{5,7},{6,4},{7,5},{8,10},{9,11},{10,... | collective-permute-start | bytes 1179656 | tf_op jit(solution)/shard_map/ppermute | solution.py:686
  439.9 49.1 %collective-permute-start.29 = (f16[4,384,128]{2,1,0:T(8,128)(2,1)S(1)}, f16[4,384,128]{2,1,0:T(8,128)(2,1)S(1)}, u32[]{:S(2)}, u32[]{:S(2)}) collective-permute-start(f16[4,384,128]{2,1,0:T(8,128)(2,1)S(1)} %multiply_convert_fusion.3), channel_id=1, source_target_pairs={{0,1},{1,2},{2,3},{3,0},{4,5},{5,6},{6,7},{7,4},{8,9},{9,10},{10,1... | collective-permute-start | bytes 1179656 | tf_op jit(solution)/shard_map/ppermute | solution.py:686
  443.0 58.6 %collective-permute-start.28 = (f16[4,384,128]{2,1,0:T(8,128)(2,1)S(1)}, f16[4,384,128]{2,1,0:T(8,128)(2,1)S(1)}, u32[]{:S(2)}, u32[]{:S(2)}) collective-permute-start(f16[4,384,128]{2,1,0:T(8,128)(2,1)S(1)} %copy-done.26), channel_id=1, source_target_pairs={{0,2},{1,3},{2,0},{3,1},{4,6},{5,7},{6,4},{7,5},{8,10},{9,11},{10,... | collective-permute-start | bytes 1179656 | tf_op jit(solution)/shard_map/ppermute | solution.py:686
  443.1 58.6 %collective-permute-start.27 = (f16[4,384,128]{2,1,0:T(8,128)(2,1)S(1)}, f16[4,384,128]{2,1,0:T(8,128)(2,1)S(1)}, u32[]{:S(2)}, u32[]{:S(2)}) collective-permute-start(f16[4,384,128]{2,1,0:T(8,128)(2,1)S(1)} %copy-done.25), channel_id=1, source_target_pairs={{0,3},{1,0},{2,1},{3,2},{4,7},{5,4},{6,5},{7,6},{8,11},{9,8},{10,9... | collective-permute-start | bytes 1179656 | tf_op jit(solution)/shard_map/ppermute | solution.py:686
  471.9 29.7 %slice-start.3 = ((s8[9437184]{0:T(1024)(128)(4,1)}), s8[4194304]{0:T(1024)(128)(4,1)S(1)}, s32[]{:S(2)}) async-start(s8[9437184]{0:T(1024)(128)(4,1)} %bitcast.57), calls=%async_computation.3 | async-start | bytes 8388608
  471.9 17.1 %copy-start.22 = (f16[4,384,128]{2,1,0:T(8,128)(2,1)S(1)}, f16[4,384,128]{2,1,0:T(8,128)(2,1)}, u32[]{:S(2)}) copy-start(f16[4,384,128]{2,1,0:T(8,128)(2,1)} %multiply_convert_fusion.8) | copy-start | bytes 1179652
  471.9 29.7 %copy-start.11 = (f32[4,384,128]{2,1,0:T(8,128)S(1)}, f32[4,384,128]{2,1,0:T(8,128)}, u32[]{:S(2)}) copy-start(f32[4,384,128]{2,1,0:T(8,128)} %copy-done.10) | copy-start | bytes 2359300
  471.9 29.7 %slice-start.4 = ((s8[9437184]{0:T(1024)(128)(4,1)}), s8[4194304]{0:T(1024)(128)(4,1)S(1)}, s32[]{:S(2)}) async-start(s8[9437184]{0:T(1024)(128)(4,1)} %bitcast.57), calls=%async_computation.4 | async-start | bytes 8388608
  471.9 29.7 %slice-start.5 = ((s8[9437184]{0:T(1024)(128)(4,1)}), s8[1048576]{0:T(1024)(128)(4,1)S(1)}, s32[]{:S(2)}) async-start(s8[9437184]{0:T(1024)(128)(4,1)} %bitcast.57), calls=%async_computation.5 | async-start | bytes 2097152
  489.0 30.2 %collective-permute-start.24 = (f16[4,384,128]{2,1,0:T(8,128)(2,1)S(1)}, f16[4,384,128]{2,1,0:T(8,128)(2,1)S(1)}, u32[]{:S(2)}, u32[]{:S(2)}) collective-permute-start(f16[4,384,128]{2,1,0:T(8,128)(2,1)S(1)} %copy-done.22), channel_id=1, source_target_pairs={{0,3},{1,0},{2,1},{3,2},{4,7},{5,4},{6,5},{7,6},{8,11},{9,8},{10,9... | collective-permute-start | bytes 1179656 | tf_op jit(solution)/shard_map/ppermute | solution.py:686
  502.1 17.1 %copy-start.9 = (f32[4,384,128]{2,1,0:T(8,128)S(1)}, f32[4,384,128]{2,1,0:T(8,128)}, u32[]{:S(2)}) copy-start(f32[4,384,128]{2,1,0:T(8,128)} %copy-done.8) | copy-start | bytes 2359300
  (8 other events, 9.6 us)

commit v4 on v3

--- a/solution.py
+++ b/solution.py
@@ -72,20 +72,27 @@
     return pl.BlockSpec(x.shape, lambda i, *_: (0,) * x.ndim, pipeline_mode=pl.Buffered(1))
 
 
-def quarter_kernel(nf, parts, me_ref, l_ref, k_ref, wt_ref, coef_ref, p_ref, far_ref, *rest):
-    r_refs, rest = rest[:parts], rest[parts:]
+def quarter_kernel(nf, parts, sets, me_ref, l_ref, k_ref, wt_ref, coef_ref, p_ref, far_ref, *rest):
+    own_ref, rest = rest[0], rest[1:]
+    came, rest = rest[: sets * (parts - 1)], rest[sets * (parts - 1) :]
     u_refs, rest = rest[:parts], rest[parts:]
     v_refs, (table, held, turned, mid, far) = rest[:parts], rest[parts:]
     own = nf // parts
-    cols = r_refs[0].shape[2]
+    cols = own_ref.shape[2]
     table[...] = dot_exact(coef_ref[...], k_ref[...])
     spread(l_ref, p_ref, far_ref, held)
 
     @pl.loop(0, table.shape[1] // LANES)
     def _(block):
         lanes = part(block, 0, LANES)
-        for v in range(nf):
-            turned[v] = r_refs[v // own][v % own, lanes, :].T
+        for v in range(own):
+            turned[v] = own_ref[v, lanes, :].T
+        for j in range(sets):
+
+            @pl.when(pl.program_id(0) == j)
+            def _():
+                for v in range(own, nf):
+                    turned[v] = came[j * (parts - 1) + v // own - 1][v % own, lanes, :].T
 
         @pl.loop(0, cols // CHUNK)
         def _(i):
@@ -110,16 +117,17 @@
             v_refs[w // own][w % own, lanes, :] = far[w].T
 
 
-def quarter_pass(me, k, first, factors, kernels, weights, coef, near, far, right_side, moved):
+def quarter_pass(me, low, factors, kernels, weights, coef, near, far, right_side, moved):
     own, pairs, cols = right_side.shape
     nf = weights.shape[0]
     parts = nf // own
     quarter = pairs // parts
     naux = factors.shape[1]
     tile = tile_of(quarter)
+    sets = len(moved)
     if tile is None:
         cut = lambda x, axis: lax.dynamic_slice_in_dim(x, me * quarter, quarter, axis)
-        here = jnp.concatenate([cut(right_side, 1)] + moved)
+        here = jnp.concatenate([cut(right_side, 1)] + moved[0][0])
         table = jnp.einsum("jt,tp->jp", coef, cut(kernels, 1), precision=EXACT)
         table = table.reshape(nf, nf, quarter)
         wide = jnp.einsum(
@@ -137,26 +145,26 @@
             [v[s * own : (s + 1) * own] for s in range(parts)],
         )
     steps = quarter // tile
-    at = lambda m: m[0] * steps + k
-    came = pl.BlockSpec((own, tile, cols), lambda i, m: (0, k - first, 0))
-    piece = pl.BlockSpec((own, tile, cols), lambda i, m: (0, 0, 0))
-    shape = jax.ShapeDtypeStruct((own, tile, cols), jnp.float32)
+    at = lambda i, m: m[0] * steps + low + i
+    here = lambda n: pl.BlockSpec((own, tile, cols), lambda i, m: (0, n, 0))
+    piece = pl.BlockSpec((own, tile, cols), lambda i, m: (0, i, 0))
+    shape = jax.ShapeDtypeStruct((own, sets * tile, cols), jnp.float32)
     out = pl.pallas_call(
-        functools.partial(quarter_kernel, nf, parts),
+        functools.partial(quarter_kernel, nf, parts, sets),
         out_shape=[shape] * (2 * parts),
         grid_spec=pltpu.PrefetchScalarGridSpec(
             num_scalar_prefetch=1,
-            grid=(1,),
+            grid=(sets,),
             in_specs=[
-                pl.BlockSpec((tile, naux), lambda i, m: (at(m), 0)),
-                pl.BlockSpec((nf, tile), lambda i, m: (0, at(m))),
-                pl.BlockSpec((nf, tile), lambda i, m: (0, at(m))),
+                pl.BlockSpec((tile, naux), lambda i, m: (at(i, m), 0)),
+                pl.BlockSpec((nf, tile), lambda i, m: (0, at(i, m))),
+                pl.BlockSpec((nf, tile), lambda i, m: (0, at(i, m))),
                 resident(coef),
                 resident(near),
                 resident(far),
-                pl.BlockSpec((own, tile, cols), lambda i, m: (0, at(m), 0)),
+                pl.BlockSpec((own, tile, cols), lambda i, m: (0, at(i, m), 0)),
             ]
-            + [came] * (parts - 1),
+            + [here(n) for _, n in moved for _ in range(parts - 1)],
             out_specs=[piece] * (2 * parts),
             scratch_shapes=[
                 VMEM((nf * nf, tile), jnp.float32),
@@ -164,17 +172,27 @@
             ]
             + [VMEM((nf, cols, LANES), jnp.float32)] * 3,
         ),
-        compiler_params=pltpu.CompilerParams(vmem_limit_bytes=36 << 20),
+        compiler_params=pltpu.CompilerParams(vmem_limit_bytes=(36 if sets == 1 else 46) << 20),
         cost_estimate=pl.CostEstimate(
-            flops=2 * nf * tile * cols * (naux + 32 * nf),
-            bytes_accessed=16 * nf * tile * cols,
+            flops=2 * nf * sets * tile * cols * (naux + 32 * nf),
+            bytes_accessed=16 * nf * sets * tile * cols,
             transcendentals=0,
         ),
-    )(me.reshape(1), factors, kernels, weights, coef, near, far, right_side, *moved)
+    )(
+        me.reshape(1),
+        factors,
+        kernels,
+        weights,
+        coef,
+        near,
+        far,
+        right_side,
+        *[x for xs, _ in moved for x in xs],
+    )
     return list(out[:parts]), list(out[parts:])
 
 
-def project_kernel(parts, me_ref, l_ref, *rest):
+def project_kernel(parts, sets, me_ref, l_ref, *rest):
     s_refs, (x_ref, o_ref) = rest[:parts], rest[parts:]
     own, _, _ = s_refs[0].shape
     i = pl.program_id(0)
@@ -185,7 +203,7 @@
 
     for s in range(parts):
 
-        @pl.when(i == s)
+        @pl.when(lax.div(i, sets) == s)
         def _():
             rounded = [s_refs[s][f].astype(jnp.bfloat16) for f in range(own)]
             o_ref[...] += lax.dot_general(
@@ -196,16 +214,17 @@
             )
 
 
-def around(parts, steps, k):
-    return lambda i, m: lax.rem(m[0] + i, parts) * steps + k
-
-
-def project(me, k, factors, pieces, total):
+def around(parts, steps, low, sets):
+    return lambda i, m: lax.rem(m[0] + lax.div(i, sets), parts) * steps + low + lax.rem(i, sets)
+
+
+def project(me, low, factors, pieces, total):
     own, size, cols = pieces[0].shape
     parts = len(pieces)
     pairs, naux = factors.shape
     quarter = pairs // parts
-    if tile_of(quarter) is None:
+    tile = tile_of(quarter)
+    if tile is None:
         for s, x in enumerate(pieces):
             rows = lax.dynamic_slice_in_dim(
                 factors, lax.rem(me + s, parts) * quarter, quarter, 0
@@ -214,15 +233,17 @@
                 "pa,fpc->fca", rows, x.astype(jnp.bfloat16), preferred_element_type=jnp.float32
             ).reshape(total.shape)
         return total
-    at = around(parts, quarter // size, k)
+    sets = size // tile
+    at = around(parts, quarter // tile, low, sets)
+    stay = lambda s: lambda i, m: (0, jnp.clip(i - s * sets, 0, sets - 1), 0)
     return pl.pallas_call(
-        functools.partial(project_kernel, parts),
+        functools.partial(project_kernel, parts, sets),
         out_shape=jax.ShapeDtypeStruct(total.shape, jnp.float32),
         grid_spec=pltpu.PrefetchScalarGridSpec(
             num_scalar_prefetch=1,
-            grid=(parts,),
-            in_specs=[pl.BlockSpec((size, naux), lambda i, m: (at(i, m), 0))]
-            + [pl.BlockSpec((own, size, cols), lambda i, m: (0, 0, 0))] * parts
+            grid=(parts * sets,),
+            in_specs=[pl.BlockSpec((tile, naux), lambda i, m: (at(i, m), 0))]
+            + [pl.BlockSpec((own, tile, cols), stay(s)) for s in range(parts)]
             + [resident(total)],
             out_specs=pl.BlockSpec(total.shape, lambda i, m: (0, 0)),
         ),
@@ -281,6 +302,10 @@
 
 class Stream:
     def __init__(self, refs, buffer, sems):
+        tile = buffer.shape[2]
+        refs = [
+            ref.at[:, n : n + tile, :] for ref in refs for n in range(0, ref.shape[1], tile)
+        ]
         self.refs, self.buffer, self.sems = refs, buffer, sems
         self.step = pl.program_id(0)
         self.slot = lax.rem(self.step, 2)
@@ -306,8 +331,8 @@
         return self.buffer.at[self.slot]
 
 
-def stream_scratch(piece):
-    return [VMEM((2,) + piece.shape, piece.dtype), pltpu.SemaphoreType.DMA((2,))]
+def stream_scratch(own, tile, cols):
+    return [VMEM((2, own, tile, cols), jnp.float32), pltpu.SemaphoreType.DMA((2,))]
 
 
 ANYWHERE = pl.BlockSpec(memory_space=pl.ANY)
@@ -328,11 +353,12 @@
 
 
 def amplitude(me, factors, pair_weight, near, sources):
-    own, size, cols = sources[0][0].shape
+    own, _, cols = sources[0][0].shape
     parts = len(sources[0])
     pairs, naux = factors.shape
     quarter = pairs // parts
-    if tile_of(quarter) is None:
+    size = tile_of(quarter)
+    if size is None:
         wide = jnp.einsum("ja,pa->jp", near, factors, preferred_element_type=jnp.float32)
         wide = jnp.transpose(wide.reshape(own, cols, pairs), (0, 2, 1))
         result = wide * pair_weight[:, :, None]
@@ -342,14 +368,24 @@
             result = lax.dynamic_update_slice_in_dim(result, part_of, at, 1)
         return result
     steps = quarter // size
-    pieces = [x for chunk in sources for x in chunk]
-    at = lambda i, m: lax.rem(m[0] + lax.rem(i, parts), parts) * steps + lax.div(i, parts)
+    pieces = [x for group in sources for x in group]
+    first = parts * (sources[0][0].shape[1] // size)
+    ranks = [around(parts, steps, 0, first // parts)]
+    if len(sources) > 1:
+        ranks.append(around(parts, steps, first // parts, steps - first // parts))
+
+    def at(i, m):
+        place = ranks[0](i, m)
+        if len(ranks) > 1:
+            place = jnp.where(i < first, place, ranks[1](jnp.maximum(i - first, 0), m))
+        return place
+
     return pl.pallas_call(
         functools.partial(amplitude_kernel, len(pieces)),
         out_shape=jax.ShapeDtypeStruct((own, pairs, cols), jnp.float32),
         grid_spec=pltpu.PrefetchScalarGridSpec(
             num_scalar_prefetch=1,
-            grid=(len(pieces),),
+            grid=(parts * steps,),
             in_specs=[
                 pl.BlockSpec((size, naux), lambda i, m: (at(i, m), 0)),
                 pl.BlockSpec((own, size), lambda i, m: (0, at(i, m))),
@@ -357,7 +393,7 @@
             ]
             + [ANYWHERE] * len(pieces),
             out_specs=pl.BlockSpec((own, size, cols), lambda i, m: (0, at(i, m), 0)),
-            scratch_shapes=stream_scratch(pieces[0]),
+            scratch_shapes=stream_scratch(own, size, cols),
         ),
         compiler_params=pltpu.CompilerParams(vmem_limit_bytes=20 << 20),
         cost_estimate=pl.CostEstimate(
@@ -396,8 +432,8 @@
             new_ref[w, lanes, :] = here[w, lanes, :] + mid[w].T
 
 
-def final(me, k, factors, kernels, weights, coef, near, far, base, outs):
-    own, size, cols = base[0].shape
+def final(me, low, factors, kernels, weights, coef, near, far, base, outs):
+    own, span, cols = base[0].shape
     parts = len(base)
     nf = weights.shape[0]
     pairs, naux = factors.shape
@@ -418,13 +454,15 @@
             part_of = lax.dynamic_slice_in_dim(new, at, quarter, 1) + base[s]
             new = lax.dynamic_update_slice_in_dim(new, part_of, at, 1)
         return [new]
-    at = around(parts, quarter // size, k)
+    size = tile
+    sets = span // size
+    at = around(parts, quarter // size, low, sets)
     result = pl.pallas_call(
         functools.partial(final_kernel, nf, parts, len(outs)),
         out_shape=jax.ShapeDtypeStruct((own, pairs, cols), jnp.float32),
         grid_spec=pltpu.PrefetchScalarGridSpec(
             num_scalar_prefetch=1,
-            grid=(parts,),
+            grid=(parts * sets,),
             in_specs=[
                 pl.BlockSpec((size, naux), lambda i, m: (at(i, m), 0)),
                 pl.BlockSpec((nf, size), lambda i, m: (0, at(i, m))),
@@ -440,13 +478,13 @@
                 VMEM((nf * cols, size), jnp.float32),
                 VMEM((own, cols, LANES), jnp.float32),
             ]
-            + stream_scratch(base[0]),
+            + stream_scratch(own, size, cols),
         ),
         input_output_aliases={7 + parts + n: n for n in range(len(outs))},
         compiler_params=pltpu.CompilerParams(vmem_limit_bytes=26 << 20),
         cost_estimate=pl.CostEstimate(
-            flops=2 * nf * parts * size * cols * naux,
-            bytes_accessed=8 * own * parts * size * cols,
+            flops=2 * nf * parts * span * cols * naux,
+            bytes_accessed=8 * own * parts * span * cols,
             transcendentals=0,
         ),
     )(me.reshape(1), factors, kernels, weights, coef, near, far, *base, *outs)
@@ -553,11 +591,18 @@
 
 def gather_kernel(chips, parts, *refs):
     x_refs, (o_ref, joined, *sems) = refs[:parts], refs[parts:]
+    kept = sems[4]
     plane = Plane(chips)
     chip, core, pal = plane.chip, plane.core, plane.pal
     plane.greet()
     wide_sems, pair_sems = sems[0:2], sems[2:4]
     pairs = []
+    copies = []
+    for s in range(parts):
+        copies.append(
+            pltpu.make_async_copy(x_refs[s], joined.at[s, chip, core], kept.at[s])
+        )
+        copies[-1].start()
     square = chips == 4
     column, row = lax.rem(chip, 2), lax.div(chip, 2)
     across, along = chip + 1 - 2 * column, chip + 2 - 4 * row
@@ -595,10 +640,11 @@
     for copy in pairs:
         copy.wait_recv()
     plane.end()
+    for copy in copies:
+        copy.wait()
     for s in range(parts):
         for c in range(chips):
             o_ref[s, c] = joined[s, c]
-        o_ref[s, chip, core] = x_refs[s][...]
 
 
 def dmas(count, pairs):
@@ -663,9 +709,11 @@
     result = pl.pallas_call(
         functools.partial(gather_kernel, chips, parts),
         out_shape=jax.ShapeDtypeStruct(flat, jnp.bfloat16),
-        in_specs=[WHOLE] * parts,
+        in_specs=[pl.BlockSpec(memory_space=pl.ANY)] * parts,
         out_specs=WHOLE,
-        scratch_shapes=[VMEM(flat, jnp.bfloat16)] + dmas(parts * chips, 2),
+        scratch_shapes=[VMEM(flat, jnp.bfloat16)]
+        + dmas(parts * chips, 2)
+        + [pltpu.SemaphoreType.DMA((parts,))],
         compiler_params=reach_params(2 if parts == 1 else 3),
         cost_estimate=reach_cost(block * width * parts * 8),
     )(*blocks)
@@ -705,6 +753,7 @@
     chunks = quarter // size
     early = max(chunks - 1, 1)
     groups = [(0, early)] + ([(early, chunks)] if early < chunks else [])
+    calls = [(0, 1)] + ([(1, chunks)] if chunks > 1 else [])
     tie = lax.optimization_barrier
     up = 8192.0
 
@@ -753,44 +802,62 @@
     def halved(blocks, top):
         return [(b * (HALF_TOP / top)).astype(jnp.float16) for b in blocks[1:]]
 
-    def added(first, rest, top, k):
+    def added(first, rest, top, group):
         rest = [b.astype(jnp.float32) * (top / HALF_TOP) for b in rest]
-        return [sliced(right_late, s, k, k + 1) + b for s, b in enumerate([first] + rest)]
-
-    us, vs, inward = [], [], []
+        return [sliced(right_late, s, *group) + b for s, b in enumerate([first] + rest)]
+
+    placed = []
     for group, moved in zip(groups, came):
         moved = [m.astype(jnp.float32) * (1.0 / up) for m in moved]
-        for k in range(*group):
-            u, v = quarter_pass(
-                me, k, group[0], factors, kernels, weights, coef, near, far, right_side, moved
-            )
-            inward.append(passed(halved(u, u_top), True))
-            us.append(u)
-            vs.append(v)
+        placed += [(moved, k - group[0]) for k in range(*group)]
+    us, vs, inward, halves = [], [], [], []
+    for low, high in calls:
+        u, v = quarter_pass(
+            me,
+            low,
+            factors,
+            kernels,
+            weights,
+            coef,
+            near,
+            far,
+            right_side,
+            placed[low:high],
+        )
+        inward.append(passed(halved(u, u_top), True))
+        halves.append(halved(v, v_top))
+        us.append(u)
+        vs.append(v)
     sources = []
     total = jnp.zeros((own * cols, naux), jnp.float32)
-    for k in range(chunks):
-        if k:
-            inward[k], total = tie((inward[k], total))
-        sources.append(added(us[k][0], inward[k], u_top, k))
-        total = project(me, k, factors, sources[k], total)
-
-    halves = []
-    for v in vs:
-        halves.append(halved(v, v_top))
+    for n, group in enumerate(calls):
+        if n:
+            inward[n], total = tie((inward[n], total))
+        sources.append(added(us[n][0], inward[n], u_top, group))
+        total = project(me, group[0], factors, sources[n], total)
+
     out, total = tie((halves[0], total))
     back = [passed(out, True)]
     near, blocks = ladder(total)
-    for k in range(1, chunks):
-        back.append(passed(halves[k], True))
+    for n in range(1, len(calls)):
+        back.append(passed(halves[n], True))
     amplitudes = amplitude(me, factors, pair_weight, near, sources)
     far = gathered_over(blocks)
     outs = []
-    for k in range(chunks):
-        back[k], outs = tie((back[k], outs))
-        base = added(vs[k][0], back[k], v_top, k)
+    for n, group in enumerate(calls):
+        back[n], outs = tie((back[n], outs))
+        base = added(vs[n][0], back[n], v_top, group)
         outs = final(
-            me, k, factors, kernels, weights, coef[: own * nf], near, far, base, outs
+            me,
+            group[0],
+            factors,
+            kernels,
+            weights,
+            coef[: own * nf],
+            near,
+            far,
+            base,
+            outs,
         )
     return amplitudes, outs[0]
 

time: 544 us -> 549 us (level)
  the two profiles are of different devices: /device:TPU:24 before, /device:TPU:0 now
where the time goes in v4:
time: 549 us; the launch traced here: 542 us
  Pallas kernels  278 us (51%)
  waiting for transfers between devices  151 us (28%)
  starting transfers between devices  56.4 us (10%)
  other arithmetic  34.2 us (6%)
  matrix products  11.4 us (2%)
  local copies, waits for them, and re-layouts  7.26 us (1%)
    ppermute x27, waiting for transfers between devices, shift(): lax.ppermute(x, 'freq', [(i, (i + by) % parts) for i in range(parts)])  151 us
    pallas_call x4, Pallas kernels, gathered_over(): pl.pallas_call(functools.partial(gather_kernel, chips, parts), out_shape=...  59.3 us
    ppermute x27, starting transfers between devices, shift(): lax.ppermute(x, 'freq', [(i, (i + by) % parts) for i in range(parts)])  56.4 us
    pallas_call x2, Pallas kernels, final(): pl.pallas_call(functools.partial(final_kernel, nf, parts, len(outs)), out...  50.7 us
    pallas_call x2, Pallas kernels, quarter_pass(): pl.pallas_call(functools.partial(quarter_kernel, nf, parts, sets), out_sh...  45 us
    pallas_call x2, Pallas kernels, summed(): pl.pallas_call(functools.partial(sum_kernel, chips), out_shape=jax.ShapeD...  39.6 us
    pallas_call x2, Pallas kernels, again(): pl.pallas_call(functools.partial(again_kernel, own), out_shape=jax.ShapeD...  31.7 us
    pallas_call x2, Pallas kernels, summed(): pl.pallas_call(functools.partial(reduce_kernel, chips), out_shape=jax.Sha...  22.5 us
  transfers between devices with their start and end apart: 27, of which 7 were waited for; matrix products, arithmetic and copies ran while one was open for 7% of the time, Pallas kernels for 32%

profile of v4, /device:TPU:0, one launch (start us, length us, event | category | flops | bytes accessed | tf_op | source)
XLA Modules:
  0.0 542.0 jit_solution(5913214684889754149)
XLA Ops:
  0.6 1.6 pad_maximum_fusion.1
  2.2 5.1 collective-permute-start.2
  7.3 10.4 %fusion = f32[4,128,1024]{2,1,0:T(8,128)S(1)} fusion(bf16[4608,1024]{1,0:T(8,128)(2,1)} %l_ref.17, f32[4,4608,128]{2,1,0:T(8,128)} %rest_0_.3), kind=kOutput, calls=%fused_computation | convolution fusion | flops 4834197504 | bytes 20971520 | tf_op jit(solution)/shard_map/pa,fpc->fca/dot_general | solution.py:773
  17.7 20.3 %shard_map.77 = bf16[4,2,64,1024]{3,2,1,0:T(8,128)(2,1)S(1)} custom-call(f32[4,2,64,1024]{3,2,1,0:T(8,128)S(1)} %bitcast.38), custom_call_target="tpu_custom_call" | custom-call | flops 20971520 | bytes 20971520 | tf_op jit(solution)/shard_map/pallas_call | solution.py:688
  38.1 15.7 %shard_map.78 = f32[512,1024]{1,0:T(8,128)S(1)} custom-call(bf16[4608,1024]{1,0:T(8,128)(2,1)} %l_ref.17, f32[4,4608]{1,0:T(4,128)S(1)} %copy-done.19, bf16[512,1024]{1,0:T(8,128)(2,1)S(1)} %bitcast.45, f32[512,1024]{1,0:T(8,128)S(1)} %bitcast.39), custom_call_target="tpu_custom_call" | custom-call | flops 9663676416 | bytes 9437184 | tf_op jit(solution)/shard_map/pallas_call | solution.py:285
  53.9 11.2 %shard_map.79.refs_0_ = bf16[64,1024]{1,0:T(8,128)(2,1)S(1)} custom-call(f32[4,2,64,1024]{3,2,1,0:T(8,128)S(1)} %bitcast.41), custom_call_target="tpu_custom_call" | custom-call | flops 10485760 | bytes 10485760 | tf_op jit(solution)/shard_map/pallas_call | solution.py:679
  65.7 2.2 collective-permute-start.4
  67.9 1.9 collective-permute-start.3
  70.6 10.7 %shard_map.80 = bf16[1,4,2,64,1024]{4,3,2,1,0:T(8,128)(2,1)S(1)} custom-call(bf16[64,1024]{1,0:T(8,128)(2,1)S(1)} %shard_map.79.refs_0_), custom_call_target="tpu_custom_call" | custom-call | flops 20971520 | bytes 20971520 | tf_op jit(solution)/shard_map/pallas_call | solution.py:709
  82.4 2.7 multiply_convert_fusion.12
  87.3 4.0 multiply_convert_fusion.6
  91.4 0.8 collective-permute-start.9
  92.2 0.7 copy-done.20
  92.8 3.6 collective-permute-start.10
  96.4 0.9 copy-done.21
  97.3 19.0 %shard_map.81 = bf16[3,4,2,64,1024]{4,3,2,1,0:T(8,128)(2,1)S(1)} custom-call(bf16[64,1024]{1,0:T(8,128)(2,1)S(1)} %copy-done.21, bf16[64,1024]{1,0:T(8,128)(2,1)S(1)} %collective-permute-done.4.refs_1_, bf16[64,1024]{1,0:T(8,128)(2,1)S(1)} %collective-permute-done.5.refs_2_), custom_call_target="tpu_custom_call" | custom-call | flops 62914560 | bytes 62914560 | tf_op jit(solution)/shard_map/pallas_call | solution.py:709
  116.3 0.7 abs_reduce_fusion
  117.0 0.9 reduce_max.29
  119.3 1.0 collective-permute-start.11
  120.3 0.8 collective-permute-start.8
  121.1 1.7 collective-permute-start.7
  122.8 1.2 pad_maximum_fusion
  124.7 1.1 convert_multiply_fusion.5.rest_4_
  125.8 1.1 convert_multiply_fusion.4.rest_5_
  126.9 6.4 %collective-permute-done.11 = f16[4,384,128]{2,1,0:T(8,128)(2,1)S(1)} collective-permute-done((f16[4,384,128]{2,1,0:T(8,128)(2,1)}, f16[4,384,128]{2,1,0:T(8,128)(2,1)S(1)}, u32[]{:S(2)}, u32[]{:S(2)}) %collective-permute-start.11) | collective-permute-done | bytes 393248 | tf_op jit(solution)/shard_map/ppermute | solution.py:734
  133.2 0.9 convert_multiply_fusion.3.rest_6_
  134.2 15.9 %collective-permute-done.8 = f16[4,768,128]{2,1,0:T(8,128)(2,1)S(1)} collective-permute-done((f16[4,768,128]{2,1,0:T(8,128)(2,1)}, f16[4,768,128]{2,1,0:T(8,128)(2,1)S(1)}, u32[]{:S(2)}, u32[]{:S(2)}) %collective-permute-start.8) | collective-permute-done | bytes 786464 | tf_op jit(solution)/shard_map/ppermute | solution.py:734
  150.2 50.4 %collective-permute-done.7 = f16[4,768,128]{2,1,0:T(8,128)(2,1)S(1)} collective-permute-done((f16[4,768,128]{2,1,0:T(8,128)(2,1)}, f16[4,768,128]{2,1,0:T(8,128)(2,1)S(1)}, u32[]{:S(2)}, u32[]{:S(2)}) %collective-permute-start.7) | collective-permute-done | bytes 786464 | tf_op jit(solution)/shard_map/ppermute | solution.py:734
  201.0 1.8 copy-done.2
  202.9 14.0 %shard_map.82 = (f32[4,384,128]{2,1,0:T(8,128)S(1)}, f32[4,384,128]{2,1,0:T(8,128)S(1)}, f32[4,384,128]{2,1,0:T(8,128)S(1)}, f32[4,384,128]{2,1,0:T(8,128)S(1)},...) custom-call(s32[1]{0:T(128)} %bitcast.me_ref, ...), custom_call_target="tpu_custom_call" | custom-call | flops 2415919104 | bytes 12582912 | tf_op jit(solution)/shard_map/pallas_call | solution.py:152
  217.8 3.8 collective-permute-start.15
  221.6 31.0 %shard_map.83 = (f32[4,768,128]{2,1,0:T(8,128)S(1)}, f32[4,768,128]{2,1,0:T(8,128)S(1)}, f32[4,768,128]{2,1,0:T(8,128)}, f32[4,768,128]{2,1,0:T(8,128)}, f32[4,7...) custom-call(s32[1]{0:T(128)} %bitcast.me_ref, ...), custom_call_target="tpu_custom_call" | custom-call | flops 4831838208 | bytes 25165824 | tf_op jit(solution)/shard_map/pallas_call | solution.py:152
  252.8 1.2 copy-done.27
  254.7 0.8 multiply_convert_fusion.17
  256.1 1.0 multiply_convert_fusion.2
  257.2 0.9 multiply_convert_fusion.16
  258.0 0.8 multiply_convert_fusion.15
  259.5 1.4 collective-permute-start.13
  260.9 3.4 collective-permute-start.12
  264.3 1.1 multiply_convert_fusion.1
  265.3 2.3 multiply_add_fusion.9
  268.0 5.2 shard_map.84.rest_4_
  273.2 8.0 %collective-permute-done.14 = f16[4,768,128]{2,1,0:T(8,128)(2,1)S(1)} collective-permute-done((f16[4,768,128]{2,1,0:T(8,128)(2,1)S(1)}, f16[4,768,128]{2,1,0:T(8,128)(2,1)S(1)}, u32[]{:S(2)}, u32[]{:S(2)}) %collective-permute-start.14) | collective-permute-done | bytes 786464 | tf_op jit(solution)/shard_map/ppermute | solution.py:734
  281.2 32.2 %collective-permute-done.13 = f16[4,768,128]{2,1,0:T(8,128)(2,1)S(1)} collective-permute-done((f16[4,768,128]{2,1,0:T(8,128)(2,1)S(1)}, f16[4,768,128]{2,1,0:T(8,128)(2,1)S(1)}, u32[]{:S(2)}, u32[]{:S(2)}) %collective-permute-start.13) | collective-permute-done | bytes 786464 | tf_op jit(solution)/shard_map/ppermute | solution.py:734
  313.4 3.8 multiply_add_fusion.3
  317.3 8.9 %shard_map.85.x_ref = f32[512,1024]{1,0:T(8,128)S(1)} custom-call(s32[1]{0:T(128)} %bitcast.me_ref, bf16[4608,1024]{1,0:T(8,128)(2,1)} %l_ref.17, f32[4,768,128]{2,1,0:T(8,128)S(1)} %get-tuple-element.83.rest_0_.rest_4_, f32[4,768,128]{2,1,0:T(8,128)S(1)} %get-tuple-element.82.rest_1_.rest_5_, f32[4,768,128]{2,1,0:T(8,128)S(1)} %get-tuple-element.81.rest_2_.rest_6_, ...), custom_call_target="tpu_custom_call" | custom-call | flops 3221225472 | bytes 12582912 | tf_op jit(solution)/shard_map/pallas_call | solution.py:239
  326.2 19.3 %shard_map.86 = bf16[4,2,64,1024]{3,2,1,0:T(8,128)(2,1)S(1)} custom-call(f32[4,2,64,1024]{3,2,1,0:T(8,128)S(1)} %bitcast.40), custom_call_target="tpu_custom_call" | custom-call | flops 20971520 | bytes 20971520 | tf_op jit(solution)/shard_map/pallas_call | solution.py:688
  345.5 16.0 %shard_map.87 = f32[512,1024]{1,0:T(8,128)S(1)} custom-call(bf16[4608,1024]{1,0:T(8,128)(2,1)} %l_ref.17, f32[4,4608]{1,0:T(4,128)S(1)} %copy-done.19, bf16[512,1024]{1,0:T(8,128)(2,1)S(1)} %bitcast.46, f32[512,1024]{1,0:T(8,128)S(1)} %shard_map.85.x_ref), custom_call_target="tpu_custom_call" | custom-call | flops 9663676416 | bytes 9437184 | tf_op jit(solution)/shard_map/pallas_call | solution.py:285
  361.6 11.3 %shard_map.88.refs_0_ = bf16[64,1024]{1,0:T(8,128)(2,1)S(1)} custom-call(f32[4,2,64,1024]{3,2,1,0:T(8,128)S(1)} %bitcast.42), custom_call_target="tpu_custom_call" | custom-call | flops 10485760 | bytes 10485760 | tf_op jit(solution)/shard_map/pallas_call | solution.py:679
  372.8 17.6 %collective-permute-start.20 = (bf16[64,1024]{1,0:T(8,128)(2,1)S(1)}, bf16[64,1024]{1,0:T(8,128)(2,1)S(1)}, u32[]{:S(2)}, u32[]{:S(2)}) collective-permute-start(bf16[64,1024]{1,0:T(8,128)(2,1)S(1)} %shard_map.88.refs_0_), channel_id=1, source_target_pairs={{0,3},{1,0},{2,1},{3,2},{4,7},{5,4},{6,5},{7,6},{8,11},{9,8},{10,9... | collective-permute-start | bytes 393224 | tf_op jit(solution)/shard_map/ppermute | solution.py:734
  390.7 0.9 collective-permute-start.19
  391.5 3.8 collective-permute-start.24
  395.7 10.7 %shard_map.89 = bf16[1,4,2,64,1024]{4,3,2,1,0:T(8,128)(2,1)S(1)} custom-call(bf16[64,1024]{1,0:T(8,128)(2,1)S(1)} %shard_map.88.refs_0_), custom_call_target="tpu_custom_call" | custom-call | flops 20971520 | bytes 20971520 | tf_op jit(solution)/shard_map/pallas_call | solution.py:709
  407.0 14.9 %shard_map.90 = f32[4,4608,128]{2,1,0:T(8,128)} custom-call(s32[1]{0:T(128)} %bitcast.me_ref, bf16[4608,1024]{1,0:T(8,128)(2,1)S(1)} %bitcast.28, f32[4,4608]{1,0:T(4,128)S(1)} %copy-done.19, bf16[512,1024]{1,0:T(8,128)(2,1)S(1)} %bitcast.35, f32[4,384,128]{2,1,0:T(8,128)S(1)} %copy-done.11, f32[4,384,128]{2,1,0:T(8,128)S(1)} %copy-done.9, ...), custom_call_target="tpu_custom_call" | custom-call | flops 4831838208 | bytes 18874368 | tf_op jit(solution)/shard_map/pallas_call | solution.py:383
  421.9 2.9 collective-permute-start.23
  424.9 1.1 collective-permute-start.22
  425.9 18.9 %shard_map.91 = bf16[3,4,2,64,1024]{4,3,2,1,0:T(8,128)(2,1)S(1)} custom-call(bf16[64,1024]{1,0:T(8,128)(2,1)S(1)} %collective-permute-done.18.refs_0_, bf16[64,1024]{1,0:T(8,128)(2,1)S(1)} %collective-permute-done.19.refs_1_, bf16[64,1024]{1,0:T(8,128)(2,1)S(1)} %collective-permute-done.20.refs_2_), custom_call_target="tpu_custom_call" | custom-call | flops 62914560 | bytes 62914560 | tf_op jit(solution)/shard_map/pallas_call | solution.py:709
  444.8 1.6 collective-permute-start.21
  446.5 25.0 %collective-permute-done.25 = f16[4,384,128]{2,1,0:T(8,128)(2,1)S(1)} collective-permute-done((f16[4,384,128]{2,1,0:T(8,128)(2,1)S(1)}, f16[4,384,128]{2,1,0:T(8,128)(2,1)S(1)}, u32[]{:S(2)}, u32[]{:S(2)}) %collective-permute-start.25) | collective-permute-done | bytes 393248 | tf_op jit(solution)/shard_map/ppermute | solution.py:734
  471.5 2.4 multiply_add_fusion.6
  473.9 17.1 %shard_map.92.rest_4_ = f32[4,4608,128]{2,1,0:T(8,128)} custom-call(s32[1]{0:T(128)} %bitcast.me_ref, bf16[4608,1024]{1,0:T(8,128)(2,1)S(1)} %bitcast.28, f32[16,4608]{1,0:T(8,128)S(1)} %copy-done.13, f32[16,4608]{1,0:T(8,128)S(1)} %get-tuple-element.94.wt_ref, f32[64,16]{1,0:T(8,128)S(1)} %bitcast.49, bf16[512,1024]{1,0:T(8,128)(2,1)S(1)} %bitcast.36, ...), custom_call_target="tpu_custom_call" | custom-call | flops 6442450944 | bytes 6291456 | tf_op jit(solution)/shard_map/pallas_call | solution.py:460
  491.1 13.3 %collective-permute-done.21 = f16[4,768,128]{2,1,0:T(8,128)(2,1)} collective-permute-done((f16[4,768,128]{2,1,0:T(8,128)(2,1)S(1)}, f16[4,768,128]{2,1,0:T(8,128)(2,1)}, u32[]{:S(2)}, u32[]{:S(2)}) %collective-permute-start.21) | collective-permute-done | bytes 786464 | tf_op jit(solution)/shard_map/ppermute | solution.py:734
  504.4 3.8 multiply_add_fusion
  508.2 33.6 %shard_map.93 = f32[4,4608,128]{2,1,0:T(8,128)} custom-call(s32[1]{0:T(128)} %bitcast.me_ref, bf16[4608,1024]{1,0:T(8,128)(2,1)S(1)} %bitcast.28, f32[16,4608]{1,0:T(8,128)S(1)} %copy-done.13, f32[16,4608]{1,0:T(8,128)S(1)} %get-tuple-element.94.wt_ref, f32[64,16]{1,0:T(8,128)S(1)} %bitcast.50, ...), custom_call_target="tpu_custom_call", output_to_operand_aliasing={{}: (11, {})} | custom-call | flops 12884901888 | bytes 12582912 | tf_op jit(solution)/shard_map/pallas_call | solution.py:460
  (132 shorter events, 9.3 us)
Async XLA Ops:
  2.2 117.0 %collective-permute-start.2 = (f32[2,4,4608]{2,1,0:T(4,128)}, f32[2,4,4608]{2,1,0:T(4,128)}, u32[]{:S(2)}, u32[]{:S(2)}) collective-permute-start(f32[2,4,4608]{2,1,0:T(4,128)} %pad_maximum_fusion.1), channel_id=1, source_target_pairs={{0,3},{1,0},{2,1},{3,2},{4,7},{5,4},{6,5},{7,6},{8,11},{9,8},{10,9... | collective-permute-start | bytes 442376 | tf_op jit(solution)/shard_map/ppermute | solution.py:734
  7.3 113.0 %collective-permute-start.1 = (f32[2,4,4608]{2,1,0:T(4,128)}, f32[2,4,4608]{2,1,0:T(4,128)}, u32[]{:S(2)}, u32[]{:S(2)}) collective-permute-start(f32[2,4,4608]{2,1,0:T(4,128)} %pad_maximum_fusion.1), channel_id=1, source_target_pairs={{0,2},{1,3},{2,0},{3,1},{4,6},{5,7},{6,4},{7,5},{8,10},{9,11},{10,... | collective-permute-start | bytes 442376 | tf_op jit(solution)/shard_map/ppermute | solution.py:734
  17.7 20.4 %copy-start.19 = (f32[4,4608]{1,0:T(4,128)S(1)}, f32[4,4608]{1,0:T(4,128)}, u32[]{:S(2)}) copy-start(f32[4,4608]{1,0:T(4,128)} %wt_ref.5) | copy-start | bytes 221188
  53.9 16.0 %copy-start.35 = (f32[16,16]{1,0:T(8,128)S(1)}, f32[16,16]{1,0:T(8,128)}, u32[]{:S(2)}) copy-start(f32[16,16]{1,0:T(8,128)} %param.10) | copy-start | bytes 3076
  53.9 16.0 %copy-start.36 = (f32[16,16]{1,0:T(8,128)S(1)}, f32[16,16]{1,0:T(8,128)}, u32[]{:S(2)}) copy-start(f32[16,16]{1,0:T(8,128)} %param.11) | copy-start | bytes 3076
  65.1 26.2 %collective-permute-start.5 = (bf16[64,1024]{1,0:T(8,128)(2,1)S(1)}, bf16[64,1024]{1,0:T(8,128)(2,1)S(1)}, u32[]{:S(2)}, u32[]{:S(2)}) collective-permute-start(bf16[64,1024]{1,0:T(8,128)(2,1)S(1)} %shard_map.79.refs_0_), channel_id=1, source_target_pairs={{0,3},{1,0},{2,1},{3,2},{4,7},{5,4},{6,5},{7,6},{8,11},{9,8},{10,9... | collective-permute-start | bytes 393224 | tf_op jit(solution)/shard_map/ppermute | solution.py:734
  65.7 25.7 %collective-permute-start.4 = (bf16[64,1024]{1,0:T(8,128)(2,1)S(1)}, bf16[64,1024]{1,0:T(8,128)(2,1)S(1)}, u32[]{:S(2)}, u32[]{:S(2)}) collective-permute-start(bf16[64,1024]{1,0:T(8,128)(2,1)S(1)} %shard_map.79.refs_0_), channel_id=1, source_target_pairs={{0,2},{1,3},{2,0},{3,1},{4,6},{5,7},{6,4},{7,5},{8,10},{9,11},{10,... | collective-permute-start | bytes 393224 | tf_op jit(solution)/shard_map/ppermute | solution.py:734
  67.9 24.2 %collective-permute-start.3 = (bf16[64,1024]{1,0:T(8,128)(2,1)S(1)}, bf16[64,1024]{1,0:T(8,128)(2,1)S(1)}, u32[]{:S(2)}, u32[]{:S(2)}) collective-permute-start(bf16[64,1024]{1,0:T(8,128)(2,1)S(1)} %shard_map.79.refs_0_), channel_id=1, source_target_pairs={{0,1},{1,2},{2,3},{3,0},{4,5},{5,6},{6,7},{7,4},{8,9},{9,10},{10,1... | collective-permute-start | bytes 393224 | tf_op jit(solution)/shard_map/ppermute | solution.py:734
  81.3 3.9 copy-start.1
  91.3 29.7 %collective-permute-start = (f32[2,4,4608]{2,1,0:T(4,128)}, f32[2,4,4608]{2,1,0:T(4,128)}, u32[]{:S(2)}, u32[]{:S(2)}) collective-permute-start(f32[2,4,4608]{2,1,0:T(4,128)} %pad_maximum_fusion.1), channel_id=1, source_target_pairs={{0,1},{1,2},{2,3},{3,0},{4,5},{5,6},{6,7},{7,4},{8,9},{9,10},{10,1... | collective-permute-start | bytes 442376 | tf_op jit(solution)/shard_map/ppermute | solution.py:734
  91.4 32.7 %collective-permute-start.9 = (f16[4,384,128]{2,1,0:T(8,128)(2,1)}, f16[4,384,128]{2,1,0:T(8,128)(2,1)}, u32[]{:S(2)}, u32[]{:S(2)}) collective-permute-start(f16[4,384,128]{2,1,0:T(8,128)(2,1)} %get-tuple-element.41), channel_id=1, source_target_pairs={{0,1},{1,2},{2,3},{3,0},{4,5},{5,6},{6,7},{7,4},{8,9},{9,10},{10,1... | collective-permute-start | bytes 1179656 | tf_op jit(solution)/shard_map/ppermute | solution.py:734
  92.8 33.0 %collective-permute-start.10 = (f16[4,384,128]{2,1,0:T(8,128)(2,1)}, f16[4,384,128]{2,1,0:T(8,128)(2,1)}, u32[]{:S(2)}, u32[]{:S(2)}) collective-permute-start(f16[4,384,128]{2,1,0:T(8,128)(2,1)} %get-tuple-element.42), channel_id=1, source_target_pairs={{0,2},{1,3},{2,0},{3,1},{4,6},{5,7},{6,4},{7,5},{8,10},{9,11},{10,... | collective-permute-start | bytes 1179656 | tf_op jit(solution)/shard_map/ppermute | solution.py:734
  96.4 0.9 copy-start.21
  116.3 84.7 %copy-start = (bf16[3,4,2,64,1024]{4,3,2,1,0:T(8,128)(2,1)}, bf16[3,4,2,64,1024]{4,3,2,1,0:T(8,128)(2,1)S(1)}, u32[]{:S(2)}) copy-start(bf16[3,4,2,64,1024]{4,3,2,1,0:T(8,128)(2,1)S(1)} %shard_map.81) | copy-start | bytes 9437188
  116.3 6.5 %copy-start.34 = (f32[4,4608]{1,0:T(4,128)S(1)}, f32[4,4608]{1,0:T(4,128)}, u32[]{:S(2)}) copy-start(f32[4,4608]{1,0:T(4,128)} %param.9) | copy-start | bytes 221188
  119.2 4.8 copy-start.30
  119.3 14.0 %collective-permute-start.11 = (f16[4,384,128]{2,1,0:T(8,128)(2,1)}, f16[4,384,128]{2,1,0:T(8,128)(2,1)S(1)}, u32[]{:S(2)}, u32[]{:S(2)}) collective-permute-start(f16[4,384,128]{2,1,0:T(8,128)(2,1)} %get-tuple-element.43), channel_id=1, source_target_pairs={{0,3},{1,0},{2,1},{3,2},{4,7},{5,4},{6,5},{7,6},{8,11},{9,8},{10,9... | collective-permute-start | bytes 1179656 | tf_op jit(solution)/shard_map/ppermute | solution.py:734
  120.3 29.7 %collective-permute-start.8 = (f16[4,768,128]{2,1,0:T(8,128)(2,1)}, f16[4,768,128]{2,1,0:T(8,128)(2,1)S(1)}, u32[]{:S(2)}, u32[]{:S(2)}) collective-permute-start(f16[4,768,128]{2,1,0:T(8,128)(2,1)} %get-tuple-element.91), channel_id=1, source_target_pairs={{0,3},{1,0},{2,1},{3,2},{4,7},{5,4},{6,5},{7,6},{8,11},{9,8},{10,9... | collective-permute-start | bytes 2359304 | tf_op jit(solution)/shard_map/ppermute | solution.py:734
  121.1 79.6 %collective-permute-start.7 = (f16[4,768,128]{2,1,0:T(8,128)(2,1)}, f16[4,768,128]{2,1,0:T(8,128)(2,1)S(1)}, u32[]{:S(2)}, u32[]{:S(2)}) collective-permute-start(f16[4,768,128]{2,1,0:T(8,128)(2,1)} %get-tuple-element.92), channel_id=1, source_target_pairs={{0,2},{1,3},{2,0},{3,1},{4,6},{5,7},{6,4},{7,5},{8,10},{9,11},{10,... | collective-permute-start | bytes 2359304 | tf_op jit(solution)/shard_map/ppermute | solution.py:734
  124.1 97.5 %copy-start.12 = (f32[16,4608]{1,0:T(8,128)}, f32[16,4608]{1,0:T(8,128)S(1)}, u32[]{:S(2)}) copy-start(f32[16,4608]{1,0:T(8,128)S(1)} %get-tuple-element.95.k_ref) | copy-start | bytes 884740
  124.1 76.7 %collective-permute-start.6 = (f16[4,768,128]{2,1,0:T(8,128)(2,1)S(1)}, f16[4,768,128]{2,1,0:T(8,128)(2,1)S(1)}, u32[]{:S(2)}, u32[]{:S(2)}) collective-permute-start(f16[4,768,128]{2,1,0:T(8,128)(2,1)S(1)} %copy-done.30), channel_id=1, source_target_pairs={{0,1},{1,2},{2,3},{3,0},{4,5},{5,6},{6,7},{7,4},{8,9},{9,10},{10,1... | collective-permute-start | bytes 2359304 | tf_op jit(solution)/shard_map/ppermute | solution.py:734
  150.2 50.8 %copy-start.3 = (f32[4,768,128]{2,1,0:T(8,128)}, f32[4,768,128]{2,1,0:T(8,128)S(1)}, u32[]{:S(2)}) copy-start(f32[4,768,128]{2,1,0:T(8,128)S(1)} %convert_multiply_fusion.rest_3_) | copy-start | bytes 4718596
  200.8 16.1 %copy-start.4 = (f32[4,768,128]{2,1,0:T(8,128)}, f32[4,768,128]{2,1,0:T(8,128)S(1)}, u32[]{:S(2)}) copy-start(f32[4,768,128]{2,1,0:T(8,128)S(1)} %convert_multiply_fusion.1.rest_2_) | copy-start | bytes 4718596
  200.8 2.0 copy-start.2
  200.8 2.1 copy-start.16
  201.0 15.9 %copy-start.5 = (f32[4,768,128]{2,1,0:T(8,128)}, f32[4,768,128]{2,1,0:T(8,128)S(1)}, u32[]{:S(2)}) copy-start(f32[4,768,128]{2,1,0:T(8,128)S(1)} %convert_multiply_fusion.2.rest_1_) | copy-start | bytes 4718596
  216.9 4.7 copy-start.14
  217.8 43.1 %collective-permute-start.17 = (f16[4,384,128]{2,1,0:T(8,128)(2,1)S(1)}, f16[4,384,128]{2,1,0:T(8,128)(2,1)S(1)}, u32[]{:S(2)}, u32[]{:S(2)}) collective-permute-start(f16[4,384,128]{2,1,0:T(8,128)(2,1)S(1)} %multiply_convert_fusion.9), channel_id=1, source_target_pairs={{0,1},{1,2},{2,3},{3,0},{4,5},{5,6},{6,7},{7,4},{8,9},{9,10},{10,1... | collective-permute-start | bytes 1179656 | tf_op jit(solution)/shard_map/ppermute | solution.py:734
  217.8 47.6 %collective-permute-start.16 = (f16[4,384,128]{2,1,0:T(8,128)(2,1)S(1)}, f16[4,384,128]{2,1,0:T(8,128)(2,1)S(1)}, u32[]{:S(2)}, u32[]{:S(2)}) collective-permute-start(f16[4,384,128]{2,1,0:T(8,128)(2,1)S(1)} %multiply_convert_fusion.10), channel_id=1, source_target_pairs={{0,2},{1,3},{2,0},{3,1},{4,6},{5,7},{6,4},{7,5},{8,10},{9,11},{10,... | collective-permute-start | bytes 1179656 | tf_op jit(solution)/shard_map/ppermute | solution.py:734
  217.8 47.6 %collective-permute-start.15 = (f16[4,384,128]{2,1,0:T(8,128)(2,1)S(1)}, f16[4,384,128]{2,1,0:T(8,128)(2,1)S(1)}, u32[]{:S(2)}, u32[]{:S(2)}) collective-permute-start(f16[4,384,128]{2,1,0:T(8,128)(2,1)S(1)} %multiply_convert_fusion.11), channel_id=1, source_target_pairs={{0,3},{1,0},{2,1},{3,2},{4,7},{5,4},{6,5},{7,6},{8,11},{9,8},{10,9... | collective-permute-start | bytes 1179656 | tf_op jit(solution)/shard_map/ppermute | solution.py:734
  252.6 1.4 copy-start.27
  252.8 1.8 copy-start.26
  254.6 1.5 copy-start.25
  257.2 7.1 %copy-start.24 = (f32[4,768,128]{2,1,0:T(8,128)S(1)}, f32[4,768,128]{2,1,0:T(8,128)}, u32[]{:S(2)}) copy-start(f32[4,768,128]{2,1,0:T(8,128)} %get-tuple-element.59) | copy-start | bytes 4718596
  258.9 22.3 %collective-permute-start.14 = (f16[4,768,128]{2,1,0:T(8,128)(2,1)S(1)}, f16[4,768,128]{2,1,0:T(8,128)(2,1)S(1)}, u32[]{:S(2)}, u32[]{:S(2)}) collective-permute-start(f16[4,768,128]{2,1,0:T(8,128)(2,1)S(1)} %multiply_convert_fusion.3), channel_id=1, source_target_pairs={{0,1},{1,2},{2,3},{3,0},{4,5},{5,6},{6,7},{7,4},{8,9},{9,10},{10,1... | collective-permute-start | bytes 2359304 | tf_op jit(solution)/shard_map/ppermute | solution.py:734
  259.5 54.0 %collective-permute-start.13 = (f16[4,768,128]{2,1,0:T(8,128)(2,1)S(1)}, f16[4,768,128]{2,1,0:T(8,128)(2,1)S(1)}, u32[]{:S(2)}, u32[]{:S(2)}) collective-permute-start(f16[4,768,128]{2,1,0:T(8,128)(2,1)S(1)} %multiply_convert_fusion.4), channel_id=1, source_target_pairs={{0,2},{1,3},{2,0},{3,1},{4,6},{5,7},{6,4},{7,5},{8,10},{9,11},{10,... | collective-permute-start | bytes 2359304 | tf_op jit(solution)/shard_map/ppermute | solution.py:734
  260.9 52.5 %collective-permute-start.12 = (f16[4,768,128]{2,1,0:T(8,128)(2,1)S(1)}, f16[4,768,128]{2,1,0:T(8,128)(2,1)S(1)}, u32[]{:S(2)}, u32[]{:S(2)}) collective-permute-start(f16[4,768,128]{2,1,0:T(8,128)(2,1)S(1)} %multiply_convert_fusion.5), channel_id=1, source_target_pairs={{0,3},{1,0},{2,1},{3,2},{4,7},{5,4},{6,5},{7,6},{8,11},{9,8},{10,9... | collective-permute-start | bytes 2359304 | tf_op jit(solution)/shard_map/ppermute | solution.py:734
  267.7 5.5 %copy-start.6 = (f32[4,384,128]{2,1,0:T(8,128)}, f32[4,384,128]{2,1,0:T(8,128)S(1)}, u32[]{:S(2)}) copy-start(f32[4,384,128]{2,1,0:T(8,128)S(1)} %get-tuple-element.85.rest_2_) | copy-start | bytes 2359300
  267.7 5.5 %copy-start.8 = (f32[4,384,128]{2,1,0:T(8,128)}, f32[4,384,128]{2,1,0:T(8,128)S(1)}, u32[]{:S(2)}) copy-start(f32[4,384,128]{2,1,0:T(8,128)S(1)} %get-tuple-element.86.rest_1_) | copy-start | bytes 2359300
  267.7 5.5 %copy-start.10 = (f32[4,384,128]{2,1,0:T(8,128)}, f32[4,384,128]{2,1,0:T(8,128)S(1)}, u32[]{:S(2)}) copy-start(f32[4,384,128]{2,1,0:T(8,128)S(1)} %get-tuple-element.87.rest_0_) | copy-start | bytes 2359300
  345.5 61.5 %slice-start = ((s8[9437184]{0:T(1024)(128)(4,1)}), s8[4194304]{0:T(1024)(128)(4,1)S(1)}, s32[]{:S(2)}) async-start(s8[9437184]{0:T(1024)(128)(4,1)} %bitcast.27), calls=%async_computation | async-start | bytes 8388608
  345.5 61.5 %slice-start.1 = ((s8[9437184]{0:T(1024)(128)(4,1)}), s8[4194304]{0:T(1024)(128)(4,1)S(1)}, s32[]{:S(2)}) async-start(s8[9437184]{0:T(1024)(128)(4,1)} %bitcast.27), calls=%async_computation.1 | async-start | bytes 8388608
  345.5 61.4 %slice-start.2 = ((s8[9437184]{0:T(1024)(128)(4,1)}), s8[1048576]{0:T(1024)(128)(4,1)S(1)}, s32[]{:S(2)}) async-start(s8[9437184]{0:T(1024)(128)(4,1)} %bitcast.27), calls=%async_computation.2 | async-start | bytes 2097152
  361.5 28.9 %copy-start.23 = (f32[4,768,128]{2,1,0:T(8,128)S(1)}, f32[4,768,128]{2,1,0:T(8,128)}, u32[]{:S(2)}) copy-start(f32[4,768,128]{2,1,0:T(8,128)} %get-tuple-element.60) | copy-start | bytes 4718596
  372.8 18.7 %copy-start.33 = (f16[4,384,128]{2,1,0:T(8,128)(2,1)S(1)}, f16[4,384,128]{2,1,0:T(8,128)(2,1)}, u32[]{:S(2)}) copy-start(f16[4,384,128]{2,1,0:T(8,128)(2,1)} %multiply_convert_fusion.17) | copy-start | bytes 1179652
  372.8 22.5 %copy-start.32 = (f16[4,384,128]{2,1,0:T(8,128)(2,1)S(1)}, f16[4,384,128]{2,1,0:T(8,128)(2,1)}, u32[]{:S(2)}) copy-start(f16[4,384,128]{2,1,0:T(8,128)(2,1)} %multiply_convert_fusion.16) | copy-start | bytes 1179652
  372.8 33.6 %collective-permute-start.20 = (bf16[64,1024]{1,0:T(8,128)(2,1)S(1)}, bf16[64,1024]{1,0:T(8,128)(2,1)S(1)}, u32[]{:S(2)}, u32[]{:S(2)}) collective-permute-start(bf16[64,1024]{1,0:T(8,128)(2,1)S(1)} %shard_map.88.refs_0_), channel_id=1, source_target_pairs={{0,3},{1,0},{2,1},{3,2},{4,7},{5,4},{6,5},{7,6},{8,11},{9,8},{10,9... | collective-permute-start | bytes 393224 | tf_op jit(solution)/shard_map/ppermute | solution.py:734
  390.5 16.0 %copy-start.31 = (f16[4,384,128]{2,1,0:T(8,128)(2,1)S(1)}, f16[4,384,128]{2,1,0:T(8,128)(2,1)}, u32[]{:S(2)}) copy-start(f16[4,384,128]{2,1,0:T(8,128)(2,1)} %multiply_convert_fusion.15) | copy-start | bytes 1179652
  390.5 16.5 %copy-start.7 = (f32[4,384,128]{2,1,0:T(8,128)S(1)}, f32[4,384,128]{2,1,0:T(8,128)}, u32[]{:S(2)}) copy-start(f32[4,384,128]{2,1,0:T(8,128)} %copy-done.6) | copy-start | bytes 2359300
  390.5 16.5 %copy-start.9 = (f32[4,384,128]{2,1,0:T(8,128)S(1)}, f32[4,384,128]{2,1,0:T(8,128)}, u32[]{:S(2)}) copy-start(f32[4,384,128]{2,1,0:T(8,128)} %copy-done.8) | copy-start | bytes 2359300
  390.5 16.5 %copy-start.11 = (f32[4,384,128]{2,1,0:T(8,128)S(1)}, f32[4,384,128]{2,1,0:T(8,128)}, u32[]{:S(2)}) copy-start(f32[4,384,128]{2,1,0:T(8,128)} %copy-done.10) | copy-start | bytes 2359300
  390.7 31.3 %collective-permute-start.19 = (bf16[64,1024]{1,0:T(8,128)(2,1)S(1)}, bf16[64,1024]{1,0:T(8,128)(2,1)S(1)}, u32[]{:S(2)}, u32[]{:S(2)}) collective-permute-start(bf16[64,1024]{1,0:T(8,128)(2,1)S(1)} %shard_map.88.refs_0_), channel_id=1, source_target_pairs={{0,2},{1,3},{2,0},{3,1},{4,6},{5,7},{6,4},{7,5},{8,10},{9,11},{10,... | collective-permute-start | bytes 393224 | tf_op jit(solution)/shard_map/ppermute | solution.py:734
  391.5 33.3 %collective-permute-start.18 = (bf16[64,1024]{1,0:T(8,128)(2,1)S(1)}, bf16[64,1024]{1,0:T(8,128)(2,1)S(1)}, u32[]{:S(2)}, u32[]{:S(2)}) collective-permute-start(bf16[64,1024]{1,0:T(8,128)(2,1)S(1)} %shard_map.88.refs_0_), channel_id=1, source_target_pairs={{0,1},{1,2},{2,3},{3,0},{4,5},{5,6},{6,7},{7,4},{8,9},{9,10},{10,1... | collective-permute-start | bytes 393224 | tf_op jit(solution)/shard_map/ppermute | solution.py:734
  391.5 53.3 %collective-permute-start.24 = (f16[4,384,128]{2,1,0:T(8,128)(2,1)S(1)}, f16[4,384,128]{2,1,0:T(8,128)(2,1)S(1)}, u32[]{:S(2)}, u32[]{:S(2)}) collective-permute-start(f16[4,384,128]{2,1,0:T(8,128)(2,1)S(1)} %copy-done.33), channel_id=1, source_target_pairs={{0,3},{1,0},{2,1},{3,2},{4,7},{5,4},{6,5},{7,6},{8,11},{9,8},{10,9... | collective-permute-start | bytes 1179656 | tf_op jit(solution)/shard_map/ppermute | solution.py:734
  395.4 76.1 %collective-permute-start.25 = (f16[4,384,128]{2,1,0:T(8,128)(2,1)S(1)}, f16[4,384,128]{2,1,0:T(8,128)(2,1)S(1)}, u32[]{:S(2)}, u32[]{:S(2)}) collective-permute-start(f16[4,384,128]{2,1,0:T(8,128)(2,1)S(1)} %copy-done.32), channel_id=1, source_target_pairs={{0,2},{1,3},{2,0},{3,1},{4,6},{5,7},{6,4},{7,5},{8,10},{9,11},{10,... | collective-permute-start | bytes 1179656 | tf_op jit(solution)/shard_map/ppermute | solution.py:734
  406.5 65.0 %collective-permute-start.26 = (f16[4,384,128]{2,1,0:T(8,128)(2,1)S(1)}, f16[4,384,128]{2,1,0:T(8,128)(2,1)S(1)}, u32[]{:S(2)}, u32[]{:S(2)}) collective-permute-start(f16[4,384,128]{2,1,0:T(8,128)(2,1)S(1)} %copy-done.31), channel_id=1, source_target_pairs={{0,1},{1,2},{2,3},{3,0},{4,5},{5,6},{6,7},{7,4},{8,9},{9,10},{10,1... | collective-permute-start | bytes 1179656 | tf_op jit(solution)/shard_map/ppermute | solution.py:734
  407.0 17.8 %copy-start.29 = (f16[4,768,128]{2,1,0:T(8,128)(2,1)S(1)}, f16[4,768,128]{2,1,0:T(8,128)(2,1)}, u32[]{:S(2)}) copy-start(f16[4,768,128]{2,1,0:T(8,128)(2,1)} %multiply_convert_fusion.1) | copy-start | bytes 2359300
  421.9 22.9 %copy-start.28 = (f16[4,768,128]{2,1,0:T(8,128)(2,1)S(1)}, f16[4,768,128]{2,1,0:T(8,128)(2,1)}, u32[]{:S(2)}) copy-start(f16[4,768,128]{2,1,0:T(8,128)(2,1)} %multiply_convert_fusion.2) | copy-start | bytes 2359300
  421.9 49.6 %copy-start.18 = (f32[4,384,128]{2,1,0:T(8,128)S(1)}, f32[4,384,128]{2,1,0:T(8,128)}, u32[]{:S(2)}) copy-start(f32[4,384,128]{2,1,0:T(8,128)} %copy-done.17) | copy-start | bytes 2359300
  421.9 69.1 %collective-permute-start.23 = (f16[4,768,128]{2,1,0:T(8,128)(2,1)S(1)}, f16[4,768,128]{2,1,0:T(8,128)(2,1)S(1)}, u32[]{:S(2)}, u32[]{:S(2)}) collective-permute-start(f16[4,768,128]{2,1,0:T(8,128)(2,1)S(1)} %multiply_convert_fusion), channel_id=1, source_target_pairs={{0,1},{1,2},{2,3},{3,0},{4,5},{5,6},{6,7},{7,4},{8,9},{9,10},{10,1... | collective-permute-start | bytes 2359304 | tf_op jit(solution)/shard_map/ppermute | solution.py:734
  424.9 66.2 %collective-permute-start.22 = (f16[4,768,128]{2,1,0:T(8,128)(2,1)S(1)}, f16[4,768,128]{2,1,0:T(8,128)(2,1)S(1)}, u32[]{:S(2)}, u32[]{:S(2)}) collective-permute-start(f16[4,768,128]{2,1,0:T(8,128)(2,1)S(1)} %copy-done.29), channel_id=1, source_target_pairs={{0,2},{1,3},{2,0},{3,1},{4,6},{5,7},{6,4},{7,5},{8,10},{9,11},{10,... | collective-permute-start | bytes 2359304 | tf_op jit(solution)/shard_map/ppermute | solution.py:734
  444.8 59.5 %collective-permute-start.21 = (f16[4,768,128]{2,1,0:T(8,128)(2,1)S(1)}, f16[4,768,128]{2,1,0:T(8,128)(2,1)}, u32[]{:S(2)}, u32[]{:S(2)}) collective-permute-start(f16[4,768,128]{2,1,0:T(8,128)(2,1)S(1)} %copy-done.28), channel_id=1, source_target_pairs={{0,3},{1,0},{2,1},{3,2},{4,7},{5,4},{6,5},{7,6},{8,11},{9,8},{10,9... | collective-permute-start | bytes 2359304 | tf_op jit(solution)/shard_map/ppermute | solution.py:734
  471.5 2.4 copy-start.13
  473.9 30.4 %copy-start.22 = (f32[4,768,128]{2,1,0:T(8,128)S(1)}, f32[4,768,128]{2,1,0:T(8,128)}, u32[]{:S(2)}) copy-start(f32[4,768,128]{2,1,0:T(8,128)} %get-tuple-element.57) | copy-start | bytes 4718596
  (3 other events, 2.2 us)

commit v5 on v4

--- a/solution.py
+++ b/solution.py
@@ -369,17 +369,7 @@
         return result
     steps = quarter // size
     pieces = [x for group in sources for x in group]
-    first = parts * (sources[0][0].shape[1] // size)
-    ranks = [around(parts, steps, 0, first // parts)]
-    if len(sources) > 1:
-        ranks.append(around(parts, steps, first // parts, steps - first // parts))
-
-    def at(i, m):
-        place = ranks[0](i, m)
-        if len(ranks) > 1:
-            place = jnp.where(i < first, place, ranks[1](jnp.maximum(i - first, 0), m))
-        return place
-
+    at = lambda i, m: lax.rem(m[0] + lax.rem(i, parts), parts) * steps + lax.div(i, parts)
     return pl.pallas_call(
         functools.partial(amplitude_kernel, len(pieces)),
         out_shape=jax.ShapeDtypeStruct((own, pairs, cols), jnp.float32),
@@ -590,7 +580,8 @@
 
 
 def gather_kernel(chips, parts, *refs):
-    x_refs, (o_ref, joined, *sems) = refs[:parts], refs[parts:]
+    x_ref, o_ref, joined, *sems = refs
+    x_refs = [x_ref.at[s] for s in range(parts)]
     kept = sems[4]
     plane = Plane(chips)
     chip, core, pal = plane.chip, plane.core, plane.pal
@@ -703,20 +694,19 @@
 def gathered_over(blocks):
     n = lax.axis_size("fac")
     chips = n // 2
-    parts = len(blocks)
-    block, width = blocks[0].shape
+    parts, block, width = blocks.shape
     flat = (parts, chips, 2, block, width)
     result = pl.pallas_call(
         functools.partial(gather_kernel, chips, parts),
         out_shape=jax.ShapeDtypeStruct(flat, jnp.bfloat16),
-        in_specs=[pl.BlockSpec(memory_space=pl.ANY)] * parts,
+        in_specs=[WHOLE],
         out_specs=WHOLE,
         scratch_shapes=[VMEM(flat, jnp.bfloat16)]
         + dmas(parts * chips, 2)
         + [pltpu.SemaphoreType.DMA((parts,))],
         compiler_params=reach_params(2 if parts == 1 else 3),
         cost_estimate=reach_cost(block * width * parts * 8),
-    )(*blocks)
+    )(blocks)
     return result.reshape(parts * n * block, width)
 
 
@@ -747,13 +737,16 @@
     )
 
     both = jnp.stack([pair_weight, second_order])
-    tables = jnp.concatenate([shift(both, s) for s in range(parts)], axis=1)
-    weights, kernels = tables[0], tables[1]
+    fine = HALF_TOP / 2.0
+    slim = (both * fine).astype(jnp.float16)
+    came = [shift(slim, s) for s in range(1, parts)]
+    tables = [both] + [x.astype(jnp.float32) * (1.0 / fine) for x in came]
+    weights, kernels = [jnp.concatenate([x[n] for x in tables]) for n in range(2)]
     size = tile_of(quarter) or quarter
     chunks = quarter // size
     early = max(chunks - 1, 1)
     groups = [(0, early)] + ([(early, chunks)] if early < chunks else [])
-    calls = [(0, 1)] + ([(1, chunks)] if chunks > 1 else [])
+    calls = [(k, k + 1) for k in range(chunks)]
     tie = lax.optimization_barrier
     up = 8192.0
 
@@ -784,13 +777,19 @@
             total = again(factors, pair_weight, mine, kept)
         block = summed(total, False)
         far = [shift(block, s) for s in range(1, parts)]
-        return gathered_over([block]), far
-
-    leaves = [leaving(*g) for g in groups]
+        return gathered_over(block[None]), far
+
+    def joined(blocks):
+        blocks = jnp.stack(blocks)
+        return gathered_over(blocks)
+
+    leaves = []
+    for g in groups:
+        leaves.append(leaving(*g))
     right_late, leaves[-1] = tie((right_side, leaves[-1]))
     came = [passed(x, False) for x in leaves]
     near, blocks = ladder(first_projection())
-    far = gathered_over(blocks)
+    far = joined(blocks)
 
     def tall(x):
         return jnp.max(jnp.sum(jnp.abs(x.astype(jnp.float32)), axis=1))
@@ -842,7 +841,7 @@
     for n in range(1, len(calls)):
         back.append(passed(halves[n], True))
     amplitudes = amplitude(me, factors, pair_weight, near, sources)
-    far = gathered_over(blocks)
+    far = joined(blocks)
     outs = []
     for n, group in enumerate(calls):
         back[n], outs = tie((back[n], outs))

time: 549 us -> 544 us (level)
  the two profiles are of different devices: /device:TPU:0 before, /device:TPU:24 now
where the time goes in v5:
time: 544 us; the launch traced here: 537 us
  Pallas kernels  276 us (51%)
  starting transfers between devices  108 us (20%)
  waiting for transfers between devices  101 us (19%)
  other arithmetic  33 us (6%)
  matrix products  11.4 us (2%)
    ppermute x33, starting transfers between devices, shift(): lax.ppermute(x, 'freq', [(i, (i + by) % parts) for i in range(parts)])  108 us
    ppermute x33, waiting for transfers between devices, shift(): lax.ppermute(x, 'freq', [(i, (i + by) % parts) for i in range(parts)])  101 us
    pallas_call x4, Pallas kernels, gathered_over(): pl.pallas_call(functools.partial(gather_kernel, chips, parts), out_shape=...  59.5 us
    pallas_call x3, Pallas kernels, final(): pl.pallas_call(functools.partial(final_kernel, nf, parts, len(outs)), out...  50.9 us
    pallas_call x3, Pallas kernels, quarter_pass(): pl.pallas_call(functools.partial(quarter_kernel, nf, parts, sets), out_sh...  41.9 us
    pallas_call x2, Pallas kernels, summed(): pl.pallas_call(functools.partial(sum_kernel, chips), out_shape=jax.ShapeD...  39.4 us
    pallas_call x2, Pallas kernels, again(): pl.pallas_call(functools.partial(again_kernel, own), out_shape=jax.ShapeD...  31.8 us
    pallas_call x2, Pallas kernels, summed(): pl.pallas_call(functools.partial(reduce_kernel, chips), out_shape=jax.Sha...  22.5 us
  transfers between devices with their start and end apart: 33, of which 6 were waited for; matrix products, arithmetic and copies ran while one was open for 8% of the time, Pallas kernels for 38%

profile of v5, /device:TPU:24, one launch (start us, length us, event | category | flops | bytes accessed | tf_op | source)
XLA Modules:
  0.0 537.0 jit_solution(8320126783062365927)
XLA Ops:
  0.6 1.0 fusion.3
  2.1 3.4 collective-permute-start
  5.5 10.4 %fusion = f32[4,128,1024]{2,1,0:T(8,128)S(1)} fusion(bf16[4608,1024]{1,0:T(8,128)(2,1)} %l_ref.23, f32[4,4608,128]{2,1,0:T(8,128)} %rest_0_.5), kind=kOutput, calls=%fused_computation | convolution fusion | flops 4834197504 | bytes 20971520 | tf_op jit(solution)/shard_map/pa,fpc->fca/dot_general | solution.py:766
  15.9 20.1 %shard_map.77 = bf16[4,2,64,1024]{3,2,1,0:T(8,128)(2,1)S(1)} custom-call(f32[4,2,64,1024]{3,2,1,0:T(8,128)S(1)} %bitcast.59), custom_call_target="tpu_custom_call" | custom-call | flops 20971520 | bytes 20971520 | tf_op jit(solution)/shard_map/pallas_call | solution.py:679
  36.0 15.8 %shard_map.78 = f32[512,1024]{1,0:T(8,128)S(1)} custom-call(bf16[4608,1024]{1,0:T(8,128)(2,1)} %l_ref.23, f32[4,4608]{1,0:T(4,128)S(1)} %copy-done.19, bf16[512,1024]{1,0:T(8,128)(2,1)S(1)} %bitcast.66, f32[512,1024]{1,0:T(8,128)S(1)} %bitcast.60), custom_call_target="tpu_custom_call" | custom-call | flops 9663676416 | bytes 9437184 | tf_op jit(solution)/shard_map/pallas_call | solution.py:285
  51.8 11.3 %shard_map.79 = bf16[64,1024]{1,0:T(8,128)(2,1)S(1)} custom-call(f32[4,2,64,1024]{3,2,1,0:T(8,128)S(1)} %bitcast.64), custom_call_target="tpu_custom_call" | custom-call | flops 10485760 | bytes 10485760 | tf_op jit(solution)/shard_map/pallas_call | solution.py:670
  63.8 1.5 collective-permute-start.4
  66.9 2.8 multiply_convert_fusion.18
  69.6 11.0 %shard_map.80 = bf16[1,4,2,64,1024]{4,3,2,1,0:T(8,128)(2,1)S(1)} custom-call(bf16[1,64,1024]{2,1,0:T(8,128)(2,1)S(1)} %bitcast.69), custom_call_target="tpu_custom_call" | custom-call | flops 20971520 | bytes 20971520 | tf_op jit(solution)/shard_map/pallas_call | solution.py:699
  80.9 1.0 copy-done
  81.9 4.0 multiply_convert_fusion
  88.0 2.7 collective-permute-start.3
  90.9 0.9 collective-permute-start.10
  92.7 2.0 collective-permute-start.11
  95.4 1.8 collective-permute-start.7
  97.2 18.6 %shard_map.81 = bf16[3,4,2,64,1024]{4,3,2,1,0:T(8,128)(2,1)S(1)} custom-call(bf16[3,64,1024]{2,1,0:T(8,128)(2,1)S(1)} %pad_maximum_fusion.refs_0_), custom_call_target="tpu_custom_call" | custom-call | flops 62914560 | bytes 62914560 | tf_op jit(solution)/shard_map/pallas_call | solution.py:699
  115.8 1.3 abs_reduce_fusion
  117.1 1.4 reduce_max.29
  119.9 3.1 collective-permute-start.6
  123.0 1.1 convert_multiply_fusion.5.rest_1_
  124.0 39.5 %collective-permute-done.10 = f16[4,384,128]{2,1,0:T(8,128)(2,1)} collective-permute-done((f16[4,384,128]{2,1,0:T(8,128)(2,1)}, f16[4,384,128]{2,1,0:T(8,128)(2,1)}, u32[]{:S(2)}, u32[]{:S(2)}) %collective-permute-start.10) | collective-permute-done | bytes 393248 | tf_op jit(solution)/shard_map/ppermute | solution.py:724
  163.5 1.1 convert_multiply_fusion.4.rest_2_
  164.6 1.1 convert_multiply_fusion.3.rest_3_
  165.7 14.0 %shard_map.83 = (f32[4,384,128]{2,1,0:T(8,128)S(1)}, f32[4,384,128]{2,1,0:T(8,128)S(1)}, f32[4,384,128]{2,1,0:T(8,128)S(1)}, f32[4,384,128]{2,1,0:T(8,128)S(1)},...) custom-call(s32[1]{0:T(128)} %bitcast.me_ref, ...), custom_call_target="tpu_custom_call" | custom-call | flops 2415919104 | bytes 12582912 | tf_op jit(solution)/shard_map/pallas_call | solution.py:152
  180.9 0.8 multiply_convert_fusion.7
  181.8 0.8 multiply_convert_fusion.6
  182.6 1.3 convert_multiply_fusion.rest_3_
  183.9 1.3 convert_multiply_fusion.1.rest_2_
  185.2 7.0 %collective-permute-done.6 = f16[4,768,128]{2,1,0:T(8,128)(2,1)S(1)} collective-permute-done((f16[4,768,128]{2,1,0:T(8,128)(2,1)}, f16[4,768,128]{2,1,0:T(8,128)(2,1)S(1)}, u32[]{:S(2)}, u32[]{:S(2)}) %collective-permute-start.6) | collective-permute-done | bytes 786464 | tf_op jit(solution)/shard_map/ppermute | solution.py:724
  192.3 14.0 %shard_map.84 = (f32[4,384,128]{2,1,0:T(8,128)S(1)}, f32[4,384,128]{2,1,0:T(8,128)S(1)}, f32[4,384,128]{2,1,0:T(8,128)S(1)}, f32[4,384,128]{2,1,0:T(8,128)S(1)},...) custom-call(s32[1]{0:T(128)} %bitcast.me_ref, ...), custom_call_target="tpu_custom_call" | custom-call | flops 2415919104 | bytes 12582912 | tf_op jit(solution)/shard_map/pallas_call | solution.py:152
  206.3 0.9 copy-done.13
  207.3 0.9 copy-done.17
  208.1 14.0 %shard_map.82 = (f32[4,384,128]{2,1,0:T(8,128)S(1)}, f32[4,384,128]{2,1,0:T(8,128)S(1)}, f32[4,384,128]{2,1,0:T(8,128)S(1)}, f32[4,384,128]{2,1,0:T(8,128)S(1)},...) custom-call(s32[1]{0:T(128)} %bitcast.me_ref, ...), custom_call_target="tpu_custom_call" | custom-call | flops 2415919104 | bytes 12582912 | tf_op jit(solution)/shard_map/pallas_call | solution.py:152
  223.4 25.6 %collective-permute-start.20 = (f16[4,384,128]{2,1,0:T(8,128)(2,1)S(1)}, f16[4,384,128]{2,1,0:T(8,128)(2,1)S(1)}, u32[]{:S(2)}, u32[]{:S(2)}) collective-permute-start(f16[4,384,128]{2,1,0:T(8,128)(2,1)S(1)} %multiply_convert_fusion.9), channel_id=1, source_target_pairs={{0,1},{1,2},{2,3},{3,0},{4,5},{5,6},{6,7},{7,4},{8,9},{9,10},{10,1... | collective-permute-start | bytes 1179656 | tf_op jit(solution)/shard_map/ppermute | solution.py:724
  249.1 0.8 collective-permute-start.18
  250.1 8.5 %collective-permute-done.20 = f16[4,384,128]{2,1,0:T(8,128)(2,1)S(1)} collective-permute-done((f16[4,384,128]{2,1,0:T(8,128)(2,1)S(1)}, f16[4,384,128]{2,1,0:T(8,128)(2,1)S(1)}, u32[]{:S(2)}, u32[]{:S(2)}) %collective-permute-start.20) | collective-permute-done | bytes 393248 | tf_op jit(solution)/shard_map/ppermute | solution.py:724
  258.6 4.3 collective-permute-start.17
  262.9 20.2 %collective-permute-done.19 = f16[4,384,128]{2,1,0:T(8,128)(2,1)S(1)} collective-permute-done((f16[4,384,128]{2,1,0:T(8,128)(2,1)S(1)}, f16[4,384,128]{2,1,0:T(8,128)(2,1)S(1)}, u32[]{:S(2)}, u32[]{:S(2)}) %collective-permute-start.19) | collective-permute-done | bytes 393248 | tf_op jit(solution)/shard_map/ppermute | solution.py:724
  283.1 18.2 %collective-permute-start.15 = (f16[4,384,128]{2,1,0:T(8,128)(2,1)S(1)}, f16[4,384,128]{2,1,0:T(8,128)(2,1)S(1)}, u32[]{:S(2)}, u32[]{:S(2)}) collective-permute-start(f16[4,384,128]{2,1,0:T(8,128)(2,1)S(1)} %multiply_convert_fusion.14), channel_id=1, source_target_pairs={{0,3},{1,0},{2,1},{3,2},{4,7},{5,4},{6,5},{7,6},{8,11},{9,8},{10,9... | collective-permute-start | bytes 1179656 | tf_op jit(solution)/shard_map/ppermute | solution.py:724
  301.3 2.4 multiply_add_fusion.15
  303.9 4.7 shard_map.85.rest_4_
  308.6 2.5 collective-permute-start.12
  311.1 13.0 %collective-permute-done.16 = f16[4,384,128]{2,1,0:T(8,128)(2,1)S(1)} collective-permute-done((f16[4,384,128]{2,1,0:T(8,128)(2,1)S(1)}, f16[4,384,128]{2,1,0:T(8,128)(2,1)S(1)}, u32[]{:S(2)}, u32[]{:S(2)}) %collective-permute-start.16) | collective-permute-done | bytes 393248 | tf_op jit(solution)/shard_map/ppermute | solution.py:724
  324.1 2.4 multiply_add_fusion.12
  326.4 4.7 shard_map.86.rest_4_
  331.2 2.4 multiply_add_fusion.9
  333.6 5.3 shard_map.87.x_ref
  338.9 19.3 %shard_map.88 = bf16[4,2,64,1024]{3,2,1,0:T(8,128)(2,1)S(1)} custom-call(f32[4,2,64,1024]{3,2,1,0:T(8,128)S(1)} %bitcast.58), custom_call_target="tpu_custom_call" | custom-call | flops 20971520 | bytes 20971520 | tf_op jit(solution)/shard_map/pallas_call | solution.py:679
  358.3 16.0 %shard_map.89 = f32[512,1024]{1,0:T(8,128)S(1)} custom-call(bf16[4608,1024]{1,0:T(8,128)(2,1)} %l_ref.23, f32[4,4608]{1,0:T(4,128)S(1)} %copy-done.19, bf16[512,1024]{1,0:T(8,128)(2,1)S(1)} %bitcast.67, f32[512,1024]{1,0:T(8,128)S(1)} %shard_map.87.x_ref), custom_call_target="tpu_custom_call" | custom-call | flops 9663676416 | bytes 9437184 | tf_op jit(solution)/shard_map/pallas_call | solution.py:285
  374.3 11.3 %shard_map.90 = bf16[64,1024]{1,0:T(8,128)(2,1)S(1)} custom-call(f32[4,2,64,1024]{3,2,1,0:T(8,128)S(1)} %bitcast.65), custom_call_target="tpu_custom_call" | custom-call | flops 10485760 | bytes 10485760 | tf_op jit(solution)/shard_map/pallas_call | solution.py:670
  385.8 3.9 collective-permute-start.21
  390.2 1.5 collective-permute-start.31
  391.6 10.8 %shard_map.91 = bf16[1,4,2,64,1024]{4,3,2,1,0:T(8,128)(2,1)S(1)} custom-call(bf16[1,64,1024]{2,1,0:T(8,128)(2,1)S(1)} %bitcast.70), custom_call_target="tpu_custom_call" | custom-call | flops 20971520 | bytes 20971520 | tf_op jit(solution)/shard_map/pallas_call | solution.py:699
  402.4 3.2 collective-permute-start.32
  405.7 14.8 %shard_map.92 = f32[4,4608,128]{2,1,0:T(8,128)} custom-call(s32[1]{0:T(128)} %bitcast.me_ref, bf16[4608,1024]{1,0:T(8,128)(2,1)S(1)} %bitcast.44, f32[4,4608]{1,0:T(4,128)S(1)} %copy-done.19, bf16[512,1024]{1,0:T(8,128)(2,1)S(1)} %bitcast.51, f32[4,384,128]{2,1,0:T(8,128)S(1)} %get-tuple-element.127.rest_0_, f32[4,384,128]{2,1,0:T(8,128)S(1)} %get-tuple-element.126.rest_1_, ...), custom_call_target="tpu_custom_call" | custom-call | flops 4831838208 | bytes 18874368 | tf_op jit(solution)/shard_map/pallas_call | solution.py:373
  420.6 1.0 collective-permute-start.25
  421.6 19.2 %shard_map.93 = bf16[3,4,2,64,1024]{4,3,2,1,0:T(8,128)(2,1)S(1)} custom-call(bf16[3,64,1024]{2,1,0:T(8,128)(2,1)S(1)} %pad_maximum_fusion.1.refs_0_), custom_call_target="tpu_custom_call" | custom-call | flops 62914560 | bytes 62914560 | tf_op jit(solution)/shard_map/pallas_call | solution.py:699
  440.9 3.1 collective-permute-start.29
  444.0 25.7 %collective-permute-start.27 = (f16[4,384,128]{2,1,0:T(8,128)(2,1)S(1)}, f16[4,384,128]{2,1,0:T(8,128)(2,1)S(1)}, u32[]{:S(2)}, u32[]{:S(2)}) collective-permute-start(f16[4,384,128]{2,1,0:T(8,128)(2,1)S(1)} %multiply_convert_fusion.5), channel_id=1, source_target_pairs={{0,3},{1,0},{2,1},{3,2},{4,7},{5,4},{6,5},{7,6},{8,11},{9,8},{10,9... | collective-permute-start | bytes 1179656 | tf_op jit(solution)/shard_map/ppermute | solution.py:724
  469.8 2.4 multiply_add_fusion.6
  472.2 17.0 %shard_map.94.rest_4_ = f32[4,4608,128]{2,1,0:T(8,128)} custom-call(s32[1]{0:T(128)} %bitcast.me_ref, bf16[4608,1024]{1,0:T(8,128)(2,1)S(1)} %bitcast.44, f32[16,4608]{1,0:T(8,128)S(1)} %copy-done.2, f32[16,4608]{1,0:T(8,128)S(1)} %pad_maximum_fusion.3.wt_ref, f32[64,16]{1,0:T(8,128)S(1)} %bitcast.71, bf16[512,1024]{1,0:T(8,128)(2,1)S(1)} %bitcast.52, ...), custom_call_target="tpu_custom_call" | custom-call | flops 6442450944 | bytes 6291456 | tf_op jit(solution)/shard_map/pallas_call | solution.py:450
  489.2 12.6 %collective-permute-done.28 = f16[4,384,128]{2,1,0:T(8,128)(2,1)S(1)} collective-permute-done((f16[4,384,128]{2,1,0:T(8,128)(2,1)S(1)}, f16[4,384,128]{2,1,0:T(8,128)(2,1)S(1)}, u32[]{:S(2)}, u32[]{:S(2)}) %collective-permute-start.28) | collective-permute-done | bytes 393248 | tf_op jit(solution)/shard_map/ppermute | solution.py:724
  502.3 17.0 %shard_map.95.rest_4_ = f32[4,4608,128]{2,1,0:T(8,128)} custom-call(s32[1]{0:T(128)} %bitcast.me_ref, bf16[4608,1024]{1,0:T(8,128)(2,1)S(1)} %bitcast.44, f32[16,4608]{1,0:T(8,128)S(1)} %copy-done.2, f32[16,4608]{1,0:T(8,128)S(1)} %pad_maximum_fusion.3.wt_ref, f32[64,16]{1,0:T(8,128)S(1)} %bitcast.72, ...), custom_call_target="tpu_custom_call", output_to_operand_aliasing={{}: (11, {})} | custom-call | flops 6442450944 | bytes 6291456 | tf_op jit(solution)/shard_map/pallas_call | solution.py:450
  519.7 17.0 %shard_map.96 = f32[4,4608,128]{2,1,0:T(8,128)} custom-call(s32[1]{0:T(128)} %bitcast.me_ref, bf16[4608,1024]{1,0:T(8,128)(2,1)S(1)} %bitcast.44, f32[16,4608]{1,0:T(8,128)S(1)} %copy-done.2, f32[16,4608]{1,0:T(8,128)S(1)} %pad_maximum_fusion.3.wt_ref, f32[64,16]{1,0:T(8,128)S(1)} %bitcast.73, ...), custom_call_target="tpu_custom_call", output_to_operand_aliasing={{}: (11, {})} | custom-call | flops 6442450944 | bytes 6291456 | tf_op jit(solution)/shard_map/pallas_call | solution.py:450
  (148 shorter events, 11.2 us)
Async XLA Ops:
  1.6 86.4 %collective-permute-start.2 = (f16[2,4,4608]{2,1,0:T(4,128)(2,1)S(1)}, f16[2,4,4608]{2,1,0:T(4,128)(2,1)S(1)}, u32[]{:S(2)}, u32[]{:S(2)}) collective-permute-start(f16[2,4,4608]{2,1,0:T(4,128)(2,1)S(1)} %fusion.3), channel_id=1, source_target_pairs={{0,3},{1,0},{2,1},{3,2},{4,7},{5,4},{6,5},{7,6},{8,11},{9,8},{10,9... | collective-permute-start | bytes 221192 | tf_op jit(solution)/shard_map/ppermute | solution.py:724
  2.1 88.6 %collective-permute-start.1 = (f16[2,4,4608]{2,1,0:T(4,128)(2,1)S(1)}, f16[2,4,4608]{2,1,0:T(4,128)(2,1)S(1)}, u32[]{:S(2)}, u32[]{:S(2)}) collective-permute-start(f16[2,4,4608]{2,1,0:T(4,128)(2,1)S(1)} %fusion.3), channel_id=1, source_target_pairs={{0,2},{1,3},{2,0},{3,1},{4,6},{5,7},{6,4},{7,5},{8,10},{9,11},{10,... | collective-permute-start | bytes 221192 | tf_op jit(solution)/shard_map/ppermute | solution.py:724
  2.1 88.7 %collective-permute-start = (f16[2,4,4608]{2,1,0:T(4,128)(2,1)S(1)}, f16[2,4,4608]{2,1,0:T(4,128)(2,1)S(1)}, u32[]{:S(2)}, u32[]{:S(2)}) collective-permute-start(f16[2,4,4608]{2,1,0:T(4,128)(2,1)S(1)} %fusion.3), channel_id=1, source_target_pairs={{0,1},{1,2},{2,3},{3,0},{4,5},{5,6},{6,7},{7,4},{8,9},{9,10},{10,1... | collective-permute-start | bytes 221192 | tf_op jit(solution)/shard_map/ppermute | solution.py:724
  15.9 20.1 %copy-start.19 = (f32[4,4608]{1,0:T(4,128)S(1)}, f32[4,4608]{1,0:T(4,128)}, u32[]{:S(2)}) copy-start(f32[4,4608]{1,0:T(4,128)} %wt_ref.5) | copy-start | bytes 221188
  51.8 13.6 %copy-start.24 = (f32[16,16]{1,0:T(8,128)S(1)}, f32[16,16]{1,0:T(8,128)}, u32[]{:S(2)}) copy-start(f32[16,16]{1,0:T(8,128)} %param.10) | copy-start | bytes 3076
  51.8 14.0 %copy-start.25 = (f32[16,16]{1,0:T(8,128)S(1)}, f32[16,16]{1,0:T(8,128)}, u32[]{:S(2)}) copy-start(f32[16,16]{1,0:T(8,128)} %param.11) | copy-start | bytes 3076
  63.1 29.6 %collective-permute-start.5 = (bf16[64,1024]{1,0:T(8,128)(2,1)S(1)}, bf16[64,1024]{1,0:T(8,128)(2,1)S(1)}, u32[]{:S(2)}, u32[]{:S(2)}) collective-permute-start(bf16[64,1024]{1,0:T(8,128)(2,1)S(1)} %shard_map.79), channel_id=1, source_target_pairs={{0,3},{1,0},{2,1},{3,2},{4,7},{5,4},{6,5},{7,6},{8,11},{9,8},{10,9... | collective-permute-start | bytes 393224 | tf_op jit(solution)/shard_map/ppermute | solution.py:724
  63.8 31.0 %collective-permute-start.4 = (bf16[64,1024]{1,0:T(8,128)(2,1)S(1)}, bf16[64,1024]{1,0:T(8,128)(2,1)S(1)}, u32[]{:S(2)}, u32[]{:S(2)}) collective-permute-start(bf16[64,1024]{1,0:T(8,128)(2,1)S(1)} %shard_map.79), channel_id=1, source_target_pairs={{0,2},{1,3},{2,0},{3,1},{4,6},{5,7},{6,4},{7,5},{8,10},{9,11},{10,... | collective-permute-start | bytes 393224 | tf_op jit(solution)/shard_map/ppermute | solution.py:724
  80.9 1.0 copy-start
  85.9 6.0 %copy-start.23 = (f32[4,4608]{1,0:T(4,128)S(1)}, f32[4,4608]{1,0:T(4,128)}, u32[]{:S(2)}) copy-start(f32[4,4608]{1,0:T(4,128)} %param.9) | copy-start | bytes 221188
  88.0 7.4 %collective-permute-start.3 = (bf16[64,1024]{1,0:T(8,128)(2,1)S(1)}, bf16[64,1024]{1,0:T(8,128)(2,1)S(1)}, u32[]{:S(2)}, u32[]{:S(2)}) collective-permute-start(bf16[64,1024]{1,0:T(8,128)(2,1)S(1)} %shard_map.79), channel_id=1, source_target_pairs={{0,1},{1,2},{2,3},{3,0},{4,5},{5,6},{6,7},{7,4},{8,9},{9,10},{10,1... | collective-permute-start | bytes 393224 | tf_op jit(solution)/shard_map/ppermute | solution.py:724
  90.7 29.1 %collective-permute-start.9 = (f16[4,384,128]{2,1,0:T(8,128)(2,1)}, f16[4,384,128]{2,1,0:T(8,128)(2,1)}, u32[]{:S(2)}, u32[]{:S(2)}) collective-permute-start(f16[4,384,128]{2,1,0:T(8,128)(2,1)} %get-tuple-element.57), channel_id=1, source_target_pairs={{0,1},{1,2},{2,3},{3,0},{4,5},{5,6},{6,7},{7,4},{8,9},{9,10},{10,1... | collective-permute-start | bytes 1179656 | tf_op jit(solution)/shard_map/ppermute | solution.py:724
  90.9 72.7 %collective-permute-start.10 = (f16[4,384,128]{2,1,0:T(8,128)(2,1)}, f16[4,384,128]{2,1,0:T(8,128)(2,1)}, u32[]{:S(2)}, u32[]{:S(2)}) collective-permute-start(f16[4,384,128]{2,1,0:T(8,128)(2,1)} %get-tuple-element.58), channel_id=1, source_target_pairs={{0,2},{1,3},{2,0},{3,1},{4,6},{5,7},{6,4},{7,5},{8,10},{9,11},{10,... | collective-permute-start | bytes 1179656 | tf_op jit(solution)/shard_map/ppermute | solution.py:724
  92.7 71.8 %collective-permute-start.11 = (f16[4,384,128]{2,1,0:T(8,128)(2,1)}, f16[4,384,128]{2,1,0:T(8,128)(2,1)}, u32[]{:S(2)}, u32[]{:S(2)}) collective-permute-start(f16[4,384,128]{2,1,0:T(8,128)(2,1)} %get-tuple-element.59), channel_id=1, source_target_pairs={{0,3},{1,0},{2,1},{3,2},{4,7},{5,4},{6,5},{7,6},{8,11},{9,8},{10,9... | collective-permute-start | bytes 1179656 | tf_op jit(solution)/shard_map/ppermute | solution.py:724
  94.7 87.9 %collective-permute-start.8 = (f16[4,768,128]{2,1,0:T(8,128)(2,1)}, f16[4,768,128]{2,1,0:T(8,128)(2,1)}, u32[]{:S(2)}, u32[]{:S(2)}) collective-permute-start(f16[4,768,128]{2,1,0:T(8,128)(2,1)} %get-tuple-element.131), channel_id=1, source_target_pairs={{0,3},{1,0},{2,1},{3,2},{4,7},{5,4},{6,5},{7,6},{8,11},{9,8},{10,9... | collective-permute-start | bytes 2359304 | tf_op jit(solution)/shard_map/ppermute | solution.py:724
  95.4 88.5 %collective-permute-start.7 = (f16[4,768,128]{2,1,0:T(8,128)(2,1)}, f16[4,768,128]{2,1,0:T(8,128)(2,1)}, u32[]{:S(2)}, u32[]{:S(2)}) collective-permute-start(f16[4,768,128]{2,1,0:T(8,128)(2,1)} %get-tuple-element.132), channel_id=1, source_target_pairs={{0,2},{1,3},{2,0},{3,1},{4,6},{5,7},{6,4},{7,5},{8,10},{9,11},{10,... | collective-permute-start | bytes 2359304 | tf_op jit(solution)/shard_map/ppermute | solution.py:724
  119.8 45.8 %copy-start.1 = (bf16[1,4,2,64,1024]{4,3,2,1,0:T(8,128)(2,1)S(1)}, bf16[1,4,2,64,1024]{4,3,2,1,0:T(8,128)(2,1)}, u32[]{:S(2)}) copy-start(bf16[1,4,2,64,1024]{4,3,2,1,0:T(8,128)(2,1)} %copy-done) | copy-start | bytes 3145732
  119.8 45.8 %copy-start.2 = (f32[16,4608]{1,0:T(8,128)S(1)}, f32[16,4608]{1,0:T(8,128)}, u32[]{:S(2)}) copy-start(f32[16,4608]{1,0:T(8,128)} %pad_maximum_fusion.2.k_ref) | copy-start | bytes 884740
  119.9 45.8 %copy-start.10 = (f32[16,16,16]{2,1,0:T(8,128)S(1)}, f32[16,16,16]{2,1,0:T(8,128)}, u32[]{:S(2)}) copy-start(f32[16,16,16]{2,1,0:T(8,128)} %copy-done.9) | copy-start | bytes 49156
  119.9 72.3 %collective-permute-start.6 = (f16[4,768,128]{2,1,0:T(8,128)(2,1)}, f16[4,768,128]{2,1,0:T(8,128)(2,1)S(1)}, u32[]{:S(2)}, u32[]{:S(2)}) collective-permute-start(f16[4,768,128]{2,1,0:T(8,128)(2,1)} %get-tuple-element.133), channel_id=1, source_target_pairs={{0,1},{1,2},{2,3},{3,0},{4,5},{5,6},{6,7},{7,4},{8,9},{9,10},{10,1... | collective-permute-start | bytes 2359304 | tf_op jit(solution)/shard_map/ppermute | solution.py:724
  179.7 1.3 copy-start.11
  180.0 151.2 %collective-permute-start.14 = (f16[4,384,128]{2,1,0:T(8,128)(2,1)S(1)}, f16[4,384,128]{2,1,0:T(8,128)(2,1)S(1)}, u32[]{:S(2)}, u32[]{:S(2)}) collective-permute-start(f16[4,384,128]{2,1,0:T(8,128)(2,1)S(1)} %multiply_convert_fusion.15), channel_id=1, source_target_pairs={{0,1},{1,2},{2,3},{3,0},{4,5},{5,6},{6,7},{7,4},{8,9},{9,10},{10,1... | collective-permute-start | bytes 1179656 | tf_op jit(solution)/shard_map/ppermute | solution.py:724
  180.0 151.1 %collective-permute-start.13 = (f16[4,384,128]{2,1,0:T(8,128)(2,1)S(1)}, f16[4,384,128]{2,1,0:T(8,128)(2,1)S(1)}, u32[]{:S(2)}, u32[]{:S(2)}) collective-permute-start(f16[4,384,128]{2,1,0:T(8,128)(2,1)S(1)} %multiply_convert_fusion.16), channel_id=1, source_target_pairs={{0,2},{1,3},{2,0},{3,1},{4,6},{5,7},{6,4},{7,5},{8,10},{9,11},{10,... | collective-permute-start | bytes 1179656 | tf_op jit(solution)/shard_map/ppermute | solution.py:724
  206.3 0.9 copy-start.13
  207.3 0.9 copy-start.17
  222.1 0.9 copy-start.15
  223.4 35.2 %collective-permute-start.20 = (f16[4,384,128]{2,1,0:T(8,128)(2,1)S(1)}, f16[4,384,128]{2,1,0:T(8,128)(2,1)S(1)}, u32[]{:S(2)}, u32[]{:S(2)}) collective-permute-start(f16[4,384,128]{2,1,0:T(8,128)(2,1)S(1)} %multiply_convert_fusion.9), channel_id=1, source_target_pairs={{0,1},{1,2},{2,3},{3,0},{4,5},{5,6},{6,7},{7,4},{8,9},{9,10},{10,1... | collective-permute-start | bytes 1179656 | tf_op jit(solution)/shard_map/ppermute | solution.py:724
  249.1 34.0 %collective-permute-start.19 = (f16[4,384,128]{2,1,0:T(8,128)(2,1)S(1)}, f16[4,384,128]{2,1,0:T(8,128)(2,1)S(1)}, u32[]{:S(2)}, u32[]{:S(2)}) collective-permute-start(f16[4,384,128]{2,1,0:T(8,128)(2,1)S(1)} %multiply_convert_fusion.10), channel_id=1, source_target_pairs={{0,2},{1,3},{2,0},{3,1},{4,6},{5,7},{6,4},{7,5},{8,10},{9,11},{10,... | collective-permute-start | bytes 1179656 | tf_op jit(solution)/shard_map/ppermute | solution.py:724
  249.1 34.0 %collective-permute-start.18 = (f16[4,384,128]{2,1,0:T(8,128)(2,1)S(1)}, f16[4,384,128]{2,1,0:T(8,128)(2,1)S(1)}, u32[]{:S(2)}, u32[]{:S(2)}) collective-permute-start(f16[4,384,128]{2,1,0:T(8,128)(2,1)S(1)} %multiply_convert_fusion.11), channel_id=1, source_target_pairs={{0,3},{1,0},{2,1},{3,2},{4,7},{5,4},{6,5},{7,6},{8,11},{9,8},{10,9... | collective-permute-start | bytes 1179656 | tf_op jit(solution)/shard_map/ppermute | solution.py:724
  258.6 50.0 %collective-permute-start.17 = (f16[4,384,128]{2,1,0:T(8,128)(2,1)S(1)}, f16[4,384,128]{2,1,0:T(8,128)(2,1)S(1)}, u32[]{:S(2)}, u32[]{:S(2)}) collective-permute-start(f16[4,384,128]{2,1,0:T(8,128)(2,1)S(1)} %multiply_convert_fusion.12), channel_id=1, source_target_pairs={{0,1},{1,2},{2,3},{3,0},{4,5},{5,6},{6,7},{7,4},{8,9},{9,10},{10,1... | collective-permute-start | bytes 1179656 | tf_op jit(solution)/shard_map/ppermute | solution.py:724
  283.1 41.0 %collective-permute-start.16 = (f16[4,384,128]{2,1,0:T(8,128)(2,1)S(1)}, f16[4,384,128]{2,1,0:T(8,128)(2,1)S(1)}, u32[]{:S(2)}, u32[]{:S(2)}) collective-permute-start(f16[4,384,128]{2,1,0:T(8,128)(2,1)S(1)} %multiply_convert_fusion.13), channel_id=1, source_target_pairs={{0,2},{1,3},{2,0},{3,1},{4,6},{5,7},{6,4},{7,5},{8,10},{9,11},{10,... | collective-permute-start | bytes 1179656 | tf_op jit(solution)/shard_map/ppermute | solution.py:724
  283.1 41.0 %collective-permute-start.15 = (f16[4,384,128]{2,1,0:T(8,128)(2,1)S(1)}, f16[4,384,128]{2,1,0:T(8,128)(2,1)S(1)}, u32[]{:S(2)}, u32[]{:S(2)}) collective-permute-start(f16[4,384,128]{2,1,0:T(8,128)(2,1)S(1)} %multiply_convert_fusion.14), channel_id=1, source_target_pairs={{0,3},{1,0},{2,1},{3,2},{4,7},{5,4},{6,5},{7,6},{8,11},{9,8},{10,9... | collective-permute-start | bytes 1179656 | tf_op jit(solution)/shard_map/ppermute | solution.py:724
  308.6 22.6 %collective-permute-start.12 = (f16[4,384,128]{2,1,0:T(8,128)(2,1)S(1)}, f16[4,384,128]{2,1,0:T(8,128)(2,1)S(1)}, u32[]{:S(2)}, u32[]{:S(2)}) collective-permute-start(f16[4,384,128]{2,1,0:T(8,128)(2,1)S(1)} %multiply_convert_fusion.17), channel_id=1, source_target_pairs={{0,3},{1,0},{2,1},{3,2},{4,7},{5,4},{6,5},{7,6},{8,11},{9,8},{10,9... | collective-permute-start | bytes 1179656 | tf_op jit(solution)/shard_map/ppermute | solution.py:724
  333.6 5.3 copy-start.3
  333.6 5.3 copy-start.5
  333.6 5.3 copy-start.7
  358.2 47.4 %slice-start = ((s8[9437184]{0:T(1024)(128)(4,1)}), s8[4194304]{0:T(1024)(128)(4,1)S(1)}, s32[]{:S(2)}) async-start(s8[9437184]{0:T(1024)(128)(4,1)} %bitcast.43), calls=%async_computation | async-start | bytes 8388608
  358.2 47.4 %slice-start.1 = ((s8[9437184]{0:T(1024)(128)(4,1)}), s8[4194304]{0:T(1024)(128)(4,1)S(1)}, s32[]{:S(2)}) async-start(s8[9437184]{0:T(1024)(128)(4,1)} %bitcast.43), calls=%async_computation.1 | async-start | bytes 8388608
  358.3 47.4 %slice-start.2 = ((s8[9437184]{0:T(1024)(128)(4,1)}), s8[1048576]{0:T(1024)(128)(4,1)S(1)}, s32[]{:S(2)}) async-start(s8[9437184]{0:T(1024)(128)(4,1)} %bitcast.43), calls=%async_computation.2 | async-start | bytes 2097152
  374.3 11.4 %copy-start.18 = (f32[4,384,128]{2,1,0:T(8,128)S(1)}, f32[4,384,128]{2,1,0:T(8,128)}, u32[]{:S(2)}) copy-start(f32[4,384,128]{2,1,0:T(8,128)} %copy-done.17) | copy-start | bytes 2359300
  374.3 31.4 %copy-start.4 = (f32[4,384,128]{2,1,0:T(8,128)S(1)}, f32[4,384,128]{2,1,0:T(8,128)}, u32[]{:S(2)}) copy-start(f32[4,384,128]{2,1,0:T(8,128)} %copy-done.3) | copy-start | bytes 2359300
  374.3 31.3 %copy-start.6 = (f32[4,384,128]{2,1,0:T(8,128)S(1)}, f32[4,384,128]{2,1,0:T(8,128)}, u32[]{:S(2)}) copy-start(f32[4,384,128]{2,1,0:T(8,128)} %copy-done.5) | copy-start | bytes 2359300
  374.3 31.3 %copy-start.8 = (f32[4,384,128]{2,1,0:T(8,128)S(1)}, f32[4,384,128]{2,1,0:T(8,128)}, u32[]{:S(2)}) copy-start(f32[4,384,128]{2,1,0:T(8,128)} %copy-done.7) | copy-start | bytes 2359300
  385.6 16.8 %collective-permute-start.23 = (bf16[64,1024]{1,0:T(8,128)(2,1)S(1)}, bf16[64,1024]{1,0:T(8,128)(2,1)S(1)}, u32[]{:S(2)}, u32[]{:S(2)}) collective-permute-start(bf16[64,1024]{1,0:T(8,128)(2,1)S(1)} %shard_map.90), channel_id=1, source_target_pairs={{0,3},{1,0},{2,1},{3,2},{4,7},{5,4},{6,5},{7,6},{8,11},{9,8},{10,9... | collective-permute-start | bytes 393224 | tf_op jit(solution)/shard_map/ppermute | solution.py:724
  385.7 34.7 %collective-permute-start.22 = (bf16[64,1024]{1,0:T(8,128)(2,1)S(1)}, bf16[64,1024]{1,0:T(8,128)(2,1)S(1)}, u32[]{:S(2)}, u32[]{:S(2)}) collective-permute-start(bf16[64,1024]{1,0:T(8,128)(2,1)S(1)} %shard_map.90), channel_id=1, source_target_pairs={{0,2},{1,3},{2,0},{3,1},{4,6},{5,7},{6,4},{7,5},{8,10},{9,11},{10,... | collective-permute-start | bytes 393224 | tf_op jit(solution)/shard_map/ppermute | solution.py:724
  385.8 34.7 %collective-permute-start.21 = (bf16[64,1024]{1,0:T(8,128)(2,1)S(1)}, bf16[64,1024]{1,0:T(8,128)(2,1)S(1)}, u32[]{:S(2)}, u32[]{:S(2)}) collective-permute-start(bf16[64,1024]{1,0:T(8,128)(2,1)S(1)} %shard_map.90), channel_id=1, source_target_pairs={{0,1},{1,2},{2,3},{3,0},{4,5},{5,6},{6,7},{7,4},{8,9},{9,10},{10,1... | collective-permute-start | bytes 393224 | tf_op jit(solution)/shard_map/ppermute | solution.py:724
  389.7 51.2 %collective-permute-start.30 = (f16[4,384,128]{2,1,0:T(8,128)(2,1)S(1)}, f16[4,384,128]{2,1,0:T(8,128)(2,1)S(1)}, u32[]{:S(2)}, u32[]{:S(2)}) collective-permute-start(f16[4,384,128]{2,1,0:T(8,128)(2,1)S(1)} %multiply_convert_fusion.23), channel_id=1, source_target_pairs={{0,3},{1,0},{2,1},{3,2},{4,7},{5,4},{6,5},{7,6},{8,11},{9,8},{10,9... | collective-permute-start | bytes 1179656 | tf_op jit(solution)/shard_map/ppermute | solution.py:724
  390.2 53.8 %collective-permute-start.31 = (f16[4,384,128]{2,1,0:T(8,128)(2,1)S(1)}, f16[4,384,128]{2,1,0:T(8,128)(2,1)S(1)}, u32[]{:S(2)}, u32[]{:S(2)}) collective-permute-start(f16[4,384,128]{2,1,0:T(8,128)(2,1)S(1)} %multiply_convert_fusion.22), channel_id=1, source_target_pairs={{0,2},{1,3},{2,0},{3,1},{4,6},{5,7},{6,4},{7,5},{8,10},{9,11},{10,... | collective-permute-start | bytes 1179656 | tf_op jit(solution)/shard_map/ppermute | solution.py:724
  402.4 41.6 %collective-permute-start.32 = (f16[4,384,128]{2,1,0:T(8,128)(2,1)S(1)}, f16[4,384,128]{2,1,0:T(8,128)(2,1)S(1)}, u32[]{:S(2)}, u32[]{:S(2)}) collective-permute-start(f16[4,384,128]{2,1,0:T(8,128)(2,1)S(1)} %multiply_convert_fusion.21), channel_id=1, source_target_pairs={{0,1},{1,2},{2,3},{3,0},{4,5},{5,6},{6,7},{7,4},{8,9},{9,10},{10,1... | collective-permute-start | bytes 1179656 | tf_op jit(solution)/shard_map/ppermute | solution.py:724
  405.6 14.8 %copy-start.22 = (f16[4,384,128]{2,1,0:T(8,128)(2,1)S(1)}, f16[4,384,128]{2,1,0:T(8,128)(2,1)}, u32[]{:S(2)}) copy-start(f16[4,384,128]{2,1,0:T(8,128)(2,1)} %multiply_convert_fusion.6) | copy-start | bytes 1179652
  405.7 14.9 %copy-start.21 = (f16[4,384,128]{2,1,0:T(8,128)(2,1)S(1)}, f16[4,384,128]{2,1,0:T(8,128)(2,1)}, u32[]{:S(2)}) copy-start(f16[4,384,128]{2,1,0:T(8,128)(2,1)} %multiply_convert_fusion.7) | copy-start | bytes 1179652
  420.5 98.8 %collective-permute-start.26 = (f16[4,384,128]{2,1,0:T(8,128)(2,1)S(1)}, f16[4,384,128]{2,1,0:T(8,128)(2,1)S(1)}, u32[]{:S(2)}, u32[]{:S(2)}) collective-permute-start(f16[4,384,128]{2,1,0:T(8,128)(2,1)S(1)} %copy-done.22), channel_id=1, source_target_pairs={{0,1},{1,2},{2,3},{3,0},{4,5},{5,6},{6,7},{7,4},{8,9},{9,10},{10,1... | collective-permute-start | bytes 1179656 | tf_op jit(solution)/shard_map/ppermute | solution.py:724
  420.6 98.7 %collective-permute-start.25 = (f16[4,384,128]{2,1,0:T(8,128)(2,1)S(1)}, f16[4,384,128]{2,1,0:T(8,128)(2,1)S(1)}, u32[]{:S(2)}, u32[]{:S(2)}) collective-permute-start(f16[4,384,128]{2,1,0:T(8,128)(2,1)S(1)} %copy-done.21), channel_id=1, source_target_pairs={{0,2},{1,3},{2,0},{3,1},{4,6},{5,7},{6,4},{7,5},{8,10},{9,11},{10,... | collective-permute-start | bytes 1179656 | tf_op jit(solution)/shard_map/ppermute | solution.py:724
  421.6 48.2 %copy-start.16 = (f32[4,384,128]{2,1,0:T(8,128)S(1)}, f32[4,384,128]{2,1,0:T(8,128)}, u32[]{:S(2)}) copy-start(f32[4,384,128]{2,1,0:T(8,128)} %copy-done.15) | copy-start | bytes 2359300
  440.9 48.3 %collective-permute-start.29 = (f16[4,384,128]{2,1,0:T(8,128)(2,1)S(1)}, f16[4,384,128]{2,1,0:T(8,128)(2,1)S(1)}, u32[]{:S(2)}, u32[]{:S(2)}) collective-permute-start(f16[4,384,128]{2,1,0:T(8,128)(2,1)S(1)} %multiply_convert_fusion.3), channel_id=1, source_target_pairs={{0,1},{1,2},{2,3},{3,0},{4,5},{5,6},{6,7},{7,4},{8,9},{9,10},{10,1... | collective-permute-start | bytes 1179656 | tf_op jit(solution)/shard_map/ppermute | solution.py:724
  444.0 57.9 %collective-permute-start.28 = (f16[4,384,128]{2,1,0:T(8,128)(2,1)S(1)}, f16[4,384,128]{2,1,0:T(8,128)(2,1)S(1)}, u32[]{:S(2)}, u32[]{:S(2)}) collective-permute-start(f16[4,384,128]{2,1,0:T(8,128)(2,1)S(1)} %multiply_convert_fusion.4), channel_id=1, source_target_pairs={{0,2},{1,3},{2,0},{3,1},{4,6},{5,7},{6,4},{7,5},{8,10},{9,11},{10,... | collective-permute-start | bytes 1179656 | tf_op jit(solution)/shard_map/ppermute | solution.py:724
  444.0 57.8 %collective-permute-start.27 = (f16[4,384,128]{2,1,0:T(8,128)(2,1)S(1)}, f16[4,384,128]{2,1,0:T(8,128)(2,1)S(1)}, u32[]{:S(2)}, u32[]{:S(2)}) collective-permute-start(f16[4,384,128]{2,1,0:T(8,128)(2,1)S(1)} %multiply_convert_fusion.5), channel_id=1, source_target_pairs={{0,3},{1,0},{2,1},{3,2},{4,7},{5,4},{6,5},{7,6},{8,11},{9,8},{10,9... | collective-permute-start | bytes 1179656 | tf_op jit(solution)/shard_map/ppermute | solution.py:724
  472.1 29.7 %slice-start.3 = ((s8[9437184]{0:T(1024)(128)(4,1)}), s8[4194304]{0:T(1024)(128)(4,1)S(1)}, s32[]{:S(2)}) async-start(s8[9437184]{0:T(1024)(128)(4,1)} %bitcast.74), calls=%async_computation.3 | async-start | bytes 8388608
  472.1 17.0 %copy-start.20 = (f16[4,384,128]{2,1,0:T(8,128)(2,1)S(1)}, f16[4,384,128]{2,1,0:T(8,128)(2,1)}, u32[]{:S(2)}) copy-start(f16[4,384,128]{2,1,0:T(8,128)(2,1)} %multiply_convert_fusion.8) | copy-start | bytes 1179652
  472.1 29.7 %copy-start.14 = (f32[4,384,128]{2,1,0:T(8,128)S(1)}, f32[4,384,128]{2,1,0:T(8,128)}, u32[]{:S(2)}) copy-start(f32[4,384,128]{2,1,0:T(8,128)} %copy-done.13) | copy-start | bytes 2359300
  472.1 29.7 %slice-start.4 = ((s8[9437184]{0:T(1024)(128)(4,1)}), s8[4194304]{0:T(1024)(128)(4,1)S(1)}, s32[]{:S(2)}) async-start(s8[9437184]{0:T(1024)(128)(4,1)} %bitcast.74), calls=%async_computation.4 | async-start | bytes 8388608
  472.2 29.7 %slice-start.5 = ((s8[9437184]{0:T(1024)(128)(4,1)}), s8[1048576]{0:T(1024)(128)(4,1)S(1)}, s32[]{:S(2)}) async-start(s8[9437184]{0:T(1024)(128)(4,1)} %bitcast.74), calls=%async_computation.5 | async-start | bytes 2097152
  489.2 30.2 %collective-permute-start.24 = (f16[4,384,128]{2,1,0:T(8,128)(2,1)S(1)}, f16[4,384,128]{2,1,0:T(8,128)(2,1)S(1)}, u32[]{:S(2)}, u32[]{:S(2)}) collective-permute-start(f16[4,384,128]{2,1,0:T(8,128)(2,1)S(1)} %copy-done.20), channel_id=1, source_target_pairs={{0,3},{1,0},{2,1},{3,2},{4,7},{5,4},{6,5},{7,6},{8,11},{9,8},{10,9... | collective-permute-start | bytes 1179656 | tf_op jit(solution)/shard_map/ppermute | solution.py:724
  502.3 17.0 %copy-start.12 = (f32[4,384,128]{2,1,0:T(8,128)S(1)}, f32[4,384,128]{2,1,0:T(8,128)}, u32[]{:S(2)}) copy-start(f32[4,384,128]{2,1,0:T(8,128)} %copy-done.11) | copy-start | bytes 2359300
  (1 other events, 0.7 us)

commit v6 on v5

--- a/solution.py
+++ b/solution.py
@@ -12,7 +12,6 @@
 LANES = 128
 MESH = pl.DeviceIdType.MESH
 CHUNK = 16
-WIDE = 32
 EXACT = lax.Precision.HIGHEST
 R_MAX = 6.0
 W_MAX = 2.0
@@ -56,12 +55,6 @@
     )
 
 
-def spread(l_ref, p_ref, far_ref, held):
-    own = p_ref.shape[0]
-    held[:own, :] = rows_times(p_ref, l_ref)
-    held[own:, :] = rows_times(far_ref, l_ref)
-
-
 def dot_exact(a, b):
     return lax.dot_general(
         a, b, (((1,), (0,)), ((), ())), precision=EXACT, preferred_element_type=jnp.float32
@@ -72,7 +65,7 @@
     return pl.BlockSpec(x.shape, lambda i, *_: (0,) * x.ndim, pipeline_mode=pl.Buffered(1))
 
 
-def quarter_kernel(nf, parts, sets, me_ref, l_ref, k_ref, wt_ref, coef_ref, p_ref, far_ref, *rest):
+def quarter_kernel(nf, parts, sets, me_ref, l_ref, k_ref, wt_ref, coef_ref, p_ref, *rest):
     own_ref, rest = rest[0], rest[1:]
     came, rest = rest[: sets * (parts - 1)], rest[sets * (parts - 1) :]
     u_refs, rest = rest[:parts], rest[parts:]
@@ -80,7 +73,7 @@
     own = nf // parts
     cols = own_ref.shape[2]
     table[...] = dot_exact(coef_ref[...], k_ref[...])
-    spread(l_ref, p_ref, far_ref, held)
+    held[...] = rows_times(p_ref, l_ref)
 
     @pl.loop(0, table.shape[1] // LANES)
     def _(block):
@@ -117,7 +110,7 @@
             v_refs[w // own][w % own, lanes, :] = far[w].T
 
 
-def quarter_pass(me, low, factors, kernels, weights, coef, near, far, right_side, moved):
+def quarter_pass(me, low, factors, kernels, weights, coef, gathered, right_side, moved):
     own, pairs, cols = right_side.shape
     nf = weights.shape[0]
     parts = nf // own
@@ -132,7 +125,7 @@
         table = table.reshape(nf, nf, quarter)
         wide = jnp.einsum(
             "ja,pa->jp",
-            jnp.concatenate([near, far]),
+            gathered,
             cut(factors, 0),
             preferred_element_type=jnp.float32,
         )
@@ -160,8 +153,7 @@
                 pl.BlockSpec((nf, tile), lambda i, m: (0, at(i, m))),
                 pl.BlockSpec((nf, tile), lambda i, m: (0, at(i, m))),
                 resident(coef),
-                resident(near),
-                resident(far),
+                resident(gathered),
                 pl.BlockSpec((own, tile, cols), lambda i, m: (0, at(i, m), 0)),
             ]
             + [here(n) for _, n in moved for _ in range(parts - 1)],
@@ -172,7 +164,7 @@
             ]
             + [VMEM((nf, cols, LANES), jnp.float32)] * 3,
         ),
-        compiler_params=pltpu.CompilerParams(vmem_limit_bytes=(36 if sets == 1 else 46) << 20),
+        compiler_params=pltpu.CompilerParams(vmem_limit_bytes=54 << 20),
         cost_estimate=pl.CostEstimate(
             flops=2 * nf * sets * tile * cols * (naux + 32 * nf),
             bytes_accessed=16 * nf * sets * tile * cols,
@@ -184,8 +176,7 @@
         kernels,
         weights,
         coef,
-        near,
-        far,
+        gathered,
         right_side,
         *[x for xs, _ in moved for x in xs],
     )
@@ -301,20 +292,20 @@
 
 
 class Stream:
-    def __init__(self, refs, buffer, sems):
+    def __init__(self, refs, buffer, sems, step):
         tile = buffer.shape[2]
         refs = [
             ref.at[:, n : n + tile, :] for ref in refs for n in range(0, ref.shape[1], tile)
         ]
         self.refs, self.buffer, self.sems = refs, buffer, sems
-        self.step = pl.program_id(0)
-        self.slot = lax.rem(self.step, 2)
+        self.step = step
+        self.slot = lax.rem(step + 2, 2)
 
     def copy(self, n):
         return pltpu.make_async_copy(self.refs[n], self.buffer.at[n % 2], self.sems.at[n % 2])
 
     def ahead(self):
-        @pl.when(self.step == 0)
+        @pl.when(pl.program_id(0) == 0)
         def _():
             self.copy(0).start()
 
@@ -341,7 +332,7 @@
 def amplitude_kernel(pieces, me_ref, l_ref, wt_ref, p_ref, *rest):
     refs, (a_ref, buffer, sems) = rest[:pieces], rest[pieces:]
     own, tile, cols = a_ref.shape
-    stream = Stream(refs, buffer, sems)
+    stream = Stream(refs, buffer, sems, pl.program_id(0))
     stream.ahead()
     wide = rows_times(p_ref, l_ref)
     here = stream.here()
@@ -394,35 +385,66 @@
     )(me.reshape(1), factors, pair_weight, near, *pieces)
 
 
-def final_kernel(nf, parts, held_outs, me_ref, l_ref, k_ref, wt_ref, coef_ref, p_ref, far_ref, *rest):
+def final_kernel(nf, held_outs, me_ref, l_ref, k_ref, wt_ref, coef_ref, p_ref, *rest):
+    parts = len(rest) - held_outs - 6
     b_refs, rest = rest[:parts], rest[parts + held_outs :]
     new_ref, table, held, mid, buffer, sems = rest
-    own, _, cols = new_ref.shape
-    stream = Stream(b_refs, buffer, sems)
+    own, tile, cols = new_ref.shape
+    i = pl.program_id(0)
+    count = pl.num_programs(0) - 1
+    stream = Stream(b_refs, buffer, sems, i - 1)
+    turns = cols // CHUNK
+    share = p_ref.shape[0] // turns
+    ahead, now = lax.rem(i, 2), lax.rem(i + 1, 2)
+
+    def multiply(r):
+        rows = part(r, 0, share)
+        held[ahead, rows, :] = lax.dot_general(
+            p_ref[rows, :], l_ref[...], (((1,), (1,)), ((), ())), preferred_element_type=jnp.float32
+        )
+
+    def blend(r):
+        rows = part(r, 0, CHUNK)
+        for k in range(0, tile, LANES):
+            lanes = slice(k, k + LANES)
+            got = mix(table, lanes, own, nf, lambda v: held[now, part(r, v * cols, CHUNK), lanes])
+            for w in range(own):
+                mid[w, rows, lanes] = got[w]
+
     stream.ahead()
-    table[...] = dot_exact(coef_ref[...], k_ref[...])
-    for w in range(own):
-        rows = slice(w * nf, (w + 1) * nf)
-        table[rows, :] = table[rows, :] * wt_ref[...]
-    spread(l_ref, p_ref, far_ref, held)
-    here = stream.here()
-
-    @pl.loop(0, table.shape[1] // LANES)
-    def _(block):
-        lanes = part(block, 0, LANES)
-
-        @pl.loop(0, cols // WIDE)
-        def _(i):
-            rows = part(i, 0, WIDE)
-            got = mix(table, lanes, own, nf, lambda v: held[part(i, v * cols, WIDE), lanes])
-            for w in range(own):
-                mid[w, rows, :] = got[w]
-
+
+    @pl.when(i > 0)
+    def _():
+        table[...] = dot_exact(coef_ref[...], k_ref[...])
         for w in range(own):
-            new_ref[w, lanes, :] = here[w, lanes, :] + mid[w].T
-
-
-def final(me, low, factors, kernels, weights, coef, near, far, base, outs):
+            rows = slice(w * nf, (w + 1) * nf)
+            table[rows, :] = table[rows, :] * wt_ref[...]
+
+    @pl.when(i == 0)
+    def _():
+        pl.loop(0, turns)(multiply)
+
+    @pl.when((i > 0) & (i < count))
+    def _():
+        @pl.loop(0, turns)
+        def _(r):
+            blend(r)
+            multiply(r)
+
+    @pl.when(i == count)
+    def _():
+        pl.loop(0, turns)(blend)
+
+    @pl.when(i > 0)
+    def _():
+        here = stream.here()
+        for w in range(own):
+            for k in range(0, tile, LANES):
+                lanes = slice(k, k + LANES)
+                new_ref[w, lanes, :] = here[w, lanes, :] + mid[w, :, lanes].T
+
+
+def final(me, low, factors, kernels, weights, coef, gathered, base, outs):
     own, span, cols = base[0].shape
     parts = len(base)
     nf = weights.shape[0]
@@ -432,7 +454,7 @@
     if tile is None:
         wide = jnp.einsum(
             "ja,pa->jp",
-            jnp.concatenate([near, far]),
+            gathered,
             factors,
             preferred_element_type=jnp.float32,
         )
@@ -447,37 +469,39 @@
     size = tile
     sets = span // size
     at = around(parts, quarter // size, low, sets)
+    count = parts * sets
+    ahead = lambda i, m: at(jnp.minimum(i, count - 1), m)
+    now = lambda i, m: at(jnp.maximum(i - 1, 0), m)
     result = pl.pallas_call(
-        functools.partial(final_kernel, nf, parts, len(outs)),
+        functools.partial(final_kernel, nf, len(outs)),
         out_shape=jax.ShapeDtypeStruct((own, pairs, cols), jnp.float32),
         grid_spec=pltpu.PrefetchScalarGridSpec(
             num_scalar_prefetch=1,
-            grid=(parts * sets,),
+            grid=(count + 1,),
             in_specs=[
-                pl.BlockSpec((size, naux), lambda i, m: (at(i, m), 0)),
-                pl.BlockSpec((nf, size), lambda i, m: (0, at(i, m))),
-                pl.BlockSpec((nf, size), lambda i, m: (0, at(i, m))),
+                pl.BlockSpec((size, naux), lambda i, m: (ahead(i, m), 0)),
+                pl.BlockSpec((nf, size), lambda i, m: (0, now(i, m))),
+                pl.BlockSpec((nf, size), lambda i, m: (0, now(i, m))),
                 resident(coef),
-                resident(near),
-                resident(far),
+                resident(gathered),
             ]
             + [ANYWHERE] * (parts + len(outs)),
-            out_specs=pl.BlockSpec((own, size, cols), lambda i, m: (0, at(i, m), 0)),
+            out_specs=pl.BlockSpec((own, size, cols), lambda i, m: (0, now(i, m), 0)),
             scratch_shapes=[
                 VMEM((own * nf, size), jnp.float32),
-                VMEM((nf * cols, size), jnp.float32),
-                VMEM((own, cols, LANES), jnp.float32),
+                VMEM((2, nf * cols, size), jnp.float32),
+                VMEM((own, cols, size), jnp.float32),
             ]
             + stream_scratch(own, size, cols),
         ),
-        input_output_aliases={7 + parts + n: n for n in range(len(outs))},
-        compiler_params=pltpu.CompilerParams(vmem_limit_bytes=26 << 20),
+        input_output_aliases={6 + parts + n: n for n in range(len(outs))},
+        compiler_params=pltpu.CompilerParams(vmem_limit_bytes=30 << 20),
         cost_estimate=pl.CostEstimate(
             flops=2 * nf * parts * span * cols * naux,
             bytes_accessed=8 * own * parts * span * cols,
             transcendentals=0,
         ),
-    )(me.reshape(1), factors, kernels, weights, coef, near, far, *base, *outs)
+    )(me.reshape(1), factors, kernels, weights, coef, gathered, *base, *outs)
     return [result]
 
 
@@ -579,8 +603,12 @@
         o_ref[c] = joined[c]
 
 
-def gather_kernel(chips, parts, *refs):
-    x_ref, o_ref, joined, *sems = refs
+def gather_kernel(chips, parts, x_ref, *refs):
+    near_ref = None
+    if len(refs) > 8:
+        near_ref, refs = refs[0], refs[1:]
+    o_ref, top_ref, joined, *sems = refs
+    skip = 0 if near_ref is None else 1
     x_refs = [x_ref.at[s] for s in range(parts)]
     kept = sems[4]
     plane = Plane(chips)
@@ -633,9 +661,22 @@
     plane.end()
     for copy in copies:
         copy.wait()
+    if skip:
+        o_ref[0] = near_ref[...]
+    top = jnp.zeros(top_ref.shape, jnp.float32)
     for s in range(parts):
-        for c in range(chips):
-            o_ref[s, c] = joined[s, c]
+
+        def fold(c, top):
+            here = joined[s, c]
+            o_ref[s + skip, c] = here
+            here = jnp.abs(here.astype(jnp.float32))
+            sums = here[..., :LANES]
+            for k in range(LANES, here.shape[-1], LANES):
+                sums = sums + here[..., k : k + LANES]
+            return jnp.maximum(top, jnp.max(sums.reshape((-1,) + top.shape), axis=0))
+
+        top = lax.fori_loop(0, chips, fold, top)
+    top_ref[...] = top
 
 
 def dmas(count, pairs):
@@ -691,23 +732,26 @@
     return result.reshape(rows, width)
 
 
-def gathered_over(blocks):
+def gathered_over(blocks, near=None):
     n = lax.axis_size("fac")
     chips = n // 2
     parts, block, width = blocks.shape
-    flat = (parts, chips, 2, block, width)
-    result = pl.pallas_call(
+    flat = (chips, 2, block, width)
+    result, top = pl.pallas_call(
         functools.partial(gather_kernel, chips, parts),
-        out_shape=jax.ShapeDtypeStruct(flat, jnp.bfloat16),
-        in_specs=[WHOLE],
-        out_specs=WHOLE,
-        scratch_shapes=[VMEM(flat, jnp.bfloat16)]
+        out_shape=(
+            jax.ShapeDtypeStruct((parts + (near is not None),) + flat, jnp.bfloat16),
+            jax.ShapeDtypeStruct((8, LANES), jnp.float32),
+        ),
+        in_specs=[WHOLE] * (1 if near is None else 2),
+        out_specs=(WHOLE, WHOLE),
+        scratch_shapes=[VMEM((parts,) + flat, jnp.bfloat16)]
         + dmas(parts * chips, 2)
         + [pltpu.SemaphoreType.DMA((parts,))],
         compiler_params=reach_params(2 if parts == 1 else 3),
         cost_estimate=reach_cost(block * width * parts * 8),
-    )(blocks)
-    return result.reshape(parts * n * block, width)
+    )(blocks, *(() if near is None else (near.reshape(flat),)))
+    return result.reshape(-1, width), top
 
 
 def shards(right_side, factors, pair_weight, second_order, forward, backward):
@@ -777,24 +821,20 @@
             total = again(factors, pair_weight, mine, kept)
         block = summed(total, False)
         far = [shift(block, s) for s in range(1, parts)]
-        return gathered_over(block[None]), far
-
-    def joined(blocks):
+        return *gathered_over(block[None]), far
+
+    def joined(blocks, near):
         blocks = jnp.stack(blocks)
-        return gathered_over(blocks)
+        return gathered_over(blocks, near)
 
     leaves = []
     for g in groups:
         leaves.append(leaving(*g))
     right_late, leaves[-1] = tie((right_side, leaves[-1]))
     came = [passed(x, False) for x in leaves]
-    near, blocks = ladder(first_projection())
-    far = joined(blocks)
-
-    def tall(x):
-        return jnp.max(jnp.sum(jnp.abs(x.astype(jnp.float32)), axis=1))
-
-    height = jnp.maximum(tall(near), tall(far))
+    near, near_top, blocks = ladder(first_projection())
+    gathered, far_top = joined(blocks, near)
+    height = jnp.sum(jnp.max(jnp.maximum(near_top, far_top), axis=0))
     u_top = jnp.maximum(1.01 * reach * (R_MAX + W_MAX * L_MAX * height), 1e-30)
     v_top = jnp.maximum(1.01 * reach * (R_MAX + u_top), 1e-30)
 
@@ -818,8 +858,7 @@
             kernels,
             weights,
             coef,
-            near,
-            far,
+            gathered,
             right_side,
             placed[low:high],
         )
@@ -837,11 +876,11 @@
 
     out, total = tie((halves[0], total))
     back = [passed(out, True)]
-    near, blocks = ladder(total)
+    near, _, blocks = ladder(total)
     for n in range(1, len(calls)):
         back.append(passed(halves[n], True))
     amplitudes = amplitude(me, factors, pair_weight, near, sources)
-    far = joined(blocks)
+    gathered, _ = joined(blocks, near)
     outs = []
     for n, group in enumerate(calls):
         back[n], outs = tie((back[n], outs))
@@ -853,8 +892,7 @@
             kernels,
             weights,
             coef[: own * nf],
-            near,
-            far,
+            gathered,
             base,
             outs,
         )

time: 544 us -> 555 us (1.020)
  the two profiles are of different devices: /device:TPU:24 before, /device:TPU:0 now
where the time goes in v6:
time: 555 us; the launch traced here: 549 us
  Pallas kernels  298 us (54%)
  starting transfers between devices  112 us (20%)
  waiting for transfers between devices  76.4 us (14%)
  other arithmetic  44.9 us (8%)
  matrix products  11.4 us (2%)
    ppermute x33, starting transfers between devices, shift(): lax.ppermute(x, 'freq', [(i, (i + by) % parts) for i in range(parts)])  112 us
    ppermute x33, waiting for transfers between devices, shift(): lax.ppermute(x, 'freq', [(i, (i + by) % parts) for i in range(parts)])  76.4 us
    pallas_call x4, Pallas kernels, gathered_over(): pl.pallas_call(functools.partial(gather_kernel, chips, parts), out_shape=...  61.7 us
    pallas_call x3, Pallas kernels, final(): pl.pallas_call(functools.partial(final_kernel, nf, len(outs)), out_shape=...  57.6 us
    pallas_call x3, Pallas kernels, quarter_pass(): pl.pallas_call(functools.partial(quarter_kernel, nf, parts, sets), out_sh...  54.9 us
    pallas_call x2, Pallas kernels, summed(): pl.pallas_call(functools.partial(sum_kernel, chips), out_shape=jax.ShapeD...  40.1 us
    pallas_call x2, Pallas kernels, again(): pl.pallas_call(functools.partial(again_kernel, own), out_shape=jax.ShapeD...  31.8 us
    pallas_call x2, Pallas kernels, summed(): pl.pallas_call(functools.partial(reduce_kernel, chips), out_shape=jax.Sha...  22.5 us
  transfers between devices with their start and end apart: 33, of which 6 were waited for; matrix products, arithmetic and copies ran while one was open for 9% of the time, Pallas kernels for 41%

profile of v6, /device:TPU:0, one launch (start us, length us, event | category | flops | bytes accessed | tf_op | source)
XLA Modules:
  0.0 548.6 jit_solution(12272362053166988697)
XLA Ops:
  1.6 5.1 collective-permute-start.2
  6.7 1.0 collective-permute-start
  7.7 10.4 %fusion = f32[4,128,1024]{2,1,0:T(8,128)S(1)} fusion(bf16[4608,1024]{1,0:T(8,128)(2,1)} %l_ref.23, f32[4,4608,128]{2,1,0:T(8,128)} %rest_0_.5), kind=kOutput, calls=%fused_computation | convolution fusion | flops 4834197504 | bytes 20971520 | tf_op jit(solution)/shard_map/pa,fpc->fca/dot_general | solution.py:810
  18.2 20.0 %shard_map.77 = bf16[4,2,64,1024]{3,2,1,0:T(8,128)(2,1)S(1)} custom-call(f32[4,2,64,1024]{3,2,1,0:T(8,128)S(1)} %bitcast.53), custom_call_target="tpu_custom_call" | custom-call | flops 20971520 | bytes 20971520 | tf_op jit(solution)/shard_map/pallas_call | solution.py:720
  38.2 15.7 %shard_map.78 = f32[512,1024]{1,0:T(8,128)S(1)} custom-call(bf16[4608,1024]{1,0:T(8,128)(2,1)} %l_ref.23, f32[4,4608]{1,0:T(4,128)S(1)} %copy-done.7, bf16[512,1024]{1,0:T(8,128)(2,1)S(1)} %bitcast.59, f32[512,1024]{1,0:T(8,128)S(1)} %bitcast.54), custom_call_target="tpu_custom_call" | custom-call | flops 9663676416 | bytes 9437184 | tf_op jit(solution)/shard_map/pallas_call | solution.py:276
  54.0 11.2 %shard_map.79 = bf16[64,1024]{1,0:T(8,128)(2,1)S(1)} custom-call(f32[4,2,64,1024]{3,2,1,0:T(8,128)S(1)} %bitcast.57), custom_call_target="tpu_custom_call" | custom-call | flops 10485760 | bytes 10485760 | tf_op jit(solution)/shard_map/pallas_call | solution.py:711
  65.2 2.9 collective-permute-start.5
  68.1 1.2 collective-permute-start.4
  70.2 2.8 multiply_convert_fusion.18
  73.0 4.0 multiply_convert_fusion
  78.5 10.9 %shard_map.80 = (bf16[1,4,2,64,1024]{4,3,2,1,0:T(8,128)(2,1)S(1)}, f32[8,128]{1,0:T(8,128)S(1)}) custom-call(bf16[1,64,1024]{2,1,0:T(8,128)(2,1)S(1)} %bitcast.63), custom_call_target="tpu_custom_call" | custom-call | flops 20971520 | bytes 20971520 | tf_op jit(solution)/shard_map/pallas_call | solution.py:740
  89.6 2.4 collective-permute-start.9
  92.0 2.1 collective-permute-start.10
  96.1 2.0 collective-permute-start.8
  98.1 1.2 collective-permute-start.7
  99.3 19.1 %shard_map.81 = (bf16[4,4,2,64,1024]{4,3,2,1,0:T(8,128)(2,1)S(1)}, f32[8,128]{1,0:T(8,128)S(1)}) custom-call(bf16[3,64,1024]{2,1,0:T(8,128)(2,1)S(1)} %pad_maximum_fusion.x_ref, bf16[4,2,64,1024]{3,2,1,0:T(8,128)(2,1)S(1)} %bitcast.61), custom_call_target="tpu_custom_call" | custom-call | flops 62914560 | bytes 62914560 | tf_op jit(solution)/shard_map/pallas_call | solution.py:740
  118.5 2.0 copy-done
  121.8 33.4 %collective-permute-start.6 = (f16[4,768,128]{2,1,0:T(8,128)(2,1)}, f16[4,768,128]{2,1,0:T(8,128)(2,1)S(1)}, u32[]{:S(2)}, u32[]{:S(2)}) collective-permute-start(f16[4,768,128]{2,1,0:T(8,128)(2,1)} %get-tuple-element.145), channel_id=1, source_target_pairs={{0,1},{1,2},{2,3},{3,0},{4,5},{5,6},{6,7},{7,4},{8,9},{9,10},{10,1... | collective-permute-start | bytes 2359304 | tf_op jit(solution)/shard_map/ppermute | solution.py:768
  156.1 2.0 convert_multiply_fusion.4.rest_2_
  158.1 1.9 convert_multiply_fusion.3.rest_3_
  160.1 18.3 %shard_map.83 = (f32[4,384,128]{2,1,0:T(8,128)}, f32[4,384,128]{2,1,0:T(8,128)}, f32[4,384,128]{2,1,0:T(8,128)}, f32[4,384,128]{2,1,0:T(8,128)}, f32[4,384,128]{...) custom-call(s32[1]{0:T(128)} %bitcast.me_ref, bf16[4608,1024]{1,0:T(8,128)(2,1)} %l_ref.23, ...), custom_call_target="tpu_custom_call" | custom-call | flops 2415919104 | bytes 12582912 | tf_op jit(solution)/shard_map/pallas_call | solution.py:145
  178.4 1.4 multiply_convert_fusion.17
  179.7 1.3 multiply_convert_fusion.16
  181.1 7.3 %collective-permute-start.14 = (f16[4,384,128]{2,1,0:T(8,128)(2,1)S(1)}, f16[4,384,128]{2,1,0:T(8,128)(2,1)S(1)}, u32[]{:S(2)}, u32[]{:S(2)}) collective-permute-start(f16[4,384,128]{2,1,0:T(8,128)(2,1)S(1)} %multiply_convert_fusion.15), channel_id=1, source_target_pairs={{0,1},{1,2},{2,3},{3,0},{4,5},{5,6},{6,7},{7,4},{8,9},{9,10},{10,1... | collective-permute-start | bytes 1179656 | tf_op jit(solution)/shard_map/ppermute | solution.py:768
  188.4 3.4 collective-permute-start.13
  194.3 1.3 convert_multiply_fusion.rest_3_
  195.6 19.6 %collective-permute-done.7 = f16[4,768,128]{2,1,0:T(8,128)(2,1)S(1)} collective-permute-done((f16[4,768,128]{2,1,0:T(8,128)(2,1)}, f16[4,768,128]{2,1,0:T(8,128)(2,1)S(1)}, u32[]{:S(2)}, u32[]{:S(2)}) %collective-permute-start.7) | collective-permute-done | bytes 786464 | tf_op jit(solution)/shard_map/ppermute | solution.py:768
  215.2 1.3 convert_multiply_fusion.1.rest_2_
  216.5 1.3 convert_multiply_fusion.2.rest_1_
  217.8 18.3 %shard_map.84 = (f32[4,384,128]{2,1,0:T(8,128)}, f32[4,384,128]{2,1,0:T(8,128)}, f32[4,384,128]{2,1,0:T(8,128)}, f32[4,384,128]{2,1,0:T(8,128)}, f32[4,384,128]{...) custom-call(s32[1]{0:T(128)} %bitcast.me_ref, bf16[4608,1024]{1,0:T(8,128)(2,1)} %l_ref.23, ...), custom_call_target="tpu_custom_call" | custom-call | flops 2415919104 | bytes 12582912 | tf_op jit(solution)/shard_map/pallas_call | solution.py:145
  236.1 18.3 %shard_map.82 = (f32[4,384,128]{2,1,0:T(8,128)}, f32[4,384,128]{2,1,0:T(8,128)}, f32[4,384,128]{2,1,0:T(8,128)}, f32[4,384,128]{2,1,0:T(8,128)}, f32[4,384,128]{...) custom-call(s32[1]{0:T(128)} %bitcast.me_ref, bf16[4608,1024]{1,0:T(8,128)(2,1)} %l_ref.23, ...), custom_call_target="tpu_custom_call" | custom-call | flops 2415919104 | bytes 12582912 | tf_op jit(solution)/shard_map/pallas_call | solution.py:145
  254.4 2.1 multiply_convert_fusion.23
  259.0 3.7 collective-permute-start.18
  264.4 8.4 %collective-permute-done.20 = f16[4,384,128]{2,1,0:T(8,128)(2,1)S(1)} collective-permute-done((f16[4,384,128]{2,1,0:T(8,128)(2,1)S(1)}, f16[4,384,128]{2,1,0:T(8,128)(2,1)S(1)}, u32[]{:S(2)}, u32[]{:S(2)}) %collective-permute-start.20) | collective-permute-done | bytes 393248 | tf_op jit(solution)/shard_map/ppermute | solution.py:768
  272.8 16.9 %collective-permute-done.19 = f16[4,384,128]{2,1,0:T(8,128)(2,1)S(1)} collective-permute-done((f16[4,384,128]{2,1,0:T(8,128)(2,1)S(1)}, f16[4,384,128]{2,1,0:T(8,128)(2,1)S(1)}, u32[]{:S(2)}, u32[]{:S(2)}) %collective-permute-start.19) | collective-permute-done | bytes 393248 | tf_op jit(solution)/shard_map/ppermute | solution.py:768
  289.6 7.5 %collective-permute-start.15 = (f16[4,384,128]{2,1,0:T(8,128)(2,1)S(1)}, f16[4,384,128]{2,1,0:T(8,128)(2,1)S(1)}, u32[]{:S(2)}, u32[]{:S(2)}) collective-permute-start(f16[4,384,128]{2,1,0:T(8,128)(2,1)S(1)} %multiply_convert_fusion.14), channel_id=1, source_target_pairs={{0,3},{1,0},{2,1},{3,2},{4,7},{5,4},{6,5},{7,6},{8,11},{9,8},{10,9... | collective-permute-start | bytes 1179656 | tf_op jit(solution)/shard_map/ppermute | solution.py:768
  297.1 2.3 multiply_add_fusion.15
  299.7 4.8 shard_map.85.rest_4_
  304.5 18.0 %collective-permute-start.12 = (f16[4,384,128]{2,1,0:T(8,128)(2,1)S(1)}, f16[4,384,128]{2,1,0:T(8,128)(2,1)S(1)}, u32[]{:S(2)}, u32[]{:S(2)}) collective-permute-start(f16[4,384,128]{2,1,0:T(8,128)(2,1)S(1)} %multiply_convert_fusion.17), channel_id=1, source_target_pairs={{0,3},{1,0},{2,1},{3,2},{4,7},{5,4},{6,5},{7,6},{8,11},{9,8},{10,9... | collective-permute-start | bytes 1179656 | tf_op jit(solution)/shard_map/ppermute | solution.py:768
  322.5 7.5 %collective-permute-done.15 = f16[4,384,128]{2,1,0:T(8,128)(2,1)S(1)} collective-permute-done((f16[4,384,128]{2,1,0:T(8,128)(2,1)S(1)}, f16[4,384,128]{2,1,0:T(8,128)(2,1)S(1)}, u32[]{:S(2)}, u32[]{:S(2)}) %collective-permute-start.15) | collective-permute-done | bytes 393248 | tf_op jit(solution)/shard_map/ppermute | solution.py:768
  329.9 2.3 multiply_add_fusion.12
  332.3 4.7 shard_map.86.rest_4_
  337.1 1.1 collective-permute-done.12
  338.2 2.3 multiply_add_fusion.9
  340.5 5.2 shard_map.87.x_ref
  345.8 20.1 %shard_map.88 = bf16[4,2,64,1024]{3,2,1,0:T(8,128)(2,1)S(1)} custom-call(f32[4,2,64,1024]{3,2,1,0:T(8,128)S(1)} %bitcast.52), custom_call_target="tpu_custom_call" | custom-call | flops 20971520 | bytes 20971520 | tf_op jit(solution)/shard_map/pallas_call | solution.py:720
  365.9 16.0 %shard_map.89 = f32[512,1024]{1,0:T(8,128)S(1)} custom-call(bf16[4608,1024]{1,0:T(8,128)(2,1)} %l_ref.23, f32[4,4608]{1,0:T(4,128)S(1)} %copy-done.7, bf16[512,1024]{1,0:T(8,128)(2,1)S(1)} %bitcast.60, f32[512,1024]{1,0:T(8,128)S(1)} %shard_map.87.x_ref), custom_call_target="tpu_custom_call" | custom-call | flops 9663676416 | bytes 9437184 | tf_op jit(solution)/shard_map/pallas_call | solution.py:276
  382.0 11.3 %shard_map.90 = bf16[64,1024]{1,0:T(8,128)(2,1)S(1)} custom-call(f32[4,2,64,1024]{3,2,1,0:T(8,128)S(1)} %bitcast.58), custom_call_target="tpu_custom_call" | custom-call | flops 10485760 | bytes 10485760 | tf_op jit(solution)/shard_map/pallas_call | solution.py:711
  393.3 6.1 %collective-permute-start.23 = (bf16[64,1024]{1,0:T(8,128)(2,1)S(1)}, bf16[64,1024]{1,0:T(8,128)(2,1)S(1)}, u32[]{:S(2)}, u32[]{:S(2)}) collective-permute-start(bf16[64,1024]{1,0:T(8,128)(2,1)S(1)} %shard_map.90), channel_id=1, source_target_pairs={{0,3},{1,0},{2,1},{3,2},{4,7},{5,4},{6,5},{7,6},{8,11},{9,8},{10,9... | collective-permute-start | bytes 393224 | tf_op jit(solution)/shard_map/ppermute | solution.py:768
  400.1 3.3 collective-permute-start.30
  403.4 1.1 collective-permute-start.31
  404.5 11.5 %shard_map.91 = (bf16[1,4,2,64,1024]{4,3,2,1,0:T(8,128)(2,1)S(1)}, f32[8,128]{1,0:T(8,128)}) custom-call(bf16[1,64,1024]{2,1,0:T(8,128)(2,1)S(1)} %bitcast.64), custom_call_target="tpu_custom_call" | custom-call | flops 20971520 | bytes 20971520 | tf_op jit(solution)/shard_map/pallas_call | solution.py:740
  416.3 14.8 %shard_map.92 = f32[4,4608,128]{2,1,0:T(8,128)} custom-call(s32[1]{0:T(128)} %bitcast.me_ref, bf16[4608,1024]{1,0:T(8,128)(2,1)S(1)} %bitcast.45, f32[4,4608]{1,0:T(4,128)S(1)} %copy-done.7, bf16[512,1024]{1,0:T(8,128)(2,1)S(1)} %bitcast.55, f32[4,384,128]{2,1,0:T(8,128)S(1)} %get-tuple-element.139.rest_0_, f32[4,384,128]{2,1,0:T(8,128)S(1)} %get-tuple-element.138.rest_1_, ...), custom_call_target="tpu_custom_call" | custom-call | flops 4831838208 | bytes 18874368 | tf_op jit(solution)/shard_map/pallas_call | solution.py:364
  431.2 2.4 collective-permute-start.26
  433.6 2.0 collective-permute-start.25
  435.6 20.2 %shard_map.93 = (bf16[4,4,2,64,1024]{4,3,2,1,0:T(8,128)(2,1)S(1)}, f32[8,128]{1,0:T(8,128)}) custom-call(bf16[3,64,1024]{2,1,0:T(8,128)(2,1)S(1)} %pad_maximum_fusion.1.x_ref, bf16[4,2,64,1024]{3,2,1,0:T(8,128)(2,1)S(1)} %bitcast.56), custom_call_target="tpu_custom_call" | custom-call | flops 62914560 | bytes 62914560 | tf_op jit(solution)/shard_map/pallas_call | solution.py:740
  456.2 22.9 %collective-permute-done.31 = f16[4,384,128]{2,1,0:T(8,128)(2,1)S(1)} collective-permute-done((f16[4,384,128]{2,1,0:T(8,128)(2,1)S(1)}, f16[4,384,128]{2,1,0:T(8,128)(2,1)S(1)}, u32[]{:S(2)}, u32[]{:S(2)}) %collective-permute-start.31) | collective-permute-done | bytes 393248 | tf_op jit(solution)/shard_map/ppermute | solution.py:768
  479.2 2.4 multiply_add_fusion.6
  481.6 19.2 %shard_map.94.rest_4_ = f32[4,4608,128]{2,1,0:T(8,128)} custom-call(s32[1]{0:T(128)} %bitcast.me_ref, bf16[4608,1024]{1,0:T(8,128)(2,1)S(1)} %bitcast.45, f32[16,4608]{1,0:T(8,128)S(1)} %copy-done.2, f32[16,4608]{1,0:T(8,128)S(1)} %copy-done.1, f32[64,16]{1,0:T(8,128)S(1)} %bitcast.65, bf16[2048,1024]{1,0:T(8,128)(2,1)S(1)} %bitcast.49, ...), custom_call_target="tpu_custom_call" | custom-call | flops 6442450944 | bytes 6291456 | tf_op jit(solution)/shard_map/pallas_call | solution.py:475
  500.9 4.3 collective-permute-start.24
  505.2 2.3 multiply_add_fusion.3
  507.6 19.2 %shard_map.95.rest_4_ = f32[4,4608,128]{2,1,0:T(8,128)} custom-call(s32[1]{0:T(128)} %bitcast.me_ref, bf16[4608,1024]{1,0:T(8,128)(2,1)S(1)} %bitcast.45, f32[16,4608]{1,0:T(8,128)S(1)} %copy-done.2, f32[16,4608]{1,0:T(8,128)S(1)} %copy-done.1, f32[64,16]{1,0:T(8,128)S(1)} %bitcast.66, ...), custom_call_target="tpu_custom_call", output_to_operand_aliasing={{}: (10, {})} | custom-call | flops 6442450944 | bytes 6291456 | tf_op jit(solution)/shard_map/pallas_call | solution.py:475
  526.8 2.3 multiply_add_fusion
  529.1 19.2 %shard_map.96 = f32[4,4608,128]{2,1,0:T(8,128)} custom-call(s32[1]{0:T(128)} %bitcast.me_ref, bf16[4608,1024]{1,0:T(8,128)(2,1)S(1)} %bitcast.45, f32[16,4608]{1,0:T(8,128)S(1)} %copy-done.2, f32[16,4608]{1,0:T(8,128)S(1)} %copy-done.1, f32[64,16]{1,0:T(8,128)S(1)} %bitcast.67, bf16[2048,1024]{1,0:T(8,128)(2,1)S(1)} %bitcast.51, ...), custom_call_target="tpu_custom_call", output_to_operand_aliasing={{}: (10, {})} | custom-call | flops 6442450944 | bytes 6291456 | tf_op jit(solution)/shard_map/pallas_call | solution.py:475
  (169 shorter events, 15.0 us)
Async XLA Ops:
  1.6 87.8 %collective-permute-start.2 = (f16[2,4,4608]{2,1,0:T(4,128)(2,1)S(1)}, f16[2,4,4608]{2,1,0:T(4,128)(2,1)S(1)}, u32[]{:S(2)}, u32[]{:S(2)}) collective-permute-start(f16[2,4,4608]{2,1,0:T(4,128)(2,1)S(1)} %fusion.3), channel_id=1, source_target_pairs={{0,3},{1,0},{2,1},{3,2},{4,7},{5,4},{6,5},{7,6},{8,11},{9,8},{10,9... | collective-permute-start | bytes 221192 | tf_op jit(solution)/shard_map/ppermute | solution.py:768
  6.7 82.9 %collective-permute-start.1 = (f16[2,4,4608]{2,1,0:T(4,128)(2,1)S(1)}, f16[2,4,4608]{2,1,0:T(4,128)(2,1)S(1)}, u32[]{:S(2)}, u32[]{:S(2)}) collective-permute-start(f16[2,4,4608]{2,1,0:T(4,128)(2,1)S(1)} %fusion.3), channel_id=1, source_target_pairs={{0,2},{1,3},{2,0},{3,1},{4,6},{5,7},{6,4},{7,5},{8,10},{9,11},{10,... | collective-permute-start | bytes 221192 | tf_op jit(solution)/shard_map/ppermute | solution.py:768
  6.7 85.3 %collective-permute-start = (f16[2,4,4608]{2,1,0:T(4,128)(2,1)S(1)}, f16[2,4,4608]{2,1,0:T(4,128)(2,1)S(1)}, u32[]{:S(2)}, u32[]{:S(2)}) collective-permute-start(f16[2,4,4608]{2,1,0:T(4,128)(2,1)S(1)} %fusion.3), channel_id=1, source_target_pairs={{0,1},{1,2},{2,3},{3,0},{4,5},{5,6},{6,7},{7,4},{8,9},{9,10},{10,1... | collective-permute-start | bytes 221192 | tf_op jit(solution)/shard_map/ppermute | solution.py:768
  18.1 20.1 %copy-start.7 = (f32[4,4608]{1,0:T(4,128)S(1)}, f32[4,4608]{1,0:T(4,128)}, u32[]{:S(2)}) copy-start(f32[4,4608]{1,0:T(4,128)} %wt_ref.5) | copy-start | bytes 221188
  54.0 15.4 %copy-start.39 = (f32[16,16]{1,0:T(8,128)S(1)}, f32[16,16]{1,0:T(8,128)}, u32[]{:S(2)}) copy-start(f32[16,16]{1,0:T(8,128)} %param.10) | copy-start | bytes 3076
  54.0 15.8 %copy-start.40 = (f32[16,16]{1,0:T(8,128)S(1)}, f32[16,16]{1,0:T(8,128)}, u32[]{:S(2)}) copy-start(f32[16,16]{1,0:T(8,128)} %param.11) | copy-start | bytes 3076
  65.2 30.5 %collective-permute-start.5 = (bf16[64,1024]{1,0:T(8,128)(2,1)S(1)}, bf16[64,1024]{1,0:T(8,128)(2,1)S(1)}, u32[]{:S(2)}, u32[]{:S(2)}) collective-permute-start(bf16[64,1024]{1,0:T(8,128)(2,1)S(1)} %shard_map.79), channel_id=1, source_target_pairs={{0,3},{1,0},{2,1},{3,2},{4,7},{5,4},{6,5},{7,6},{8,11},{9,8},{10,9... | collective-permute-start | bytes 393224 | tf_op jit(solution)/shard_map/ppermute | solution.py:768
  68.1 28.0 %collective-permute-start.4 = (bf16[64,1024]{1,0:T(8,128)(2,1)S(1)}, bf16[64,1024]{1,0:T(8,128)(2,1)S(1)}, u32[]{:S(2)}, u32[]{:S(2)}) collective-permute-start(bf16[64,1024]{1,0:T(8,128)(2,1)S(1)} %shard_map.79), channel_id=1, source_target_pairs={{0,2},{1,3},{2,0},{3,1},{4,6},{5,7},{6,4},{7,5},{8,10},{9,11},{10,... | collective-permute-start | bytes 393224 | tf_op jit(solution)/shard_map/ppermute | solution.py:768
  70.2 6.8 %copy-start.8 = (f32[16,16,16]{2,1,0:T(8,128)}, f32[16,16,16]{2,1,0:T(8,128)S(1)}, u32[]{:S(2)}) copy-start(f32[16,16,16]{2,1,0:T(8,128)S(1)} %broadcast_multiply_fusion) | copy-start | bytes 49156
  77.0 18.0 %copy-start.38 = (f32[4,4608]{1,0:T(4,128)S(1)}, f32[4,4608]{1,0:T(4,128)}, u32[]{:S(2)}) copy-start(f32[4,4608]{1,0:T(4,128)} %param.9) | copy-start | bytes 221188
  89.5 8.7 %collective-permute-start.3 = (bf16[64,1024]{1,0:T(8,128)(2,1)S(1)}, bf16[64,1024]{1,0:T(8,128)(2,1)S(1)}, u32[]{:S(2)}, u32[]{:S(2)}) collective-permute-start(bf16[64,1024]{1,0:T(8,128)(2,1)S(1)} %shard_map.79), channel_id=1, source_target_pairs={{0,1},{1,2},{2,3},{3,0},{4,5},{5,6},{6,7},{7,4},{8,9},{9,10},{10,1... | collective-permute-start | bytes 393224 | tf_op jit(solution)/shard_map/ppermute | solution.py:768
  89.6 32.2 %collective-permute-start.9 = (f16[4,384,128]{2,1,0:T(8,128)(2,1)S(1)}, f16[4,384,128]{2,1,0:T(8,128)(2,1)S(1)}, u32[]{:S(2)}, u32[]{:S(2)}) collective-permute-start(f16[4,384,128]{2,1,0:T(8,128)(2,1)S(1)} %get-tuple-element.67), channel_id=1, source_target_pairs={{0,1},{1,2},{2,3},{3,0},{4,5},{5,6},{6,7},{7,4},{8,9},{9,10},{10,1... | collective-permute-start | bytes 1179656 | tf_op jit(solution)/shard_map/ppermute | solution.py:768
  92.0 64.1 %collective-permute-start.10 = (f16[4,384,128]{2,1,0:T(8,128)(2,1)}, f16[4,384,128]{2,1,0:T(8,128)(2,1)}, u32[]{:S(2)}, u32[]{:S(2)}) collective-permute-start(f16[4,384,128]{2,1,0:T(8,128)(2,1)} %get-tuple-element.68), channel_id=1, source_target_pairs={{0,2},{1,3},{2,0},{3,1},{4,6},{5,7},{6,4},{7,5},{8,10},{9,11},{10,... | collective-permute-start | bytes 1179656 | tf_op jit(solution)/shard_map/ppermute | solution.py:768
  95.8 62.3 %collective-permute-start.11 = (f16[4,384,128]{2,1,0:T(8,128)(2,1)}, f16[4,384,128]{2,1,0:T(8,128)(2,1)}, u32[]{:S(2)}, u32[]{:S(2)}) collective-permute-start(f16[4,384,128]{2,1,0:T(8,128)(2,1)} %get-tuple-element.69), channel_id=1, source_target_pairs={{0,3},{1,0},{2,1},{3,2},{4,7},{5,4},{6,5},{7,6},{8,11},{9,8},{10,9... | collective-permute-start | bytes 1179656 | tf_op jit(solution)/shard_map/ppermute | solution.py:768
  96.1 98.2 %collective-permute-start.8 = (f16[4,768,128]{2,1,0:T(8,128)(2,1)}, f16[4,768,128]{2,1,0:T(8,128)(2,1)S(1)}, u32[]{:S(2)}, u32[]{:S(2)}) collective-permute-start(f16[4,768,128]{2,1,0:T(8,128)(2,1)} %get-tuple-element.143), channel_id=1, source_target_pairs={{0,3},{1,0},{2,1},{3,2},{4,7},{5,4},{6,5},{7,6},{8,11},{9,8},{10,9... | collective-permute-start | bytes 2359304 | tf_op jit(solution)/shard_map/ppermute | solution.py:768
  98.1 117.1 %collective-permute-start.7 = (f16[4,768,128]{2,1,0:T(8,128)(2,1)}, f16[4,768,128]{2,1,0:T(8,128)(2,1)S(1)}, u32[]{:S(2)}, u32[]{:S(2)}) collective-permute-start(f16[4,768,128]{2,1,0:T(8,128)(2,1)} %get-tuple-element.144), channel_id=1, source_target_pairs={{0,2},{1,3},{2,0},{3,1},{4,6},{5,7},{6,4},{7,5},{8,10},{9,11},{10,... | collective-permute-start | bytes 2359304 | tf_op jit(solution)/shard_map/ppermute | solution.py:768
  121.8 94.7 %collective-permute-start.6 = (f16[4,768,128]{2,1,0:T(8,128)(2,1)}, f16[4,768,128]{2,1,0:T(8,128)(2,1)S(1)}, u32[]{:S(2)}, u32[]{:S(2)}) collective-permute-start(f16[4,768,128]{2,1,0:T(8,128)(2,1)} %get-tuple-element.145), channel_id=1, source_target_pairs={{0,1},{1,2},{2,3},{3,0},{4,5},{5,6},{6,7},{7,4},{8,9},{9,10},{10,1... | collective-permute-start | bytes 2359304 | tf_op jit(solution)/shard_map/ppermute | solution.py:768
  178.3 13.5 %copy-start.28 = (f32[4,384,128]{2,1,0:T(8,128)S(1)}, f32[4,384,128]{2,1,0:T(8,128)}, u32[]{:S(2)}) copy-start(f32[4,384,128]{2,1,0:T(8,128)} %get-tuple-element.94) | copy-start | bytes 2359300
  178.3 14.3 %copy-start.27 = (f32[4,384,128]{2,1,0:T(8,128)S(1)}, f32[4,384,128]{2,1,0:T(8,128)}, u32[]{:S(2)}) copy-start(f32[4,384,128]{2,1,0:T(8,128)} %get-tuple-element.95) | copy-start | bytes 2359300
  179.7 13.8 %copy-start.24 = (f32[4,384,128]{2,1,0:T(8,128)S(1)}, f32[4,384,128]{2,1,0:T(8,128)}, u32[]{:S(2)}) copy-start(f32[4,384,128]{2,1,0:T(8,128)} %get-tuple-element.96) | copy-start | bytes 2359300
  181.1 155.9 %collective-permute-start.14 = (f16[4,384,128]{2,1,0:T(8,128)(2,1)S(1)}, f16[4,384,128]{2,1,0:T(8,128)(2,1)S(1)}, u32[]{:S(2)}, u32[]{:S(2)}) collective-permute-start(f16[4,384,128]{2,1,0:T(8,128)(2,1)S(1)} %multiply_convert_fusion.15), channel_id=1, source_target_pairs={{0,1},{1,2},{2,3},{3,0},{4,5},{5,6},{6,7},{7,4},{8,9},{9,10},{10,1... | collective-permute-start | bytes 1179656 | tf_op jit(solution)/shard_map/ppermute | solution.py:768
  188.4 148.7 %collective-permute-start.13 = (f16[4,384,128]{2,1,0:T(8,128)(2,1)S(1)}, f16[4,384,128]{2,1,0:T(8,128)(2,1)S(1)}, u32[]{:S(2)}, u32[]{:S(2)}) collective-permute-start(f16[4,384,128]{2,1,0:T(8,128)(2,1)S(1)} %multiply_convert_fusion.16), channel_id=1, source_target_pairs={{0,2},{1,3},{2,0},{3,1},{4,6},{5,7},{6,4},{7,5},{8,10},{9,11},{10,... | collective-permute-start | bytes 1179656 | tf_op jit(solution)/shard_map/ppermute | solution.py:768
  236.1 20.4 %copy-start.25 = (f32[4,384,128]{2,1,0:T(8,128)S(1)}, f32[4,384,128]{2,1,0:T(8,128)}, u32[]{:S(2)}) copy-start(f32[4,384,128]{2,1,0:T(8,128)} %get-tuple-element.75) | copy-start | bytes 2359300
  258.6 38.5 %copy-start.14 = (f32[4,384,128]{2,1,0:T(8,128)S(1)}, f32[4,384,128]{2,1,0:T(8,128)}, u32[]{:S(2)}) copy-start(f32[4,384,128]{2,1,0:T(8,128)} %get-tuple-element.78) | copy-start | bytes 2359300
  258.8 13.9 %collective-permute-start.20 = (f16[4,384,128]{2,1,0:T(8,128)(2,1)S(1)}, f16[4,384,128]{2,1,0:T(8,128)(2,1)S(1)}, u32[]{:S(2)}, u32[]{:S(2)}) collective-permute-start(f16[4,384,128]{2,1,0:T(8,128)(2,1)S(1)} %multiply_convert_fusion.9), channel_id=1, source_target_pairs={{0,1},{1,2},{2,3},{3,0},{4,5},{5,6},{6,7},{7,4},{8,9},{9,10},{10,1... | collective-permute-start | bytes 1179656 | tf_op jit(solution)/shard_map/ppermute | solution.py:768
  258.9 30.7 %collective-permute-start.19 = (f16[4,384,128]{2,1,0:T(8,128)(2,1)S(1)}, f16[4,384,128]{2,1,0:T(8,128)(2,1)S(1)}, u32[]{:S(2)}, u32[]{:S(2)}) collective-permute-start(f16[4,384,128]{2,1,0:T(8,128)(2,1)S(1)} %multiply_convert_fusion.10), channel_id=1, source_target_pairs={{0,2},{1,3},{2,0},{3,1},{4,6},{5,7},{6,4},{7,5},{8,10},{9,11},{10,... | collective-permute-start | bytes 1179656 | tf_op jit(solution)/shard_map/ppermute | solution.py:768
  259.0 30.7 %collective-permute-start.18 = (f16[4,384,128]{2,1,0:T(8,128)(2,1)S(1)}, f16[4,384,128]{2,1,0:T(8,128)(2,1)S(1)}, u32[]{:S(2)}, u32[]{:S(2)}) collective-permute-start(f16[4,384,128]{2,1,0:T(8,128)(2,1)S(1)} %multiply_convert_fusion.11), channel_id=1, source_target_pairs={{0,3},{1,0},{2,1},{3,2},{4,7},{5,4},{6,5},{7,6},{8,11},{9,8},{10,9... | collective-permute-start | bytes 1179656 | tf_op jit(solution)/shard_map/ppermute | solution.py:768
  272.8 31.7 %collective-permute-start.17 = (f16[4,384,128]{2,1,0:T(8,128)(2,1)S(1)}, f16[4,384,128]{2,1,0:T(8,128)(2,1)S(1)}, u32[]{:S(2)}, u32[]{:S(2)}) collective-permute-start(f16[4,384,128]{2,1,0:T(8,128)(2,1)S(1)} %multiply_convert_fusion.12), channel_id=1, source_target_pairs={{0,1},{1,2},{2,3},{3,0},{4,5},{5,6},{6,7},{7,4},{8,9},{9,10},{10,1... | collective-permute-start | bytes 1179656 | tf_op jit(solution)/shard_map/ppermute | solution.py:768
  289.6 32.8 %collective-permute-start.16 = (f16[4,384,128]{2,1,0:T(8,128)(2,1)S(1)}, f16[4,384,128]{2,1,0:T(8,128)(2,1)S(1)}, u32[]{:S(2)}, u32[]{:S(2)}) collective-permute-start(f16[4,384,128]{2,1,0:T(8,128)(2,1)S(1)} %multiply_convert_fusion.13), channel_id=1, source_target_pairs={{0,2},{1,3},{2,0},{3,1},{4,6},{5,7},{6,4},{7,5},{8,10},{9,11},{10,... | collective-permute-start | bytes 1179656 | tf_op jit(solution)/shard_map/ppermute | solution.py:768
  289.6 40.3 %collective-permute-start.15 = (f16[4,384,128]{2,1,0:T(8,128)(2,1)S(1)}, f16[4,384,128]{2,1,0:T(8,128)(2,1)S(1)}, u32[]{:S(2)}, u32[]{:S(2)}) collective-permute-start(f16[4,384,128]{2,1,0:T(8,128)(2,1)S(1)} %multiply_convert_fusion.14), channel_id=1, source_target_pairs={{0,3},{1,0},{2,1},{3,2},{4,7},{5,4},{6,5},{7,6},{8,11},{9,8},{10,9... | collective-permute-start | bytes 1179656 | tf_op jit(solution)/shard_map/ppermute | solution.py:768
  299.7 30.3 %copy-start.13 = (f32[4,384,128]{2,1,0:T(8,128)S(1)}, f32[4,384,128]{2,1,0:T(8,128)}, u32[]{:S(2)}) copy-start(f32[4,384,128]{2,1,0:T(8,128)} %get-tuple-element.74) | copy-start | bytes 2359300
  304.5 33.7 %collective-permute-start.12 = (f16[4,384,128]{2,1,0:T(8,128)(2,1)S(1)}, f16[4,384,128]{2,1,0:T(8,128)(2,1)S(1)}, u32[]{:S(2)}, u32[]{:S(2)}) collective-permute-start(f16[4,384,128]{2,1,0:T(8,128)(2,1)S(1)} %multiply_convert_fusion.17), channel_id=1, source_target_pairs={{0,3},{1,0},{2,1},{3,2},{4,7},{5,4},{6,5},{7,6},{8,11},{9,8},{10,9... | collective-permute-start | bytes 1179656 | tf_op jit(solution)/shard_map/ppermute | solution.py:768
  332.3 5.9 %copy-start.12 = (f32[4,384,128]{2,1,0:T(8,128)S(1)}, f32[4,384,128]{2,1,0:T(8,128)}, u32[]{:S(2)}) copy-start(f32[4,384,128]{2,1,0:T(8,128)} %get-tuple-element.70) | copy-start | bytes 2359300
  340.5 5.3 copy-start.3
  340.5 5.3 copy-start.5
  365.9 50.4 %slice-start = ((s8[9437184]{0:T(1024)(128)(4,1)}), s8[4194304]{0:T(1024)(128)(4,1)S(1)}, s32[]{:S(2)}) async-start(s8[9437184]{0:T(1024)(128)(4,1)} %bitcast.44), calls=%async_computation | async-start | bytes 8388608
  365.9 33.4 %copy-start.15 = (f32[4,384,128]{2,1,0:T(8,128)S(1)}, f32[4,384,128]{2,1,0:T(8,128)}, u32[]{:S(2)}) copy-start(f32[4,384,128]{2,1,0:T(8,128)} %get-tuple-element.100) | copy-start | bytes 2359300
  365.9 50.3 %slice-start.1 = ((s8[9437184]{0:T(1024)(128)(4,1)}), s8[4194304]{0:T(1024)(128)(4,1)S(1)}, s32[]{:S(2)}) async-start(s8[9437184]{0:T(1024)(128)(4,1)} %bitcast.44), calls=%async_computation.1 | async-start | bytes 8388608
  365.9 50.3 %slice-start.2 = ((s8[9437184]{0:T(1024)(128)(4,1)}), s8[1048576]{0:T(1024)(128)(4,1)S(1)}, s32[]{:S(2)}) async-start(s8[9437184]{0:T(1024)(128)(4,1)} %bitcast.44), calls=%async_computation.2 | async-start | bytes 2097152
  382.0 18.1 %copy-start.35 = (f16[4,384,128]{2,1,0:T(8,128)(2,1)S(1)}, f16[4,384,128]{2,1,0:T(8,128)(2,1)}, u32[]{:S(2)}) copy-start(f16[4,384,128]{2,1,0:T(8,128)(2,1)} %multiply_convert_fusion.23) | copy-start | bytes 1179652
  382.0 21.4 %copy-start.37 = (f16[4,384,128]{2,1,0:T(8,128)(2,1)S(1)}, f16[4,384,128]{2,1,0:T(8,128)(2,1)}, u32[]{:S(2)}) copy-start(f16[4,384,128]{2,1,0:T(8,128)(2,1)} %multiply_convert_fusion.22) | copy-start | bytes 1179652
  382.0 34.0 %copy-start.36 = (f16[4,384,128]{2,1,0:T(8,128)(2,1)S(1)}, f16[4,384,128]{2,1,0:T(8,128)(2,1)}, u32[]{:S(2)}) copy-start(f16[4,384,128]{2,1,0:T(8,128)(2,1)} %multiply_convert_fusion.21) | copy-start | bytes 1179652
  382.0 34.3 %copy-start.4 = (f32[4,384,128]{2,1,0:T(8,128)S(1)}, f32[4,384,128]{2,1,0:T(8,128)}, u32[]{:S(2)}) copy-start(f32[4,384,128]{2,1,0:T(8,128)} %copy-done.3) | copy-start | bytes 2359300
  382.0 34.3 %copy-start.6 = (f32[4,384,128]{2,1,0:T(8,128)S(1)}, f32[4,384,128]{2,1,0:T(8,128)}, u32[]{:S(2)}) copy-start(f32[4,384,128]{2,1,0:T(8,128)} %copy-done.5) | copy-start | bytes 2359300
  393.3 22.7 %collective-permute-start.23 = (bf16[64,1024]{1,0:T(8,128)(2,1)S(1)}, bf16[64,1024]{1,0:T(8,128)(2,1)S(1)}, u32[]{:S(2)}, u32[]{:S(2)}) collective-permute-start(bf16[64,1024]{1,0:T(8,128)(2,1)S(1)} %shard_map.90), channel_id=1, source_target_pairs={{0,3},{1,0},{2,1},{3,2},{4,7},{5,4},{6,5},{7,6},{8,11},{9,8},{10,9... | collective-permute-start | bytes 393224 | tf_op jit(solution)/shard_map/ppermute | solution.py:768
  399.4 31.7 %collective-permute-start.22 = (bf16[64,1024]{1,0:T(8,128)(2,1)S(1)}, bf16[64,1024]{1,0:T(8,128)(2,1)S(1)}, u32[]{:S(2)}, u32[]{:S(2)}) collective-permute-start(bf16[64,1024]{1,0:T(8,128)(2,1)S(1)} %shard_map.90), channel_id=1, source_target_pairs={{0,2},{1,3},{2,0},{3,1},{4,6},{5,7},{6,4},{7,5},{8,10},{9,11},{10,... | collective-permute-start | bytes 393224 | tf_op jit(solution)/shard_map/ppermute | solution.py:768
  399.5 34.1 %collective-permute-start.21 = (bf16[64,1024]{1,0:T(8,128)(2,1)S(1)}, bf16[64,1024]{1,0:T(8,128)(2,1)S(1)}, u32[]{:S(2)}, u32[]{:S(2)}) collective-permute-start(bf16[64,1024]{1,0:T(8,128)(2,1)S(1)} %shard_map.90), channel_id=1, source_target_pairs={{0,1},{1,2},{2,3},{3,0},{4,5},{5,6},{6,7},{7,4},{8,9},{9,10},{10,1... | collective-permute-start | bytes 393224 | tf_op jit(solution)/shard_map/ppermute | solution.py:768
  400.1 55.7 %collective-permute-start.30 = (f16[4,384,128]{2,1,0:T(8,128)(2,1)S(1)}, f16[4,384,128]{2,1,0:T(8,128)(2,1)S(1)}, u32[]{:S(2)}, u32[]{:S(2)}) collective-permute-start(f16[4,384,128]{2,1,0:T(8,128)(2,1)S(1)} %copy-done.35), channel_id=1, source_target_pairs={{0,3},{1,0},{2,1},{3,2},{4,7},{5,4},{6,5},{7,6},{8,11},{9,8},{10,9... | collective-permute-start | bytes 1179656 | tf_op jit(solution)/shard_map/ppermute | solution.py:768
  403.4 75.7 %collective-permute-start.31 = (f16[4,384,128]{2,1,0:T(8,128)(2,1)S(1)}, f16[4,384,128]{2,1,0:T(8,128)(2,1)S(1)}, u32[]{:S(2)}, u32[]{:S(2)}) collective-permute-start(f16[4,384,128]{2,1,0:T(8,128)(2,1)S(1)} %copy-done.37), channel_id=1, source_target_pairs={{0,2},{1,3},{2,0},{3,1},{4,6},{5,7},{6,4},{7,5},{8,10},{9,11},{10,... | collective-permute-start | bytes 1179656 | tf_op jit(solution)/shard_map/ppermute | solution.py:768
  416.0 63.1 %collective-permute-start.32 = (f16[4,384,128]{2,1,0:T(8,128)(2,1)S(1)}, f16[4,384,128]{2,1,0:T(8,128)(2,1)S(1)}, u32[]{:S(2)}, u32[]{:S(2)}) collective-permute-start(f16[4,384,128]{2,1,0:T(8,128)(2,1)S(1)} %copy-done.36), channel_id=1, source_target_pairs={{0,1},{1,2},{2,3},{3,0},{4,5},{5,6},{6,7},{7,4},{8,9},{9,10},{10,1... | collective-permute-start | bytes 1179656 | tf_op jit(solution)/shard_map/ppermute | solution.py:768
  416.3 14.8 %copy-start.32 = (f16[4,384,128]{2,1,0:T(8,128)(2,1)S(1)}, f16[4,384,128]{2,1,0:T(8,128)(2,1)}, u32[]{:S(2)}) copy-start(f16[4,384,128]{2,1,0:T(8,128)(2,1)} %multiply_convert_fusion.6) | copy-start | bytes 1179652
  416.3 17.3 %copy-start.31 = (f16[4,384,128]{2,1,0:T(8,128)(2,1)S(1)}, f16[4,384,128]{2,1,0:T(8,128)(2,1)}, u32[]{:S(2)}) copy-start(f16[4,384,128]{2,1,0:T(8,128)(2,1)} %multiply_convert_fusion.7) | copy-start | bytes 1179652
  431.1 48.0 %copy-start.34 = (f16[4,384,128]{2,1,0:T(8,128)(2,1)S(1)}, f16[4,384,128]{2,1,0:T(8,128)(2,1)}, u32[]{:S(2)}) copy-start(f16[4,384,128]{2,1,0:T(8,128)(2,1)} %multiply_convert_fusion.4) | copy-start | bytes 1179652
  431.1 48.0 %copy-start.33 = (f16[4,384,128]{2,1,0:T(8,128)(2,1)S(1)}, f16[4,384,128]{2,1,0:T(8,128)(2,1)}, u32[]{:S(2)}) copy-start(f16[4,384,128]{2,1,0:T(8,128)(2,1)} %multiply_convert_fusion.5) | copy-start | bytes 1179652
  431.1 48.0 %copy-start.11 = (f32[4,384,128]{2,1,0:T(8,128)S(1)}, f32[4,384,128]{2,1,0:T(8,128)}, u32[]{:S(2)}) copy-start(f32[4,384,128]{2,1,0:T(8,128)} %get-tuple-element.101) | copy-start | bytes 2359300
  431.2 95.6 %collective-permute-start.26 = (f16[4,384,128]{2,1,0:T(8,128)(2,1)S(1)}, f16[4,384,128]{2,1,0:T(8,128)(2,1)S(1)}, u32[]{:S(2)}, u32[]{:S(2)}) collective-permute-start(f16[4,384,128]{2,1,0:T(8,128)(2,1)S(1)} %copy-done.32), channel_id=1, source_target_pairs={{0,1},{1,2},{2,3},{3,0},{4,5},{5,6},{6,7},{7,4},{8,9},{9,10},{10,1... | collective-permute-start | bytes 1179656 | tf_op jit(solution)/shard_map/ppermute | solution.py:768
  433.6 93.2 %collective-permute-start.25 = (f16[4,384,128]{2,1,0:T(8,128)(2,1)S(1)}, f16[4,384,128]{2,1,0:T(8,128)(2,1)S(1)}, u32[]{:S(2)}, u32[]{:S(2)}) collective-permute-start(f16[4,384,128]{2,1,0:T(8,128)(2,1)S(1)} %copy-done.31), channel_id=1, source_target_pairs={{0,2},{1,3},{2,0},{3,1},{4,6},{5,7},{6,4},{7,5},{8,10},{9,11},{10,... | collective-permute-start | bytes 1179656 | tf_op jit(solution)/shard_map/ppermute | solution.py:768
  455.8 45.1 %collective-permute-start.29 = (f16[4,384,128]{2,1,0:T(8,128)(2,1)S(1)}, f16[4,384,128]{2,1,0:T(8,128)(2,1)S(1)}, u32[]{:S(2)}, u32[]{:S(2)}) collective-permute-start(f16[4,384,128]{2,1,0:T(8,128)(2,1)S(1)} %multiply_convert_fusion.3), channel_id=1, source_target_pairs={{0,1},{1,2},{2,3},{3,0},{4,5},{5,6},{6,7},{7,4},{8,9},{9,10},{10,1... | collective-permute-start | bytes 1179656 | tf_op jit(solution)/shard_map/ppermute | solution.py:768
  479.1 26.1 %collective-permute-start.28 = (f16[4,384,128]{2,1,0:T(8,128)(2,1)S(1)}, f16[4,384,128]{2,1,0:T(8,128)(2,1)S(1)}, u32[]{:S(2)}, u32[]{:S(2)}) collective-permute-start(f16[4,384,128]{2,1,0:T(8,128)(2,1)S(1)} %copy-done.34), channel_id=1, source_target_pairs={{0,2},{1,3},{2,0},{3,1},{4,6},{5,7},{6,4},{7,5},{8,10},{9,11},{10,... | collective-permute-start | bytes 1179656 | tf_op jit(solution)/shard_map/ppermute | solution.py:768
  479.1 26.1 %collective-permute-start.27 = (f16[4,384,128]{2,1,0:T(8,128)(2,1)S(1)}, f16[4,384,128]{2,1,0:T(8,128)(2,1)S(1)}, u32[]{:S(2)}, u32[]{:S(2)}) collective-permute-start(f16[4,384,128]{2,1,0:T(8,128)(2,1)S(1)} %copy-done.33), channel_id=1, source_target_pairs={{0,3},{1,0},{2,1},{3,2},{4,7},{5,4},{6,5},{7,6},{8,11},{9,8},{10,9... | collective-permute-start | bytes 1179656 | tf_op jit(solution)/shard_map/ppermute | solution.py:768
  481.6 19.3 %copy-start.30 = (f16[4,384,128]{2,1,0:T(8,128)(2,1)S(1)}, f16[4,384,128]{2,1,0:T(8,128)(2,1)}, u32[]{:S(2)}) copy-start(f16[4,384,128]{2,1,0:T(8,128)(2,1)} %multiply_convert_fusion.8) | copy-start | bytes 1179652
  481.6 23.6 %copy-start.10 = (f32[4,384,128]{2,1,0:T(8,128)S(1)}, f32[4,384,128]{2,1,0:T(8,128)}, u32[]{:S(2)}) copy-start(f32[4,384,128]{2,1,0:T(8,128)} %get-tuple-element.97) | copy-start | bytes 2359300
  500.9 25.9 %collective-permute-start.24 = (f16[4,384,128]{2,1,0:T(8,128)(2,1)S(1)}, f16[4,384,128]{2,1,0:T(8,128)(2,1)S(1)}, u32[]{:S(2)}, u32[]{:S(2)}) collective-permute-start(f16[4,384,128]{2,1,0:T(8,128)(2,1)S(1)} %copy-done.30), channel_id=1, source_target_pairs={{0,3},{1,0},{2,1},{3,2},{4,7},{5,4},{6,5},{7,6},{8,11},{9,8},{10,9... | collective-permute-start | bytes 1179656 | tf_op jit(solution)/shard_map/ppermute | solution.py:768
  507.5 19.2 %copy-start.9 = (f32[4,384,128]{2,1,0:T(8,128)S(1)}, f32[4,384,128]{2,1,0:T(8,128)}, u32[]{:S(2)}) copy-start(f32[4,384,128]{2,1,0:T(8,128)} %get-tuple-element.93) | copy-start | bytes 2359300
  (13 other events, 33.5 us)

commit v7 on v6

--- a/solution.py
+++ b/solution.py
@@ -12,6 +12,7 @@
 LANES = 128
 MESH = pl.DeviceIdType.MESH
 CHUNK = 16
+WIDE = 32
 EXACT = lax.Precision.HIGHEST
 R_MAX = 6.0
 W_MAX = 2.0
@@ -144,7 +145,7 @@
     shape = jax.ShapeDtypeStruct((own, sets * tile, cols), jnp.float32)
     out = pl.pallas_call(
         functools.partial(quarter_kernel, nf, parts, sets),
-        out_shape=[shape] * (2 * parts),
+        out_shape=[shape] * parts + [pltpu.HBM(shape.shape, shape.dtype)] * parts,
         grid_spec=pltpu.PrefetchScalarGridSpec(
             num_scalar_prefetch=1,
             grid=(sets,),
@@ -164,7 +165,7 @@
             ]
             + [VMEM((nf, cols, LANES), jnp.float32)] * 3,
         ),
-        compiler_params=pltpu.CompilerParams(vmem_limit_bytes=54 << 20),
+        compiler_params=pltpu.CompilerParams(vmem_limit_bytes=36 << 20),
         cost_estimate=pl.CostEstimate(
             flops=2 * nf * sets * tile * cols * (naux + 32 * nf),
             bytes_accessed=16 * nf * sets * tile * cols,
@@ -385,63 +386,32 @@
     )(me.reshape(1), factors, pair_weight, near, *pieces)
 
 
-def final_kernel(nf, held_outs, me_ref, l_ref, k_ref, wt_ref, coef_ref, p_ref, *rest):
-    parts = len(rest) - held_outs - 6
+def final_kernel(nf, parts, held_outs, me_ref, l_ref, k_ref, wt_ref, coef_ref, p_ref, *rest):
     b_refs, rest = rest[:parts], rest[parts + held_outs :]
     new_ref, table, held, mid, buffer, sems = rest
-    own, tile, cols = new_ref.shape
-    i = pl.program_id(0)
-    count = pl.num_programs(0) - 1
-    stream = Stream(b_refs, buffer, sems, i - 1)
-    turns = cols // CHUNK
-    share = p_ref.shape[0] // turns
-    ahead, now = lax.rem(i, 2), lax.rem(i + 1, 2)
-
-    def multiply(r):
-        rows = part(r, 0, share)
-        held[ahead, rows, :] = lax.dot_general(
-            p_ref[rows, :], l_ref[...], (((1,), (1,)), ((), ())), preferred_element_type=jnp.float32
-        )
-
-    def blend(r):
-        rows = part(r, 0, CHUNK)
-        for k in range(0, tile, LANES):
-            lanes = slice(k, k + LANES)
-            got = mix(table, lanes, own, nf, lambda v: held[now, part(r, v * cols, CHUNK), lanes])
+    own, _, cols = new_ref.shape
+    stream = Stream(b_refs, buffer, sems, pl.program_id(0))
+    stream.ahead()
+    table[...] = dot_exact(coef_ref[...], k_ref[...])
+    for w in range(own):
+        rows = slice(w * nf, (w + 1) * nf)
+        table[rows, :] = table[rows, :] * wt_ref[...]
+    held[...] = rows_times(p_ref, l_ref)
+    here = stream.here()
+
+    @pl.loop(0, table.shape[1] // LANES)
+    def _(block):
+        lanes = part(block, 0, LANES)
+
+        @pl.loop(0, cols // WIDE)
+        def _(i):
+            rows = part(i, 0, WIDE)
+            got = mix(table, lanes, own, nf, lambda v: held[part(i, v * cols, WIDE), lanes])
             for w in range(own):
-                mid[w, rows, lanes] = got[w]
-
-    stream.ahead()
-
-    @pl.when(i > 0)
-    def _():
-        table[...] = dot_exact(coef_ref[...], k_ref[...])
+                mid[w, rows, :] = got[w]
+
         for w in range(own):
-            rows = slice(w * nf, (w + 1) * nf)
-            table[rows, :] = table[rows, :] * wt_ref[...]
-
-    @pl.when(i == 0)
-    def _():
-        pl.loop(0, turns)(multiply)
-
-    @pl.when((i > 0) & (i < count))
-    def _():
-        @pl.loop(0, turns)
-        def _(r):
-            blend(r)
-            multiply(r)
-
-    @pl.when(i == count)
-    def _():
-        pl.loop(0, turns)(blend)
-
-    @pl.when(i > 0)
-    def _():
-        here = stream.here()
-        for w in range(own):
-            for k in range(0, tile, LANES):
-                lanes = slice(k, k + LANES)
-                new_ref[w, lanes, :] = here[w, lanes, :] + mid[w, :, lanes].T
+            new_ref[w, lanes, :] = here[w, lanes, :] + mid[w].T
 
 
 def final(me, low, factors, kernels, weights, coef, gathered, base, outs):
@@ -469,33 +439,30 @@
     size = tile
     sets = span // size
     at = around(parts, quarter // size, low, sets)
-    count = parts * sets
-    ahead = lambda i, m: at(jnp.minimum(i, count - 1), m)
-    now = lambda i, m: at(jnp.maximum(i - 1, 0), m)
     result = pl.pallas_call(
-        functools.partial(final_kernel, nf, len(outs)),
+        functools.partial(final_kernel, nf, parts, len(outs)),
         out_shape=jax.ShapeDtypeStruct((own, pairs, cols), jnp.float32),
         grid_spec=pltpu.PrefetchScalarGridSpec(
             num_scalar_prefetch=1,
-            grid=(count + 1,),
+            grid=(parts * sets,),
             in_specs=[
-                pl.BlockSpec((size, naux), lambda i, m: (ahead(i, m), 0)),
-                pl.BlockSpec((nf, size), lambda i, m: (0, now(i, m))),
-                pl.BlockSpec((nf, size), lambda i, m: (0, now(i, m))),
+                pl.BlockSpec((size, naux), lambda i, m: (at(i, m), 0)),
+                pl.BlockSpec((nf, size), lambda i, m: (0, at(i, m))),
+                pl.BlockSpec((nf, size), lambda i, m: (0, at(i, m))),
                 resident(coef),
                 resident(gathered),
             ]
             + [ANYWHERE] * (parts + len(outs)),
-            out_specs=pl.BlockSpec((own, size, cols), lambda i, m: (0, now(i, m), 0)),
+            out_specs=pl.BlockSpec((own, size, cols), lambda i, m: (0, at(i, m), 0)),
             scratch_shapes=[
                 VMEM((own * nf, size), jnp.float32),
-                VMEM((2, nf * cols, size), jnp.float32),
-                VMEM((own, cols, size), jnp.float32),
+                VMEM((nf * cols, size), jnp.float32),
+                VMEM((own, cols, LANES), jnp.float32),
             ]
             + stream_scratch(own, size, cols),
         ),
         input_output_aliases={6 + parts + n: n for n in range(len(outs))},
-        compiler_params=pltpu.CompilerParams(vmem_limit_bytes=30 << 20),
+        compiler_params=pltpu.CompilerParams(vmem_limit_bytes=26 << 20),
         cost_estimate=pl.CostEstimate(
             flops=2 * nf * parts * span * cols * naux,
             bytes_accessed=8 * own * parts * span * cols,

time: 555 us -> 549 us (0.989)
  the two profiles are of different devices: /device:TPU:0 before, /device:TPU:24 now
where the time goes in v7:
time: 549 us; the launch traced here: 542 us
  Pallas kernels  282 us (51%)
  starting transfers between devices  106 us (19%)
  waiting for transfers between devices  98.3 us (18%)
  other arithmetic  34.9 us (6%)
  matrix products  11.4 us (2%)
  local copies, waits for them, and re-layouts  5.52 us (1%)
    ppermute x33, starting transfers between devices, shift(): lax.ppermute(x, 'freq', [(i, (i + by) % parts) for i in range(parts)])  106 us
    ppermute x33, waiting for transfers between devices, shift(): lax.ppermute(x, 'freq', [(i, (i + by) % parts) for i in range(parts)])  98.3 us
    pallas_call x4, Pallas kernels, gathered_over(): pl.pallas_call(functools.partial(gather_kernel, chips, parts), out_shape=...  62.2 us
    pallas_call x3, Pallas kernels, final(): pl.pallas_call(functools.partial(final_kernel, nf, parts, len(outs)), out...  51.3 us
    pallas_call x3, Pallas kernels, quarter_pass(): pl.pallas_call(functools.partial(quarter_kernel, nf, parts, sets), out_sh...  45.7 us
    pallas_call x2, Pallas kernels, summed(): pl.pallas_call(functools.partial(sum_kernel, chips), out_shape=jax.ShapeD...  39.4 us
    pallas_call x2, Pallas kernels, again(): pl.pallas_call(functools.partial(again_kernel, own), out_shape=jax.ShapeD...  31.7 us
    pallas_call x2, Pallas kernels, summed(): pl.pallas_call(functools.partial(reduce_kernel, chips), out_shape=jax.Sha...  22.5 us
  transfers between devices with their start and end apart: 33, of which 6 were waited for; matrix products, arithmetic and copies ran while one was open for 8% of the time, Pallas kernels for 39%

profile of v7, /device:TPU:24, one launch (start us, length us, event | category | flops | bytes accessed | tf_op | source)
XLA Modules:
  0.0 541.9 jit_solution(3398695921205510165)
XLA Ops:
  0.6 1.0 fusion.3
  2.1 3.4 collective-permute-start
  5.5 10.4 %fusion = f32[4,128,1024]{2,1,0:T(8,128)S(1)} fusion(bf16[4608,1024]{1,0:T(8,128)(2,1)} %l_ref.23, f32[4,4608,128]{2,1,0:T(8,128)} %rest_0_.5), kind=kOutput, calls=%fused_computation | convolution fusion | flops 4834197504 | bytes 20971520 | tf_op jit(solution)/shard_map/pa,fpc->fca/dot_general | solution.py:777
  15.9 20.0 %shard_map.77 = bf16[4,2,64,1024]{3,2,1,0:T(8,128)(2,1)S(1)} custom-call(f32[4,2,64,1024]{3,2,1,0:T(8,128)S(1)} %bitcast.53), custom_call_target="tpu_custom_call" | custom-call | flops 20971520 | bytes 20971520 | tf_op jit(solution)/shard_map/pallas_call | solution.py:687
  36.0 15.7 %shard_map.78 = f32[512,1024]{1,0:T(8,128)S(1)} custom-call(bf16[4608,1024]{1,0:T(8,128)(2,1)} %l_ref.23, f32[4,4608]{1,0:T(4,128)S(1)} %copy-done.10, bf16[512,1024]{1,0:T(8,128)(2,1)S(1)} %bitcast.62, f32[512,1024]{1,0:T(8,128)S(1)} %bitcast.54), custom_call_target="tpu_custom_call" | custom-call | flops 9663676416 | bytes 9437184 | tf_op jit(solution)/shard_map/pallas_call | solution.py:277
  51.7 11.2 %shard_map.79 = bf16[64,1024]{1,0:T(8,128)(2,1)S(1)} custom-call(f32[4,2,64,1024]{3,2,1,0:T(8,128)S(1)} %bitcast.60), custom_call_target="tpu_custom_call" | custom-call | flops 10485760 | bytes 10485760 | tf_op jit(solution)/shard_map/pallas_call | solution.py:678
  63.6 1.5 collective-permute-start.4
  66.1 2.6 multiply_convert_fusion.18
  68.7 4.0 multiply_convert_fusion
  74.2 11.2 %shard_map.80 = (bf16[1,4,2,64,1024]{4,3,2,1,0:T(8,128)(2,1)S(1)}, f32[8,128]{1,0:T(8,128)S(1)}) custom-call(bf16[1,64,1024]{2,1,0:T(8,128)(2,1)S(1)} %bitcast.66), custom_call_target="tpu_custom_call" | custom-call | flops 20971520 | bytes 20971520 | tf_op jit(solution)/shard_map/pallas_call | solution.py:707
  85.4 2.7 collective-permute-start.3
  88.3 0.9 collective-permute-start.10
  89.4 2.1 collective-permute-start.11
  92.1 1.8 collective-permute-start.7
  93.9 1.0 pad_maximum_fusion.x_ref
  94.9 19.1 %shard_map.81 = (bf16[4,4,2,64,1024]{4,3,2,1,0:T(8,128)(2,1)S(1)}, f32[8,128]{1,0:T(8,128)S(1)}) custom-call(bf16[3,64,1024]{2,1,0:T(8,128)(2,1)S(1)} %pad_maximum_fusion.x_ref, bf16[4,2,64,1024]{3,2,1,0:T(8,128)(2,1)S(1)} %bitcast.64), custom_call_target="tpu_custom_call" | custom-call | flops 62914560 | bytes 62914560 | tf_op jit(solution)/shard_map/pallas_call | solution.py:707
  114.1 2.0 copy-done
  117.5 3.1 collective-permute-start.6
  120.6 40.2 %collective-permute-done.10 = f16[4,384,128]{2,1,0:T(8,128)(2,1)S(1)} collective-permute-done((f16[4,384,128]{2,1,0:T(8,128)(2,1)S(1)}, f16[4,384,128]{2,1,0:T(8,128)(2,1)S(1)}, u32[]{:S(2)}, u32[]{:S(2)}) %collective-permute-start.10) | collective-permute-done | bytes 393248 | tf_op jit(solution)/shard_map/ppermute | solution.py:735
  161.0 2.2 copy-done.1
  163.2 15.3 %shard_map.83 = (f32[4,384,128]{2,1,0:T(8,128)S(1)}, f32[4,384,128]{2,1,0:T(8,128)S(1)}, f32[4,384,128]{2,1,0:T(8,128)S(1)}, f32[4,384,128]{2,1,0:T(8,128)S(1)},...) custom-call(s32[1]{0:T(128)} %bitcast.me_ref, ...), custom_call_target="tpu_custom_call" | custom-call | flops 2415919104 | bytes 12582912 | tf_op jit(solution)/shard_map/pallas_call | solution.py:146
  179.8 0.8 multiply_convert_fusion.7
  180.6 0.8 multiply_convert_fusion.6
  181.5 1.3 convert_multiply_fusion.rest_3_
  182.8 1.3 convert_multiply_fusion.1.rest_2_
  184.0 5.6 %collective-permute-done.6 = f16[4,768,128]{2,1,0:T(8,128)(2,1)S(1)} collective-permute-done((f16[4,768,128]{2,1,0:T(8,128)(2,1)}, f16[4,768,128]{2,1,0:T(8,128)(2,1)S(1)}, u32[]{:S(2)}, u32[]{:S(2)}) %collective-permute-start.6) | collective-permute-done | bytes 786464 | tf_op jit(solution)/shard_map/ppermute | solution.py:735
  189.8 15.3 %shard_map.84 = (f32[4,384,128]{2,1,0:T(8,128)S(1)}, f32[4,384,128]{2,1,0:T(8,128)S(1)}, f32[4,384,128]{2,1,0:T(8,128)S(1)}, f32[4,384,128]{2,1,0:T(8,128)S(1)},...) custom-call(s32[1]{0:T(128)} %bitcast.me_ref, ...), custom_call_target="tpu_custom_call" | custom-call | flops 2415919104 | bytes 12582912 | tf_op jit(solution)/shard_map/pallas_call | solution.py:146
  205.0 15.2 %shard_map.82 = (f32[4,384,128]{2,1,0:T(8,128)S(1)}, f32[4,384,128]{2,1,0:T(8,128)S(1)}, f32[4,384,128]{2,1,0:T(8,128)S(1)}, f32[4,384,128]{2,1,0:T(8,128)S(1)},...) custom-call(s32[1]{0:T(128)} %bitcast.me_ref, ...), custom_call_target="tpu_custom_call" | custom-call | flops 2415919104 | bytes 12582912 | tf_op jit(solution)/shard_map/pallas_call | solution.py:146
  220.2 2.0 multiply_convert_fusion.23
  222.5 0.8 multiply_convert_fusion.5
  224.5 25.6 %collective-permute-start.20 = (f16[4,384,128]{2,1,0:T(8,128)(2,1)S(1)}, f16[4,384,128]{2,1,0:T(8,128)(2,1)S(1)}, u32[]{:S(2)}, u32[]{:S(2)}) collective-permute-start(f16[4,384,128]{2,1,0:T(8,128)(2,1)S(1)} %multiply_convert_fusion.9), channel_id=1, source_target_pairs={{0,1},{1,2},{2,3},{3,0},{4,5},{5,6},{6,7},{7,4},{8,9},{9,10},{10,1... | collective-permute-start | bytes 1179656 | tf_op jit(solution)/shard_map/ppermute | solution.py:735
  250.7 0.9 multiply_convert_fusion.22
  251.6 0.8 multiply_convert_fusion.21
  252.5 7.2 %collective-permute-done.20 = f16[4,384,128]{2,1,0:T(8,128)(2,1)S(1)} collective-permute-done((f16[4,384,128]{2,1,0:T(8,128)(2,1)S(1)}, f16[4,384,128]{2,1,0:T(8,128)(2,1)S(1)}, u32[]{:S(2)}, u32[]{:S(2)}) %collective-permute-start.20) | collective-permute-done | bytes 393248 | tf_op jit(solution)/shard_map/ppermute | solution.py:735
  259.7 4.3 collective-permute-start.17
  264.0 20.2 %collective-permute-done.19 = f16[4,384,128]{2,1,0:T(8,128)(2,1)S(1)} collective-permute-done((f16[4,384,128]{2,1,0:T(8,128)(2,1)S(1)}, f16[4,384,128]{2,1,0:T(8,128)(2,1)S(1)}, u32[]{:S(2)}, u32[]{:S(2)}) %collective-permute-start.19) | collective-permute-done | bytes 393248 | tf_op jit(solution)/shard_map/ppermute | solution.py:735
  284.2 18.1 %collective-permute-start.15 = (f16[4,384,128]{2,1,0:T(8,128)(2,1)S(1)}, f16[4,384,128]{2,1,0:T(8,128)(2,1)S(1)}, u32[]{:S(2)}, u32[]{:S(2)}) collective-permute-start(f16[4,384,128]{2,1,0:T(8,128)(2,1)S(1)} %multiply_convert_fusion.14), channel_id=1, source_target_pairs={{0,3},{1,0},{2,1},{3,2},{4,7},{5,4},{6,5},{7,6},{8,11},{9,8},{10,9... | collective-permute-start | bytes 1179656 | tf_op jit(solution)/shard_map/ppermute | solution.py:735
  302.3 2.3 multiply_add_fusion.15
  304.9 4.7 shard_map.85.rest_4_
  309.6 2.7 collective-permute-start.12
  312.3 12.8 %collective-permute-done.16 = f16[4,384,128]{2,1,0:T(8,128)(2,1)S(1)} collective-permute-done((f16[4,384,128]{2,1,0:T(8,128)(2,1)S(1)}, f16[4,384,128]{2,1,0:T(8,128)(2,1)S(1)}, u32[]{:S(2)}, u32[]{:S(2)}) %collective-permute-start.16) | collective-permute-done | bytes 393248 | tf_op jit(solution)/shard_map/ppermute | solution.py:735
  325.1 2.3 multiply_add_fusion.12
  327.4 4.7 shard_map.86.rest_4_
  332.1 2.4 multiply_add_fusion.9
  334.5 5.2 shard_map.87.x_ref
  339.8 19.3 %shard_map.88 = bf16[4,2,64,1024]{3,2,1,0:T(8,128)(2,1)S(1)} custom-call(f32[4,2,64,1024]{3,2,1,0:T(8,128)S(1)} %bitcast.52), custom_call_target="tpu_custom_call" | custom-call | flops 20971520 | bytes 20971520 | tf_op jit(solution)/shard_map/pallas_call | solution.py:687
  359.2 16.0 %shard_map.89 = f32[512,1024]{1,0:T(8,128)S(1)} custom-call(bf16[4608,1024]{1,0:T(8,128)(2,1)} %l_ref.23, f32[4,4608]{1,0:T(4,128)S(1)} %copy-done.10, bf16[512,1024]{1,0:T(8,128)(2,1)S(1)} %bitcast.63, f32[512,1024]{1,0:T(8,128)S(1)} %shard_map.87.x_ref), custom_call_target="tpu_custom_call" | custom-call | flops 9663676416 | bytes 9437184 | tf_op jit(solution)/shard_map/pallas_call | solution.py:277
  375.3 11.3 %shard_map.90 = bf16[64,1024]{1,0:T(8,128)(2,1)S(1)} custom-call(f32[4,2,64,1024]{3,2,1,0:T(8,128)S(1)} %bitcast.61), custom_call_target="tpu_custom_call" | custom-call | flops 10485760 | bytes 10485760 | tf_op jit(solution)/shard_map/pallas_call | solution.py:678
  386.8 3.9 collective-permute-start.21
  391.1 1.5 collective-permute-start.31
  392.7 11.5 %shard_map.91 = (bf16[1,4,2,64,1024]{4,3,2,1,0:T(8,128)(2,1)S(1)}, f32[8,128]{1,0:T(8,128)}) custom-call(bf16[1,64,1024]{2,1,0:T(8,128)(2,1)S(1)} %bitcast.67), custom_call_target="tpu_custom_call" | custom-call | flops 20971520 | bytes 20971520 | tf_op jit(solution)/shard_map/pallas_call | solution.py:707
  404.2 2.9 collective-permute-start.32
  407.2 14.8 %shard_map.92 = f32[4,4608,128]{2,1,0:T(8,128)} custom-call(s32[1]{0:T(128)} %bitcast.me_ref, bf16[4608,1024]{1,0:T(8,128)(2,1)S(1)} %bitcast.45, f32[4,4608]{1,0:T(4,128)S(1)} %copy-done.10, bf16[512,1024]{1,0:T(8,128)(2,1)S(1)} %bitcast.55, f32[4,384,128]{2,1,0:T(8,128)S(1)} %get-tuple-element.139.rest_0_, f32[4,384,128]{2,1,0:T(8,128)S(1)} %get-tuple-element.138.rest_1_, ...), custom_call_target="tpu_custom_call" | custom-call | flops 4831838208 | bytes 18874368 | tf_op jit(solution)/shard_map/pallas_call | solution.py:365
  422.1 1.0 collective-permute-start.25
  423.2 20.4 %shard_map.93 = (bf16[4,4,2,64,1024]{4,3,2,1,0:T(8,128)(2,1)S(1)}, f32[8,128]{1,0:T(8,128)}) custom-call(bf16[3,64,1024]{2,1,0:T(8,128)(2,1)S(1)} %pad_maximum_fusion.1.x_ref, bf16[4,2,64,1024]{3,2,1,0:T(8,128)(2,1)S(1)} %bitcast.56), custom_call_target="tpu_custom_call" | custom-call | flops 62914560 | bytes 62914560 | tf_op jit(solution)/shard_map/pallas_call | solution.py:707
  443.6 3.1 collective-permute-start.29
  446.8 24.1 %collective-permute-start.27 = (f16[4,384,128]{2,1,0:T(8,128)(2,1)S(1)}, f16[4,384,128]{2,1,0:T(8,128)(2,1)S(1)}, u32[]{:S(2)}, u32[]{:S(2)}) collective-permute-start(f16[4,384,128]{2,1,0:T(8,128)(2,1)S(1)} %copy-done.24), channel_id=1, source_target_pairs={{0,3},{1,0},{2,1},{3,2},{4,7},{5,4},{6,5},{7,6},{8,11},{9,8},{10,9... | collective-permute-start | bytes 1179656 | tf_op jit(solution)/shard_map/ppermute | solution.py:735
  470.9 2.3 multiply_add_fusion.6
  473.2 17.1 %shard_map.94.rest_4_ = f32[4,4608,128]{2,1,0:T(8,128)} custom-call(s32[1]{0:T(128)} %bitcast.me_ref, bf16[4608,1024]{1,0:T(8,128)(2,1)S(1)} %bitcast.45, f32[16,4608]{1,0:T(8,128)S(1)} %pad_maximum_fusion.2.k_ref, f32[16,4608]{1,0:T(8,128)S(1)} %pad_maximum_fusion.3.wt_ref, f32[64,16]{1,0:T(8,128)S(1)} %bitcast.68, bf16[2048,1024]{1,0:T(8,128)(2,1)S(1)} %bitcast.49, ...), custom_call_target="tpu_custom_call" | custom-call | flops 6442450944 | bytes 6291456 | tf_op jit(solution)/shard_map/pallas_call | solution.py:442
  490.5 12.3 %collective-permute-done.28 = f16[4,384,128]{2,1,0:T(8,128)(2,1)S(1)} collective-permute-done((f16[4,384,128]{2,1,0:T(8,128)(2,1)S(1)}, f16[4,384,128]{2,1,0:T(8,128)(2,1)S(1)}, u32[]{:S(2)}, u32[]{:S(2)}) %collective-permute-start.28) | collective-permute-done | bytes 393248 | tf_op jit(solution)/shard_map/ppermute | solution.py:735
  502.8 2.3 multiply_add_fusion.3
  505.1 17.1 %shard_map.95.rest_4_ = f32[4,4608,128]{2,1,0:T(8,128)} custom-call(s32[1]{0:T(128)} %bitcast.me_ref, bf16[4608,1024]{1,0:T(8,128)(2,1)S(1)} %bitcast.45, f32[16,4608]{1,0:T(8,128)S(1)} %pad_maximum_fusion.2.k_ref, f32[16,4608]{1,0:T(8,128)S(1)} %pad_maximum_fusion.3.wt_ref, f32[64,16]{1,0:T(8,128)S(1)} %bitcast.69, ...), custom_call_target="tpu_custom_call", output_to_operand_aliasing={{}: (10, {})} | custom-call | flops 6442450944 | bytes 6291456 | tf_op jit(solution)/shard_map/pallas_call | solution.py:442
  522.2 2.3 multiply_add_fusion
  524.5 17.1 %shard_map.96 = f32[4,4608,128]{2,1,0:T(8,128)} custom-call(s32[1]{0:T(128)} %bitcast.me_ref, bf16[4608,1024]{1,0:T(8,128)(2,1)S(1)} %bitcast.45, f32[16,4608]{1,0:T(8,128)S(1)} %pad_maximum_fusion.2.k_ref, f32[16,4608]{1,0:T(8,128)S(1)} %pad_maximum_fusion.3.wt_ref, f32[64,16]{1,0:T(8,128)S(1)} %bitcast.70, ...), custom_call_target="tpu_custom_call", output_to_operand_aliasing={{}: (10, {})} | custom-call | flops 6442450944 | bytes 6291456 | tf_op jit(solution)/shard_map/pallas_call | solution.py:442
  (151 shorter events, 9.6 us)
Async XLA Ops:
  1.6 83.8 %collective-permute-start.2 = (f16[2,4,4608]{2,1,0:T(4,128)(2,1)S(1)}, f16[2,4,4608]{2,1,0:T(4,128)(2,1)S(1)}, u32[]{:S(2)}, u32[]{:S(2)}) collective-permute-start(f16[2,4,4608]{2,1,0:T(4,128)(2,1)S(1)} %fusion.3), channel_id=1, source_target_pairs={{0,3},{1,0},{2,1},{3,2},{4,7},{5,4},{6,5},{7,6},{8,11},{9,8},{10,9... | collective-permute-start | bytes 221192 | tf_op jit(solution)/shard_map/ppermute | solution.py:735
  2.1 86.0 %collective-permute-start.1 = (f16[2,4,4608]{2,1,0:T(4,128)(2,1)S(1)}, f16[2,4,4608]{2,1,0:T(4,128)(2,1)S(1)}, u32[]{:S(2)}, u32[]{:S(2)}) collective-permute-start(f16[2,4,4608]{2,1,0:T(4,128)(2,1)S(1)} %fusion.3), channel_id=1, source_target_pairs={{0,2},{1,3},{2,0},{3,1},{4,6},{5,7},{6,4},{7,5},{8,10},{9,11},{10,... | collective-permute-start | bytes 221192 | tf_op jit(solution)/shard_map/ppermute | solution.py:735
  2.1 86.2 %collective-permute-start = (f16[2,4,4608]{2,1,0:T(4,128)(2,1)S(1)}, f16[2,4,4608]{2,1,0:T(4,128)(2,1)S(1)}, u32[]{:S(2)}, u32[]{:S(2)}) collective-permute-start(f16[2,4,4608]{2,1,0:T(4,128)(2,1)S(1)} %fusion.3), channel_id=1, source_target_pairs={{0,1},{1,2},{2,3},{3,0},{4,5},{5,6},{6,7},{7,4},{8,9},{9,10},{10,1... | collective-permute-start | bytes 221192 | tf_op jit(solution)/shard_map/ppermute | solution.py:735
  15.9 20.1 %copy-start.10 = (f32[4,4608]{1,0:T(4,128)S(1)}, f32[4,4608]{1,0:T(4,128)}, u32[]{:S(2)}) copy-start(f32[4,4608]{1,0:T(4,128)} %wt_ref.5) | copy-start | bytes 221188
  51.7 13.6 %copy-start.30 = (f32[16,16]{1,0:T(8,128)S(1)}, f32[16,16]{1,0:T(8,128)}, u32[]{:S(2)}) copy-start(f32[16,16]{1,0:T(8,128)} %param.10) | copy-start | bytes 3076
  51.7 13.9 %copy-start.31 = (f32[16,16]{1,0:T(8,128)S(1)}, f32[16,16]{1,0:T(8,128)}, u32[]{:S(2)}) copy-start(f32[16,16]{1,0:T(8,128)} %param.11) | copy-start | bytes 3076
  63.0 26.4 %collective-permute-start.5 = (bf16[64,1024]{1,0:T(8,128)(2,1)S(1)}, bf16[64,1024]{1,0:T(8,128)(2,1)}, u32[]{:S(2)}, u32[]{:S(2)}) collective-permute-start(bf16[64,1024]{1,0:T(8,128)(2,1)S(1)} %shard_map.79), channel_id=1, source_target_pairs={{0,3},{1,0},{2,1},{3,2},{4,7},{5,4},{6,5},{7,6},{8,11},{9,8},{10,9... | collective-permute-start | bytes 393224 | tf_op jit(solution)/shard_map/ppermute | solution.py:735
  63.6 27.8 %collective-permute-start.4 = (bf16[64,1024]{1,0:T(8,128)(2,1)S(1)}, bf16[64,1024]{1,0:T(8,128)(2,1)}, u32[]{:S(2)}, u32[]{:S(2)}) collective-permute-start(bf16[64,1024]{1,0:T(8,128)(2,1)S(1)} %shard_map.79), channel_id=1, source_target_pairs={{0,2},{1,3},{2,0},{3,1},{4,6},{5,7},{6,4},{7,5},{8,10},{9,11},{10,... | collective-permute-start | bytes 393224 | tf_op jit(solution)/shard_map/ppermute | solution.py:735
  72.7 16.6 %copy-start.29 = (f32[4,4608]{1,0:T(4,128)S(1)}, f32[4,4608]{1,0:T(4,128)}, u32[]{:S(2)}) copy-start(f32[4,4608]{1,0:T(4,128)} %param.9) | copy-start | bytes 221188
  85.4 6.7 %collective-permute-start.3 = (bf16[64,1024]{1,0:T(8,128)(2,1)S(1)}, bf16[64,1024]{1,0:T(8,128)(2,1)S(1)}, u32[]{:S(2)}, u32[]{:S(2)}) collective-permute-start(bf16[64,1024]{1,0:T(8,128)(2,1)S(1)} %shard_map.79), channel_id=1, source_target_pairs={{0,1},{1,2},{2,3},{3,0},{4,5},{5,6},{6,7},{7,4},{8,9},{9,10},{10,1... | collective-permute-start | bytes 393224 | tf_op jit(solution)/shard_map/ppermute | solution.py:735
  88.1 29.3 %collective-permute-start.9 = (f16[4,384,128]{2,1,0:T(8,128)(2,1)}, f16[4,384,128]{2,1,0:T(8,128)(2,1)S(1)}, u32[]{:S(2)}, u32[]{:S(2)}) collective-permute-start(f16[4,384,128]{2,1,0:T(8,128)(2,1)} %get-tuple-element.67), channel_id=1, source_target_pairs={{0,1},{1,2},{2,3},{3,0},{4,5},{5,6},{6,7},{7,4},{8,9},{9,10},{10,1... | collective-permute-start | bytes 1179656 | tf_op jit(solution)/shard_map/ppermute | solution.py:735
  88.3 72.6 %collective-permute-start.10 = (f16[4,384,128]{2,1,0:T(8,128)(2,1)S(1)}, f16[4,384,128]{2,1,0:T(8,128)(2,1)S(1)}, u32[]{:S(2)}, u32[]{:S(2)}) collective-permute-start(f16[4,384,128]{2,1,0:T(8,128)(2,1)S(1)} %get-tuple-element.68), channel_id=1, source_target_pairs={{0,2},{1,3},{2,0},{3,1},{4,6},{5,7},{6,4},{7,5},{8,10},{9,11},{10,... | collective-permute-start | bytes 1179656 | tf_op jit(solution)/shard_map/ppermute | solution.py:735
  89.4 71.5 %collective-permute-start.11 = (f16[4,384,128]{2,1,0:T(8,128)(2,1)S(1)}, f16[4,384,128]{2,1,0:T(8,128)(2,1)S(1)}, u32[]{:S(2)}, u32[]{:S(2)}) collective-permute-start(f16[4,384,128]{2,1,0:T(8,128)(2,1)S(1)} %get-tuple-element.69), channel_id=1, source_target_pairs={{0,3},{1,0},{2,1},{3,2},{4,7},{5,4},{6,5},{7,6},{8,11},{9,8},{10,9... | collective-permute-start | bytes 1179656 | tf_op jit(solution)/shard_map/ppermute | solution.py:735
  91.5 90.0 %collective-permute-start.8 = (f16[4,768,128]{2,1,0:T(8,128)(2,1)}, f16[4,768,128]{2,1,0:T(8,128)(2,1)}, u32[]{:S(2)}, u32[]{:S(2)}) collective-permute-start(f16[4,768,128]{2,1,0:T(8,128)(2,1)} %get-tuple-element.143), channel_id=1, source_target_pairs={{0,3},{1,0},{2,1},{3,2},{4,7},{5,4},{6,5},{7,6},{8,11},{9,8},{10,9... | collective-permute-start | bytes 2359304 | tf_op jit(solution)/shard_map/ppermute | solution.py:735
  92.1 90.6 %collective-permute-start.7 = (f16[4,768,128]{2,1,0:T(8,128)(2,1)}, f16[4,768,128]{2,1,0:T(8,128)(2,1)}, u32[]{:S(2)}, u32[]{:S(2)}) collective-permute-start(f16[4,768,128]{2,1,0:T(8,128)(2,1)} %get-tuple-element.144), channel_id=1, source_target_pairs={{0,2},{1,3},{2,0},{3,1},{4,6},{5,7},{6,4},{7,5},{8,10},{9,11},{10,... | collective-permute-start | bytes 2359304 | tf_op jit(solution)/shard_map/ppermute | solution.py:735
  117.5 72.1 %collective-permute-start.6 = (f16[4,768,128]{2,1,0:T(8,128)(2,1)}, f16[4,768,128]{2,1,0:T(8,128)(2,1)S(1)}, u32[]{:S(2)}, u32[]{:S(2)}) collective-permute-start(f16[4,768,128]{2,1,0:T(8,128)(2,1)} %get-tuple-element.145), channel_id=1, source_target_pairs={{0,1},{1,2},{2,3},{3,0},{4,5},{5,6},{6,7},{7,4},{8,9},{9,10},{10,1... | collective-permute-start | bytes 2359304 | tf_op jit(solution)/shard_map/ppermute | solution.py:735
  161.0 2.2 copy-start.1
  178.5 2.1 copy-start.19
  178.7 153.4 %collective-permute-start.14 = (f16[4,384,128]{2,1,0:T(8,128)(2,1)S(1)}, f16[4,384,128]{2,1,0:T(8,128)(2,1)S(1)}, u32[]{:S(2)}, u32[]{:S(2)}) collective-permute-start(f16[4,384,128]{2,1,0:T(8,128)(2,1)S(1)} %multiply_convert_fusion.15), channel_id=1, source_target_pairs={{0,1},{1,2},{2,3},{3,0},{4,5},{5,6},{6,7},{7,4},{8,9},{9,10},{10,1... | collective-permute-start | bytes 1179656 | tf_op jit(solution)/shard_map/ppermute | solution.py:735
  178.8 153.3 %collective-permute-start.13 = (f16[4,384,128]{2,1,0:T(8,128)(2,1)S(1)}, f16[4,384,128]{2,1,0:T(8,128)(2,1)S(1)}, u32[]{:S(2)}, u32[]{:S(2)}) collective-permute-start(f16[4,384,128]{2,1,0:T(8,128)(2,1)S(1)} %multiply_convert_fusion.16), channel_id=1, source_target_pairs={{0,2},{1,3},{2,0},{3,1},{4,6},{5,7},{6,4},{7,5},{8,10},{9,11},{10,... | collective-permute-start | bytes 1179656 | tf_op jit(solution)/shard_map/ppermute | solution.py:735
  220.2 2.3 copy-start.18
  223.4 27.3 %copy-start.16 = (f32[4,384,128]{2,1,0:T(8,128)S(1)}, f32[4,384,128]{2,1,0:T(8,128)}, u32[]{:S(2)}) copy-start(f32[4,384,128]{2,1,0:T(8,128)} %get-tuple-element.64) | copy-start | bytes 2359300
  224.2 27.4 %copy-start.15 = (f32[4,384,128]{2,1,0:T(8,128)S(1)}, f32[4,384,128]{2,1,0:T(8,128)}, u32[]{:S(2)}) copy-start(f32[4,384,128]{2,1,0:T(8,128)} %get-tuple-element.65) | copy-start | bytes 2359300
  224.5 35.2 %collective-permute-start.20 = (f16[4,384,128]{2,1,0:T(8,128)(2,1)S(1)}, f16[4,384,128]{2,1,0:T(8,128)(2,1)S(1)}, u32[]{:S(2)}, u32[]{:S(2)}) collective-permute-start(f16[4,384,128]{2,1,0:T(8,128)(2,1)S(1)} %multiply_convert_fusion.9), channel_id=1, source_target_pairs={{0,1},{1,2},{2,3},{3,0},{4,5},{5,6},{6,7},{7,4},{8,9},{9,10},{10,1... | collective-permute-start | bytes 1179656 | tf_op jit(solution)/shard_map/ppermute | solution.py:735
  250.1 34.0 %collective-permute-start.19 = (f16[4,384,128]{2,1,0:T(8,128)(2,1)S(1)}, f16[4,384,128]{2,1,0:T(8,128)(2,1)S(1)}, u32[]{:S(2)}, u32[]{:S(2)}) collective-permute-start(f16[4,384,128]{2,1,0:T(8,128)(2,1)S(1)} %multiply_convert_fusion.10), channel_id=1, source_target_pairs={{0,2},{1,3},{2,0},{3,1},{4,6},{5,7},{6,4},{7,5},{8,10},{9,11},{10,... | collective-permute-start | bytes 1179656 | tf_op jit(solution)/shard_map/ppermute | solution.py:735
  250.1 34.1 %collective-permute-start.18 = (f16[4,384,128]{2,1,0:T(8,128)(2,1)S(1)}, f16[4,384,128]{2,1,0:T(8,128)(2,1)S(1)}, u32[]{:S(2)}, u32[]{:S(2)}) collective-permute-start(f16[4,384,128]{2,1,0:T(8,128)(2,1)S(1)} %multiply_convert_fusion.11), channel_id=1, source_target_pairs={{0,3},{1,0},{2,1},{3,2},{4,7},{5,4},{6,5},{7,6},{8,11},{9,8},{10,9... | collective-permute-start | bytes 1179656 | tf_op jit(solution)/shard_map/ppermute | solution.py:735
  259.7 49.9 %collective-permute-start.17 = (f16[4,384,128]{2,1,0:T(8,128)(2,1)S(1)}, f16[4,384,128]{2,1,0:T(8,128)(2,1)S(1)}, u32[]{:S(2)}, u32[]{:S(2)}) collective-permute-start(f16[4,384,128]{2,1,0:T(8,128)(2,1)S(1)} %multiply_convert_fusion.12), channel_id=1, source_target_pairs={{0,1},{1,2},{2,3},{3,0},{4,5},{5,6},{6,7},{7,4},{8,9},{9,10},{10,1... | collective-permute-start | bytes 1179656 | tf_op jit(solution)/shard_map/ppermute | solution.py:735
  284.2 41.0 %collective-permute-start.16 = (f16[4,384,128]{2,1,0:T(8,128)(2,1)S(1)}, f16[4,384,128]{2,1,0:T(8,128)(2,1)S(1)}, u32[]{:S(2)}, u32[]{:S(2)}) collective-permute-start(f16[4,384,128]{2,1,0:T(8,128)(2,1)S(1)} %multiply_convert_fusion.13), channel_id=1, source_target_pairs={{0,2},{1,3},{2,0},{3,1},{4,6},{5,7},{6,4},{7,5},{8,10},{9,11},{10,... | collective-permute-start | bytes 1179656 | tf_op jit(solution)/shard_map/ppermute | solution.py:735
  284.2 41.0 %collective-permute-start.15 = (f16[4,384,128]{2,1,0:T(8,128)(2,1)S(1)}, f16[4,384,128]{2,1,0:T(8,128)(2,1)S(1)}, u32[]{:S(2)}, u32[]{:S(2)}) collective-permute-start(f16[4,384,128]{2,1,0:T(8,128)(2,1)S(1)} %multiply_convert_fusion.14), channel_id=1, source_target_pairs={{0,3},{1,0},{2,1},{3,2},{4,7},{5,4},{6,5},{7,6},{8,11},{9,8},{10,9... | collective-permute-start | bytes 1179656 | tf_op jit(solution)/shard_map/ppermute | solution.py:735
  309.6 22.5 %collective-permute-start.12 = (f16[4,384,128]{2,1,0:T(8,128)(2,1)S(1)}, f16[4,384,128]{2,1,0:T(8,128)(2,1)S(1)}, u32[]{:S(2)}, u32[]{:S(2)}) collective-permute-start(f16[4,384,128]{2,1,0:T(8,128)(2,1)S(1)} %multiply_convert_fusion.17), channel_id=1, source_target_pairs={{0,3},{1,0},{2,1},{3,2},{4,7},{5,4},{6,5},{7,6},{8,11},{9,8},{10,9... | collective-permute-start | bytes 1179656 | tf_op jit(solution)/shard_map/ppermute | solution.py:735
  334.5 5.3 copy-start.2
  334.5 5.3 copy-start.4
  334.5 5.3 copy-start.6
  334.5 5.3 copy-start.8
  359.2 47.9 %slice-start = ((s8[9437184]{0:T(1024)(128)(4,1)}), s8[4194304]{0:T(1024)(128)(4,1)S(1)}, s32[]{:S(2)}) async-start(s8[9437184]{0:T(1024)(128)(4,1)} %bitcast.44), calls=%async_computation | async-start | bytes 8388608
  359.2 27.4 %copy-start.14 = (f32[4,384,128]{2,1,0:T(8,128)S(1)}, f32[4,384,128]{2,1,0:T(8,128)}, u32[]{:S(2)}) copy-start(f32[4,384,128]{2,1,0:T(8,128)} %get-tuple-element.100) | copy-start | bytes 2359300
  359.2 31.5 %copy-start.26 = (f16[4,384,128]{2,1,0:T(8,128)(2,1)S(1)}, f16[4,384,128]{2,1,0:T(8,128)(2,1)}, u32[]{:S(2)}) copy-start(f16[4,384,128]{2,1,0:T(8,128)(2,1)} %multiply_convert_fusion.23) | copy-start | bytes 1179652
  359.2 32.0 %copy-start.28 = (f16[4,384,128]{2,1,0:T(8,128)(2,1)S(1)}, f16[4,384,128]{2,1,0:T(8,128)(2,1)}, u32[]{:S(2)}) copy-start(f16[4,384,128]{2,1,0:T(8,128)(2,1)} %multiply_convert_fusion.22) | copy-start | bytes 1179652
  359.2 47.9 %slice-start.1 = ((s8[9437184]{0:T(1024)(128)(4,1)}), s8[4194304]{0:T(1024)(128)(4,1)S(1)}, s32[]{:S(2)}) async-start(s8[9437184]{0:T(1024)(128)(4,1)} %bitcast.44), calls=%async_computation.1 | async-start | bytes 8388608
  359.2 47.9 %slice-start.2 = ((s8[9437184]{0:T(1024)(128)(4,1)}), s8[1048576]{0:T(1024)(128)(4,1)S(1)}, s32[]{:S(2)}) async-start(s8[9437184]{0:T(1024)(128)(4,1)} %bitcast.44), calls=%async_computation.2 | async-start | bytes 2097152
  375.2 29.0 %copy-start.27 = (f16[4,384,128]{2,1,0:T(8,128)(2,1)S(1)}, f16[4,384,128]{2,1,0:T(8,128)(2,1)}, u32[]{:S(2)}) copy-start(f16[4,384,128]{2,1,0:T(8,128)(2,1)} %multiply_convert_fusion.21) | copy-start | bytes 1179652
  375.2 31.9 %copy-start.3 = (f32[4,384,128]{2,1,0:T(8,128)S(1)}, f32[4,384,128]{2,1,0:T(8,128)}, u32[]{:S(2)}) copy-start(f32[4,384,128]{2,1,0:T(8,128)} %copy-done.2) | copy-start | bytes 2359300
  375.2 31.9 %copy-start.5 = (f32[4,384,128]{2,1,0:T(8,128)S(1)}, f32[4,384,128]{2,1,0:T(8,128)}, u32[]{:S(2)}) copy-start(f32[4,384,128]{2,1,0:T(8,128)} %copy-done.4) | copy-start | bytes 2359300
  375.2 31.9 %copy-start.7 = (f32[4,384,128]{2,1,0:T(8,128)S(1)}, f32[4,384,128]{2,1,0:T(8,128)}, u32[]{:S(2)}) copy-start(f32[4,384,128]{2,1,0:T(8,128)} %copy-done.6) | copy-start | bytes 2359300
  375.3 31.9 %copy-start.9 = (f32[4,384,128]{2,1,0:T(8,128)S(1)}, f32[4,384,128]{2,1,0:T(8,128)}, u32[]{:S(2)}) copy-start(f32[4,384,128]{2,1,0:T(8,128)} %copy-done.8) | copy-start | bytes 2359300
  386.5 17.6 %collective-permute-start.23 = (bf16[64,1024]{1,0:T(8,128)(2,1)S(1)}, bf16[64,1024]{1,0:T(8,128)(2,1)S(1)}, u32[]{:S(2)}, u32[]{:S(2)}) collective-permute-start(bf16[64,1024]{1,0:T(8,128)(2,1)S(1)} %shard_map.90), channel_id=1, source_target_pairs={{0,3},{1,0},{2,1},{3,2},{4,7},{5,4},{6,5},{7,6},{8,11},{9,8},{10,9... | collective-permute-start | bytes 393224 | tf_op jit(solution)/shard_map/ppermute | solution.py:735
  386.7 35.3 %collective-permute-start.22 = (bf16[64,1024]{1,0:T(8,128)(2,1)S(1)}, bf16[64,1024]{1,0:T(8,128)(2,1)S(1)}, u32[]{:S(2)}, u32[]{:S(2)}) collective-permute-start(bf16[64,1024]{1,0:T(8,128)(2,1)S(1)} %shard_map.90), channel_id=1, source_target_pairs={{0,2},{1,3},{2,0},{3,1},{4,6},{5,7},{6,4},{7,5},{8,10},{9,11},{10,... | collective-permute-start | bytes 393224 | tf_op jit(solution)/shard_map/ppermute | solution.py:735
  386.8 35.3 %collective-permute-start.21 = (bf16[64,1024]{1,0:T(8,128)(2,1)S(1)}, bf16[64,1024]{1,0:T(8,128)(2,1)S(1)}, u32[]{:S(2)}, u32[]{:S(2)}) collective-permute-start(bf16[64,1024]{1,0:T(8,128)(2,1)S(1)} %shard_map.90), channel_id=1, source_target_pairs={{0,1},{1,2},{2,3},{3,0},{4,5},{5,6},{6,7},{7,4},{8,9},{9,10},{10,1... | collective-permute-start | bytes 393224 | tf_op jit(solution)/shard_map/ppermute | solution.py:735
  390.6 53.0 %collective-permute-start.30 = (f16[4,384,128]{2,1,0:T(8,128)(2,1)S(1)}, f16[4,384,128]{2,1,0:T(8,128)(2,1)S(1)}, u32[]{:S(2)}, u32[]{:S(2)}) collective-permute-start(f16[4,384,128]{2,1,0:T(8,128)(2,1)S(1)} %copy-done.26), channel_id=1, source_target_pairs={{0,3},{1,0},{2,1},{3,2},{4,7},{5,4},{6,5},{7,6},{8,11},{9,8},{10,9... | collective-permute-start | bytes 1179656 | tf_op jit(solution)/shard_map/ppermute | solution.py:735
  391.1 55.6 %collective-permute-start.31 = (f16[4,384,128]{2,1,0:T(8,128)(2,1)S(1)}, f16[4,384,128]{2,1,0:T(8,128)(2,1)S(1)}, u32[]{:S(2)}, u32[]{:S(2)}) collective-permute-start(f16[4,384,128]{2,1,0:T(8,128)(2,1)S(1)} %copy-done.28), channel_id=1, source_target_pairs={{0,2},{1,3},{2,0},{3,1},{4,6},{5,7},{6,4},{7,5},{8,10},{9,11},{10,... | collective-permute-start | bytes 1179656 | tf_op jit(solution)/shard_map/ppermute | solution.py:735
  404.2 42.6 %collective-permute-start.32 = (f16[4,384,128]{2,1,0:T(8,128)(2,1)S(1)}, f16[4,384,128]{2,1,0:T(8,128)(2,1)S(1)}, u32[]{:S(2)}, u32[]{:S(2)}) collective-permute-start(f16[4,384,128]{2,1,0:T(8,128)(2,1)S(1)} %copy-done.27), channel_id=1, source_target_pairs={{0,1},{1,2},{2,3},{3,0},{4,5},{5,6},{6,7},{7,4},{8,9},{9,10},{10,1... | collective-permute-start | bytes 1179656 | tf_op jit(solution)/shard_map/ppermute | solution.py:735
  407.1 14.9 %copy-start.23 = (f16[4,384,128]{2,1,0:T(8,128)(2,1)S(1)}, f16[4,384,128]{2,1,0:T(8,128)(2,1)}, u32[]{:S(2)}) copy-start(f16[4,384,128]{2,1,0:T(8,128)(2,1)} %multiply_convert_fusion.6) | copy-start | bytes 1179652
  407.2 14.9 %copy-start.22 = (f16[4,384,128]{2,1,0:T(8,128)(2,1)S(1)}, f16[4,384,128]{2,1,0:T(8,128)(2,1)}, u32[]{:S(2)}) copy-start(f16[4,384,128]{2,1,0:T(8,128)(2,1)} %multiply_convert_fusion.7) | copy-start | bytes 1179652
  422.0 24.8 %copy-start.25 = (f16[4,384,128]{2,1,0:T(8,128)(2,1)S(1)}, f16[4,384,128]{2,1,0:T(8,128)(2,1)}, u32[]{:S(2)}) copy-start(f16[4,384,128]{2,1,0:T(8,128)(2,1)} %multiply_convert_fusion.4) | copy-start | bytes 1179652
  422.0 24.8 %copy-start.24 = (f16[4,384,128]{2,1,0:T(8,128)(2,1)S(1)}, f16[4,384,128]{2,1,0:T(8,128)(2,1)}, u32[]{:S(2)}) copy-start(f16[4,384,128]{2,1,0:T(8,128)(2,1)} %multiply_convert_fusion.5) | copy-start | bytes 1179652
  422.0 48.9 %copy-start.13 = (f32[4,384,128]{2,1,0:T(8,128)S(1)}, f32[4,384,128]{2,1,0:T(8,128)}, u32[]{:S(2)}) copy-start(f32[4,384,128]{2,1,0:T(8,128)} %get-tuple-element.101) | copy-start | bytes 2359300
  422.0 100.2 %collective-permute-start.26 = (f16[4,384,128]{2,1,0:T(8,128)(2,1)S(1)}, f16[4,384,128]{2,1,0:T(8,128)(2,1)S(1)}, u32[]{:S(2)}, u32[]{:S(2)}) collective-permute-start(f16[4,384,128]{2,1,0:T(8,128)(2,1)S(1)} %copy-done.23), channel_id=1, source_target_pairs={{0,1},{1,2},{2,3},{3,0},{4,5},{5,6},{6,7},{7,4},{8,9},{9,10},{10,1... | collective-permute-start | bytes 1179656 | tf_op jit(solution)/shard_map/ppermute | solution.py:735
  422.1 100.1 %collective-permute-start.25 = (f16[4,384,128]{2,1,0:T(8,128)(2,1)S(1)}, f16[4,384,128]{2,1,0:T(8,128)(2,1)S(1)}, u32[]{:S(2)}, u32[]{:S(2)}) collective-permute-start(f16[4,384,128]{2,1,0:T(8,128)(2,1)S(1)} %copy-done.22), channel_id=1, source_target_pairs={{0,2},{1,3},{2,0},{3,1},{4,6},{5,7},{6,4},{7,5},{8,10},{9,11},{10,... | collective-permute-start | bytes 1179656 | tf_op jit(solution)/shard_map/ppermute | solution.py:735
  443.6 46.7 %collective-permute-start.29 = (f16[4,384,128]{2,1,0:T(8,128)(2,1)S(1)}, f16[4,384,128]{2,1,0:T(8,128)(2,1)S(1)}, u32[]{:S(2)}, u32[]{:S(2)}) collective-permute-start(f16[4,384,128]{2,1,0:T(8,128)(2,1)S(1)} %multiply_convert_fusion.3), channel_id=1, source_target_pairs={{0,1},{1,2},{2,3},{3,0},{4,5},{5,6},{6,7},{7,4},{8,9},{9,10},{10,1... | collective-permute-start | bytes 1179656 | tf_op jit(solution)/shard_map/ppermute | solution.py:735
  446.7 56.1 %collective-permute-start.28 = (f16[4,384,128]{2,1,0:T(8,128)(2,1)S(1)}, f16[4,384,128]{2,1,0:T(8,128)(2,1)S(1)}, u32[]{:S(2)}, u32[]{:S(2)}) collective-permute-start(f16[4,384,128]{2,1,0:T(8,128)(2,1)S(1)} %copy-done.25), channel_id=1, source_target_pairs={{0,2},{1,3},{2,0},{3,1},{4,6},{5,7},{6,4},{7,5},{8,10},{9,11},{10,... | collective-permute-start | bytes 1179656 | tf_op jit(solution)/shard_map/ppermute | solution.py:735
  446.8 56.0 %collective-permute-start.27 = (f16[4,384,128]{2,1,0:T(8,128)(2,1)S(1)}, f16[4,384,128]{2,1,0:T(8,128)(2,1)S(1)}, u32[]{:S(2)}, u32[]{:S(2)}) collective-permute-start(f16[4,384,128]{2,1,0:T(8,128)(2,1)S(1)} %copy-done.24), channel_id=1, source_target_pairs={{0,3},{1,0},{2,1},{3,2},{4,7},{5,4},{6,5},{7,6},{8,11},{9,8},{10,9... | collective-permute-start | bytes 1179656 | tf_op jit(solution)/shard_map/ppermute | solution.py:735
  473.2 29.5 %copy-start.12 = (f32[4,384,128]{2,1,0:T(8,128)S(1)}, f32[4,384,128]{2,1,0:T(8,128)}, u32[]{:S(2)}) copy-start(f32[4,384,128]{2,1,0:T(8,128)} %get-tuple-element.97) | copy-start | bytes 2359300
  490.4 31.8 %collective-permute-start.24 = (f16[4,384,128]{2,1,0:T(8,128)(2,1)S(1)}, f16[4,384,128]{2,1,0:T(8,128)(2,1)S(1)}, u32[]{:S(2)}, u32[]{:S(2)}) collective-permute-start(f16[4,384,128]{2,1,0:T(8,128)(2,1)S(1)} %multiply_convert_fusion.8), channel_id=1, source_target_pairs={{0,3},{1,0},{2,1},{3,2},{4,7},{5,4},{6,5},{7,6},{8,11},{9,8},{10,9... | collective-permute-start | bytes 1179656 | tf_op jit(solution)/shard_map/ppermute | solution.py:735
  505.0 17.2 %copy-start.11 = (f32[4,384,128]{2,1,0:T(8,128)S(1)}, f32[4,384,128]{2,1,0:T(8,128)}, u32[]{:S(2)}) copy-start(f32[4,384,128]{2,1,0:T(8,128)} %get-tuple-element.93) | copy-start | bytes 2359300
  (4 other events, 5.7 us)

commit v8 on v7

--- a/solution.py
+++ b/solution.py
@@ -69,8 +69,7 @@
 def quarter_kernel(nf, parts, sets, me_ref, l_ref, k_ref, wt_ref, coef_ref, p_ref, *rest):
     own_ref, rest = rest[0], rest[1:]
     came, rest = rest[: sets * (parts - 1)], rest[sets * (parts - 1) :]
-    u_refs, rest = rest[:parts], rest[parts:]
-    v_refs, (table, held, turned, mid, far) = rest[:parts], rest[parts:]
+    mine_u, far_u, mine_v, far_v, table, held, turned, mid, far = rest
     own = nf // parts
     cols = own_ref.shape[2]
     table[...] = dot_exact(coef_ref[...], k_ref[...])
@@ -107,8 +106,9 @@
                 far[w, rows, :] = got[w]
 
         for w in range(nf):
-            u_refs[w // own][w % own, lanes, :] = mid[w].T
-            v_refs[w // own][w % own, lanes, :] = far[w].T
+            u_ref, v_ref, row = (mine_u, mine_v, w) if w < own else (far_u, far_v, w - own)
+            u_ref[row, lanes, :] = mid[w].T
+            v_ref[row, lanes, :] = far[w].T
 
 
 def quarter_pass(me, low, factors, kernels, weights, coef, gathered, right_side, moved):
@@ -134,18 +134,16 @@
         wide = here + cut(weights, 1)[:, :, None] * wide
         u = jnp.einsum("wvp,vpc->wpc", table, wide, precision=EXACT)
         v = jnp.einsum("wvp,vpc->wpc", table, here + u, precision=EXACT)
-        return (
-            [u[s * own : (s + 1) * own] for s in range(parts)],
-            [v[s * own : (s + 1) * own] for s in range(parts)],
-        )
+        return u[:own], u[own:], v[:own], v[own:]
     steps = quarter // tile
     at = lambda i, m: m[0] * steps + low + i
     here = lambda n: pl.BlockSpec((own, tile, cols), lambda i, m: (0, n, 0))
-    piece = pl.BlockSpec((own, tile, cols), lambda i, m: (0, i, 0))
-    shape = jax.ShapeDtypeStruct((own, sets * tile, cols), jnp.float32)
-    out = pl.pallas_call(
+    outs = [(rows, sets * tile, cols) for rows in (own, nf - own)]
+    pieces = [pl.BlockSpec((x[0], tile, cols), lambda i, m: (0, i, 0)) for x in outs]
+    return pl.pallas_call(
         functools.partial(quarter_kernel, nf, parts, sets),
-        out_shape=[shape] * parts + [pltpu.HBM(shape.shape, shape.dtype)] * parts,
+        out_shape=[jax.ShapeDtypeStruct(x, jnp.float32) for x in outs]
+        + [pltpu.HBM(x, jnp.float32) for x in outs],
         grid_spec=pltpu.PrefetchScalarGridSpec(
             num_scalar_prefetch=1,
             grid=(sets,),
@@ -158,7 +156,7 @@
                 pl.BlockSpec((own, tile, cols), lambda i, m: (0, at(i, m), 0)),
             ]
             + [here(n) for _, n in moved for _ in range(parts - 1)],
-            out_specs=[piece] * (2 * parts),
+            out_specs=pieces * 2,
             scratch_shapes=[
                 VMEM((nf * nf, tile), jnp.float32),
                 VMEM((nf * cols, tile), jnp.float32),
@@ -181,7 +179,6 @@
         right_side,
         *[x for xs, _ in moved for x in xs],
     )
-    return list(out[:parts]), list(out[parts:])
 
 
 def project_kernel(parts, sets, me_ref, l_ref, *rest):
@@ -805,20 +802,25 @@
     u_top = jnp.maximum(1.01 * reach * (R_MAX + W_MAX * L_MAX * height), 1e-30)
     v_top = jnp.maximum(1.01 * reach * (R_MAX + u_top), 1e-30)
 
-    def halved(blocks, top):
-        return [(b * (HALF_TOP / top)).astype(jnp.float16) for b in blocks[1:]]
+    def halved(far, top):
+        blocks = [far[s * own : (s + 1) * own] for s in range(parts - 1)]
+        return [(b * (HALF_TOP / top)).astype(jnp.float16) for b in blocks]
 
     def added(first, rest, top, group):
         rest = [b.astype(jnp.float32) * (top / HALF_TOP) for b in rest]
         return [sliced(right_late, s, *group) + b for s, b in enumerate([first] + rest)]
 
-    placed = []
-    for group, moved in zip(groups, came):
-        moved = [m.astype(jnp.float32) * (1.0 / up) for m in moved]
-        placed += [(moved, k - group[0]) for k in range(*group)]
     us, vs, inward, halves = [], [], [], []
-    for low, high in calls:
-        u, v = quarter_pass(
+    for n, (low, high) in enumerate(calls):
+        at = next(g for g, (first, end) in enumerate(groups) if first <= low < end)
+        moved = came[at]
+        if n:
+            moved, _ = tie((moved, us[-1][1]))
+        start = (low - groups[at][0]) * size
+        moved = [
+            m[:, start : start + size].astype(jnp.float32) * (1.0 / up) for m in moved
+        ]
+        mine_u, far_u, mine_v, far_v = quarter_pass(
             me,
             low,
             factors,
@@ -827,12 +829,12 @@
             coef,
             gathered,
             right_side,
-            placed[low:high],
+            [(moved, 0)],
         )
-        inward.append(passed(halved(u, u_top), True))
-        halves.append(halved(v, v_top))
-        us.append(u)
-        vs.append(v)
+        inward.append(passed(halved(far_u, u_top), True))
+        halves.append(halved(far_v, v_top))
+        us.append((mine_u, far_u))
+        vs.append((mine_v, far_v))
     sources = []
     total = jnp.zeros((own * cols, naux), jnp.float32)
     for n, group in enumerate(calls):
@@ -841,16 +843,13 @@
         sources.append(added(us[n][0], inward[n], u_top, group))
         total = project(me, group[0], factors, sources[n], total)
 
-    out, total = tie((halves[0], total))
-    back = [passed(out, True)]
     near, _, blocks = ladder(total)
-    for n in range(1, len(calls)):
-        back.append(passed(halves[n], True))
+    back = [passed(x, True) for x in halves]
     amplitudes = amplitude(me, factors, pair_weight, near, sources)
     gathered, _ = joined(blocks, near)
     outs = []
     for n, group in enumerate(calls):
-        back[n], outs = tie((back[n], outs))
+        back[n], outs, gathered = tie((back[n], outs, gathered))
         base = added(vs[n][0], back[n], v_top, group)
         outs = final(
             me,

time: 549 us -> 533 us (0.971)
  waiting for transfers between devices: 98.3 us -> 46.1 us
  starting transfers between devices: 106 us -> 148 us
  other arithmetic: 34.9 us -> 27 us
    ppermute x33, waiting for transfers between devices: 98.3 us -> 46.1 us  [shift(): lax.ppermute(x, 'freq', [(i, (i + by) % parts) for i in range(parts)])]
    ppermute x33, starting transfers between devices: 106 us -> 148 us  [shift(): lax.ppermute(x, 'freq', [(i, (i + by) % parts) for i in range(parts)])]
  transfers between devices with their start and end apart: 33 -> 33, of which waited for: 6 -> 4; matrix products, arithmetic and copies ran while one was open for 8% -> 7% of each run, Pallas kernels for 39% -> 51%
where the time goes in v8:
time: 533 us; the launch traced here: 527 us
  Pallas kernels  284 us (53%)
  starting transfers between devices  148 us (28%)
  waiting for transfers between devices  46.1 us (9%)
  other arithmetic  27 us (5%)
  matrix products  11.4 us (2%)
  local copies, waits for them, and re-layouts  7.41 us (1%)
    ppermute x33, starting transfers between devices, shift(): lax.ppermute(x, 'freq', [(i, (i + by) % parts) for i in range(parts)])  148 us
    pallas_call x4, Pallas kernels, gathered_over(): pl.pallas_call(functools.partial(gather_kernel, chips, parts), out_shape=...  62.8 us
    pallas_call x3, Pallas kernels, final(): pl.pallas_call(functools.partial(final_kernel, nf, parts, len(outs)), out...  51.6 us
    pallas_call x3, Pallas kernels, quarter_pass(): pl.pallas_call(functools.partial(quarter_kernel, nf, parts, sets), out_sh...  46.2 us
    ppermute x33, waiting for transfers between devices, shift(): lax.ppermute(x, 'freq', [(i, (i + by) % parts) for i in range(parts)])  46.1 us
    pallas_call x2, Pallas kernels, summed(): pl.pallas_call(functools.partial(sum_kernel, chips), out_shape=jax.ShapeD...  39.4 us
    pallas_call x2, Pallas kernels, again(): pl.pallas_call(functools.partial(again_kernel, own), out_shape=jax.ShapeD...  31.8 us
    pallas_call x2, Pallas kernels, summed(): pl.pallas_call(functools.partial(reduce_kernel, chips), out_shape=jax.Sha...  22.5 us
  transfers between devices with their start and end apart: 33, of which 4 were waited for; matrix products, arithmetic and copies ran while one was open for 7% of the time, Pallas kernels for 51%

profile of v8, /device:TPU:24, one launch (start us, length us, event | category | flops | bytes accessed | tf_op | source)
XLA Modules:
  0.0 526.6 jit_solution(12618217316883303312)
XLA Ops:
  0.6 1.0 fusion.3
  2.1 3.4 collective-permute-start
  5.5 10.4 %fusion = f32[4,128,1024]{2,1,0:T(8,128)S(1)} fusion(bf16[4608,1024]{1,0:T(8,128)(2,1)} %l_ref.23, f32[4,4608,128]{2,1,0:T(8,128)} %rest_0_.5), kind=kOutput, calls=%fused_computation | convolution fusion | flops 4834197504 | bytes 20971520 | tf_op jit(solution)/shard_map/pa,fpc->fca/dot_general | solution.py:774
  15.9 20.1 %shard_map.77 = bf16[4,2,64,1024]{3,2,1,0:T(8,128)(2,1)S(1)} custom-call(f32[4,2,64,1024]{3,2,1,0:T(8,128)S(1)} %bitcast.53), custom_call_target="tpu_custom_call" | custom-call | flops 20971520 | bytes 20971520 | tf_op jit(solution)/shard_map/pallas_call | solution.py:684
  36.0 15.8 %shard_map.78 = f32[512,1024]{1,0:T(8,128)S(1)} custom-call(bf16[4608,1024]{1,0:T(8,128)(2,1)} %l_ref.23, f32[4,4608]{1,0:T(4,128)S(1)} %copy-done.10, bf16[512,1024]{1,0:T(8,128)(2,1)S(1)} %bitcast.62, f32[512,1024]{1,0:T(8,128)S(1)} %bitcast.54), custom_call_target="tpu_custom_call" | custom-call | flops 9663676416 | bytes 9437184 | tf_op jit(solution)/shard_map/pallas_call | solution.py:274
  51.9 11.3 %shard_map.79 = bf16[64,1024]{1,0:T(8,128)(2,1)S(1)} custom-call(f32[4,2,64,1024]{3,2,1,0:T(8,128)S(1)} %bitcast.60), custom_call_target="tpu_custom_call" | custom-call | flops 10485760 | bytes 10485760 | tf_op jit(solution)/shard_map/pallas_call | solution.py:675
  63.2 0.6 collective-permute-start.5
  63.7 1.6 collective-permute-start.4
  66.3 2.8 multiply_convert_fusion.21
  69.0 4.0 multiply_convert_fusion
  73.2 0.6 reduce_max.18
  74.5 11.2 %shard_map.80 = (bf16[1,4,2,64,1024]{4,3,2,1,0:T(8,128)(2,1)S(1)}, f32[8,128]{1,0:T(8,128)S(1)}) custom-call(bf16[1,64,1024]{2,1,0:T(8,128)(2,1)S(1)} %bitcast.66), custom_call_target="tpu_custom_call" | custom-call | flops 20971520 | bytes 20971520 | tf_op jit(solution)/shard_map/pallas_call | solution.py:704
  85.7 2.7 collective-permute-start.3
  88.6 1.0 collective-permute-start.10
  89.7 3.0 collective-permute-start.9
  92.8 0.6 collective-permute-start.6
  93.4 1.5 collective-permute-start.7
  94.9 0.9 pad_maximum_fusion.x_ref
  95.9 19.1 %shard_map.81 = (bf16[4,4,2,64,1024]{4,3,2,1,0:T(8,128)(2,1)S(1)}, f32[8,128]{1,0:T(8,128)S(1)}) custom-call(bf16[3,64,1024]{2,1,0:T(8,128)(2,1)S(1)} %pad_maximum_fusion.x_ref, bf16[4,2,64,1024]{3,2,1,0:T(8,128)(2,1)S(1)} %bitcast.64), custom_call_target="tpu_custom_call" | custom-call | flops 62914560 | bytes 62914560 | tf_op jit(solution)/shard_map/pallas_call | solution.py:704
  115.0 2.0 copy-done
  117.0 0.7 reduce_sum.19
  118.5 33.1 %collective-permute-start.8 = (f16[4,384,128]{2,1,0:T(8,128)(2,1)}, f16[4,384,128]{2,1,0:T(8,128)(2,1)S(1)}, u32[]{:S(2)}, u32[]{:S(2)}) collective-permute-start(f16[4,384,128]{2,1,0:T(8,128)(2,1)} %get-tuple-element.57), channel_id=1, source_target_pairs={{0,3},{1,0},{2,1},{3,2},{4,7},{5,4},{6,5},{7,6},{8,11},{9,8},{10,9... | collective-permute-start | bytes 1179656 | tf_op jit(solution)/shard_map/ppermute | solution.py:732
  151.8 2.2 copy-done.1
  154.0 15.4 %shard_map.82 = (f32[4,384,128]{2,1,0:T(8,128)S(1)}, f32[12,384,128]{2,1,0:T(8,128)S(1)}, f32[4,384,128]{2,1,0:T(8,128)}, f32[12,384,128]{2,1,0:T(8,128)}) custom-call(s32[1]{0:T(128)} %bitcast.me_ref, bf16[4608,1024]{1,0:T(8,128)(2,1)} %l_ref.23, f32[16,4608]{1,0:T(8,128)S(1)} %pad_maximum_fusion.2.k_ref, f32[16,4608]{1,0:T(8,128)S(1)} %pad_maximum_fusion.3.wt_ref, ...), custom_call_target="tpu_custom_call" | custom-call | flops 2415919104 | bytes 12582912 | tf_op jit(solution)/shard_map/pallas_call | solution.py:143
  169.6 1.4 copy-done.13
  171.1 1.1 multiply_convert_fusion.3
  172.2 28.8 %collective-permute-start.29 = (f16[4,384,128]{2,1,0:T(8,128)(2,1)}, f16[4,384,128]{2,1,0:T(8,128)(2,1)S(1)}, u32[]{:S(2)}, u32[]{:S(2)}) collective-permute-start(f16[4,384,128]{2,1,0:T(8,128)(2,1)} %get-tuple-element.132), channel_id=1, source_target_pairs={{0,1},{1,2},{2,3},{3,0},{4,5},{5,6},{6,7},{7,4},{8,9},{9,10},{10,1... | collective-permute-start | bytes 1179656 | tf_op jit(solution)/shard_map/ppermute | solution.py:732
  201.2 15.4 %shard_map.83 = (f32[4,384,128]{2,1,0:T(8,128)S(1)}, f32[12,384,128]{2,1,0:T(8,128)S(1)}, f32[4,384,128]{2,1,0:T(8,128)}, f32[12,384,128]{2,1,0:T(8,128)}) custom-call(s32[1]{0:T(128)} %bitcast.me_ref, bf16[4608,1024]{1,0:T(8,128)(2,1)} %l_ref.23, f32[16,4608]{1,0:T(8,128)S(1)} %pad_maximum_fusion.2.k_ref, f32[16,4608]{1,0:T(8,128)S(1)} %pad_maximum_fusion.3.wt_ref, ...), custom_call_target="tpu_custom_call" | custom-call | flops 2415919104 | bytes 12582912 | tf_op jit(solution)/shard_map/pallas_call | solution.py:143
  217.4 2.6 collective-permute-start.19
  220.0 2.1 collective-permute-start.18
  222.1 1.1 convert_multiply_fusion.2.rest_1_
  223.2 1.1 convert_multiply_fusion.1.rest_2_
  224.3 15.4 %shard_map.84 = (f32[4,384,128]{2,1,0:T(8,128)S(1)}, f32[12,384,128]{2,1,0:T(8,128)S(1)}, f32[4,384,128]{2,1,0:T(8,128)}, f32[12,384,128]{2,1,0:T(8,128)}) custom-call(s32[1]{0:T(128)} %bitcast.me_ref, bf16[4608,1024]{1,0:T(8,128)(2,1)} %l_ref.23, f32[16,4608]{1,0:T(8,128)S(1)} %pad_maximum_fusion.2.k_ref, f32[16,4608]{1,0:T(8,128)S(1)} %pad_maximum_fusion.3.wt_ref, ...), custom_call_target="tpu_custom_call" | custom-call | flops 2415919104 | bytes 12582912 | tf_op jit(solution)/shard_map/pallas_call | solution.py:143
  240.0 1.4 copy-done.12
  241.4 1.2 multiply_convert_fusion.9
  242.6 1.9 collective-permute-start.17
  244.5 16.8 %collective-permute-done.19 = f16[4,384,128]{2,1,0:T(8,128)(2,1)S(1)} collective-permute-done((f16[4,384,128]{2,1,0:T(8,128)(2,1)S(1)}, f16[4,384,128]{2,1,0:T(8,128)(2,1)S(1)}, u32[]{:S(2)}, u32[]{:S(2)}) %collective-permute-start.19) | collective-permute-done | bytes 393248 | tf_op jit(solution)/shard_map/ppermute | solution.py:732
  261.3 17.3 %collective-permute-start.15 = (f16[4,384,128]{2,1,0:T(8,128)(2,1)S(1)}, f16[4,384,128]{2,1,0:T(8,128)(2,1)S(1)}, u32[]{:S(2)}, u32[]{:S(2)}) collective-permute-start(f16[4,384,128]{2,1,0:T(8,128)(2,1)S(1)} %get-tuple-element.146), channel_id=1, source_target_pairs={{0,3},{1,0},{2,1},{3,2},{4,7},{5,4},{6,5},{7,6},{8,11},{9,8},{10,9... | collective-permute-start | bytes 1179656 | tf_op jit(solution)/shard_map/ppermute | solution.py:732
  278.6 2.4 multiply_add_fusion.15
  281.2 4.7 shard_map.85.rest_4_
  286.0 9.0 %collective-permute-done.16 = f16[4,384,128]{2,1,0:T(8,128)(2,1)S(1)} collective-permute-done((f16[4,384,128]{2,1,0:T(8,128)(2,1)S(1)}, f16[4,384,128]{2,1,0:T(8,128)(2,1)S(1)}, u32[]{:S(2)}, u32[]{:S(2)}) %collective-permute-start.16) | collective-permute-done | bytes 393248 | tf_op jit(solution)/shard_map/ppermute | solution.py:732
  295.0 17.3 %collective-permute-start.12 = (f16[4,384,128]{2,1,0:T(8,128)(2,1)S(1)}, f16[4,384,128]{2,1,0:T(8,128)(2,1)S(1)}, u32[]{:S(2)}, u32[]{:S(2)}) collective-permute-start(f16[4,384,128]{2,1,0:T(8,128)(2,1)S(1)} %get-tuple-element.149), channel_id=1, source_target_pairs={{0,3},{1,0},{2,1},{3,2},{4,7},{5,4},{6,5},{7,6},{8,11},{9,8},{10,9... | collective-permute-start | bytes 1179656 | tf_op jit(solution)/shard_map/ppermute | solution.py:732
  312.4 2.4 multiply_add_fusion.12
  314.7 4.7 shard_map.86.rest_4_
  319.4 2.7 collective-permute-start.27
  322.2 13.2 %collective-permute-done.13 = f16[4,384,128]{2,1,0:T(8,128)(2,1)S(1)} collective-permute-done((f16[4,384,128]{2,1,0:T(8,128)(2,1)S(1)}, f16[4,384,128]{2,1,0:T(8,128)(2,1)S(1)}, u32[]{:S(2)}, u32[]{:S(2)}) %collective-permute-start.13) | collective-permute-done | bytes 393248 | tf_op jit(solution)/shard_map/ppermute | solution.py:732
  335.3 2.4 multiply_add_fusion.9
  337.8 5.3 shard_map.87.x_ref
  343.1 19.3 %shard_map.88 = bf16[4,2,64,1024]{3,2,1,0:T(8,128)(2,1)S(1)} custom-call(f32[4,2,64,1024]{3,2,1,0:T(8,128)S(1)} %bitcast.52), custom_call_target="tpu_custom_call" | custom-call | flops 20971520 | bytes 20971520 | tf_op jit(solution)/shard_map/pallas_call | solution.py:684
  362.4 16.0 %shard_map.89 = f32[512,1024]{1,0:T(8,128)S(1)} custom-call(bf16[4608,1024]{1,0:T(8,128)(2,1)} %l_ref.23, f32[4,4608]{1,0:T(4,128)S(1)} %copy-done.10, bf16[512,1024]{1,0:T(8,128)(2,1)S(1)} %bitcast.63, f32[512,1024]{1,0:T(8,128)S(1)} %shard_map.87.x_ref), custom_call_target="tpu_custom_call" | custom-call | flops 9663676416 | bytes 9437184 | tf_op jit(solution)/shard_map/pallas_call | solution.py:274
  378.5 11.3 %shard_map.90 = bf16[64,1024]{1,0:T(8,128)(2,1)S(1)} custom-call(f32[4,2,64,1024]{3,2,1,0:T(8,128)S(1)} %bitcast.61), custom_call_target="tpu_custom_call" | custom-call | flops 10485760 | bytes 10485760 | tf_op jit(solution)/shard_map/pallas_call | solution.py:675
  390.2 12.1 %shard_map.91 = (bf16[1,4,2,64,1024]{4,3,2,1,0:T(8,128)(2,1)S(1)}, f32[8,128]{1,0:T(8,128)}) custom-call(bf16[1,64,1024]{2,1,0:T(8,128)(2,1)S(1)} %bitcast.67), custom_call_target="tpu_custom_call" | custom-call | flops 20971520 | bytes 20971520 | tf_op jit(solution)/shard_map/pallas_call | solution.py:704
  402.3 3.6 collective-permute-start.30
  405.9 14.8 %shard_map.92 = f32[4,4608,128]{2,1,0:T(8,128)} custom-call(s32[1]{0:T(128)} %bitcast.me_ref, bf16[4608,1024]{1,0:T(8,128)(2,1)S(1)} %bitcast.45, f32[4,4608]{1,0:T(4,128)S(1)} %copy-done.10, bf16[512,1024]{1,0:T(8,128)(2,1)S(1)} %bitcast.55, f32[4,384,128]{2,1,0:T(8,128)S(1)} %get-tuple-element.125.rest_0_, f32[4,384,128]{2,1,0:T(8,128)S(1)} %get-tuple-element.124.rest_1_, ...), custom_call_target="tpu_custom_call" | custom-call | flops 4831838208 | bytes 18874368 | tf_op jit(solution)/shard_map/pallas_call | solution.py:362
  421.3 1.3 collective-permute-start.22
  422.7 20.4 %shard_map.93 = (bf16[4,4,2,64,1024]{4,3,2,1,0:T(8,128)(2,1)S(1)}, f32[8,128]{1,0:T(8,128)}) custom-call(bf16[3,64,1024]{2,1,0:T(8,128)(2,1)S(1)} %pad_maximum_fusion.1.x_ref, bf16[4,2,64,1024]{3,2,1,0:T(8,128)(2,1)S(1)} %bitcast.56), custom_call_target="tpu_custom_call" | custom-call | flops 62914560 | bytes 62914560 | tf_op jit(solution)/shard_map/pallas_call | solution.py:704
  443.1 2.1 collective-permute-start.26
  445.2 1.1 collective-permute-start.25
  446.3 2.7 multiply_add_fusion.6
  449.1 17.2 %shard_map.94.rest_4_ = f32[4,4608,128]{2,1,0:T(8,128)} custom-call(s32[1]{0:T(128)} %bitcast.me_ref, bf16[4608,1024]{1,0:T(8,128)(2,1)S(1)} %bitcast.45, f32[16,4608]{1,0:T(8,128)S(1)} %pad_maximum_fusion.2.k_ref, f32[16,4608]{1,0:T(8,128)S(1)} %pad_maximum_fusion.3.wt_ref, f32[64,16]{1,0:T(8,128)S(1)} %bitcast.68, bf16[2048,1024]{1,0:T(8,128)(2,1)S(1)} %bitcast.49, ...), custom_call_target="tpu_custom_call" | custom-call | flops 6442450944 | bytes 6291456 | tf_op jit(solution)/shard_map/pallas_call | solution.py:439
  466.3 17.6 %collective-permute-start.21 = (f16[4,384,128]{2,1,0:T(8,128)(2,1)S(1)}, f16[4,384,128]{2,1,0:T(8,128)(2,1)S(1)}, u32[]{:S(2)}, u32[]{:S(2)}) collective-permute-start(f16[4,384,128]{2,1,0:T(8,128)(2,1)S(1)} %copy-done.17), channel_id=1, source_target_pairs={{0,3},{1,0},{2,1},{3,2},{4,7},{5,4},{6,5},{7,6},{8,11},{9,8},{10,9... | collective-permute-start | bytes 1179656 | tf_op jit(solution)/shard_map/ppermute | solution.py:732
  483.9 7.0 %collective-permute-done.25 = f16[4,384,128]{2,1,0:T(8,128)(2,1)S(1)} collective-permute-done((f16[4,384,128]{2,1,0:T(8,128)(2,1)S(1)}, f16[4,384,128]{2,1,0:T(8,128)(2,1)S(1)}, u32[]{:S(2)}, u32[]{:S(2)}) %collective-permute-start.25) | collective-permute-done | bytes 393248 | tf_op jit(solution)/shard_map/ppermute | solution.py:732
  491.4 17.2 %shard_map.95.rest_4_ = f32[4,4608,128]{2,1,0:T(8,128)} custom-call(s32[1]{0:T(128)} %bitcast.me_ref, bf16[4608,1024]{1,0:T(8,128)(2,1)S(1)} %bitcast.45, f32[16,4608]{1,0:T(8,128)S(1)} %pad_maximum_fusion.2.k_ref, f32[16,4608]{1,0:T(8,128)S(1)} %pad_maximum_fusion.3.wt_ref, f32[64,16]{1,0:T(8,128)S(1)} %bitcast.69, ...), custom_call_target="tpu_custom_call", output_to_operand_aliasing={{}: (10, {})} | custom-call | flops 6442450944 | bytes 6291456 | tf_op jit(solution)/shard_map/pallas_call | solution.py:439
  509.1 17.2 %shard_map.96 = f32[4,4608,128]{2,1,0:T(8,128)} custom-call(s32[1]{0:T(128)} %bitcast.me_ref, bf16[4608,1024]{1,0:T(8,128)(2,1)S(1)} %bitcast.45, f32[16,4608]{1,0:T(8,128)S(1)} %pad_maximum_fusion.2.k_ref, f32[16,4608]{1,0:T(8,128)S(1)} %pad_maximum_fusion.3.wt_ref, f32[64,16]{1,0:T(8,128)S(1)} %bitcast.70, ...), custom_call_target="tpu_custom_call", output_to_operand_aliasing={{}: (10, {})} | custom-call | flops 6442450944 | bytes 6291456 | tf_op jit(solution)/shard_map/pallas_call | solution.py:439
  (131 shorter events, 6.1 us)
Async XLA Ops:
  1.6 84.1 %collective-permute-start.2 = (f16[2,4,4608]{2,1,0:T(4,128)(2,1)S(1)}, f16[2,4,4608]{2,1,0:T(4,128)(2,1)S(1)}, u32[]{:S(2)}, u32[]{:S(2)}) collective-permute-start(f16[2,4,4608]{2,1,0:T(4,128)(2,1)S(1)} %fusion.3), channel_id=1, source_target_pairs={{0,3},{1,0},{2,1},{3,2},{4,7},{5,4},{6,5},{7,6},{8,11},{9,8},{10,9... | collective-permute-start | bytes 221192 | tf_op jit(solution)/shard_map/ppermute | solution.py:732
  2.1 86.3 %collective-permute-start.1 = (f16[2,4,4608]{2,1,0:T(4,128)(2,1)S(1)}, f16[2,4,4608]{2,1,0:T(4,128)(2,1)S(1)}, u32[]{:S(2)}, u32[]{:S(2)}) collective-permute-start(f16[2,4,4608]{2,1,0:T(4,128)(2,1)S(1)} %fusion.3), channel_id=1, source_target_pairs={{0,2},{1,3},{2,0},{3,1},{4,6},{5,7},{6,4},{7,5},{8,10},{9,11},{10,... | collective-permute-start | bytes 221192 | tf_op jit(solution)/shard_map/ppermute | solution.py:732
  2.1 86.5 %collective-permute-start = (f16[2,4,4608]{2,1,0:T(4,128)(2,1)S(1)}, f16[2,4,4608]{2,1,0:T(4,128)(2,1)S(1)}, u32[]{:S(2)}, u32[]{:S(2)}) collective-permute-start(f16[2,4,4608]{2,1,0:T(4,128)(2,1)S(1)} %fusion.3), channel_id=1, source_target_pairs={{0,1},{1,2},{2,3},{3,0},{4,5},{5,6},{6,7},{7,4},{8,9},{9,10},{10,1... | collective-permute-start | bytes 221192 | tf_op jit(solution)/shard_map/ppermute | solution.py:732
  15.9 20.1 %copy-start.10 = (f32[4,4608]{1,0:T(4,128)S(1)}, f32[4,4608]{1,0:T(4,128)}, u32[]{:S(2)}) copy-start(f32[4,4608]{1,0:T(4,128)} %wt_ref.5) | copy-start | bytes 221188
  51.9 13.5 %copy-start.21 = (f32[16,16]{1,0:T(8,128)S(1)}, f32[16,16]{1,0:T(8,128)}, u32[]{:S(2)}) copy-start(f32[16,16]{1,0:T(8,128)} %param.10) | copy-start | bytes 3076
  51.9 13.9 %copy-start.22 = (f32[16,16]{1,0:T(8,128)S(1)}, f32[16,16]{1,0:T(8,128)}, u32[]{:S(2)}) copy-start(f32[16,16]{1,0:T(8,128)} %param.11) | copy-start | bytes 3076
  63.2 26.5 %collective-permute-start.5 = (bf16[64,1024]{1,0:T(8,128)(2,1)S(1)}, bf16[64,1024]{1,0:T(8,128)(2,1)S(1)}, u32[]{:S(2)}, u32[]{:S(2)}) collective-permute-start(bf16[64,1024]{1,0:T(8,128)(2,1)S(1)} %shard_map.79), channel_id=1, source_target_pairs={{0,3},{1,0},{2,1},{3,2},{4,7},{5,4},{6,5},{7,6},{8,11},{9,8},{10,9... | collective-permute-start | bytes 393224 | tf_op jit(solution)/shard_map/ppermute | solution.py:732
  63.7 29.0 %collective-permute-start.4 = (bf16[64,1024]{1,0:T(8,128)(2,1)S(1)}, bf16[64,1024]{1,0:T(8,128)(2,1)}, u32[]{:S(2)}, u32[]{:S(2)}) collective-permute-start(bf16[64,1024]{1,0:T(8,128)(2,1)S(1)} %shard_map.79), channel_id=1, source_target_pairs={{0,2},{1,3},{2,0},{3,1},{4,6},{5,7},{6,4},{7,5},{8,10},{9,11},{10,... | collective-permute-start | bytes 393224 | tf_op jit(solution)/shard_map/ppermute | solution.py:732
  73.0 19.6 %copy-start.20 = (f32[4,4608]{1,0:T(4,128)S(1)}, f32[4,4608]{1,0:T(4,128)}, u32[]{:S(2)}) copy-start(f32[4,4608]{1,0:T(4,128)} %param.9) | copy-start | bytes 221188
  85.7 7.7 %collective-permute-start.3 = (bf16[64,1024]{1,0:T(8,128)(2,1)S(1)}, bf16[64,1024]{1,0:T(8,128)(2,1)S(1)}, u32[]{:S(2)}, u32[]{:S(2)}) collective-permute-start(bf16[64,1024]{1,0:T(8,128)(2,1)S(1)} %shard_map.79), channel_id=1, source_target_pairs={{0,1},{1,2},{2,3},{3,0},{4,5},{5,6},{6,7},{7,4},{8,9},{9,10},{10,1... | collective-permute-start | bytes 393224 | tf_op jit(solution)/shard_map/ppermute | solution.py:732
  88.4 30.0 %collective-permute-start.11 = (f16[4,768,128]{2,1,0:T(8,128)(2,1)}, f16[4,768,128]{2,1,0:T(8,128)(2,1)S(1)}, u32[]{:S(2)}, u32[]{:S(2)}) collective-permute-start(f16[4,768,128]{2,1,0:T(8,128)(2,1)} %get-tuple-element.126), channel_id=1, source_target_pairs={{0,3},{1,0},{2,1},{3,2},{4,7},{5,4},{6,5},{7,6},{8,11},{9,8},{10,9... | collective-permute-start | bytes 2359304 | tf_op jit(solution)/shard_map/ppermute | solution.py:732
  88.6 63.0 %collective-permute-start.10 = (f16[4,768,128]{2,1,0:T(8,128)(2,1)}, f16[4,768,128]{2,1,0:T(8,128)(2,1)S(1)}, u32[]{:S(2)}, u32[]{:S(2)}) collective-permute-start(f16[4,768,128]{2,1,0:T(8,128)(2,1)} %get-tuple-element.127), channel_id=1, source_target_pairs={{0,2},{1,3},{2,0},{3,1},{4,6},{5,7},{6,4},{7,5},{8,10},{9,11},{10,... | collective-permute-start | bytes 2359304 | tf_op jit(solution)/shard_map/ppermute | solution.py:732
  89.7 62.0 %collective-permute-start.9 = (f16[4,768,128]{2,1,0:T(8,128)(2,1)}, f16[4,768,128]{2,1,0:T(8,128)(2,1)S(1)}, u32[]{:S(2)}, u32[]{:S(2)}) collective-permute-start(f16[4,768,128]{2,1,0:T(8,128)(2,1)} %get-tuple-element.128), channel_id=1, source_target_pairs={{0,1},{1,2},{2,3},{3,0},{4,5},{5,6},{6,7},{7,4},{8,9},{9,10},{10,1... | collective-permute-start | bytes 2359304 | tf_op jit(solution)/shard_map/ppermute | solution.py:732
  92.8 124.2 %collective-permute-start.6 = (f16[4,384,128]{2,1,0:T(8,128)(2,1)}, f16[4,384,128]{2,1,0:T(8,128)(2,1)}, u32[]{:S(2)}, u32[]{:S(2)}) collective-permute-start(f16[4,384,128]{2,1,0:T(8,128)(2,1)} %get-tuple-element.55), channel_id=1, source_target_pairs={{0,1},{1,2},{2,3},{3,0},{4,5},{5,6},{6,7},{7,4},{8,9},{9,10},{10,1... | collective-permute-start | bytes 1179656 | tf_op jit(solution)/shard_map/ppermute | solution.py:732
  93.4 124.0 %collective-permute-start.7 = (f16[4,384,128]{2,1,0:T(8,128)(2,1)}, f16[4,384,128]{2,1,0:T(8,128)(2,1)}, u32[]{:S(2)}, u32[]{:S(2)}) collective-permute-start(f16[4,384,128]{2,1,0:T(8,128)(2,1)} %get-tuple-element.56), channel_id=1, source_target_pairs={{0,2},{1,3},{2,0},{3,1},{4,6},{5,7},{6,4},{7,5},{8,10},{9,11},{10,... | collective-permute-start | bytes 1179656 | tf_op jit(solution)/shard_map/ppermute | solution.py:732
  115.0 2.0 copy-start
  118.5 101.6 %collective-permute-start.8 = (f16[4,384,128]{2,1,0:T(8,128)(2,1)}, f16[4,384,128]{2,1,0:T(8,128)(2,1)S(1)}, u32[]{:S(2)}, u32[]{:S(2)}) collective-permute-start(f16[4,384,128]{2,1,0:T(8,128)(2,1)} %get-tuple-element.57), channel_id=1, source_target_pairs={{0,3},{1,0},{2,1},{3,2},{4,7},{5,4},{6,5},{7,6},{8,11},{9,8},{10,9... | collective-permute-start | bytes 1179656 | tf_op jit(solution)/shard_map/ppermute | solution.py:732
  151.8 2.2 copy-start.1
  169.4 1.7 copy-start.13
  172.2 270.9 %collective-permute-start.29 = (f16[4,384,128]{2,1,0:T(8,128)(2,1)}, f16[4,384,128]{2,1,0:T(8,128)(2,1)S(1)}, u32[]{:S(2)}, u32[]{:S(2)}) collective-permute-start(f16[4,384,128]{2,1,0:T(8,128)(2,1)} %get-tuple-element.132), channel_id=1, source_target_pairs={{0,1},{1,2},{2,3},{3,0},{4,5},{5,6},{6,7},{7,4},{8,9},{9,10},{10,1... | collective-permute-start | bytes 1179656 | tf_op jit(solution)/shard_map/ppermute | solution.py:732
  200.9 244.3 %collective-permute-start.28 = (f16[4,384,128]{2,1,0:T(8,128)(2,1)}, f16[4,384,128]{2,1,0:T(8,128)(2,1)}, u32[]{:S(2)}, u32[]{:S(2)}) collective-permute-start(f16[4,384,128]{2,1,0:T(8,128)(2,1)} %get-tuple-element.133), channel_id=1, source_target_pairs={{0,2},{1,3},{2,0},{3,1},{4,6},{5,7},{6,4},{7,5},{8,10},{9,11},{10,... | collective-permute-start | bytes 1179656 | tf_op jit(solution)/shard_map/ppermute | solution.py:732
  216.9 25.6 %collective-permute-start.20 = (f16[4,384,128]{2,1,0:T(8,128)(2,1)S(1)}, f16[4,384,128]{2,1,0:T(8,128)(2,1)S(1)}, u32[]{:S(2)}, u32[]{:S(2)}) collective-permute-start(f16[4,384,128]{2,1,0:T(8,128)(2,1)S(1)} %get-tuple-element.141), channel_id=1, source_target_pairs={{0,1},{1,2},{2,3},{3,0},{4,5},{5,6},{6,7},{7,4},{8,9},{9,10},{10,1... | collective-permute-start | bytes 1179656 | tf_op jit(solution)/shard_map/ppermute | solution.py:732
  217.4 43.9 %collective-permute-start.19 = (f16[4,384,128]{2,1,0:T(8,128)(2,1)S(1)}, f16[4,384,128]{2,1,0:T(8,128)(2,1)S(1)}, u32[]{:S(2)}, u32[]{:S(2)}) collective-permute-start(f16[4,384,128]{2,1,0:T(8,128)(2,1)S(1)} %get-tuple-element.142), channel_id=1, source_target_pairs={{0,2},{1,3},{2,0},{3,1},{4,6},{5,7},{6,4},{7,5},{8,10},{9,11},{10,... | collective-permute-start | bytes 1179656 | tf_op jit(solution)/shard_map/ppermute | solution.py:732
  220.0 41.3 %collective-permute-start.18 = (f16[4,384,128]{2,1,0:T(8,128)(2,1)S(1)}, f16[4,384,128]{2,1,0:T(8,128)(2,1)S(1)}, u32[]{:S(2)}, u32[]{:S(2)}) collective-permute-start(f16[4,384,128]{2,1,0:T(8,128)(2,1)S(1)} %get-tuple-element.143), channel_id=1, source_target_pairs={{0,3},{1,0},{2,1},{3,2},{4,7},{5,4},{6,5},{7,6},{8,11},{9,8},{10,9... | collective-permute-start | bytes 1179656 | tf_op jit(solution)/shard_map/ppermute | solution.py:732
  239.7 1.7 copy-start.12
  242.6 43.4 %collective-permute-start.17 = (f16[4,384,128]{2,1,0:T(8,128)(2,1)S(1)}, f16[4,384,128]{2,1,0:T(8,128)(2,1)S(1)}, u32[]{:S(2)}, u32[]{:S(2)}) collective-permute-start(f16[4,384,128]{2,1,0:T(8,128)(2,1)S(1)} %get-tuple-element.144), channel_id=1, source_target_pairs={{0,1},{1,2},{2,3},{3,0},{4,5},{5,6},{6,7},{7,4},{8,9},{9,10},{10,1... | collective-permute-start | bytes 1179656 | tf_op jit(solution)/shard_map/ppermute | solution.py:732
  261.3 33.7 %collective-permute-start.16 = (f16[4,384,128]{2,1,0:T(8,128)(2,1)S(1)}, f16[4,384,128]{2,1,0:T(8,128)(2,1)S(1)}, u32[]{:S(2)}, u32[]{:S(2)}) collective-permute-start(f16[4,384,128]{2,1,0:T(8,128)(2,1)S(1)} %get-tuple-element.145), channel_id=1, source_target_pairs={{0,2},{1,3},{2,0},{3,1},{4,6},{5,7},{6,4},{7,5},{8,10},{9,11},{10,... | collective-permute-start | bytes 1179656 | tf_op jit(solution)/shard_map/ppermute | solution.py:732
  261.3 33.7 %collective-permute-start.15 = (f16[4,384,128]{2,1,0:T(8,128)(2,1)S(1)}, f16[4,384,128]{2,1,0:T(8,128)(2,1)S(1)}, u32[]{:S(2)}, u32[]{:S(2)}) collective-permute-start(f16[4,384,128]{2,1,0:T(8,128)(2,1)S(1)} %get-tuple-element.146), channel_id=1, source_target_pairs={{0,3},{1,0},{2,1},{3,2},{4,7},{5,4},{6,5},{7,6},{8,11},{9,8},{10,9... | collective-permute-start | bytes 1179656 | tf_op jit(solution)/shard_map/ppermute | solution.py:732
  285.9 33.5 %collective-permute-start.14 = (f16[4,384,128]{2,1,0:T(8,128)(2,1)S(1)}, f16[4,384,128]{2,1,0:T(8,128)(2,1)S(1)}, u32[]{:S(2)}, u32[]{:S(2)}) collective-permute-start(f16[4,384,128]{2,1,0:T(8,128)(2,1)S(1)} %get-tuple-element.147), channel_id=1, source_target_pairs={{0,1},{1,2},{2,3},{3,0},{4,5},{5,6},{6,7},{7,4},{8,9},{9,10},{10,1... | collective-permute-start | bytes 1179656 | tf_op jit(solution)/shard_map/ppermute | solution.py:732
  295.0 40.3 %collective-permute-start.13 = (f16[4,384,128]{2,1,0:T(8,128)(2,1)S(1)}, f16[4,384,128]{2,1,0:T(8,128)(2,1)S(1)}, u32[]{:S(2)}, u32[]{:S(2)}) collective-permute-start(f16[4,384,128]{2,1,0:T(8,128)(2,1)S(1)} %get-tuple-element.148), channel_id=1, source_target_pairs={{0,2},{1,3},{2,0},{3,1},{4,6},{5,7},{6,4},{7,5},{8,10},{9,11},{10,... | collective-permute-start | bytes 1179656 | tf_op jit(solution)/shard_map/ppermute | solution.py:732
  295.0 40.3 %collective-permute-start.12 = (f16[4,384,128]{2,1,0:T(8,128)(2,1)S(1)}, f16[4,384,128]{2,1,0:T(8,128)(2,1)S(1)}, u32[]{:S(2)}, u32[]{:S(2)}) collective-permute-start(f16[4,384,128]{2,1,0:T(8,128)(2,1)S(1)} %get-tuple-element.149), channel_id=1, source_target_pairs={{0,3},{1,0},{2,1},{3,2},{4,7},{5,4},{6,5},{7,6},{8,11},{9,8},{10,9... | collective-permute-start | bytes 1179656 | tf_op jit(solution)/shard_map/ppermute | solution.py:732
  319.4 126.9 %collective-permute-start.27 = (f16[4,384,128]{2,1,0:T(8,128)(2,1)}, f16[4,384,128]{2,1,0:T(8,128)(2,1)}, u32[]{:S(2)}, u32[]{:S(2)}) collective-permute-start(f16[4,384,128]{2,1,0:T(8,128)(2,1)} %get-tuple-element.134), channel_id=1, source_target_pairs={{0,3},{1,0},{2,1},{3,2},{4,7},{5,4},{6,5},{7,6},{8,11},{9,8},{10,9... | collective-permute-start | bytes 1179656 | tf_op jit(solution)/shard_map/ppermute | solution.py:732
  337.7 5.3 %copy-start.2 = (f32[4,384,128]{2,1,0:T(8,128)}, f32[4,384,128]{2,1,0:T(8,128)S(1)}, u32[]{:S(2)}) copy-start(f32[4,384,128]{2,1,0:T(8,128)S(1)} %get-tuple-element.114.rest_3_.rest_11_) | copy-start | bytes 2359300
  337.7 5.3 %copy-start.4 = (f32[4,384,128]{2,1,0:T(8,128)}, f32[4,384,128]{2,1,0:T(8,128)S(1)}, u32[]{:S(2)}) copy-start(f32[4,384,128]{2,1,0:T(8,128)S(1)} %get-tuple-element.115.rest_2_.rest_10_) | copy-start | bytes 2359300
  337.7 5.3 %copy-start.6 = (f32[4,384,128]{2,1,0:T(8,128)}, f32[4,384,128]{2,1,0:T(8,128)S(1)}, u32[]{:S(2)}) copy-start(f32[4,384,128]{2,1,0:T(8,128)S(1)} %get-tuple-element.116.rest_1_.rest_9_) | copy-start | bytes 2359300
  337.7 5.3 %copy-start.8 = (f32[4,384,128]{2,1,0:T(8,128)}, f32[4,384,128]{2,1,0:T(8,128)S(1)}, u32[]{:S(2)}) copy-start(f32[4,384,128]{2,1,0:T(8,128)S(1)} %get-tuple-element.117.rest_0_.rest_8_) | copy-start | bytes 2359300
  362.4 43.5 %slice-start = ((s8[9437184]{0:T(1024)(128)(4,1)}), s8[4194304]{0:T(1024)(128)(4,1)S(1)}, s32[]{:S(2)}) async-start(s8[9437184]{0:T(1024)(128)(4,1)} %bitcast.44), calls=%async_computation | async-start | bytes 8388608
  362.4 27.4 %copy-start.11 = (f32[12,384,128]{2,1,0:T(8,128)S(1)}, f32[12,384,128]{2,1,0:T(8,128)}, u32[]{:S(2)}) copy-start(f32[12,384,128]{2,1,0:T(8,128)} %get-tuple-element.82) | copy-start | bytes 7077892
  362.4 43.5 %slice-start.1 = ((s8[9437184]{0:T(1024)(128)(4,1)}), s8[4194304]{0:T(1024)(128)(4,1)S(1)}, s32[]{:S(2)}) async-start(s8[9437184]{0:T(1024)(128)(4,1)} %bitcast.44), calls=%async_computation.1 | async-start | bytes 8388608
  362.4 43.5 %slice-start.2 = ((s8[9437184]{0:T(1024)(128)(4,1)}), s8[1048576]{0:T(1024)(128)(4,1)S(1)}, s32[]{:S(2)}) async-start(s8[9437184]{0:T(1024)(128)(4,1)} %bitcast.44), calls=%async_computation.2 | async-start | bytes 2097152
  389.7 16.2 %copy-start.3 = (f32[4,384,128]{2,1,0:T(8,128)S(1)}, f32[4,384,128]{2,1,0:T(8,128)}, u32[]{:S(2)}) copy-start(f32[4,384,128]{2,1,0:T(8,128)} %copy-done.2) | copy-start | bytes 2359300
  389.7 16.1 %copy-start.5 = (f32[4,384,128]{2,1,0:T(8,128)S(1)}, f32[4,384,128]{2,1,0:T(8,128)}, u32[]{:S(2)}) copy-start(f32[4,384,128]{2,1,0:T(8,128)} %copy-done.4) | copy-start | bytes 2359300
  389.8 16.1 %copy-start.7 = (f32[4,384,128]{2,1,0:T(8,128)S(1)}, f32[4,384,128]{2,1,0:T(8,128)}, u32[]{:S(2)}) copy-start(f32[4,384,128]{2,1,0:T(8,128)} %copy-done.6) | copy-start | bytes 2359300
  389.8 16.1 %copy-start.9 = (f32[4,384,128]{2,1,0:T(8,128)S(1)}, f32[4,384,128]{2,1,0:T(8,128)}, u32[]{:S(2)}) copy-start(f32[4,384,128]{2,1,0:T(8,128)} %copy-done.8) | copy-start | bytes 2359300
  389.8 12.5 %collective-permute-start.32 = (bf16[64,1024]{1,0:T(8,128)(2,1)S(1)}, bf16[64,1024]{1,0:T(8,128)(2,1)S(1)}, u32[]{:S(2)}, u32[]{:S(2)}) collective-permute-start(bf16[64,1024]{1,0:T(8,128)(2,1)S(1)} %shard_map.90), channel_id=1, source_target_pairs={{0,3},{1,0},{2,1},{3,2},{4,7},{5,4},{6,5},{7,6},{8,11},{9,8},{10,9... | collective-permute-start | bytes 393224 | tf_op jit(solution)/shard_map/ppermute | solution.py:732
  390.1 30.6 %collective-permute-start.31 = (bf16[64,1024]{1,0:T(8,128)(2,1)S(1)}, bf16[64,1024]{1,0:T(8,128)(2,1)S(1)}, u32[]{:S(2)}, u32[]{:S(2)}) collective-permute-start(bf16[64,1024]{1,0:T(8,128)(2,1)S(1)} %shard_map.90), channel_id=1, source_target_pairs={{0,2},{1,3},{2,0},{3,1},{4,6},{5,7},{6,4},{7,5},{8,10},{9,11},{10,... | collective-permute-start | bytes 393224 | tf_op jit(solution)/shard_map/ppermute | solution.py:732
  402.3 19.0 %collective-permute-start.30 = (bf16[64,1024]{1,0:T(8,128)(2,1)S(1)}, bf16[64,1024]{1,0:T(8,128)(2,1)S(1)}, u32[]{:S(2)}, u32[]{:S(2)}) collective-permute-start(bf16[64,1024]{1,0:T(8,128)(2,1)S(1)} %shard_map.90), channel_id=1, source_target_pairs={{0,1},{1,2},{2,3},{3,0},{4,5},{5,6},{6,7},{7,4},{8,9},{9,10},{10,1... | collective-permute-start | bytes 393224 | tf_op jit(solution)/shard_map/ppermute | solution.py:732
  405.9 14.8 %copy-start.19 = (f16[4,384,128]{2,1,0:T(8,128)(2,1)S(1)}, f16[4,384,128]{2,1,0:T(8,128)(2,1)}, u32[]{:S(2)}) copy-start(f16[4,384,128]{2,1,0:T(8,128)(2,1)} %get-tuple-element.138) | copy-start | bytes 1179652
  405.9 15.4 %copy-start.18 = (f16[4,384,128]{2,1,0:T(8,128)(2,1)S(1)}, f16[4,384,128]{2,1,0:T(8,128)(2,1)}, u32[]{:S(2)}) copy-start(f16[4,384,128]{2,1,0:T(8,128)(2,1)} %get-tuple-element.139) | copy-start | bytes 1179652
  420.7 25.6 %copy-start.15 = (f32[4,384,128]{2,1,0:T(8,128)S(1)}, f32[4,384,128]{2,1,0:T(8,128)}, u32[]{:S(2)}) copy-start(f32[4,384,128]{2,1,0:T(8,128)} %get-tuple-element.86) | copy-start | bytes 2359300
  420.8 87.9 %collective-permute-start.23 = (f16[4,384,128]{2,1,0:T(8,128)(2,1)S(1)}, f16[4,384,128]{2,1,0:T(8,128)(2,1)S(1)}, u32[]{:S(2)}, u32[]{:S(2)}) collective-permute-start(f16[4,384,128]{2,1,0:T(8,128)(2,1)S(1)} %copy-done.19), channel_id=1, source_target_pairs={{0,1},{1,2},{2,3},{3,0},{4,5},{5,6},{6,7},{7,4},{8,9},{9,10},{10,1... | collective-permute-start | bytes 1179656 | tf_op jit(solution)/shard_map/ppermute | solution.py:732
  421.3 87.3 %collective-permute-start.22 = (f16[4,384,128]{2,1,0:T(8,128)(2,1)S(1)}, f16[4,384,128]{2,1,0:T(8,128)(2,1)S(1)}, u32[]{:S(2)}, u32[]{:S(2)}) collective-permute-start(f16[4,384,128]{2,1,0:T(8,128)(2,1)S(1)} %copy-done.18), channel_id=1, source_target_pairs={{0,2},{1,3},{2,0},{3,1},{4,6},{5,7},{6,4},{7,5},{8,10},{9,11},{10,... | collective-permute-start | bytes 1179656 | tf_op jit(solution)/shard_map/ppermute | solution.py:732
  443.1 23.2 %collective-permute-start.26 = (f16[4,384,128]{2,1,0:T(8,128)(2,1)S(1)}, f16[4,384,128]{2,1,0:T(8,128)(2,1)S(1)}, u32[]{:S(2)}, u32[]{:S(2)}) collective-permute-start(f16[4,384,128]{2,1,0:T(8,128)(2,1)S(1)} %get-tuple-element.135), channel_id=1, source_target_pairs={{0,1},{1,2},{2,3},{3,0},{4,5},{5,6},{6,7},{7,4},{8,9},{9,10},{10,1... | collective-permute-start | bytes 1179656 | tf_op jit(solution)/shard_map/ppermute | solution.py:732
  445.2 45.7 %collective-permute-start.25 = (f16[4,384,128]{2,1,0:T(8,128)(2,1)S(1)}, f16[4,384,128]{2,1,0:T(8,128)(2,1)S(1)}, u32[]{:S(2)}, u32[]{:S(2)}) collective-permute-start(f16[4,384,128]{2,1,0:T(8,128)(2,1)S(1)} %get-tuple-element.136), channel_id=1, source_target_pairs={{0,2},{1,3},{2,0},{3,1},{4,6},{5,7},{6,4},{7,5},{8,10},{9,11},{10,... | collective-permute-start | bytes 1179656 | tf_op jit(solution)/shard_map/ppermute | solution.py:732
  446.3 44.7 %collective-permute-start.24 = (f16[4,384,128]{2,1,0:T(8,128)(2,1)S(1)}, f16[4,384,128]{2,1,0:T(8,128)(2,1)S(1)}, u32[]{:S(2)}, u32[]{:S(2)}) collective-permute-start(f16[4,384,128]{2,1,0:T(8,128)(2,1)S(1)} %get-tuple-element.137), channel_id=1, source_target_pairs={{0,3},{1,0},{2,1},{3,2},{4,7},{5,4},{6,5},{7,6},{8,11},{9,8},{10,9... | collective-permute-start | bytes 1179656 | tf_op jit(solution)/shard_map/ppermute | solution.py:732
  446.3 44.6 %slice-start.3 = ((s8[9437184]{0:T(1024)(128)(4,1)}), s8[4194304]{0:T(1024)(128)(4,1)S(1)}, s32[]{:S(2)}) async-start(s8[9437184]{0:T(1024)(128)(4,1)} %bitcast.71), calls=%async_computation.3 | async-start | bytes 8388608
  449.1 17.3 %copy-start.17 = (f16[4,384,128]{2,1,0:T(8,128)(2,1)S(1)}, f16[4,384,128]{2,1,0:T(8,128)(2,1)}, u32[]{:S(2)}) copy-start(f16[4,384,128]{2,1,0:T(8,128)(2,1)} %get-tuple-element.140) | copy-start | bytes 1179652
  449.1 41.9 %slice-start.4 = ((s8[9437184]{0:T(1024)(128)(4,1)}), s8[4194304]{0:T(1024)(128)(4,1)S(1)}, s32[]{:S(2)}) async-start(s8[9437184]{0:T(1024)(128)(4,1)} %bitcast.71), calls=%async_computation.4 | async-start | bytes 8388608
  449.1 41.9 %slice-start.5 = ((s8[9437184]{0:T(1024)(128)(4,1)}), s8[1048576]{0:T(1024)(128)(4,1)S(1)}, s32[]{:S(2)}) async-start(s8[9437184]{0:T(1024)(128)(4,1)} %bitcast.71), calls=%async_computation.5 | async-start | bytes 2097152
  449.1 41.9 %copy-start.14 = (f32[4,384,128]{2,1,0:T(8,128)S(1)}, f32[4,384,128]{2,1,0:T(8,128)}, u32[]{:S(2)}) copy-start(f32[4,384,128]{2,1,0:T(8,128)} %get-tuple-element.91) | copy-start | bytes 2359300
  466.3 42.3 %collective-permute-start.21 = (f16[4,384,128]{2,1,0:T(8,128)(2,1)S(1)}, f16[4,384,128]{2,1,0:T(8,128)(2,1)S(1)}, u32[]{:S(2)}, u32[]{:S(2)}) collective-permute-start(f16[4,384,128]{2,1,0:T(8,128)(2,1)S(1)} %copy-done.17), channel_id=1, source_target_pairs={{0,3},{1,0},{2,1},{3,2},{4,7},{5,4},{6,5},{7,6},{8,11},{9,8},{10,9... | collective-permute-start | bytes 1179656 | tf_op jit(solution)/shard_map/ppermute | solution.py:732
  491.4 17.3 %copy-start.16 = (f32[4,384,128]{2,1,0:T(8,128)S(1)}, f32[4,384,128]{2,1,0:T(8,128)}, u32[]{:S(2)}) copy-start(f32[4,384,128]{2,1,0:T(8,128)} %get-tuple-element.97) | copy-start | bytes 2359300

commit v9 on v8

--- a/solution.py
+++ b/solution.py
@@ -810,7 +810,7 @@
         rest = [b.astype(jnp.float32) * (top / HALF_TOP) for b in rest]
         return [sliced(right_late, s, *group) + b for s, b in enumerate([first] + rest)]
 
-    us, vs, inward, halves = [], [], [], []
+    us, vs, inward = [], [], []
     for n, (low, high) in enumerate(calls):
         at = next(g for g, (first, end) in enumerate(groups) if first <= low < end)
         moved = came[at]
@@ -832,7 +832,6 @@
             [(moved, 0)],
         )
         inward.append(passed(halved(far_u, u_top), True))
-        halves.append(halved(far_v, v_top))
         us.append((mine_u, far_u))
         vs.append((mine_v, far_v))
     sources = []
@@ -843,17 +842,30 @@
         sources.append(added(us[n][0], inward[n], u_top, group))
         total = project(me, group[0], factors, sources[n], total)
 
+    order = [*range(1, chunks), 0]
+    lots = [order[:-1], order[-1:]] if chunks > 1 else [order]
+    halves, back = [], {}
+    for lot in lots:
+        halves.append(halved(jnp.concatenate([vs[k][1] for k in lot], axis=1), v_top))
+
+    def returned(n):
+        back[n] = passed(halves[n], True)
+
+    halves[0], total = tie((halves[0], total))
+    returned(0)
     near, _, blocks = ladder(total)
-    back = [passed(x, True) for x in halves]
+    if len(lots) > 1:
+        returned(1)
     amplitudes = amplitude(me, factors, pair_weight, near, sources)
     gathered, _ = joined(blocks, near)
     outs = []
-    for n, group in enumerate(calls):
+    for n, j, k in [(n, j, k) for n, lot in enumerate(lots) for j, k in enumerate(lot)]:
         back[n], outs, gathered = tie((back[n], outs, gathered))
-        base = added(vs[n][0], back[n], v_top, group)
+        base = [m[:, j * size : (j + 1) * size] for m in back[n]]
+        base = added(vs[k][0], base, v_top, calls[k])
         outs = final(
             me,
-            group[0],
+            k,
             factors,
             kernels,
             weights,

time: 533 us -> 501 us (0.940)
  the two profiles are of different devices: /device:TPU:24 before, /device:TPU:0 now
where the time goes in v9:
time: 501 us; the launch traced here: 495 us
  Pallas kernels  283 us (56%)
  starting transfers between devices  91.4 us (18%)
  waiting for transfers between devices  74.9 us (15%)
  other arithmetic  24.5 us (5%)
  matrix products  11.4 us (2%)
  local copies, waits for them, and re-layouts  6.44 us (1%)
    ppermute x30, starting transfers between devices, shift(): lax.ppermute(x, 'freq', [(i, (i + by) % parts) for i in range(parts)])  91.4 us
    ppermute x30, waiting for transfers between devices, shift(): lax.ppermute(x, 'freq', [(i, (i + by) % parts) for i in range(parts)])  74.9 us
    pallas_call x4, Pallas kernels, gathered_over(): pl.pallas_call(functools.partial(gather_kernel, chips, parts), out_shape=...  61.4 us
    pallas_call x3, Pallas kernels, final(): pl.pallas_call(functools.partial(final_kernel, nf, parts, len(outs)), out...  51.6 us
    pallas_call x3, Pallas kernels, quarter_pass(): pl.pallas_call(functools.partial(quarter_kernel, nf, parts, sets), out_sh...  46.3 us
    pallas_call x2, Pallas kernels, summed(): pl.pallas_call(functools.partial(sum_kernel, chips), out_shape=jax.ShapeD...  39.7 us
    pallas_call x2, Pallas kernels, again(): pl.pallas_call(functools.partial(again_kernel, own), out_shape=jax.ShapeD...  31.8 us
    pallas_call x2, Pallas kernels, summed(): pl.pallas_call(functools.partial(reduce_kernel, chips), out_shape=jax.Sha...  22.5 us
  transfers between devices with their start and end apart: 30, of which 5 were waited for; matrix products, arithmetic and copies ran while one was open for 7% of the time, Pallas kernels for 53%

profile of v9, /device:TPU:0, one launch (start us, length us, event | category | flops | bytes accessed | tf_op | source)
XLA Modules:
  0.0 494.6 jit_solution(2006237233604284692)
XLA Ops:
  0.6 1.0 fusion.6
  1.6 5.1 %collective-permute-start.2 = (f16[2,4,4608]{2,1,0:T(4,128)(2,1)S(1)}, f16[2,4,4608]{2,1,0:T(4,128)(2,1)S(1)}, u32[]{:S(2)}, u32[]{:S(2)}) collective-permute-start(f16[2,4,4608]{2,1,0:T(4,128)(2,1)S(1)} %fusion.6), channel_id=1, source_target_pairs={{0,3},{1,0},{2,1},{3,2},{4,7},{5,4},{6,5},{7,6},{8,11},{9,8},{10,9... | collective-permute-start | bytes 221192 | tf_op jit(solution)/shard_map/ppermute | solution.py:732
  6.7 1.0 collective-permute-start
  7.7 10.4 %fusion = f32[4,128,1024]{2,1,0:T(8,128)S(1)} fusion(bf16[4608,1024]{1,0:T(8,128)(2,1)} %l_ref.23, f32[4,4608,128]{2,1,0:T(8,128)} %rest_0_.5), kind=kOutput, calls=%fused_computation | convolution fusion | flops 4834197504 | bytes 20971520 | tf_op jit(solution)/shard_map/pa,fpc->fca/dot_general | solution.py:774
  18.2 20.1 %shard_map.77 = bf16[4,2,64,1024]{3,2,1,0:T(8,128)(2,1)S(1)} custom-call(f32[4,2,64,1024]{3,2,1,0:T(8,128)S(1)} %bitcast.53), custom_call_target="tpu_custom_call" | custom-call | flops 20971520 | bytes 20971520 | tf_op jit(solution)/shard_map/pallas_call | solution.py:684
  38.2 15.8 %shard_map.78 = f32[512,1024]{1,0:T(8,128)S(1)} custom-call(bf16[4608,1024]{1,0:T(8,128)(2,1)} %l_ref.23, f32[4,4608]{1,0:T(4,128)S(1)} %copy-done.10, bf16[512,1024]{1,0:T(8,128)(2,1)S(1)} %bitcast.62, f32[512,1024]{1,0:T(8,128)S(1)} %bitcast.54), custom_call_target="tpu_custom_call" | custom-call | flops 9663676416 | bytes 9437184 | tf_op jit(solution)/shard_map/pallas_call | solution.py:274
  54.1 11.3 %shard_map.79 = bf16[64,1024]{1,0:T(8,128)(2,1)S(1)} custom-call(f32[4,2,64,1024]{3,2,1,0:T(8,128)S(1)} %bitcast.60), custom_call_target="tpu_custom_call" | custom-call | flops 10485760 | bytes 10485760 | tf_op jit(solution)/shard_map/pallas_call | solution.py:675
  65.4 2.9 collective-permute-start.5
  68.2 1.2 collective-permute-start.4
  70.4 2.8 multiply_convert_fusion.15
  73.1 4.0 multiply_convert_fusion
  77.3 0.6 reduce_max.18
  78.6 10.9 %shard_map.80 = (bf16[1,4,2,64,1024]{4,3,2,1,0:T(8,128)(2,1)S(1)}, f32[8,128]{1,0:T(8,128)S(1)}) custom-call(bf16[1,64,1024]{2,1,0:T(8,128)(2,1)S(1)} %bitcast.66), custom_call_target="tpu_custom_call" | custom-call | flops 20971520 | bytes 20971520 | tf_op jit(solution)/shard_map/pallas_call | solution.py:704
  89.7 3.9 collective-permute-start.8
  93.9 0.6 collective-permute-start.6
  94.6 3.0 collective-permute-start.9
  97.8 33.0 %collective-permute-start.10 = (f16[4,384,128]{2,1,0:T(8,128)(2,1)}, f16[4,384,128]{2,1,0:T(8,128)(2,1)}, u32[]{:S(2)}, u32[]{:S(2)}) collective-permute-start(f16[4,384,128]{2,1,0:T(8,128)(2,1)} %get-tuple-element.64), channel_id=1, source_target_pairs={{0,2},{1,3},{2,0},{3,1},{4,6},{5,7},{6,4},{7,5},{8,10},{9,11},{10,... | collective-permute-start | bytes 1179656 | tf_op jit(solution)/shard_map/ppermute | solution.py:732
  130.8 0.9 pad_maximum_fusion.x_ref
  131.8 19.3 %shard_map.81 = (bf16[4,4,2,64,1024]{4,3,2,1,0:T(8,128)(2,1)S(1)}, f32[8,128]{1,0:T(8,128)S(1)}) custom-call(bf16[3,64,1024]{2,1,0:T(8,128)(2,1)S(1)} %pad_maximum_fusion.x_ref, bf16[4,2,64,1024]{3,2,1,0:T(8,128)(2,1)S(1)} %bitcast.64), custom_call_target="tpu_custom_call" | custom-call | flops 62914560 | bytes 62914560 | tf_op jit(solution)/shard_map/pallas_call | solution.py:704
  151.1 2.0 copy-done
  153.1 0.7 reduce_sum.19
  154.5 0.5 collective-permute-start.11
  155.1 26.5 %collective-permute-done.7 = f16[4,768,128]{2,1,0:T(8,128)(2,1)S(1)} collective-permute-done((f16[4,768,128]{2,1,0:T(8,128)(2,1)}, f16[4,768,128]{2,1,0:T(8,128)(2,1)S(1)}, u32[]{:S(2)}, u32[]{:S(2)}) %collective-permute-start.7) | collective-permute-done | bytes 786464 | tf_op jit(solution)/shard_map/ppermute | solution.py:732
  181.8 2.2 copy-done.1
  184.0 15.4 %shard_map.82 = (f32[4,384,128]{2,1,0:T(8,128)S(1)}, f32[12,384,128]{2,1,0:T(8,128)S(1)}, f32[4,384,128]{2,1,0:T(8,128)}, f32[12,384,128]{2,1,0:T(8,128)}) custom-call(s32[1]{0:T(128)} %bitcast.me_ref, bf16[4608,1024]{1,0:T(8,128)(2,1)} %l_ref.23, f32[16,4608]{1,0:T(8,128)S(1)} %pad_maximum_fusion.2.k_ref, f32[16,4608]{1,0:T(8,128)S(1)} %pad_maximum_fusion.3.wt_ref, ...), custom_call_target="tpu_custom_call" | custom-call | flops 2415919104 | bytes 12582912 | tf_op jit(solution)/shard_map/pallas_call | solution.py:143
  200.3 15.4 %shard_map.83 = (f32[4,384,128]{2,1,0:T(8,128)S(1)}, f32[12,384,128]{2,1,0:T(8,128)S(1)}, f32[4,384,128]{2,1,0:T(8,128)}, f32[12,384,128]{2,1,0:T(8,128)}) custom-call(s32[1]{0:T(128)} %bitcast.me_ref, bf16[4608,1024]{1,0:T(8,128)(2,1)} %l_ref.23, f32[16,4608]{1,0:T(8,128)S(1)} %pad_maximum_fusion.2.k_ref, f32[16,4608]{1,0:T(8,128)S(1)} %pad_maximum_fusion.3.wt_ref, ...), custom_call_target="tpu_custom_call" | custom-call | flops 2415919104 | bytes 12582912 | tf_op jit(solution)/shard_map/pallas_call | solution.py:143
  215.8 1.1 multiply_convert_fusion.9
  216.8 3.4 collective-permute-start.18
  220.3 1.1 convert_multiply_fusion.2.rest_1_
  221.3 1.1 convert_multiply_fusion.1.rest_2_
  222.5 15.6 %shard_map.84 = (f32[4,384,128]{2,1,0:T(8,128)S(1)}, f32[12,384,128]{2,1,0:T(8,128)S(1)}, f32[4,384,128]{2,1,0:T(8,128)}, f32[12,384,128]{2,1,0:T(8,128)}) custom-call(s32[1]{0:T(128)} %bitcast.me_ref, bf16[4608,1024]{1,0:T(8,128)(2,1)} %l_ref.23, f32[16,4608]{1,0:T(8,128)S(1)} %pad_maximum_fusion.2.k_ref, f32[16,4608]{1,0:T(8,128)S(1)} %pad_maximum_fusion.3.wt_ref, ...), custom_call_target="tpu_custom_call" | custom-call | flops 2415919104 | bytes 12582912 | tf_op jit(solution)/shard_map/pallas_call | solution.py:143
  238.1 1.2 multiply_convert_fusion.12
  239.3 0.7 collective-permute-start.14
  240.0 1.5 collective-permute-start.13
  241.7 1.5 copy-done.12
  243.4 1.6 fusion.3
  245.0 2.3 collective-permute-start.17
  247.3 1.1 collective-permute-start.16
  248.4 1.3 collective-permute-start.15
  250.4 4.7 shard_map.85.rest_4_
  255.1 15.2 %collective-permute-done.17 = f16[4,384,128]{2,1,0:T(8,128)(2,1)S(1)} collective-permute-done((f16[4,384,128]{2,1,0:T(8,128)(2,1)S(1)}, f16[4,384,128]{2,1,0:T(8,128)(2,1)S(1)}, u32[]{:S(2)}, u32[]{:S(2)}) %collective-permute-start.17) | collective-permute-done | bytes 393248 | tf_op jit(solution)/shard_map/ppermute | solution.py:732
  270.3 23.7 %collective-permute-done.16 = f16[4,384,128]{2,1,0:T(8,128)(2,1)S(1)} collective-permute-done((f16[4,384,128]{2,1,0:T(8,128)(2,1)}, f16[4,384,128]{2,1,0:T(8,128)(2,1)S(1)}, u32[]{:S(2)}, u32[]{:S(2)}) %collective-permute-start.16) | collective-permute-done | bytes 393248 | tf_op jit(solution)/shard_map/ppermute | solution.py:732
  294.0 0.4 multiply_add_fusion.12
  294.4 4.7 shard_map.86.rest_4_
  299.1 9.1 %collective-permute-done.12 = f16[4,384,128]{2,1,0:T(8,128)(2,1)S(1)} collective-permute-done((f16[4,384,128]{2,1,0:T(8,128)(2,1)}, f16[4,384,128]{2,1,0:T(8,128)(2,1)S(1)}, u32[]{:S(2)}, u32[]{:S(2)}) %collective-permute-start.12) | collective-permute-done | bytes 393248 | tf_op jit(solution)/shard_map/ppermute | solution.py:732
  308.2 2.4 multiply_add_fusion.9
  310.6 5.3 %shard_map.87.x_ref = f32[512,1024]{1,0:T(8,128)S(1)} custom-call(s32[1]{0:T(128)} %bitcast.me_ref, bf16[4608,1024]{1,0:T(8,128)(2,1)} %l_ref.23, f32[4,384,128]{2,1,0:T(8,128)S(1)} %get-tuple-element.125.rest_0_.rest_8_, f32[4,384,128]{2,1,0:T(8,128)S(1)} %get-tuple-element.124.rest_1_.rest_9_, f32[4,384,128]{2,1,0:T(8,128)S(1)} %get-tuple-element.123.rest_2_.rest_10_, ...), custom_call_target="tpu_custom_call" | custom-call | flops 1610612736 | bytes 6291456 | tf_op jit(solution)/shard_map/pallas_call | solution.py:228
  315.9 8.6 %collective-permute-start.24 = (f16[4,768,128]{2,1,0:T(8,128)(2,1)}, f16[4,768,128]{2,1,0:T(8,128)(2,1)}, u32[]{:S(2)}, u32[]{:S(2)}) collective-permute-start(f16[4,768,128]{2,1,0:T(8,128)(2,1)} %get-tuple-element.89), channel_id=1, source_target_pairs={{0,3},{1,0},{2,1},{3,2},{4,7},{5,4},{6,5},{7,6},{8,11},{9,8},{10,9... | collective-permute-start | bytes 2359304 | tf_op jit(solution)/shard_map/ppermute | solution.py:732
  324.5 0.6 collective-permute-start.26
  325.2 19.6 %shard_map.88 = bf16[4,2,64,1024]{3,2,1,0:T(8,128)(2,1)S(1)} custom-call(f32[4,2,64,1024]{3,2,1,0:T(8,128)S(1)} %bitcast.52), custom_call_target="tpu_custom_call" | custom-call | flops 20971520 | bytes 20971520 | tf_op jit(solution)/shard_map/pallas_call | solution.py:684
  344.8 16.0 %shard_map.89 = f32[512,1024]{1,0:T(8,128)S(1)} custom-call(bf16[4608,1024]{1,0:T(8,128)(2,1)} %l_ref.23, f32[4,4608]{1,0:T(4,128)S(1)} %copy-done.10, bf16[512,1024]{1,0:T(8,128)(2,1)S(1)} %bitcast.63, f32[512,1024]{1,0:T(8,128)S(1)} %shard_map.87.x_ref), custom_call_target="tpu_custom_call" | custom-call | flops 9663676416 | bytes 9437184 | tf_op jit(solution)/shard_map/pallas_call | solution.py:274
  360.9 11.3 %shard_map.90 = bf16[64,1024]{1,0:T(8,128)(2,1)S(1)} custom-call(f32[4,2,64,1024]{3,2,1,0:T(8,128)S(1)} %bitcast.61), custom_call_target="tpu_custom_call" | custom-call | flops 10485760 | bytes 10485760 | tf_op jit(solution)/shard_map/pallas_call | solution.py:675
  372.2 3.4 collective-permute-start.29
  375.9 1.2 collective-permute-start.28
  377.1 11.5 %shard_map.91 = (bf16[1,4,2,64,1024]{4,3,2,1,0:T(8,128)(2,1)S(1)}, f32[8,128]{1,0:T(8,128)}) custom-call(bf16[1,64,1024]{2,1,0:T(8,128)(2,1)S(1)} %bitcast.67), custom_call_target="tpu_custom_call" | custom-call | flops 20971520 | bytes 20971520 | tf_op jit(solution)/shard_map/pallas_call | solution.py:704
  388.7 11.5 %collective-permute-start.27 = (bf16[64,1024]{1,0:T(8,128)(2,1)S(1)}, bf16[64,1024]{1,0:T(8,128)(2,1)S(1)}, u32[]{:S(2)}, u32[]{:S(2)}) collective-permute-start(bf16[64,1024]{1,0:T(8,128)(2,1)S(1)} %shard_map.90), channel_id=1, source_target_pairs={{0,1},{1,2},{2,3},{3,0},{4,5},{5,6},{6,7},{7,4},{8,9},{9,10},{10,1... | collective-permute-start | bytes 393224 | tf_op jit(solution)/shard_map/ppermute | solution.py:732
  400.2 14.8 %shard_map.92 = f32[4,4608,128]{2,1,0:T(8,128)} custom-call(s32[1]{0:T(128)} %bitcast.me_ref, bf16[4608,1024]{1,0:T(8,128)(2,1)S(1)} %bitcast.45, f32[4,4608]{1,0:T(4,128)S(1)} %copy-done.10, bf16[512,1024]{1,0:T(8,128)(2,1)S(1)} %bitcast.55, f32[4,384,128]{2,1,0:T(8,128)S(1)} %get-tuple-element.133.rest_0_, f32[4,384,128]{2,1,0:T(8,128)S(1)} %get-tuple-element.132.rest_1_, ...), custom_call_target="tpu_custom_call" | custom-call | flops 4831838208 | bytes 18874368 | tf_op jit(solution)/shard_map/pallas_call | solution.py:362
  415.2 19.7 %shard_map.93 = (bf16[4,4,2,64,1024]{4,3,2,1,0:T(8,128)(2,1)S(1)}, f32[8,128]{1,0:T(8,128)}) custom-call(bf16[3,64,1024]{2,1,0:T(8,128)(2,1)S(1)} %pad_maximum_fusion.1.x_ref, bf16[4,2,64,1024]{3,2,1,0:T(8,128)(2,1)S(1)} %bitcast.56), custom_call_target="tpu_custom_call" | custom-call | flops 62914560 | bytes 62914560 | tf_op jit(solution)/shard_map/pallas_call | solution.py:704
  434.9 3.8 collective-permute-start.21
  438.7 1.7 multiply_add_fusion.6
  440.5 17.2 %shard_map.94.rest_4_ = f32[4,4608,128]{2,1,0:T(8,128)} custom-call(s32[1]{0:T(128)} %bitcast.me_ref, bf16[4608,1024]{1,0:T(8,128)(2,1)S(1)} %bitcast.45, f32[16,4608]{1,0:T(8,128)S(1)} %pad_maximum_fusion.2.k_ref, f32[16,4608]{1,0:T(8,128)S(1)} %pad_maximum_fusion.3.wt_ref, f32[64,16]{1,0:T(8,128)S(1)} %bitcast.68, bf16[2048,1024]{1,0:T(8,128)(2,1)S(1)} %bitcast.49, ...), custom_call_target="tpu_custom_call" | custom-call | flops 6442450944 | bytes 6291456 | tf_op jit(solution)/shard_map/pallas_call | solution.py:439
  457.7 1.7 multiply_add_fusion.3
  459.5 17.2 %shard_map.95.rest_4_ = f32[4,4608,128]{2,1,0:T(8,128)} custom-call(s32[1]{0:T(128)} %bitcast.me_ref, bf16[4608,1024]{1,0:T(8,128)(2,1)S(1)} %bitcast.45, f32[16,4608]{1,0:T(8,128)S(1)} %pad_maximum_fusion.2.k_ref, f32[16,4608]{1,0:T(8,128)S(1)} %pad_maximum_fusion.3.wt_ref, f32[64,16]{1,0:T(8,128)S(1)} %bitcast.69, ...), custom_call_target="tpu_custom_call", output_to_operand_aliasing={{}: (10, {})} | custom-call | flops 6442450944 | bytes 6291456 | tf_op jit(solution)/shard_map/pallas_call | solution.py:439
  477.1 17.2 %shard_map.96 = f32[4,4608,128]{2,1,0:T(8,128)} custom-call(s32[1]{0:T(128)} %bitcast.me_ref, bf16[4608,1024]{1,0:T(8,128)(2,1)S(1)} %bitcast.45, f32[16,4608]{1,0:T(8,128)S(1)} %pad_maximum_fusion.2.k_ref, f32[16,4608]{1,0:T(8,128)S(1)} %pad_maximum_fusion.3.wt_ref, f32[64,16]{1,0:T(8,128)S(1)} %bitcast.70, ...), custom_call_target="tpu_custom_call", output_to_operand_aliasing={{}: (10, {})} | custom-call | flops 6442450944 | bytes 6291456 | tf_op jit(solution)/shard_map/pallas_call | solution.py:439
  (127 shorter events, 5.1 us)
Async XLA Ops:
  1.6 88.0 %collective-permute-start.2 = (f16[2,4,4608]{2,1,0:T(4,128)(2,1)S(1)}, f16[2,4,4608]{2,1,0:T(4,128)(2,1)S(1)}, u32[]{:S(2)}, u32[]{:S(2)}) collective-permute-start(f16[2,4,4608]{2,1,0:T(4,128)(2,1)S(1)} %fusion.6), channel_id=1, source_target_pairs={{0,3},{1,0},{2,1},{3,2},{4,7},{5,4},{6,5},{7,6},{8,11},{9,8},{10,9... | collective-permute-start | bytes 221192 | tf_op jit(solution)/shard_map/ppermute | solution.py:732
  6.7 83.0 %collective-permute-start.1 = (f16[2,4,4608]{2,1,0:T(4,128)(2,1)S(1)}, f16[2,4,4608]{2,1,0:T(4,128)(2,1)S(1)}, u32[]{:S(2)}, u32[]{:S(2)}) collective-permute-start(f16[2,4,4608]{2,1,0:T(4,128)(2,1)S(1)} %fusion.6), channel_id=1, source_target_pairs={{0,2},{1,3},{2,0},{3,1},{4,6},{5,7},{6,4},{7,5},{8,10},{9,11},{10,... | collective-permute-start | bytes 221192 | tf_op jit(solution)/shard_map/ppermute | solution.py:732
  6.7 86.9 %collective-permute-start = (f16[2,4,4608]{2,1,0:T(4,128)(2,1)S(1)}, f16[2,4,4608]{2,1,0:T(4,128)(2,1)S(1)}, u32[]{:S(2)}, u32[]{:S(2)}) collective-permute-start(f16[2,4,4608]{2,1,0:T(4,128)(2,1)S(1)} %fusion.6), channel_id=1, source_target_pairs={{0,1},{1,2},{2,3},{3,0},{4,5},{5,6},{6,7},{7,4},{8,9},{9,10},{10,1... | collective-permute-start | bytes 221192 | tf_op jit(solution)/shard_map/ppermute | solution.py:732
  18.1 20.1 %copy-start.10 = (f32[4,4608]{1,0:T(4,128)S(1)}, f32[4,4608]{1,0:T(4,128)}, u32[]{:S(2)}) copy-start(f32[4,4608]{1,0:T(4,128)} %wt_ref.5) | copy-start | bytes 221188
  54.1 15.4 %copy-start.18 = (f32[16,16]{1,0:T(8,128)S(1)}, f32[16,16]{1,0:T(8,128)}, u32[]{:S(2)}) copy-start(f32[16,16]{1,0:T(8,128)} %param.10) | copy-start | bytes 3076
  54.1 15.8 %copy-start.19 = (f32[16,16]{1,0:T(8,128)S(1)}, f32[16,16]{1,0:T(8,128)}, u32[]{:S(2)}) copy-start(f32[16,16]{1,0:T(8,128)} %param.11) | copy-start | bytes 3076
  65.4 28.5 %collective-permute-start.5 = (bf16[64,1024]{1,0:T(8,128)(2,1)S(1)}, bf16[64,1024]{1,0:T(8,128)(2,1)S(1)}, u32[]{:S(2)}, u32[]{:S(2)}) collective-permute-start(bf16[64,1024]{1,0:T(8,128)(2,1)S(1)} %shard_map.79), channel_id=1, source_target_pairs={{0,3},{1,0},{2,1},{3,2},{4,7},{5,4},{6,5},{7,6},{8,11},{9,8},{10,9... | collective-permute-start | bytes 393224 | tf_op jit(solution)/shard_map/ppermute | solution.py:732
  68.2 26.3 %collective-permute-start.4 = (bf16[64,1024]{1,0:T(8,128)(2,1)S(1)}, bf16[64,1024]{1,0:T(8,128)(2,1)}, u32[]{:S(2)}, u32[]{:S(2)}) collective-permute-start(bf16[64,1024]{1,0:T(8,128)(2,1)S(1)} %shard_map.79), channel_id=1, source_target_pairs={{0,2},{1,3},{2,0},{3,1},{4,6},{5,7},{6,4},{7,5},{8,10},{9,11},{10,... | collective-permute-start | bytes 393224 | tf_op jit(solution)/shard_map/ppermute | solution.py:732
  77.1 17.4 %copy-start.17 = (f32[4,4608]{1,0:T(4,128)S(1)}, f32[4,4608]{1,0:T(4,128)}, u32[]{:S(2)}) copy-start(f32[4,4608]{1,0:T(4,128)} %param.9) | copy-start | bytes 221188
  89.6 8.3 %collective-permute-start.3 = (bf16[64,1024]{1,0:T(8,128)(2,1)S(1)}, bf16[64,1024]{1,0:T(8,128)(2,1)S(1)}, u32[]{:S(2)}, u32[]{:S(2)}) collective-permute-start(bf16[64,1024]{1,0:T(8,128)(2,1)S(1)} %shard_map.79), channel_id=1, source_target_pairs={{0,1},{1,2},{2,3},{3,0},{4,5},{5,6},{6,7},{7,4},{8,9},{9,10},{10,1... | collective-permute-start | bytes 393224 | tf_op jit(solution)/shard_map/ppermute | solution.py:732
  89.7 64.8 %collective-permute-start.8 = (f16[4,768,128]{2,1,0:T(8,128)(2,1)}, f16[4,768,128]{2,1,0:T(8,128)(2,1)S(1)}, u32[]{:S(2)}, u32[]{:S(2)}) collective-permute-start(f16[4,768,128]{2,1,0:T(8,128)(2,1)} %get-tuple-element.137), channel_id=1, source_target_pairs={{0,3},{1,0},{2,1},{3,2},{4,7},{5,4},{6,5},{7,6},{8,11},{9,8},{10,9... | collective-permute-start | bytes 2359304 | tf_op jit(solution)/shard_map/ppermute | solution.py:732
  93.6 88.0 %collective-permute-start.7 = (f16[4,768,128]{2,1,0:T(8,128)(2,1)}, f16[4,768,128]{2,1,0:T(8,128)(2,1)S(1)}, u32[]{:S(2)}, u32[]{:S(2)}) collective-permute-start(f16[4,768,128]{2,1,0:T(8,128)(2,1)} %get-tuple-element.138), channel_id=1, source_target_pairs={{0,2},{1,3},{2,0},{3,1},{4,6},{5,7},{6,4},{7,5},{8,10},{9,11},{10,... | collective-permute-start | bytes 2359304 | tf_op jit(solution)/shard_map/ppermute | solution.py:732
  93.9 87.9 %collective-permute-start.6 = (f16[4,768,128]{2,1,0:T(8,128)(2,1)}, f16[4,768,128]{2,1,0:T(8,128)(2,1)S(1)}, u32[]{:S(2)}, u32[]{:S(2)}) collective-permute-start(f16[4,768,128]{2,1,0:T(8,128)(2,1)} %get-tuple-element.139), channel_id=1, source_target_pairs={{0,1},{1,2},{2,3},{3,0},{4,5},{5,6},{6,7},{7,4},{8,9},{9,10},{10,1... | collective-permute-start | bytes 2359304 | tf_op jit(solution)/shard_map/ppermute | solution.py:732
  94.6 122.3 %collective-permute-start.9 = (f16[4,384,128]{2,1,0:T(8,128)(2,1)}, f16[4,384,128]{2,1,0:T(8,128)(2,1)}, u32[]{:S(2)}, u32[]{:S(2)}) collective-permute-start(f16[4,384,128]{2,1,0:T(8,128)(2,1)} %get-tuple-element.63), channel_id=1, source_target_pairs={{0,1},{1,2},{2,3},{3,0},{4,5},{5,6},{6,7},{7,4},{8,9},{9,10},{10,1... | collective-permute-start | bytes 1179656 | tf_op jit(solution)/shard_map/ppermute | solution.py:732
  97.8 122.4 %collective-permute-start.10 = (f16[4,384,128]{2,1,0:T(8,128)(2,1)}, f16[4,384,128]{2,1,0:T(8,128)(2,1)}, u32[]{:S(2)}, u32[]{:S(2)}) collective-permute-start(f16[4,384,128]{2,1,0:T(8,128)(2,1)} %get-tuple-element.64), channel_id=1, source_target_pairs={{0,2},{1,3},{2,0},{3,1},{4,6},{5,7},{6,4},{7,5},{8,10},{9,11},{10,... | collective-permute-start | bytes 1179656 | tf_op jit(solution)/shard_map/ppermute | solution.py:732
  151.1 2.0 copy-start
  154.5 65.8 %collective-permute-start.11 = (f16[4,384,128]{2,1,0:T(8,128)(2,1)}, f16[4,384,128]{2,1,0:T(8,128)(2,1)S(1)}, u32[]{:S(2)}, u32[]{:S(2)}) collective-permute-start(f16[4,384,128]{2,1,0:T(8,128)(2,1)} %get-tuple-element.65), channel_id=1, source_target_pairs={{0,3},{1,0},{2,1},{3,2},{4,7},{5,4},{6,5},{7,6},{8,11},{9,8},{10,9... | collective-permute-start | bytes 1179656 | tf_op jit(solution)/shard_map/ppermute | solution.py:732
  181.8 2.2 copy-start.1
  199.9 45.1 %collective-permute-start.20 = (f16[4,384,128]{2,1,0:T(8,128)(2,1)S(1)}, f16[4,384,128]{2,1,0:T(8,128)(2,1)S(1)}, u32[]{:S(2)}, u32[]{:S(2)}) collective-permute-start(f16[4,384,128]{2,1,0:T(8,128)(2,1)S(1)} %get-tuple-element.146), channel_id=1, source_target_pairs={{0,1},{1,2},{2,3},{3,0},{4,5},{5,6},{6,7},{7,4},{8,9},{9,10},{10,1... | collective-permute-start | bytes 1179656 | tf_op jit(solution)/shard_map/ppermute | solution.py:732
  200.0 47.3 %collective-permute-start.19 = (f16[4,384,128]{2,1,0:T(8,128)(2,1)S(1)}, f16[4,384,128]{2,1,0:T(8,128)(2,1)S(1)}, u32[]{:S(2)}, u32[]{:S(2)}) collective-permute-start(f16[4,384,128]{2,1,0:T(8,128)(2,1)S(1)} %get-tuple-element.147), channel_id=1, source_target_pairs={{0,2},{1,3},{2,0},{3,1},{4,6},{5,7},{6,4},{7,5},{8,10},{9,11},{10,... | collective-permute-start | bytes 1179656 | tf_op jit(solution)/shard_map/ppermute | solution.py:732
  216.8 31.6 %collective-permute-start.18 = (f16[4,384,128]{2,1,0:T(8,128)(2,1)S(1)}, f16[4,384,128]{2,1,0:T(8,128)(2,1)S(1)}, u32[]{:S(2)}, u32[]{:S(2)}) collective-permute-start(f16[4,384,128]{2,1,0:T(8,128)(2,1)S(1)} %get-tuple-element.148), channel_id=1, source_target_pairs={{0,3},{1,0},{2,1},{3,2},{4,7},{5,4},{6,5},{7,6},{8,11},{9,8},{10,9... | collective-permute-start | bytes 1179656 | tf_op jit(solution)/shard_map/ppermute | solution.py:732
  222.5 27.2 %slice-start.3 = ((s8[9437184]{0:T(1024)(128)(4,1)}), s8[4194304]{0:T(1024)(128)(4,1)S(1)}, s32[]{:S(2)}) async-start(s8[9437184]{0:T(1024)(128)(4,1)} %bitcast.71), calls=%async_computation.3 | async-start | bytes 8388608
  222.5 27.2 %slice-start.4 = ((s8[9437184]{0:T(1024)(128)(4,1)}), s8[4194304]{0:T(1024)(128)(4,1)S(1)}, s32[]{:S(2)}) async-start(s8[9437184]{0:T(1024)(128)(4,1)} %bitcast.71), calls=%async_computation.4 | async-start | bytes 8388608
  238.1 3.4 copy-start.11
  239.3 59.9 %collective-permute-start.14 = (f16[4,384,128]{2,1,0:T(8,128)(2,1)}, f16[4,384,128]{2,1,0:T(8,128)(2,1)S(1)}, u32[]{:S(2)}, u32[]{:S(2)}) collective-permute-start(f16[4,384,128]{2,1,0:T(8,128)(2,1)} %get-tuple-element.152), channel_id=1, source_target_pairs={{0,1},{1,2},{2,3},{3,0},{4,5},{5,6},{6,7},{7,4},{8,9},{9,10},{10,1... | collective-permute-start | bytes 1179656 | tf_op jit(solution)/shard_map/ppermute | solution.py:732
  240.0 59.1 %collective-permute-start.13 = (f16[4,384,128]{2,1,0:T(8,128)(2,1)}, f16[4,384,128]{2,1,0:T(8,128)(2,1)S(1)}, u32[]{:S(2)}, u32[]{:S(2)}) collective-permute-start(f16[4,384,128]{2,1,0:T(8,128)(2,1)} %get-tuple-element.153), channel_id=1, source_target_pairs={{0,2},{1,3},{2,0},{3,1},{4,6},{5,7},{6,4},{7,5},{8,10},{9,11},{10,... | collective-permute-start | bytes 1179656 | tf_op jit(solution)/shard_map/ppermute | solution.py:732
  241.5 1.7 copy-start.12
  241.5 8.2 %slice-start.5 = ((s8[9437184]{0:T(1024)(128)(4,1)}), s8[1048576]{0:T(1024)(128)(4,1)S(1)}, s32[]{:S(2)}) async-start(s8[9437184]{0:T(1024)(128)(4,1)} %bitcast.71), calls=%async_computation.5 | async-start | bytes 2097152
  245.0 25.3 %collective-permute-start.17 = (f16[4,384,128]{2,1,0:T(8,128)(2,1)S(1)}, f16[4,384,128]{2,1,0:T(8,128)(2,1)S(1)}, u32[]{:S(2)}, u32[]{:S(2)}) collective-permute-start(f16[4,384,128]{2,1,0:T(8,128)(2,1)S(1)} %get-tuple-element.149), channel_id=1, source_target_pairs={{0,1},{1,2},{2,3},{3,0},{4,5},{5,6},{6,7},{7,4},{8,9},{9,10},{10,1... | collective-permute-start | bytes 1179656 | tf_op jit(solution)/shard_map/ppermute | solution.py:732
  247.3 46.7 %collective-permute-start.16 = (f16[4,384,128]{2,1,0:T(8,128)(2,1)}, f16[4,384,128]{2,1,0:T(8,128)(2,1)S(1)}, u32[]{:S(2)}, u32[]{:S(2)}) collective-permute-start(f16[4,384,128]{2,1,0:T(8,128)(2,1)} %get-tuple-element.150), channel_id=1, source_target_pairs={{0,2},{1,3},{2,0},{3,1},{4,6},{5,7},{6,4},{7,5},{8,10},{9,11},{10,... | collective-permute-start | bytes 1179656 | tf_op jit(solution)/shard_map/ppermute | solution.py:732
  248.4 45.6 %collective-permute-start.15 = (f16[4,384,128]{2,1,0:T(8,128)(2,1)S(1)}, f16[4,384,128]{2,1,0:T(8,128)(2,1)S(1)}, u32[]{:S(2)}, u32[]{:S(2)}) collective-permute-start(f16[4,384,128]{2,1,0:T(8,128)(2,1)S(1)} %get-tuple-element.151), channel_id=1, source_target_pairs={{0,3},{1,0},{2,1},{3,2},{4,7},{5,4},{6,5},{7,6},{8,11},{9,8},{10,9... | collective-permute-start | bytes 1179656 | tf_op jit(solution)/shard_map/ppermute | solution.py:732
  270.3 37.9 %collective-permute-start.12 = (f16[4,384,128]{2,1,0:T(8,128)(2,1)}, f16[4,384,128]{2,1,0:T(8,128)(2,1)S(1)}, u32[]{:S(2)}, u32[]{:S(2)}) collective-permute-start(f16[4,384,128]{2,1,0:T(8,128)(2,1)} %get-tuple-element.154), channel_id=1, source_target_pairs={{0,3},{1,0},{2,1},{3,2},{4,7},{5,4},{6,5},{7,6},{8,11},{9,8},{10,9... | collective-permute-start | bytes 1179656 | tf_op jit(solution)/shard_map/ppermute | solution.py:732
  310.6 5.3 %copy-start.2 = (f32[4,384,128]{2,1,0:T(8,128)}, f32[4,384,128]{2,1,0:T(8,128)S(1)}, u32[]{:S(2)}) copy-start(f32[4,384,128]{2,1,0:T(8,128)S(1)} %get-tuple-element.122.rest_3_.rest_11_) | copy-start | bytes 2359300
  310.6 5.3 %copy-start.4 = (f32[4,384,128]{2,1,0:T(8,128)}, f32[4,384,128]{2,1,0:T(8,128)S(1)}, u32[]{:S(2)}) copy-start(f32[4,384,128]{2,1,0:T(8,128)S(1)} %get-tuple-element.123.rest_2_.rest_10_) | copy-start | bytes 2359300
  310.6 5.3 %copy-start.6 = (f32[4,384,128]{2,1,0:T(8,128)}, f32[4,384,128]{2,1,0:T(8,128)S(1)}, u32[]{:S(2)}) copy-start(f32[4,384,128]{2,1,0:T(8,128)S(1)} %get-tuple-element.124.rest_1_.rest_9_) | copy-start | bytes 2359300
  310.6 5.3 %copy-start.8 = (f32[4,384,128]{2,1,0:T(8,128)}, f32[4,384,128]{2,1,0:T(8,128)S(1)}, u32[]{:S(2)}) copy-start(f32[4,384,128]{2,1,0:T(8,128)S(1)} %get-tuple-element.125.rest_0_.rest_8_) | copy-start | bytes 2359300
  315.9 119.0 %collective-permute-start.24 = (f16[4,768,128]{2,1,0:T(8,128)(2,1)}, f16[4,768,128]{2,1,0:T(8,128)(2,1)}, u32[]{:S(2)}, u32[]{:S(2)}) collective-permute-start(f16[4,768,128]{2,1,0:T(8,128)(2,1)} %get-tuple-element.89), channel_id=1, source_target_pairs={{0,3},{1,0},{2,1},{3,2},{4,7},{5,4},{6,5},{7,6},{8,11},{9,8},{10,9... | collective-permute-start | bytes 2359304 | tf_op jit(solution)/shard_map/ppermute | solution.py:732
  324.5 114.2 %collective-permute-start.25 = (f16[4,768,128]{2,1,0:T(8,128)(2,1)}, f16[4,768,128]{2,1,0:T(8,128)(2,1)}, u32[]{:S(2)}, u32[]{:S(2)}) collective-permute-start(f16[4,768,128]{2,1,0:T(8,128)(2,1)} %get-tuple-element.90), channel_id=1, source_target_pairs={{0,2},{1,3},{2,0},{3,1},{4,6},{5,7},{6,4},{7,5},{8,10},{9,11},{10,... | collective-permute-start | bytes 2359304 | tf_op jit(solution)/shard_map/ppermute | solution.py:732
  324.5 114.2 %collective-permute-start.26 = (f16[4,768,128]{2,1,0:T(8,128)(2,1)}, f16[4,768,128]{2,1,0:T(8,128)(2,1)}, u32[]{:S(2)}, u32[]{:S(2)}) collective-permute-start(f16[4,768,128]{2,1,0:T(8,128)(2,1)} %get-tuple-element.91), channel_id=1, source_target_pairs={{0,1},{1,2},{2,3},{3,0},{4,5},{5,6},{6,7},{7,4},{8,9},{9,10},{10,1... | collective-permute-start | bytes 2359304 | tf_op jit(solution)/shard_map/ppermute | solution.py:732
  344.8 55.3 %slice-start = ((s8[9437184]{0:T(1024)(128)(4,1)}), s8[4194304]{0:T(1024)(128)(4,1)S(1)}, s32[]{:S(2)}) async-start(s8[9437184]{0:T(1024)(128)(4,1)} %bitcast.44), calls=%async_computation | async-start | bytes 8388608
  344.8 30.8 %copy-start.13 = (f32[12,384,128]{2,1,0:T(8,128)S(1)}, f32[12,384,128]{2,1,0:T(8,128)}, u32[]{:S(2)}) copy-start(f32[12,384,128]{2,1,0:T(8,128)} %get-tuple-element.88) | copy-start | bytes 7077892
  344.8 55.3 %slice-start.1 = ((s8[9437184]{0:T(1024)(128)(4,1)}), s8[4194304]{0:T(1024)(128)(4,1)S(1)}, s32[]{:S(2)}) async-start(s8[9437184]{0:T(1024)(128)(4,1)} %bitcast.44), calls=%async_computation.1 | async-start | bytes 8388608
  344.8 55.3 %slice-start.2 = ((s8[9437184]{0:T(1024)(128)(4,1)}), s8[1048576]{0:T(1024)(128)(4,1)S(1)}, s32[]{:S(2)}) async-start(s8[9437184]{0:T(1024)(128)(4,1)} %bitcast.44), calls=%async_computation.2 | async-start | bytes 2097152
  372.1 28.0 %copy-start.3 = (f32[4,384,128]{2,1,0:T(8,128)S(1)}, f32[4,384,128]{2,1,0:T(8,128)}, u32[]{:S(2)}) copy-start(f32[4,384,128]{2,1,0:T(8,128)} %copy-done.2) | copy-start | bytes 2359300
  372.2 28.0 %copy-start.5 = (f32[4,384,128]{2,1,0:T(8,128)S(1)}, f32[4,384,128]{2,1,0:T(8,128)}, u32[]{:S(2)}) copy-start(f32[4,384,128]{2,1,0:T(8,128)} %copy-done.4) | copy-start | bytes 2359300
  372.2 28.0 %copy-start.7 = (f32[4,384,128]{2,1,0:T(8,128)S(1)}, f32[4,384,128]{2,1,0:T(8,128)}, u32[]{:S(2)}) copy-start(f32[4,384,128]{2,1,0:T(8,128)} %copy-done.6) | copy-start | bytes 2359300
  372.2 28.0 %copy-start.9 = (f32[4,384,128]{2,1,0:T(8,128)S(1)}, f32[4,384,128]{2,1,0:T(8,128)}, u32[]{:S(2)}) copy-start(f32[4,384,128]{2,1,0:T(8,128)} %copy-done.8) | copy-start | bytes 2359300
  372.2 16.5 %collective-permute-start.29 = (bf16[64,1024]{1,0:T(8,128)(2,1)S(1)}, bf16[64,1024]{1,0:T(8,128)(2,1)S(1)}, u32[]{:S(2)}, u32[]{:S(2)}) collective-permute-start(bf16[64,1024]{1,0:T(8,128)(2,1)S(1)} %shard_map.90), channel_id=1, source_target_pairs={{0,3},{1,0},{2,1},{3,2},{4,7},{5,4},{6,5},{7,6},{8,11},{9,8},{10,9... | collective-permute-start | bytes 393224 | tf_op jit(solution)/shard_map/ppermute | solution.py:732
  375.9 39.1 %collective-permute-start.28 = (bf16[64,1024]{1,0:T(8,128)(2,1)S(1)}, bf16[64,1024]{1,0:T(8,128)(2,1)S(1)}, u32[]{:S(2)}, u32[]{:S(2)}) collective-permute-start(bf16[64,1024]{1,0:T(8,128)(2,1)S(1)} %shard_map.90), channel_id=1, source_target_pairs={{0,2},{1,3},{2,0},{3,1},{4,6},{5,7},{6,4},{7,5},{8,10},{9,11},{10,... | collective-permute-start | bytes 393224 | tf_op jit(solution)/shard_map/ppermute | solution.py:732
  388.7 26.4 %collective-permute-start.27 = (bf16[64,1024]{1,0:T(8,128)(2,1)S(1)}, bf16[64,1024]{1,0:T(8,128)(2,1)S(1)}, u32[]{:S(2)}, u32[]{:S(2)}) collective-permute-start(bf16[64,1024]{1,0:T(8,128)(2,1)S(1)} %shard_map.90), channel_id=1, source_target_pairs={{0,1},{1,2},{2,3},{3,0},{4,5},{5,6},{6,7},{7,4},{8,9},{9,10},{10,1... | collective-permute-start | bytes 393224 | tf_op jit(solution)/shard_map/ppermute | solution.py:732
  400.1 38.6 %slice-start.6 = ((s8[9437184]{0:T(1024)(128)(4,1)}), s8[4194304]{0:T(1024)(128)(4,1)S(1)}, s32[]{:S(2)}) async-start(s8[9437184]{0:T(1024)(128)(4,1)} %bitcast.73), calls=%async_computation.6 | async-start | bytes 8388608
  400.2 38.5 %slice-start.7 = ((s8[9437184]{0:T(1024)(128)(4,1)}), s8[4194304]{0:T(1024)(128)(4,1)S(1)}, s32[]{:S(2)}) async-start(s8[9437184]{0:T(1024)(128)(4,1)} %bitcast.73), calls=%async_computation.7 | async-start | bytes 8388608
  400.2 38.5 %slice-start.8 = ((s8[9437184]{0:T(1024)(128)(4,1)}), s8[1048576]{0:T(1024)(128)(4,1)S(1)}, s32[]{:S(2)}) async-start(s8[9437184]{0:T(1024)(128)(4,1)} %bitcast.73), calls=%async_computation.8 | async-start | bytes 2097152
  415.0 23.7 %copy-start.15 = (f32[4,384,128]{2,1,0:T(8,128)S(1)}, f32[4,384,128]{2,1,0:T(8,128)}, u32[]{:S(2)}) copy-start(f32[4,384,128]{2,1,0:T(8,128)} %get-tuple-element.97) | copy-start | bytes 2359300
  415.0 61.7 %collective-permute-start.23 = (f16[4,384,128]{2,1,0:T(8,128)(2,1)S(1)}, f16[4,384,128]{2,1,0:T(8,128)(2,1)S(1)}, u32[]{:S(2)}, u32[]{:S(2)}) collective-permute-start(f16[4,384,128]{2,1,0:T(8,128)(2,1)S(1)} %get-tuple-element.143), channel_id=1, source_target_pairs={{0,1},{1,2},{2,3},{3,0},{4,5},{5,6},{6,7},{7,4},{8,9},{9,10},{10,1... | collective-permute-start | bytes 1179656 | tf_op jit(solution)/shard_map/ppermute | solution.py:732
  415.1 61.6 %collective-permute-start.22 = (f16[4,384,128]{2,1,0:T(8,128)(2,1)S(1)}, f16[4,384,128]{2,1,0:T(8,128)(2,1)S(1)}, u32[]{:S(2)}, u32[]{:S(2)}) collective-permute-start(f16[4,384,128]{2,1,0:T(8,128)(2,1)S(1)} %get-tuple-element.144), channel_id=1, source_target_pairs={{0,2},{1,3},{2,0},{3,1},{4,6},{5,7},{6,4},{7,5},{8,10},{9,11},{10,... | collective-permute-start | bytes 1179656 | tf_op jit(solution)/shard_map/ppermute | solution.py:732
  434.9 41.8 %collective-permute-start.21 = (f16[4,384,128]{2,1,0:T(8,128)(2,1)S(1)}, f16[4,384,128]{2,1,0:T(8,128)(2,1)S(1)}, u32[]{:S(2)}, u32[]{:S(2)}) collective-permute-start(f16[4,384,128]{2,1,0:T(8,128)(2,1)S(1)} %get-tuple-element.145), channel_id=1, source_target_pairs={{0,3},{1,0},{2,1},{3,2},{4,7},{5,4},{6,5},{7,6},{8,11},{9,8},{10,9... | collective-permute-start | bytes 1179656 | tf_op jit(solution)/shard_map/ppermute | solution.py:732
  440.5 17.2 %copy-start.16 = (f32[4,384,128]{2,1,0:T(8,128)S(1)}, f32[4,384,128]{2,1,0:T(8,128)}, u32[]{:S(2)}) copy-start(f32[4,384,128]{2,1,0:T(8,128)} %get-tuple-element.99) | copy-start | bytes 2359300
  459.5 17.3 %copy-start.14 = (f32[4,384,128]{2,1,0:T(8,128)S(1)}, f32[4,384,128]{2,1,0:T(8,128)}, u32[]{:S(2)}) copy-start(f32[4,384,128]{2,1,0:T(8,128)} %get-tuple-element.105) | copy-start | bytes 2359300

commit v10 on v9

--- a/solution.py
+++ b/solution.py
@@ -842,11 +842,9 @@
         sources.append(added(us[n][0], inward[n], u_top, group))
         total = project(me, group[0], factors, sources[n], total)
 
-    order = [*range(1, chunks), 0]
-    lots = [order[:-1], order[-1:]] if chunks > 1 else [order]
     halves, back = [], {}
-    for lot in lots:
-        halves.append(halved(jnp.concatenate([vs[k][1] for k in lot], axis=1), v_top))
+    for n in range(chunks):
+        halves.append(halved(vs[n][1], v_top))
 
     def returned(n):
         back[n] = passed(halves[n], True)
@@ -854,15 +852,14 @@
     halves[0], total = tie((halves[0], total))
     returned(0)
     near, _, blocks = ladder(total)
-    if len(lots) > 1:
-        returned(1)
+    for n in range(1, chunks):
+        returned(n)
     amplitudes = amplitude(me, factors, pair_weight, near, sources)
     gathered, _ = joined(blocks, near)
     outs = []
-    for n, j, k in [(n, j, k) for n, lot in enumerate(lots) for j, k in enumerate(lot)]:
-        back[n], outs, gathered = tie((back[n], outs, gathered))
-        base = [m[:, j * size : (j + 1) * size] for m in back[n]]
-        base = added(vs[k][0], base, v_top, calls[k])
+    for k in range(chunks):
+        back[k], outs = tie((back[k], outs))
+        base = added(vs[k][0], back[k], v_top, calls[k])
         outs = final(
             me,
             k,

time: 501 us -> 525 us (1.048)
  the two profiles are of different devices: /device:TPU:0 before, /device:TPU:24 now
where the time goes in v10:
time: 525 us; the launch traced here: 518 us
  Pallas kernels  283 us (54%)
  starting transfers between devices  159 us (30%)
  waiting for transfers between devices  30.2 us (6%)
  other arithmetic  26.8 us (5%)
  matrix products  11.4 us (2%)
    ppermute x33, starting transfers between devices, shift(): lax.ppermute(x, 'freq', [(i, (i + by) % parts) for i in range(parts)])  159 us
    pallas_call x4, Pallas kernels, gathered_over(): pl.pallas_call(functools.partial(gather_kernel, chips, parts), out_shape=...  62.2 us
    pallas_call x3, Pallas kernels, final(): pl.pallas_call(functools.partial(final_kernel, nf, parts, len(outs)), out...  51.6 us
    pallas_call x3, Pallas kernels, quarter_pass(): pl.pallas_call(functools.partial(quarter_kernel, nf, parts, sets), out_sh...  46.2 us
    pallas_call x2, Pallas kernels, summed(): pl.pallas_call(functools.partial(sum_kernel, chips), out_shape=jax.ShapeD...  39.4 us
    pallas_call x2, Pallas kernels, again(): pl.pallas_call(functools.partial(again_kernel, own), out_shape=jax.ShapeD...  31.8 us
    ppermute x33, waiting for transfers between devices, shift(): lax.ppermute(x, 'freq', [(i, (i + by) % parts) for i in range(parts)])  30.2 us
    pallas_call x2, Pallas kernels, summed(): pl.pallas_call(functools.partial(reduce_kernel, chips), out_shape=jax.Sha...  22.5 us
  transfers between devices with their start and end apart: 33, of which 3 were waited for; matrix products, arithmetic and copies ran while one was open for 7% of the time, Pallas kernels for 41%

profile of v10, /device:TPU:24, one launch (start us, length us, event | category | flops | bytes accessed | tf_op | source)
XLA Modules:
  0.0 518.1 jit_solution(16155978470900531941)
XLA Ops:
  0.6 1.0 fusion.3
  1.6 0.5 collective-permute-start.2
  2.1 3.4 collective-permute-start
  5.5 10.4 %fusion = f32[4,128,1024]{2,1,0:T(8,128)S(1)} fusion(bf16[4608,1024]{1,0:T(8,128)(2,1)} %l_ref.23, f32[4,4608,128]{2,1,0:T(8,128)} %rest_0_.5), kind=kOutput, calls=%fused_computation | convolution fusion | flops 4834197504 | bytes 20971520 | tf_op jit(solution)/shard_map/pa,fpc->fca/dot_general | solution.py:774
  15.9 20.1 %shard_map.77 = bf16[4,2,64,1024]{3,2,1,0:T(8,128)(2,1)S(1)} custom-call(f32[4,2,64,1024]{3,2,1,0:T(8,128)S(1)} %bitcast.53), custom_call_target="tpu_custom_call" | custom-call | flops 20971520 | bytes 20971520 | tf_op jit(solution)/shard_map/pallas_call | solution.py:684
  36.0 15.8 %shard_map.78 = f32[512,1024]{1,0:T(8,128)S(1)} custom-call(bf16[4608,1024]{1,0:T(8,128)(2,1)} %l_ref.23, f32[4,4608]{1,0:T(4,128)S(1)} %copy-done.10, bf16[512,1024]{1,0:T(8,128)(2,1)S(1)} %bitcast.62, f32[512,1024]{1,0:T(8,128)S(1)} %bitcast.54), custom_call_target="tpu_custom_call" | custom-call | flops 9663676416 | bytes 9437184 | tf_op jit(solution)/shard_map/pallas_call | solution.py:274
  51.8 11.3 %shard_map.79 = bf16[64,1024]{1,0:T(8,128)(2,1)S(1)} custom-call(f32[4,2,64,1024]{3,2,1,0:T(8,128)S(1)} %bitcast.60), custom_call_target="tpu_custom_call" | custom-call | flops 10485760 | bytes 10485760 | tf_op jit(solution)/shard_map/pallas_call | solution.py:675
  63.1 0.7 collective-permute-start.5
  63.8 1.5 collective-permute-start.4
  66.3 2.8 multiply_convert_fusion.18
  69.0 4.0 multiply_convert_fusion
  73.2 0.6 reduce_max.18
  74.5 11.2 %shard_map.80 = (bf16[1,4,2,64,1024]{4,3,2,1,0:T(8,128)(2,1)S(1)}, f32[8,128]{1,0:T(8,128)S(1)}) custom-call(bf16[1,64,1024]{2,1,0:T(8,128)(2,1)S(1)} %bitcast.66), custom_call_target="tpu_custom_call" | custom-call | flops 20971520 | bytes 20971520 | tf_op jit(solution)/shard_map/pallas_call | solution.py:704
  85.7 2.7 collective-permute-start.3
  88.6 0.9 collective-permute-start.7
  89.7 3.0 collective-permute-start.6
  92.8 0.6 collective-permute-start.9
  93.4 1.5 collective-permute-start.10
  94.9 0.9 pad_maximum_fusion.x_ref
  95.9 19.1 %shard_map.81 = (bf16[4,4,2,64,1024]{4,3,2,1,0:T(8,128)(2,1)S(1)}, f32[8,128]{1,0:T(8,128)S(1)}) custom-call(bf16[3,64,1024]{2,1,0:T(8,128)(2,1)S(1)} %pad_maximum_fusion.x_ref, bf16[4,2,64,1024]{3,2,1,0:T(8,128)(2,1)S(1)} %bitcast.64), custom_call_target="tpu_custom_call" | custom-call | flops 62914560 | bytes 62914560 | tf_op jit(solution)/shard_map/pallas_call | solution.py:704
  115.0 2.0 copy-done
  117.0 0.7 reduce_sum.19
  118.5 33.0 %collective-permute-start.11 = (f16[4,384,128]{2,1,0:T(8,128)(2,1)}, f16[4,384,128]{2,1,0:T(8,128)(2,1)S(1)}, u32[]{:S(2)}, u32[]{:S(2)}) collective-permute-start(f16[4,384,128]{2,1,0:T(8,128)(2,1)} %get-tuple-element.61), channel_id=1, source_target_pairs={{0,3},{1,0},{2,1},{3,2},{4,7},{5,4},{6,5},{7,6},{8,11},{9,8},{10,9... | collective-permute-start | bytes 1179656 | tf_op jit(solution)/shard_map/ppermute | solution.py:732
  151.8 2.2 copy-done.1
  153.9 15.4 %shard_map.82 = (f32[4,384,128]{2,1,0:T(8,128)S(1)}, f32[12,384,128]{2,1,0:T(8,128)S(1)}, f32[4,384,128]{2,1,0:T(8,128)}, f32[12,384,128]{2,1,0:T(8,128)}) custom-call(s32[1]{0:T(128)} %bitcast.me_ref, bf16[4608,1024]{1,0:T(8,128)(2,1)} %l_ref.23, f32[16,4608]{1,0:T(8,128)S(1)} %pad_maximum_fusion.2.k_ref, f32[16,4608]{1,0:T(8,128)S(1)} %pad_maximum_fusion.3.wt_ref, ...), custom_call_target="tpu_custom_call" | custom-call | flops 2415919104 | bytes 12582912 | tf_op jit(solution)/shard_map/pallas_call | solution.py:143
  169.8 28.9 %collective-permute-start.20 = (f16[4,384,128]{2,1,0:T(8,128)(2,1)S(1)}, f16[4,384,128]{2,1,0:T(8,128)(2,1)S(1)}, u32[]{:S(2)}, u32[]{:S(2)}) collective-permute-start(f16[4,384,128]{2,1,0:T(8,128)(2,1)S(1)} %get-tuple-element.140), channel_id=1, source_target_pairs={{0,1},{1,2},{2,3},{3,0},{4,5},{5,6},{6,7},{7,4},{8,9},{9,10},{10,1... | collective-permute-start | bytes 1179656 | tf_op jit(solution)/shard_map/ppermute | solution.py:732
  198.7 15.4 %shard_map.83 = (f32[4,384,128]{2,1,0:T(8,128)S(1)}, f32[12,384,128]{2,1,0:T(8,128)S(1)}, f32[4,384,128]{2,1,0:T(8,128)}, f32[12,384,128]{2,1,0:T(8,128)}) custom-call(s32[1]{0:T(128)} %bitcast.me_ref, bf16[4608,1024]{1,0:T(8,128)(2,1)} %l_ref.23, f32[16,4608]{1,0:T(8,128)S(1)} %pad_maximum_fusion.2.k_ref, f32[16,4608]{1,0:T(8,128)S(1)} %pad_maximum_fusion.3.wt_ref, ...), custom_call_target="tpu_custom_call" | custom-call | flops 2415919104 | bytes 12582912 | tf_op jit(solution)/shard_map/pallas_call | solution.py:143
  214.4 0.7 collective-permute-start.18
  215.1 1.1 convert_multiply_fusion.2.rest_1_
  216.1 1.1 convert_multiply_fusion.1.rest_2_
  217.3 15.4 %shard_map.84 = (f32[4,384,128]{2,1,0:T(8,128)S(1)}, f32[12,384,128]{2,1,0:T(8,128)S(1)}, f32[4,384,128]{2,1,0:T(8,128)}, f32[12,384,128]{2,1,0:T(8,128)}) custom-call(s32[1]{0:T(128)} %bitcast.me_ref, bf16[4608,1024]{1,0:T(8,128)(2,1)} %l_ref.23, f32[16,4608]{1,0:T(8,128)S(1)} %pad_maximum_fusion.2.k_ref, f32[16,4608]{1,0:T(8,128)S(1)} %pad_maximum_fusion.3.wt_ref, ...), custom_call_target="tpu_custom_call" | custom-call | flops 2415919104 | bytes 12582912 | tf_op jit(solution)/shard_map/pallas_call | solution.py:143
  233.0 3.4 collective-permute-start.14
  236.4 1.1 collective-permute-start.13
  237.5 1.1 multiply_convert_fusion.21
  238.7 1.2 multiply_convert_fusion.6
  239.9 1.0 collective-permute-start.17
  240.9 0.9 collective-permute-start.16
  241.8 2.0 collective-permute-start.15
  243.7 2.4 multiply_add_fusion.15
  246.3 4.7 shard_map.85.rest_4_
  251.0 11.8 %collective-permute-done.17 = f16[4,384,128]{2,1,0:T(8,128)(2,1)S(1)} collective-permute-done((f16[4,384,128]{2,1,0:T(8,128)(2,1)S(1)}, f16[4,384,128]{2,1,0:T(8,128)(2,1)S(1)}, u32[]{:S(2)}, u32[]{:S(2)}) %collective-permute-start.17) | collective-permute-done | bytes 393248 | tf_op jit(solution)/shard_map/ppermute | solution.py:732
  262.8 35.8 %collective-permute-start.12 = (f16[4,384,128]{2,1,0:T(8,128)(2,1)S(1)}, f16[4,384,128]{2,1,0:T(8,128)(2,1)S(1)}, u32[]{:S(2)}, u32[]{:S(2)}) collective-permute-start(f16[4,384,128]{2,1,0:T(8,128)(2,1)S(1)} %get-tuple-element.148), channel_id=1, source_target_pairs={{0,3},{1,0},{2,1},{3,2},{4,7},{5,4},{6,5},{7,6},{8,11},{9,8},{10,9... | collective-permute-start | bytes 1179656 | tf_op jit(solution)/shard_map/ppermute | solution.py:732
  298.6 5.9 %collective-permute-done.16 = f16[4,384,128]{2,1,0:T(8,128)(2,1)S(1)} collective-permute-done((f16[4,384,128]{2,1,0:T(8,128)(2,1)S(1)}, f16[4,384,128]{2,1,0:T(8,128)(2,1)S(1)}, u32[]{:S(2)}, u32[]{:S(2)}) %collective-permute-start.16) | collective-permute-done | bytes 393248 | tf_op jit(solution)/shard_map/ppermute | solution.py:732
  304.6 2.4 multiply_add_fusion.12
  306.9 4.7 shard_map.86.rest_4_
  311.7 2.4 multiply_add_fusion.9
  314.1 5.3 %shard_map.87.x_ref = f32[512,1024]{1,0:T(8,128)S(1)} custom-call(s32[1]{0:T(128)} %bitcast.me_ref, bf16[4608,1024]{1,0:T(8,128)(2,1)} %l_ref.23, f32[4,384,128]{2,1,0:T(8,128)S(1)} %get-tuple-element.119.rest_0_.rest_8_, f32[4,384,128]{2,1,0:T(8,128)S(1)} %get-tuple-element.118.rest_1_.rest_9_, f32[4,384,128]{2,1,0:T(8,128)S(1)} %get-tuple-element.117.rest_2_.rest_10_, ...), custom_call_target="tpu_custom_call" | custom-call | flops 1610612736 | bytes 6291456 | tf_op jit(solution)/shard_map/pallas_call | solution.py:228
  319.4 19.3 %shard_map.88 = bf16[4,2,64,1024]{3,2,1,0:T(8,128)(2,1)S(1)} custom-call(f32[4,2,64,1024]{3,2,1,0:T(8,128)S(1)} %bitcast.52), custom_call_target="tpu_custom_call" | custom-call | flops 20971520 | bytes 20971520 | tf_op jit(solution)/shard_map/pallas_call | solution.py:684
  338.8 16.0 %shard_map.89 = f32[512,1024]{1,0:T(8,128)S(1)} custom-call(bf16[4608,1024]{1,0:T(8,128)(2,1)} %l_ref.23, f32[4,4608]{1,0:T(4,128)S(1)} %copy-done.10, bf16[512,1024]{1,0:T(8,128)(2,1)S(1)} %bitcast.63, f32[512,1024]{1,0:T(8,128)S(1)} %shard_map.87.x_ref), custom_call_target="tpu_custom_call" | custom-call | flops 9663676416 | bytes 9437184 | tf_op jit(solution)/shard_map/pallas_call | solution.py:274
  354.8 11.3 %shard_map.90 = bf16[64,1024]{1,0:T(8,128)(2,1)S(1)} custom-call(f32[4,2,64,1024]{3,2,1,0:T(8,128)S(1)} %bitcast.61), custom_call_target="tpu_custom_call" | custom-call | flops 10485760 | bytes 10485760 | tf_op jit(solution)/shard_map/pallas_call | solution.py:675
  366.6 3.9 collective-permute-start.21
  370.9 1.5 collective-permute-start.31
  372.5 11.5 %shard_map.91 = (bf16[1,4,2,64,1024]{4,3,2,1,0:T(8,128)(2,1)S(1)}, f32[8,128]{1,0:T(8,128)}) custom-call(bf16[1,64,1024]{2,1,0:T(8,128)(2,1)S(1)} %bitcast.67), custom_call_target="tpu_custom_call" | custom-call | flops 20971520 | bytes 20971520 | tf_op jit(solution)/shard_map/pallas_call | solution.py:704
  384.0 3.1 collective-permute-start.32
  387.2 14.8 %shard_map.92 = f32[4,4608,128]{2,1,0:T(8,128)} custom-call(s32[1]{0:T(128)} %bitcast.me_ref, bf16[4608,1024]{1,0:T(8,128)(2,1)S(1)} %bitcast.45, f32[4,4608]{1,0:T(4,128)S(1)} %copy-done.10, bf16[512,1024]{1,0:T(8,128)(2,1)S(1)} %bitcast.55, f32[4,384,128]{2,1,0:T(8,128)S(1)} %get-tuple-element.127.rest_0_, f32[4,384,128]{2,1,0:T(8,128)S(1)} %get-tuple-element.126.rest_1_, ...), custom_call_target="tpu_custom_call" | custom-call | flops 4831838208 | bytes 18874368 | tf_op jit(solution)/shard_map/pallas_call | solution.py:362
  402.1 1.0 collective-permute-start.25
  403.2 20.4 %shard_map.93 = (bf16[4,4,2,64,1024]{4,3,2,1,0:T(8,128)(2,1)S(1)}, f32[8,128]{1,0:T(8,128)}) custom-call(bf16[3,64,1024]{2,1,0:T(8,128)(2,1)S(1)} %pad_maximum_fusion.1.x_ref, bf16[4,2,64,1024]{3,2,1,0:T(8,128)(2,1)S(1)} %bitcast.56), custom_call_target="tpu_custom_call" | custom-call | flops 62914560 | bytes 62914560 | tf_op jit(solution)/shard_map/pallas_call | solution.py:704
  423.6 3.1 collective-permute-start.29
  426.8 23.5 %collective-permute-start.27 = (f16[4,384,128]{2,1,0:T(8,128)(2,1)S(1)}, f16[4,384,128]{2,1,0:T(8,128)(2,1)S(1)}, u32[]{:S(2)}, u32[]{:S(2)}) collective-permute-start(f16[4,384,128]{2,1,0:T(8,128)(2,1)S(1)} %get-tuple-element.136), channel_id=1, source_target_pairs={{0,3},{1,0},{2,1},{3,2},{4,7},{5,4},{6,5},{7,6},{8,11},{9,8},{10,9... | collective-permute-start | bytes 1179656 | tf_op jit(solution)/shard_map/ppermute | solution.py:732
  450.3 2.5 multiply_add_fusion.6
  452.9 17.2 %shard_map.94.rest_4_ = f32[4,4608,128]{2,1,0:T(8,128)} custom-call(s32[1]{0:T(128)} %bitcast.me_ref, bf16[4608,1024]{1,0:T(8,128)(2,1)S(1)} %bitcast.45, f32[16,4608]{1,0:T(8,128)S(1)} %pad_maximum_fusion.2.k_ref, f32[16,4608]{1,0:T(8,128)S(1)} %pad_maximum_fusion.3.wt_ref, f32[64,16]{1,0:T(8,128)S(1)} %bitcast.68, bf16[2048,1024]{1,0:T(8,128)(2,1)S(1)} %bitcast.49, ...), custom_call_target="tpu_custom_call" | custom-call | flops 6442450944 | bytes 6291456 | tf_op jit(solution)/shard_map/pallas_call | solution.py:439
  470.2 12.4 %collective-permute-done.28 = f16[4,384,128]{2,1,0:T(8,128)(2,1)S(1)} collective-permute-done((f16[4,384,128]{2,1,0:T(8,128)(2,1)S(1)}, f16[4,384,128]{2,1,0:T(8,128)(2,1)S(1)}, u32[]{:S(2)}, u32[]{:S(2)}) %collective-permute-start.28) | collective-permute-done | bytes 393248 | tf_op jit(solution)/shard_map/ppermute | solution.py:732
  483.0 17.2 %shard_map.95.rest_4_ = f32[4,4608,128]{2,1,0:T(8,128)} custom-call(s32[1]{0:T(128)} %bitcast.me_ref, bf16[4608,1024]{1,0:T(8,128)(2,1)S(1)} %bitcast.45, f32[16,4608]{1,0:T(8,128)S(1)} %pad_maximum_fusion.2.k_ref, f32[16,4608]{1,0:T(8,128)S(1)} %pad_maximum_fusion.3.wt_ref, f32[64,16]{1,0:T(8,128)S(1)} %bitcast.69, ...), custom_call_target="tpu_custom_call", output_to_operand_aliasing={{}: (10, {})} | custom-call | flops 6442450944 | bytes 6291456 | tf_op jit(solution)/shard_map/pallas_call | solution.py:439
  500.7 17.2 %shard_map.96 = f32[4,4608,128]{2,1,0:T(8,128)} custom-call(s32[1]{0:T(128)} %bitcast.me_ref, bf16[4608,1024]{1,0:T(8,128)(2,1)S(1)} %bitcast.45, f32[16,4608]{1,0:T(8,128)S(1)} %pad_maximum_fusion.2.k_ref, f32[16,4608]{1,0:T(8,128)S(1)} %pad_maximum_fusion.3.wt_ref, f32[64,16]{1,0:T(8,128)S(1)} %bitcast.70, ...), custom_call_target="tpu_custom_call", output_to_operand_aliasing={{}: (10, {})} | custom-call | flops 6442450944 | bytes 6291456 | tf_op jit(solution)/shard_map/pallas_call | solution.py:439
  (135 shorter events, 5.2 us)
Async XLA Ops:
  1.6 84.1 %collective-permute-start.2 = (f16[2,4,4608]{2,1,0:T(4,128)(2,1)S(1)}, f16[2,4,4608]{2,1,0:T(4,128)(2,1)S(1)}, u32[]{:S(2)}, u32[]{:S(2)}) collective-permute-start(f16[2,4,4608]{2,1,0:T(4,128)(2,1)S(1)} %fusion.3), channel_id=1, source_target_pairs={{0,3},{1,0},{2,1},{3,2},{4,7},{5,4},{6,5},{7,6},{8,11},{9,8},{10,9... | collective-permute-start | bytes 221192 | tf_op jit(solution)/shard_map/ppermute | solution.py:732
  2.1 86.3 %collective-permute-start.1 = (f16[2,4,4608]{2,1,0:T(4,128)(2,1)S(1)}, f16[2,4,4608]{2,1,0:T(4,128)(2,1)S(1)}, u32[]{:S(2)}, u32[]{:S(2)}) collective-permute-start(f16[2,4,4608]{2,1,0:T(4,128)(2,1)S(1)} %fusion.3), channel_id=1, source_target_pairs={{0,2},{1,3},{2,0},{3,1},{4,6},{5,7},{6,4},{7,5},{8,10},{9,11},{10,... | collective-permute-start | bytes 221192 | tf_op jit(solution)/shard_map/ppermute | solution.py:732
  2.1 86.5 %collective-permute-start = (f16[2,4,4608]{2,1,0:T(4,128)(2,1)S(1)}, f16[2,4,4608]{2,1,0:T(4,128)(2,1)S(1)}, u32[]{:S(2)}, u32[]{:S(2)}) collective-permute-start(f16[2,4,4608]{2,1,0:T(4,128)(2,1)S(1)} %fusion.3), channel_id=1, source_target_pairs={{0,1},{1,2},{2,3},{3,0},{4,5},{5,6},{6,7},{7,4},{8,9},{9,10},{10,1... | collective-permute-start | bytes 221192 | tf_op jit(solution)/shard_map/ppermute | solution.py:732
  15.9 20.1 %copy-start.10 = (f32[4,4608]{1,0:T(4,128)S(1)}, f32[4,4608]{1,0:T(4,128)}, u32[]{:S(2)}) copy-start(f32[4,4608]{1,0:T(4,128)} %wt_ref.5) | copy-start | bytes 221188
  51.8 13.6 %copy-start.23 = (f32[16,16]{1,0:T(8,128)S(1)}, f32[16,16]{1,0:T(8,128)}, u32[]{:S(2)}) copy-start(f32[16,16]{1,0:T(8,128)} %param.10) | copy-start | bytes 3076
  51.8 14.0 %copy-start.24 = (f32[16,16]{1,0:T(8,128)S(1)}, f32[16,16]{1,0:T(8,128)}, u32[]{:S(2)}) copy-start(f32[16,16]{1,0:T(8,128)} %param.11) | copy-start | bytes 3076
  63.1 26.5 %collective-permute-start.5 = (bf16[64,1024]{1,0:T(8,128)(2,1)S(1)}, bf16[64,1024]{1,0:T(8,128)(2,1)S(1)}, u32[]{:S(2)}, u32[]{:S(2)}) collective-permute-start(bf16[64,1024]{1,0:T(8,128)(2,1)S(1)} %shard_map.79), channel_id=1, source_target_pairs={{0,3},{1,0},{2,1},{3,2},{4,7},{5,4},{6,5},{7,6},{8,11},{9,8},{10,9... | collective-permute-start | bytes 393224 | tf_op jit(solution)/shard_map/ppermute | solution.py:732
  63.8 29.0 %collective-permute-start.4 = (bf16[64,1024]{1,0:T(8,128)(2,1)S(1)}, bf16[64,1024]{1,0:T(8,128)(2,1)}, u32[]{:S(2)}, u32[]{:S(2)}) collective-permute-start(bf16[64,1024]{1,0:T(8,128)(2,1)S(1)} %shard_map.79), channel_id=1, source_target_pairs={{0,2},{1,3},{2,0},{3,1},{4,6},{5,7},{6,4},{7,5},{8,10},{9,11},{10,... | collective-permute-start | bytes 393224 | tf_op jit(solution)/shard_map/ppermute | solution.py:732
  73.0 19.6 %copy-start.22 = (f32[4,4608]{1,0:T(4,128)S(1)}, f32[4,4608]{1,0:T(4,128)}, u32[]{:S(2)}) copy-start(f32[4,4608]{1,0:T(4,128)} %param.9) | copy-start | bytes 221188
  85.7 7.7 %collective-permute-start.3 = (bf16[64,1024]{1,0:T(8,128)(2,1)S(1)}, bf16[64,1024]{1,0:T(8,128)(2,1)S(1)}, u32[]{:S(2)}, u32[]{:S(2)}) collective-permute-start(bf16[64,1024]{1,0:T(8,128)(2,1)S(1)} %shard_map.79), channel_id=1, source_target_pairs={{0,1},{1,2},{2,3},{3,0},{4,5},{5,6},{6,7},{7,4},{8,9},{9,10},{10,1... | collective-permute-start | bytes 393224 | tf_op jit(solution)/shard_map/ppermute | solution.py:732
  88.4 30.0 %collective-permute-start.8 = (f16[4,768,128]{2,1,0:T(8,128)(2,1)}, f16[4,768,128]{2,1,0:T(8,128)(2,1)S(1)}, u32[]{:S(2)}, u32[]{:S(2)}) collective-permute-start(f16[4,768,128]{2,1,0:T(8,128)(2,1)} %get-tuple-element.131), channel_id=1, source_target_pairs={{0,3},{1,0},{2,1},{3,2},{4,7},{5,4},{6,5},{7,6},{8,11},{9,8},{10,9... | collective-permute-start | bytes 2359304 | tf_op jit(solution)/shard_map/ppermute | solution.py:732
  88.6 63.0 %collective-permute-start.7 = (f16[4,768,128]{2,1,0:T(8,128)(2,1)}, f16[4,768,128]{2,1,0:T(8,128)(2,1)S(1)}, u32[]{:S(2)}, u32[]{:S(2)}) collective-permute-start(f16[4,768,128]{2,1,0:T(8,128)(2,1)} %get-tuple-element.132), channel_id=1, source_target_pairs={{0,2},{1,3},{2,0},{3,1},{4,6},{5,7},{6,4},{7,5},{8,10},{9,11},{10,... | collective-permute-start | bytes 2359304 | tf_op jit(solution)/shard_map/ppermute | solution.py:732
  89.7 62.0 %collective-permute-start.6 = (f16[4,768,128]{2,1,0:T(8,128)(2,1)}, f16[4,768,128]{2,1,0:T(8,128)(2,1)S(1)}, u32[]{:S(2)}, u32[]{:S(2)}) collective-permute-start(f16[4,768,128]{2,1,0:T(8,128)(2,1)} %get-tuple-element.133), channel_id=1, source_target_pairs={{0,1},{1,2},{2,3},{3,0},{4,5},{5,6},{6,7},{7,4},{8,9},{9,10},{10,1... | collective-permute-start | bytes 2359304 | tf_op jit(solution)/shard_map/ppermute | solution.py:732
  92.8 121.6 %collective-permute-start.9 = (f16[4,384,128]{2,1,0:T(8,128)(2,1)}, f16[4,384,128]{2,1,0:T(8,128)(2,1)}, u32[]{:S(2)}, u32[]{:S(2)}) collective-permute-start(f16[4,384,128]{2,1,0:T(8,128)(2,1)} %get-tuple-element.59), channel_id=1, source_target_pairs={{0,1},{1,2},{2,3},{3,0},{4,5},{5,6},{6,7},{7,4},{8,9},{9,10},{10,1... | collective-permute-start | bytes 1179656 | tf_op jit(solution)/shard_map/ppermute | solution.py:732
  93.4 121.7 %collective-permute-start.10 = (f16[4,384,128]{2,1,0:T(8,128)(2,1)}, f16[4,384,128]{2,1,0:T(8,128)(2,1)}, u32[]{:S(2)}, u32[]{:S(2)}) collective-permute-start(f16[4,384,128]{2,1,0:T(8,128)(2,1)} %get-tuple-element.60), channel_id=1, source_target_pairs={{0,2},{1,3},{2,0},{3,1},{4,6},{5,7},{6,4},{7,5},{8,10},{9,11},{10,... | collective-permute-start | bytes 1179656 | tf_op jit(solution)/shard_map/ppermute | solution.py:732
  115.0 2.0 copy-start
  118.5 96.6 %collective-permute-start.11 = (f16[4,384,128]{2,1,0:T(8,128)(2,1)}, f16[4,384,128]{2,1,0:T(8,128)(2,1)S(1)}, u32[]{:S(2)}, u32[]{:S(2)}) collective-permute-start(f16[4,384,128]{2,1,0:T(8,128)(2,1)} %get-tuple-element.61), channel_id=1, source_target_pairs={{0,3},{1,0},{2,1},{3,2},{4,7},{5,4},{6,5},{7,6},{8,11},{9,8},{10,9... | collective-permute-start | bytes 1179656 | tf_op jit(solution)/shard_map/ppermute | solution.py:732
  151.7 2.2 copy-start.1
  169.8 70.0 %collective-permute-start.20 = (f16[4,384,128]{2,1,0:T(8,128)(2,1)S(1)}, f16[4,384,128]{2,1,0:T(8,128)(2,1)S(1)}, u32[]{:S(2)}, u32[]{:S(2)}) collective-permute-start(f16[4,384,128]{2,1,0:T(8,128)(2,1)S(1)} %get-tuple-element.140), channel_id=1, source_target_pairs={{0,1},{1,2},{2,3},{3,0},{4,5},{5,6},{6,7},{7,4},{8,9},{9,10},{10,1... | collective-permute-start | bytes 1179656 | tf_op jit(solution)/shard_map/ppermute | solution.py:732
  198.7 42.1 %collective-permute-start.19 = (f16[4,384,128]{2,1,0:T(8,128)(2,1)S(1)}, f16[4,384,128]{2,1,0:T(8,128)(2,1)S(1)}, u32[]{:S(2)}, u32[]{:S(2)}) collective-permute-start(f16[4,384,128]{2,1,0:T(8,128)(2,1)S(1)} %get-tuple-element.141), channel_id=1, source_target_pairs={{0,2},{1,3},{2,0},{3,1},{4,6},{5,7},{6,4},{7,5},{8,10},{9,11},{10,... | collective-permute-start | bytes 1179656 | tf_op jit(solution)/shard_map/ppermute | solution.py:732
  214.4 27.4 %collective-permute-start.18 = (f16[4,384,128]{2,1,0:T(8,128)(2,1)S(1)}, f16[4,384,128]{2,1,0:T(8,128)(2,1)S(1)}, u32[]{:S(2)}, u32[]{:S(2)}) collective-permute-start(f16[4,384,128]{2,1,0:T(8,128)(2,1)S(1)} %get-tuple-element.142), channel_id=1, source_target_pairs={{0,3},{1,0},{2,1},{3,2},{4,7},{5,4},{6,5},{7,6},{8,11},{9,8},{10,9... | collective-permute-start | bytes 1179656 | tf_op jit(solution)/shard_map/ppermute | solution.py:732
  232.7 4.8 copy-start.12
  233.0 5.7 %copy-start.13 = (f32[12,384,128]{2,1,0:T(8,128)S(1)}, f32[12,384,128]{2,1,0:T(8,128)}, u32[]{:S(2)}) copy-start(f32[12,384,128]{2,1,0:T(8,128)} %get-tuple-element.86) | copy-start | bytes 7077892
  233.0 78.6 %collective-permute-start.14 = (f16[4,384,128]{2,1,0:T(8,128)(2,1)S(1)}, f16[4,384,128]{2,1,0:T(8,128)(2,1)S(1)}, u32[]{:S(2)}, u32[]{:S(2)}) collective-permute-start(f16[4,384,128]{2,1,0:T(8,128)(2,1)S(1)} %get-tuple-element.146), channel_id=1, source_target_pairs={{0,1},{1,2},{2,3},{3,0},{4,5},{5,6},{6,7},{7,4},{8,9},{9,10},{10,1... | collective-permute-start | bytes 1179656 | tf_op jit(solution)/shard_map/ppermute | solution.py:732
  236.4 75.2 %collective-permute-start.13 = (f16[4,384,128]{2,1,0:T(8,128)(2,1)S(1)}, f16[4,384,128]{2,1,0:T(8,128)(2,1)S(1)}, u32[]{:S(2)}, u32[]{:S(2)}) collective-permute-start(f16[4,384,128]{2,1,0:T(8,128)(2,1)S(1)} %get-tuple-element.147), channel_id=1, source_target_pairs={{0,2},{1,3},{2,0},{3,1},{4,6},{5,7},{6,4},{7,5},{8,10},{9,11},{10,... | collective-permute-start | bytes 1179656 | tf_op jit(solution)/shard_map/ppermute | solution.py:732
  239.9 22.9 %collective-permute-start.17 = (f16[4,384,128]{2,1,0:T(8,128)(2,1)S(1)}, f16[4,384,128]{2,1,0:T(8,128)(2,1)S(1)}, u32[]{:S(2)}, u32[]{:S(2)}) collective-permute-start(f16[4,384,128]{2,1,0:T(8,128)(2,1)S(1)} %get-tuple-element.143), channel_id=1, source_target_pairs={{0,1},{1,2},{2,3},{3,0},{4,5},{5,6},{6,7},{7,4},{8,9},{9,10},{10,1... | collective-permute-start | bytes 1179656 | tf_op jit(solution)/shard_map/ppermute | solution.py:732
  240.9 63.7 %collective-permute-start.16 = (f16[4,384,128]{2,1,0:T(8,128)(2,1)S(1)}, f16[4,384,128]{2,1,0:T(8,128)(2,1)S(1)}, u32[]{:S(2)}, u32[]{:S(2)}) collective-permute-start(f16[4,384,128]{2,1,0:T(8,128)(2,1)S(1)} %get-tuple-element.144), channel_id=1, source_target_pairs={{0,2},{1,3},{2,0},{3,1},{4,6},{5,7},{6,4},{7,5},{8,10},{9,11},{10,... | collective-permute-start | bytes 1179656 | tf_op jit(solution)/shard_map/ppermute | solution.py:732
  241.8 62.8 %collective-permute-start.15 = (f16[4,384,128]{2,1,0:T(8,128)(2,1)S(1)}, f16[4,384,128]{2,1,0:T(8,128)(2,1)S(1)}, u32[]{:S(2)}, u32[]{:S(2)}) collective-permute-start(f16[4,384,128]{2,1,0:T(8,128)(2,1)S(1)} %get-tuple-element.145), channel_id=1, source_target_pairs={{0,3},{1,0},{2,1},{3,2},{4,7},{5,4},{6,5},{7,6},{8,11},{9,8},{10,9... | collective-permute-start | bytes 1179656 | tf_op jit(solution)/shard_map/ppermute | solution.py:732
  262.8 48.8 %collective-permute-start.12 = (f16[4,384,128]{2,1,0:T(8,128)(2,1)S(1)}, f16[4,384,128]{2,1,0:T(8,128)(2,1)S(1)}, u32[]{:S(2)}, u32[]{:S(2)}) collective-permute-start(f16[4,384,128]{2,1,0:T(8,128)(2,1)S(1)} %get-tuple-element.148), channel_id=1, source_target_pairs={{0,3},{1,0},{2,1},{3,2},{4,7},{5,4},{6,5},{7,6},{8,11},{9,8},{10,9... | collective-permute-start | bytes 1179656 | tf_op jit(solution)/shard_map/ppermute | solution.py:732
  314.1 5.3 %copy-start.2 = (f32[4,384,128]{2,1,0:T(8,128)}, f32[4,384,128]{2,1,0:T(8,128)S(1)}, u32[]{:S(2)}) copy-start(f32[4,384,128]{2,1,0:T(8,128)S(1)} %get-tuple-element.116.rest_3_.rest_11_) | copy-start | bytes 2359300
  314.1 5.3 %copy-start.4 = (f32[4,384,128]{2,1,0:T(8,128)}, f32[4,384,128]{2,1,0:T(8,128)S(1)}, u32[]{:S(2)}) copy-start(f32[4,384,128]{2,1,0:T(8,128)S(1)} %get-tuple-element.117.rest_2_.rest_10_) | copy-start | bytes 2359300
  314.1 5.3 %copy-start.6 = (f32[4,384,128]{2,1,0:T(8,128)}, f32[4,384,128]{2,1,0:T(8,128)S(1)}, u32[]{:S(2)}) copy-start(f32[4,384,128]{2,1,0:T(8,128)S(1)} %get-tuple-element.118.rest_1_.rest_9_) | copy-start | bytes 2359300
  314.1 5.3 %copy-start.8 = (f32[4,384,128]{2,1,0:T(8,128)}, f32[4,384,128]{2,1,0:T(8,128)S(1)}, u32[]{:S(2)}) copy-start(f32[4,384,128]{2,1,0:T(8,128)S(1)} %get-tuple-element.119.rest_0_.rest_8_) | copy-start | bytes 2359300
  338.7 48.4 %slice-start = ((s8[9437184]{0:T(1024)(128)(4,1)}), s8[4194304]{0:T(1024)(128)(4,1)S(1)}, s32[]{:S(2)}) async-start(s8[9437184]{0:T(1024)(128)(4,1)} %bitcast.44), calls=%async_computation | async-start | bytes 8388608
  338.7 27.5 %copy-start.11 = (f32[12,384,128]{2,1,0:T(8,128)S(1)}, f32[12,384,128]{2,1,0:T(8,128)}, u32[]{:S(2)}) copy-start(f32[12,384,128]{2,1,0:T(8,128)} %get-tuple-element.88) | copy-start | bytes 7077892
  338.8 48.4 %slice-start.1 = ((s8[9437184]{0:T(1024)(128)(4,1)}), s8[4194304]{0:T(1024)(128)(4,1)S(1)}, s32[]{:S(2)}) async-start(s8[9437184]{0:T(1024)(128)(4,1)} %bitcast.44), calls=%async_computation.1 | async-start | bytes 8388608
  338.8 48.3 %slice-start.2 = ((s8[9437184]{0:T(1024)(128)(4,1)}), s8[1048576]{0:T(1024)(128)(4,1)S(1)}, s32[]{:S(2)}) async-start(s8[9437184]{0:T(1024)(128)(4,1)} %bitcast.44), calls=%async_computation.2 | async-start | bytes 2097152
  354.8 15.7 %copy-start.21 = (f16[4,384,128]{2,1,0:T(8,128)(2,1)S(1)}, f16[4,384,128]{2,1,0:T(8,128)(2,1)}, u32[]{:S(2)}) copy-start(f16[4,384,128]{2,1,0:T(8,128)(2,1)} %get-tuple-element.90) | copy-start | bytes 1179652
  354.8 16.1 %copy-start.20 = (f16[4,384,128]{2,1,0:T(8,128)(2,1)S(1)}, f16[4,384,128]{2,1,0:T(8,128)(2,1)}, u32[]{:S(2)}) copy-start(f16[4,384,128]{2,1,0:T(8,128)(2,1)} %get-tuple-element.91) | copy-start | bytes 1179652
  366.1 17.9 %copy-start.19 = (f16[4,384,128]{2,1,0:T(8,128)(2,1)S(1)}, f16[4,384,128]{2,1,0:T(8,128)(2,1)}, u32[]{:S(2)}) copy-start(f16[4,384,128]{2,1,0:T(8,128)(2,1)} %get-tuple-element.92) | copy-start | bytes 1179652
  366.1 21.0 %copy-start.3 = (f32[4,384,128]{2,1,0:T(8,128)S(1)}, f32[4,384,128]{2,1,0:T(8,128)}, u32[]{:S(2)}) copy-start(f32[4,384,128]{2,1,0:T(8,128)} %copy-done.2) | copy-start | bytes 2359300
  366.1 21.0 %copy-start.5 = (f32[4,384,128]{2,1,0:T(8,128)S(1)}, f32[4,384,128]{2,1,0:T(8,128)}, u32[]{:S(2)}) copy-start(f32[4,384,128]{2,1,0:T(8,128)} %copy-done.4) | copy-start | bytes 2359300
  366.1 21.0 %copy-start.7 = (f32[4,384,128]{2,1,0:T(8,128)S(1)}, f32[4,384,128]{2,1,0:T(8,128)}, u32[]{:S(2)}) copy-start(f32[4,384,128]{2,1,0:T(8,128)} %copy-done.6) | copy-start | bytes 2359300
  366.1 21.0 %copy-start.9 = (f32[4,384,128]{2,1,0:T(8,128)S(1)}, f32[4,384,128]{2,1,0:T(8,128)}, u32[]{:S(2)}) copy-start(f32[4,384,128]{2,1,0:T(8,128)} %copy-done.8) | copy-start | bytes 2359300
  366.1 17.8 %collective-permute-start.23 = (bf16[64,1024]{1,0:T(8,128)(2,1)S(1)}, bf16[64,1024]{1,0:T(8,128)(2,1)S(1)}, u32[]{:S(2)}, u32[]{:S(2)}) collective-permute-start(bf16[64,1024]{1,0:T(8,128)(2,1)S(1)} %shard_map.90), channel_id=1, source_target_pairs={{0,3},{1,0},{2,1},{3,2},{4,7},{5,4},{6,5},{7,6},{8,11},{9,8},{10,9... | collective-permute-start | bytes 393224 | tf_op jit(solution)/shard_map/ppermute | solution.py:732
  366.5 35.5 %collective-permute-start.22 = (bf16[64,1024]{1,0:T(8,128)(2,1)S(1)}, bf16[64,1024]{1,0:T(8,128)(2,1)S(1)}, u32[]{:S(2)}, u32[]{:S(2)}) collective-permute-start(bf16[64,1024]{1,0:T(8,128)(2,1)S(1)} %shard_map.90), channel_id=1, source_target_pairs={{0,2},{1,3},{2,0},{3,1},{4,6},{5,7},{6,4},{7,5},{8,10},{9,11},{10,... | collective-permute-start | bytes 393224 | tf_op jit(solution)/shard_map/ppermute | solution.py:732
  366.6 35.5 %collective-permute-start.21 = (bf16[64,1024]{1,0:T(8,128)(2,1)S(1)}, bf16[64,1024]{1,0:T(8,128)(2,1)S(1)}, u32[]{:S(2)}, u32[]{:S(2)}) collective-permute-start(bf16[64,1024]{1,0:T(8,128)(2,1)S(1)} %shard_map.90), channel_id=1, source_target_pairs={{0,1},{1,2},{2,3},{3,0},{4,5},{5,6},{6,7},{7,4},{8,9},{9,10},{10,1... | collective-permute-start | bytes 393224 | tf_op jit(solution)/shard_map/ppermute | solution.py:732
  370.4 53.2 %collective-permute-start.30 = (f16[4,384,128]{2,1,0:T(8,128)(2,1)S(1)}, f16[4,384,128]{2,1,0:T(8,128)(2,1)S(1)}, u32[]{:S(2)}, u32[]{:S(2)}) collective-permute-start(f16[4,384,128]{2,1,0:T(8,128)(2,1)S(1)} %copy-done.21), channel_id=1, source_target_pairs={{0,3},{1,0},{2,1},{3,2},{4,7},{5,4},{6,5},{7,6},{8,11},{9,8},{10,9... | collective-permute-start | bytes 1179656 | tf_op jit(solution)/shard_map/ppermute | solution.py:732
  370.9 55.8 %collective-permute-start.31 = (f16[4,384,128]{2,1,0:T(8,128)(2,1)S(1)}, f16[4,384,128]{2,1,0:T(8,128)(2,1)S(1)}, u32[]{:S(2)}, u32[]{:S(2)}) collective-permute-start(f16[4,384,128]{2,1,0:T(8,128)(2,1)S(1)} %copy-done.20), channel_id=1, source_target_pairs={{0,2},{1,3},{2,0},{3,1},{4,6},{5,7},{6,4},{7,5},{8,10},{9,11},{10,... | collective-permute-start | bytes 1179656 | tf_op jit(solution)/shard_map/ppermute | solution.py:732
  384.0 42.8 %collective-permute-start.32 = (f16[4,384,128]{2,1,0:T(8,128)(2,1)S(1)}, f16[4,384,128]{2,1,0:T(8,128)(2,1)S(1)}, u32[]{:S(2)}, u32[]{:S(2)}) collective-permute-start(f16[4,384,128]{2,1,0:T(8,128)(2,1)S(1)} %copy-done.19), channel_id=1, source_target_pairs={{0,1},{1,2},{2,3},{3,0},{4,5},{5,6},{6,7},{7,4},{8,9},{9,10},{10,1... | collective-permute-start | bytes 1179656 | tf_op jit(solution)/shard_map/ppermute | solution.py:732
  387.2 14.8 %copy-start.18 = (f16[4,384,128]{2,1,0:T(8,128)(2,1)S(1)}, f16[4,384,128]{2,1,0:T(8,128)(2,1)}, u32[]{:S(2)}) copy-start(f16[4,384,128]{2,1,0:T(8,128)(2,1)} %get-tuple-element.137) | copy-start | bytes 1179652
  387.2 14.9 %copy-start.17 = (f16[4,384,128]{2,1,0:T(8,128)(2,1)S(1)}, f16[4,384,128]{2,1,0:T(8,128)(2,1)}, u32[]{:S(2)}) copy-start(f16[4,384,128]{2,1,0:T(8,128)(2,1)} %get-tuple-element.138) | copy-start | bytes 1179652
  402.0 48.4 %copy-start.16 = (f32[4,384,128]{2,1,0:T(8,128)S(1)}, f32[4,384,128]{2,1,0:T(8,128)}, u32[]{:S(2)}) copy-start(f32[4,384,128]{2,1,0:T(8,128)} %get-tuple-element.89) | copy-start | bytes 2359300
  402.0 98.2 %collective-permute-start.26 = (f16[4,384,128]{2,1,0:T(8,128)(2,1)S(1)}, f16[4,384,128]{2,1,0:T(8,128)(2,1)S(1)}, u32[]{:S(2)}, u32[]{:S(2)}) collective-permute-start(f16[4,384,128]{2,1,0:T(8,128)(2,1)S(1)} %copy-done.18), channel_id=1, source_target_pairs={{0,1},{1,2},{2,3},{3,0},{4,5},{5,6},{6,7},{7,4},{8,9},{9,10},{10,1... | collective-permute-start | bytes 1179656 | tf_op jit(solution)/shard_map/ppermute | solution.py:732
  402.1 98.2 %collective-permute-start.25 = (f16[4,384,128]{2,1,0:T(8,128)(2,1)S(1)}, f16[4,384,128]{2,1,0:T(8,128)(2,1)S(1)}, u32[]{:S(2)}, u32[]{:S(2)}) collective-permute-start(f16[4,384,128]{2,1,0:T(8,128)(2,1)S(1)} %copy-done.17), channel_id=1, source_target_pairs={{0,2},{1,3},{2,0},{3,1},{4,6},{5,7},{6,4},{7,5},{8,10},{9,11},{10,... | collective-permute-start | bytes 1179656 | tf_op jit(solution)/shard_map/ppermute | solution.py:732
  423.6 46.5 %collective-permute-start.29 = (f16[4,384,128]{2,1,0:T(8,128)(2,1)S(1)}, f16[4,384,128]{2,1,0:T(8,128)(2,1)S(1)}, u32[]{:S(2)}, u32[]{:S(2)}) collective-permute-start(f16[4,384,128]{2,1,0:T(8,128)(2,1)S(1)} %get-tuple-element.134), channel_id=1, source_target_pairs={{0,1},{1,2},{2,3},{3,0},{4,5},{5,6},{6,7},{7,4},{8,9},{9,10},{10,1... | collective-permute-start | bytes 1179656 | tf_op jit(solution)/shard_map/ppermute | solution.py:732
  426.7 55.8 %collective-permute-start.28 = (f16[4,384,128]{2,1,0:T(8,128)(2,1)S(1)}, f16[4,384,128]{2,1,0:T(8,128)(2,1)S(1)}, u32[]{:S(2)}, u32[]{:S(2)}) collective-permute-start(f16[4,384,128]{2,1,0:T(8,128)(2,1)S(1)} %get-tuple-element.135), channel_id=1, source_target_pairs={{0,2},{1,3},{2,0},{3,1},{4,6},{5,7},{6,4},{7,5},{8,10},{9,11},{10,... | collective-permute-start | bytes 1179656 | tf_op jit(solution)/shard_map/ppermute | solution.py:732
  426.8 55.8 %collective-permute-start.27 = (f16[4,384,128]{2,1,0:T(8,128)(2,1)S(1)}, f16[4,384,128]{2,1,0:T(8,128)(2,1)S(1)}, u32[]{:S(2)}, u32[]{:S(2)}) collective-permute-start(f16[4,384,128]{2,1,0:T(8,128)(2,1)S(1)} %get-tuple-element.136), channel_id=1, source_target_pairs={{0,3},{1,0},{2,1},{3,2},{4,7},{5,4},{6,5},{7,6},{8,11},{9,8},{10,9... | collective-permute-start | bytes 1179656 | tf_op jit(solution)/shard_map/ppermute | solution.py:732
  450.3 32.2 %slice-start.3 = ((s8[9437184]{0:T(1024)(128)(4,1)}), s8[4194304]{0:T(1024)(128)(4,1)S(1)}, s32[]{:S(2)}) async-start(s8[9437184]{0:T(1024)(128)(4,1)} %bitcast.71), calls=%async_computation.3 | async-start | bytes 8388608
  452.8 29.7 %slice-start.4 = ((s8[9437184]{0:T(1024)(128)(4,1)}), s8[4194304]{0:T(1024)(128)(4,1)S(1)}, s32[]{:S(2)}) async-start(s8[9437184]{0:T(1024)(128)(4,1)} %bitcast.71), calls=%async_computation.4 | async-start | bytes 8388608
  452.8 29.7 %slice-start.5 = ((s8[9437184]{0:T(1024)(128)(4,1)}), s8[1048576]{0:T(1024)(128)(4,1)S(1)}, s32[]{:S(2)}) async-start(s8[9437184]{0:T(1024)(128)(4,1)} %bitcast.71), calls=%async_computation.5 | async-start | bytes 2097152
  452.9 29.7 %copy-start.14 = (f32[4,384,128]{2,1,0:T(8,128)S(1)}, f32[4,384,128]{2,1,0:T(8,128)}, u32[]{:S(2)}) copy-start(f32[4,384,128]{2,1,0:T(8,128)} %get-tuple-element.87) | copy-start | bytes 2359300
  470.1 30.2 %collective-permute-start.24 = (f16[4,384,128]{2,1,0:T(8,128)(2,1)S(1)}, f16[4,384,128]{2,1,0:T(8,128)(2,1)S(1)}, u32[]{:S(2)}, u32[]{:S(2)}) collective-permute-start(f16[4,384,128]{2,1,0:T(8,128)(2,1)S(1)} %get-tuple-element.139), channel_id=1, source_target_pairs={{0,3},{1,0},{2,1},{3,2},{4,7},{5,4},{6,5},{7,6},{8,11},{9,8},{10,9... | collective-permute-start | bytes 1179656 | tf_op jit(solution)/shard_map/ppermute | solution.py:732
  483.0 17.3 %copy-start.15 = (f32[4,384,128]{2,1,0:T(8,128)S(1)}, f32[4,384,128]{2,1,0:T(8,128)}, u32[]{:S(2)}) copy-start(f32[4,384,128]{2,1,0:T(8,128)} %get-tuple-element.85) | copy-start | bytes 2359300

commit v11 on v10

--- a/solution.py
+++ b/solution.py
@@ -236,7 +236,7 @@
             + [resident(total)],
             out_specs=pl.BlockSpec(total.shape, lambda i, m: (0, 0)),
         ),
-        compiler_params=pltpu.CompilerParams(vmem_limit_bytes=40 << 20),
+        compiler_params=pltpu.CompilerParams(vmem_limit_bytes=18 << 20),
         cost_estimate=pl.CostEstimate(
             flops=2 * own * parts * size * cols * naux,
             bytes_accessed=8 * own * parts * size * cols,
@@ -282,7 +282,7 @@
             resident(kept),
         ],
         out_specs=pl.BlockSpec(kept.shape, lambda i: (0, 0)),
-        compiler_params=pltpu.CompilerParams(vmem_limit_bytes=40 << 20),
+        compiler_params=pltpu.CompilerParams(vmem_limit_bytes=18 << 20),
         cost_estimate=pl.CostEstimate(
             flops=4 * kept.size * pairs, bytes_accessed=2 * factors.size, transcendentals=0
         ),
@@ -374,7 +374,7 @@
             out_specs=pl.BlockSpec((own, size, cols), lambda i, m: (0, at(i, m), 0)),
             scratch_shapes=stream_scratch(own, size, cols),
         ),
-        compiler_params=pltpu.CompilerParams(vmem_limit_bytes=20 << 20),
+        compiler_params=pltpu.CompilerParams(vmem_limit_bytes=13 << 20),
         cost_estimate=pl.CostEstimate(
             flops=2 * own * pairs * cols * naux,
             bytes_accessed=8 * own * pairs * cols,
@@ -459,7 +459,7 @@
             + stream_scratch(own, size, cols),
         ),
         input_output_aliases={6 + parts + n: n for n in range(len(outs))},
-        compiler_params=pltpu.CompilerParams(vmem_limit_bytes=26 << 20),
+        compiler_params=pltpu.CompilerParams(vmem_limit_bytes=18 << 20),
         cost_estimate=pl.CostEstimate(
             flops=2 * nf * parts * span * cols * naux,
             bytes_accessed=8 * own * parts * span * cols,
@@ -545,15 +545,12 @@
     plane.end()
 
 
-def sum_kernel(chips, x_ref, o_ref, near, red, land, mine, joined, *sems):
+def sum_kernel(chips, x_ref, o_ref, near, red, land, joined, *sems):
     plane = Plane(chips)
     chip, core = plane.chip, plane.core
     plane.greet()
-    reduced(plane, x_ref, near, red, land, mine, sems[0:2], sems[2:4])
     here = joined.at[chip, core]
-    keep = pltpu.make_async_copy(mine, here, sems[8])
-    keep.start()
-    keep.wait()
+    reduced(plane, x_ref, near, red, land, here, sems[0:2], sems[2:4])
     wides = [plane.send(here, here, sems[4:6], d, plane.at(d)) for d in range(1, chips)]
     pairs = [plane.send(here, here, sems[6:8], 0, plane.pal)]
     for d, copy in enumerate(wides, 1):
@@ -687,9 +684,8 @@
         in_specs=[WHOLE],
         out_specs=WHOLE,
         scratch_shapes=landing
-        + [VMEM((block, width), jnp.bfloat16), VMEM(flat, jnp.bfloat16)]
-        + dmas(chips, 4)
-        + [pltpu.SemaphoreType.DMA],
+        + [VMEM(flat, jnp.bfloat16)]
+        + dmas(chips, 4),
         compiler_params=reach_params(0),
         cost_estimate=reach_cost(x.size),
     )(x.reshape(flat))

time: 525 us -> 515 us (0.981)
  other arithmetic: 26.8 us -> 17.2 us
  Pallas kernels: 283 us -> 274 us
  waiting for transfers between devices: 30.2 us -> 37 us
    add x6, other arithmetic: 10.4 us -> 2.39 us  [added(): sliced(right_late, s, *group) + b]
    ppermute x33, waiting for transfers between devices: 30.2 us -> 37 us  [shift(): lax.ppermute(x, 'freq', [(i, (i + by) % parts) for i in range(parts)])]
    pallas_call x3, Pallas kernels: 14.6 us -> 9.18 us  [project(): pl.pallas_call(functools.partial(project_kernel, parts, sets), out_shape=...]
  transfers between devices with their start and end apart: 33 -> 33, of which waited for: 3 -> 3; matrix products, arithmetic and copies ran while one was open for 7% -> 6% of each run, Pallas kernels for 41% -> 41%
where the time goes in v11:
time: 515 us; the launch traced here: 508 us
  Pallas kernels  274 us (53%)
  starting transfers between devices  159 us (31%)
  waiting for transfers between devices  37 us (7%)
  other arithmetic  17.2 us (3%)
  matrix products  12.6 us (2%)
    ppermute x33, starting transfers between devices, shift(): lax.ppermute(x, 'freq', [(i, (i + by) % parts) for i in range(parts)])  159 us
    pallas_call x4, Pallas kernels, gathered_over(): pl.pallas_call(functools.partial(gather_kernel, chips, parts), out_shape=...  62.2 us
    pallas_call x3, Pallas kernels, final(): pl.pallas_call(functools.partial(final_kernel, nf, parts, len(outs)), out...  51.6 us
    pallas_call x3, Pallas kernels, quarter_pass(): pl.pallas_call(functools.partial(quarter_kernel, nf, parts, sets), out_sh...  46.4 us
    pallas_call x2, Pallas kernels, summed(): pl.pallas_call(functools.partial(sum_kernel, chips), out_shape=jax.ShapeD...  39 us
    ppermute x33, waiting for transfers between devices, shift(): lax.ppermute(x, 'freq', [(i, (i + by) % parts) for i in range(parts)])  37 us
    pallas_call x2, Pallas kernels, again(): pl.pallas_call(functools.partial(again_kernel, own), out_shape=jax.ShapeD...  28.7 us
    pallas_call x2, Pallas kernels, summed(): pl.pallas_call(functools.partial(reduce_kernel, chips), out_shape=jax.Sha...  22.5 us
  transfers between devices with their start and end apart: 33, of which 3 were waited for; matrix products, arithmetic and copies ran while one was open for 6% of the time, Pallas kernels for 41%

profile of v11, /device:TPU:24, one launch (start us, length us, event | category | flops | bytes accessed | tf_op | source)
XLA Modules:
  0.0 508.2 jit_solution(11884960947445118989)
XLA Ops:
  0.6 1.0 fusion.3
  1.6 0.5 collective-permute-start.2
  2.1 3.4 collective-permute-start
  5.5 11.6 %fusion = f32[4,128,1024]{2,1,0:T(8,128)S(1)} fusion(bf16[4608,1024]{1,0:T(8,128)(2,1)} %l_ref.23, f32[4,4608,128]{2,1,0:T(8,128)} %rest_0_.5), kind=kOutput, calls=%fused_computation | convolution fusion | flops 4834197504 | bytes 20971520 | tf_op jit(solution)/shard_map/pa,fpc->fca/dot_general | solution.py:770
  17.1 19.8 %shard_map.77 = bf16[4,2,64,1024]{3,2,1,0:T(8,128)(2,1)S(1)} custom-call(f32[4,2,64,1024]{3,2,1,0:T(8,128)S(1)} %bitcast.53), custom_call_target="tpu_custom_call" | custom-call | flops 20971520 | bytes 20971520 | tf_op jit(solution)/shard_map/pallas_call | solution.py:681
  37.0 14.4 %shard_map.78 = f32[512,1024]{1,0:T(8,128)S(1)} custom-call(bf16[4608,1024]{1,0:T(8,128)(2,1)S(1)} %copy-done, f32[4,4608]{1,0:T(4,128)S(1)} %copy-done.3, bf16[512,1024]{1,0:T(8,128)(2,1)S(1)} %bitcast.62, f32[512,1024]{1,0:T(8,128)S(1)} %bitcast.54), custom_call_target="tpu_custom_call" | custom-call | flops 9663676416 | bytes 9437184 | tf_op jit(solution)/shard_map/pallas_call | solution.py:274
  51.4 11.3 %shard_map.79 = bf16[64,1024]{1,0:T(8,128)(2,1)S(1)} custom-call(f32[4,2,64,1024]{3,2,1,0:T(8,128)S(1)} %bitcast.60), custom_call_target="tpu_custom_call" | custom-call | flops 10485760 | bytes 10485760 | tf_op jit(solution)/shard_map/pallas_call | solution.py:672
  62.6 0.6 collective-permute-start.5
  63.3 1.6 collective-permute-start.4
  65.8 2.8 multiply_convert_fusion.18
  68.5 4.0 multiply_convert_fusion
  72.8 0.6 reduce_max.18
  74.0 11.2 %shard_map.80 = (bf16[1,4,2,64,1024]{4,3,2,1,0:T(8,128)(2,1)S(1)}, f32[8,128]{1,0:T(8,128)S(1)}) custom-call(bf16[1,64,1024]{2,1,0:T(8,128)(2,1)S(1)} %bitcast.66), custom_call_target="tpu_custom_call" | custom-call | flops 20971520 | bytes 20971520 | tf_op jit(solution)/shard_map/pallas_call | solution.py:700
  85.2 2.7 collective-permute-start.3
  88.1 0.9 collective-permute-start.7
  89.2 3.0 collective-permute-start.6
  92.3 0.6 collective-permute-start.9
  92.9 1.5 collective-permute-start.10
  94.4 0.9 pad_maximum_fusion.x_ref
  95.4 19.1 %shard_map.81 = (bf16[4,4,2,64,1024]{4,3,2,1,0:T(8,128)(2,1)S(1)}, f32[8,128]{1,0:T(8,128)S(1)}) custom-call(bf16[3,64,1024]{2,1,0:T(8,128)(2,1)S(1)} %pad_maximum_fusion.x_ref, bf16[4,2,64,1024]{3,2,1,0:T(8,128)(2,1)S(1)} %bitcast.64), custom_call_target="tpu_custom_call" | custom-call | flops 62914560 | bytes 62914560 | tf_op jit(solution)/shard_map/pallas_call | solution.py:700
  114.5 2.0 copy-done.1
  116.5 0.6 reduce_sum.19
  117.8 33.0 %collective-permute-start.11 = (f16[4,384,128]{2,1,0:T(8,128)(2,1)}, f16[4,384,128]{2,1,0:T(8,128)(2,1)S(1)}, u32[]{:S(2)}, u32[]{:S(2)}) collective-permute-start(f16[4,384,128]{2,1,0:T(8,128)(2,1)} %get-tuple-element.61), channel_id=1, source_target_pairs={{0,3},{1,0},{2,1},{3,2},{4,7},{5,4},{6,5},{7,6},{8,11},{9,8},{10,9... | collective-permute-start | bytes 1179656 | tf_op jit(solution)/shard_map/ppermute | solution.py:728
  151.1 2.2 copy-done.2
  153.3 15.4 %shard_map.82 = (f32[4,384,128]{2,1,0:T(8,128)S(1)}, f32[12,384,128]{2,1,0:T(8,128)S(1)}, f32[4,384,128]{2,1,0:T(8,128)}, f32[12,384,128]{2,1,0:T(8,128)}) custom-call(s32[1]{0:T(128)} %bitcast.me_ref, bf16[4608,1024]{1,0:T(8,128)(2,1)} %l_ref.23, f32[16,4608]{1,0:T(8,128)S(1)} %pad_maximum_fusion.2.k_ref, f32[16,4608]{1,0:T(8,128)S(1)} %pad_maximum_fusion.3.wt_ref, ...), custom_call_target="tpu_custom_call" | custom-call | flops 2415919104 | bytes 12582912 | tf_op jit(solution)/shard_map/pallas_call | solution.py:143
  169.2 29.1 %collective-permute-start.20 = (f16[4,384,128]{2,1,0:T(8,128)(2,1)S(1)}, f16[4,384,128]{2,1,0:T(8,128)(2,1)S(1)}, u32[]{:S(2)}, u32[]{:S(2)}) collective-permute-start(f16[4,384,128]{2,1,0:T(8,128)(2,1)S(1)} %get-tuple-element.140), channel_id=1, source_target_pairs={{0,1},{1,2},{2,3},{3,0},{4,5},{5,6},{6,7},{7,4},{8,9},{9,10},{10,1... | collective-permute-start | bytes 1179656 | tf_op jit(solution)/shard_map/ppermute | solution.py:728
  198.3 15.4 %shard_map.83 = (f32[4,384,128]{2,1,0:T(8,128)S(1)}, f32[12,384,128]{2,1,0:T(8,128)S(1)}, f32[4,384,128]{2,1,0:T(8,128)}, f32[12,384,128]{2,1,0:T(8,128)}) custom-call(s32[1]{0:T(128)} %bitcast.me_ref, bf16[4608,1024]{1,0:T(8,128)(2,1)} %l_ref.23, f32[16,4608]{1,0:T(8,128)S(1)} %pad_maximum_fusion.2.k_ref, f32[16,4608]{1,0:T(8,128)S(1)} %pad_maximum_fusion.3.wt_ref, ...), custom_call_target="tpu_custom_call" | custom-call | flops 2415919104 | bytes 12582912 | tf_op jit(solution)/shard_map/pallas_call | solution.py:143
  214.0 0.7 collective-permute-start.18
  214.7 1.1 convert_multiply_fusion.2.rest_1_
  215.7 1.2 convert_multiply_fusion.1.rest_2_
  217.1 15.6 %shard_map.84 = (f32[4,384,128]{2,1,0:T(8,128)S(1)}, f32[12,384,128]{2,1,0:T(8,128)S(1)}, f32[4,384,128]{2,1,0:T(8,128)}, f32[12,384,128]{2,1,0:T(8,128)}) custom-call(s32[1]{0:T(128)} %bitcast.me_ref, bf16[4608,1024]{1,0:T(8,128)(2,1)} %l_ref.23, f32[16,4608]{1,0:T(8,128)S(1)} %pad_maximum_fusion.2.k_ref, f32[16,4608]{1,0:T(8,128)S(1)} %pad_maximum_fusion.3.wt_ref, ...), custom_call_target="tpu_custom_call" | custom-call | flops 2415919104 | bytes 12582912 | tf_op jit(solution)/shard_map/pallas_call | solution.py:143
  232.9 3.4 collective-permute-start.14
  236.3 1.1 collective-permute-start.13
  238.1 1.0 collective-permute-start.17
  239.1 0.9 collective-permute-start.16
  240.0 1.9 collective-permute-start.15
  242.0 0.4 multiply_add_fusion.15
  242.7 0.5 slice-done.2
  243.2 3.0 shard_map.85.rest_4_
  246.2 16.5 %collective-permute-done.17 = f16[4,384,128]{2,1,0:T(8,128)(2,1)S(1)} collective-permute-done((f16[4,384,128]{2,1,0:T(8,128)(2,1)S(1)}, f16[4,384,128]{2,1,0:T(8,128)(2,1)S(1)}, u32[]{:S(2)}, u32[]{:S(2)}) %collective-permute-start.17) | collective-permute-done | bytes 393248 | tf_op jit(solution)/shard_map/ppermute | solution.py:728
  262.7 35.8 %collective-permute-start.12 = (f16[4,384,128]{2,1,0:T(8,128)(2,1)S(1)}, f16[4,384,128]{2,1,0:T(8,128)(2,1)S(1)}, u32[]{:S(2)}, u32[]{:S(2)}) collective-permute-start(f16[4,384,128]{2,1,0:T(8,128)(2,1)S(1)} %get-tuple-element.148), channel_id=1, source_target_pairs={{0,3},{1,0},{2,1},{3,2},{4,7},{5,4},{6,5},{7,6},{8,11},{9,8},{10,9... | collective-permute-start | bytes 1179656 | tf_op jit(solution)/shard_map/ppermute | solution.py:728
  298.5 5.9 %collective-permute-done.16 = f16[4,384,128]{2,1,0:T(8,128)(2,1)S(1)} collective-permute-done((f16[4,384,128]{2,1,0:T(8,128)(2,1)S(1)}, f16[4,384,128]{2,1,0:T(8,128)(2,1)S(1)}, u32[]{:S(2)}, u32[]{:S(2)}) %collective-permute-start.16) | collective-permute-done | bytes 393248 | tf_op jit(solution)/shard_map/ppermute | solution.py:728
  304.5 0.4 multiply_add_fusion.12
  304.9 3.1 shard_map.86.rest_4_
  308.0 0.4 multiply_add_fusion.9
  308.4 3.1 shard_map.87.x_ref
  311.5 19.2 %shard_map.88 = bf16[4,2,64,1024]{3,2,1,0:T(8,128)(2,1)S(1)} custom-call(f32[4,2,64,1024]{3,2,1,0:T(8,128)S(1)} %bitcast.52), custom_call_target="tpu_custom_call" | custom-call | flops 20971520 | bytes 20971520 | tf_op jit(solution)/shard_map/pallas_call | solution.py:681
  330.7 14.4 %shard_map.89 = f32[512,1024]{1,0:T(8,128)S(1)} custom-call(bf16[4608,1024]{1,0:T(8,128)(2,1)S(1)} %bitcast.45, f32[4,4608]{1,0:T(4,128)S(1)} %copy-done.3, bf16[512,1024]{1,0:T(8,128)(2,1)S(1)} %bitcast.63, f32[512,1024]{1,0:T(8,128)S(1)} %shard_map.87.x_ref), custom_call_target="tpu_custom_call" | custom-call | flops 9663676416 | bytes 9437184 | tf_op jit(solution)/shard_map/pallas_call | solution.py:274
  345.0 11.3 %shard_map.90 = bf16[64,1024]{1,0:T(8,128)(2,1)S(1)} custom-call(f32[4,2,64,1024]{3,2,1,0:T(8,128)S(1)} %bitcast.61), custom_call_target="tpu_custom_call" | custom-call | flops 10485760 | bytes 10485760 | tf_op jit(solution)/shard_map/pallas_call | solution.py:672
  356.7 3.9 collective-permute-start.21
  360.6 0.5 collective-permute-start.30
  361.1 1.5 collective-permute-start.31
  362.6 11.5 %shard_map.91 = (bf16[1,4,2,64,1024]{4,3,2,1,0:T(8,128)(2,1)S(1)}, f32[8,128]{1,0:T(8,128)}) custom-call(bf16[1,64,1024]{2,1,0:T(8,128)(2,1)S(1)} %bitcast.67), custom_call_target="tpu_custom_call" | custom-call | flops 20971520 | bytes 20971520 | tf_op jit(solution)/shard_map/pallas_call | solution.py:700
  374.1 3.2 collective-permute-start.32
  377.3 14.7 %shard_map.92 = f32[4,4608,128]{2,1,0:T(8,128)} custom-call(s32[1]{0:T(128)} %bitcast.me_ref, bf16[4608,1024]{1,0:T(8,128)(2,1)S(1)} %bitcast.45, f32[4,4608]{1,0:T(4,128)S(1)} %copy-done.3, bf16[512,1024]{1,0:T(8,128)(2,1)S(1)} %bitcast.55, f32[4,384,128]{2,1,0:T(8,128)S(1)} %get-tuple-element.127.rest_0_, f32[4,384,128]{2,1,0:T(8,128)S(1)} %get-tuple-element.126.rest_1_, ...), custom_call_target="tpu_custom_call" | custom-call | flops 4831838208 | bytes 18874368 | tf_op jit(solution)/shard_map/pallas_call | solution.py:362
  392.1 1.0 collective-permute-start.25
  393.1 20.4 %shard_map.93 = (bf16[4,4,2,64,1024]{4,3,2,1,0:T(8,128)(2,1)S(1)}, f32[8,128]{1,0:T(8,128)}) custom-call(bf16[3,64,1024]{2,1,0:T(8,128)(2,1)S(1)} %pad_maximum_fusion.1.x_ref, bf16[4,2,64,1024]{3,2,1,0:T(8,128)(2,1)S(1)} %bitcast.56), custom_call_target="tpu_custom_call" | custom-call | flops 62914560 | bytes 62914560 | tf_op jit(solution)/shard_map/pallas_call | solution.py:700
  413.6 3.1 collective-permute-start.29
  416.7 23.7 %collective-permute-start.27 = (f16[4,384,128]{2,1,0:T(8,128)(2,1)S(1)}, f16[4,384,128]{2,1,0:T(8,128)(2,1)S(1)}, u32[]{:S(2)}, u32[]{:S(2)}) collective-permute-start(f16[4,384,128]{2,1,0:T(8,128)(2,1)S(1)} %get-tuple-element.136), channel_id=1, source_target_pairs={{0,3},{1,0},{2,1},{3,2},{4,7},{5,4},{6,5},{7,6},{8,11},{9,8},{10,9... | collective-permute-start | bytes 1179656 | tf_op jit(solution)/shard_map/ppermute | solution.py:728
  440.9 17.2 %shard_map.94.rest_4_ = f32[4,4608,128]{2,1,0:T(8,128)} custom-call(s32[1]{0:T(128)} %bitcast.me_ref, bf16[4608,1024]{1,0:T(8,128)(2,1)S(1)} %bitcast.45, f32[16,4608]{1,0:T(8,128)S(1)} %pad_maximum_fusion.2.k_ref, f32[16,4608]{1,0:T(8,128)S(1)} %pad_maximum_fusion.3.wt_ref, f32[64,16]{1,0:T(8,128)S(1)} %bitcast.68, bf16[2048,1024]{1,0:T(8,128)(2,1)S(1)} %bitcast.49, ...), custom_call_target="tpu_custom_call" | custom-call | flops 6442450944 | bytes 6291456 | tf_op jit(solution)/shard_map/pallas_call | solution.py:439
  458.2 14.5 %collective-permute-done.28 = f16[4,384,128]{2,1,0:T(8,128)(2,1)S(1)} collective-permute-done((f16[4,384,128]{2,1,0:T(8,128)(2,1)S(1)}, f16[4,384,128]{2,1,0:T(8,128)(2,1)S(1)}, u32[]{:S(2)}, u32[]{:S(2)}) %collective-permute-start.28) | collective-permute-done | bytes 393248 | tf_op jit(solution)/shard_map/ppermute | solution.py:728
  472.7 0.4 multiply_add_fusion.3
  473.1 17.2 %shard_map.95.rest_4_ = f32[4,4608,128]{2,1,0:T(8,128)} custom-call(s32[1]{0:T(128)} %bitcast.me_ref, bf16[4608,1024]{1,0:T(8,128)(2,1)S(1)} %bitcast.45, f32[16,4608]{1,0:T(8,128)S(1)} %pad_maximum_fusion.2.k_ref, f32[16,4608]{1,0:T(8,128)S(1)} %pad_maximum_fusion.3.wt_ref, f32[64,16]{1,0:T(8,128)S(1)} %bitcast.69, ...), custom_call_target="tpu_custom_call", output_to_operand_aliasing={{}: (10, {})} | custom-call | flops 6442450944 | bytes 6291456 | tf_op jit(solution)/shard_map/pallas_call | solution.py:439
  490.8 17.2 %shard_map.96 = f32[4,4608,128]{2,1,0:T(8,128)} custom-call(s32[1]{0:T(128)} %bitcast.me_ref, bf16[4608,1024]{1,0:T(8,128)(2,1)S(1)} %bitcast.45, f32[16,4608]{1,0:T(8,128)S(1)} %pad_maximum_fusion.2.k_ref, f32[16,4608]{1,0:T(8,128)S(1)} %pad_maximum_fusion.3.wt_ref, f32[64,16]{1,0:T(8,128)S(1)} %bitcast.70, ...), custom_call_target="tpu_custom_call", output_to_operand_aliasing={{}: (10, {})} | custom-call | flops 6442450944 | bytes 6291456 | tf_op jit(solution)/shard_map/pallas_call | solution.py:439
  (111 shorter events, 5.3 us)
Async XLA Ops:
  1.6 83.6 %collective-permute-start.2 = (f16[2,4,4608]{2,1,0:T(4,128)(2,1)S(1)}, f16[2,4,4608]{2,1,0:T(4,128)(2,1)S(1)}, u32[]{:S(2)}, u32[]{:S(2)}) collective-permute-start(f16[2,4,4608]{2,1,0:T(4,128)(2,1)S(1)} %fusion.3), channel_id=1, source_target_pairs={{0,3},{1,0},{2,1},{3,2},{4,7},{5,4},{6,5},{7,6},{8,11},{9,8},{10,9... | collective-permute-start | bytes 221192 | tf_op jit(solution)/shard_map/ppermute | solution.py:728
  2.1 85.8 %collective-permute-start.1 = (f16[2,4,4608]{2,1,0:T(4,128)(2,1)S(1)}, f16[2,4,4608]{2,1,0:T(4,128)(2,1)S(1)}, u32[]{:S(2)}, u32[]{:S(2)}) collective-permute-start(f16[2,4,4608]{2,1,0:T(4,128)(2,1)S(1)} %fusion.3), channel_id=1, source_target_pairs={{0,2},{1,3},{2,0},{3,1},{4,6},{5,7},{6,4},{7,5},{8,10},{9,11},{10,... | collective-permute-start | bytes 221192 | tf_op jit(solution)/shard_map/ppermute | solution.py:728
  2.1 86.0 %collective-permute-start = (f16[2,4,4608]{2,1,0:T(4,128)(2,1)S(1)}, f16[2,4,4608]{2,1,0:T(4,128)(2,1)S(1)}, u32[]{:S(2)}, u32[]{:S(2)}) collective-permute-start(f16[2,4,4608]{2,1,0:T(4,128)(2,1)S(1)} %fusion.3), channel_id=1, source_target_pairs={{0,1},{1,2},{2,3},{3,0},{4,5},{5,6},{6,7},{7,4},{8,9},{9,10},{10,1... | collective-permute-start | bytes 221192 | tf_op jit(solution)/shard_map/ppermute | solution.py:728
  5.5 31.5 %copy-start = (bf16[4608,1024]{1,0:T(8,128)(2,1)S(1)}, bf16[4608,1024]{1,0:T(8,128)(2,1)}, u32[]{:S(2)}) copy-start(bf16[4608,1024]{1,0:T(8,128)(2,1)} %l_ref.23) | copy-start | bytes 28311556
  17.1 19.9 %copy-start.3 = (f32[4,4608]{1,0:T(4,128)S(1)}, f32[4,4608]{1,0:T(4,128)}, u32[]{:S(2)}) copy-start(f32[4,4608]{1,0:T(4,128)} %wt_ref.5) | copy-start | bytes 221188
  51.3 13.6 %copy-start.11 = (f32[16,16]{1,0:T(8,128)S(1)}, f32[16,16]{1,0:T(8,128)}, u32[]{:S(2)}) copy-start(f32[16,16]{1,0:T(8,128)} %param.10) | copy-start | bytes 3076
  51.4 14.0 %copy-start.12 = (f32[16,16]{1,0:T(8,128)S(1)}, f32[16,16]{1,0:T(8,128)}, u32[]{:S(2)}) copy-start(f32[16,16]{1,0:T(8,128)} %param.11) | copy-start | bytes 3076
  62.6 26.5 %collective-permute-start.5 = (bf16[64,1024]{1,0:T(8,128)(2,1)S(1)}, bf16[64,1024]{1,0:T(8,128)(2,1)S(1)}, u32[]{:S(2)}, u32[]{:S(2)}) collective-permute-start(bf16[64,1024]{1,0:T(8,128)(2,1)S(1)} %shard_map.79), channel_id=1, source_target_pairs={{0,3},{1,0},{2,1},{3,2},{4,7},{5,4},{6,5},{7,6},{8,11},{9,8},{10,9... | collective-permute-start | bytes 393224 | tf_op jit(solution)/shard_map/ppermute | solution.py:728
  63.3 29.0 %collective-permute-start.4 = (bf16[64,1024]{1,0:T(8,128)(2,1)S(1)}, bf16[64,1024]{1,0:T(8,128)(2,1)}, u32[]{:S(2)}, u32[]{:S(2)}) collective-permute-start(bf16[64,1024]{1,0:T(8,128)(2,1)S(1)} %shard_map.79), channel_id=1, source_target_pairs={{0,2},{1,3},{2,0},{3,1},{4,6},{5,7},{6,4},{7,5},{8,10},{9,11},{10,... | collective-permute-start | bytes 393224 | tf_op jit(solution)/shard_map/ppermute | solution.py:728
  72.6 19.6 %copy-start.10 = (f32[4,4608]{1,0:T(4,128)S(1)}, f32[4,4608]{1,0:T(4,128)}, u32[]{:S(2)}) copy-start(f32[4,4608]{1,0:T(4,128)} %param.9) | copy-start | bytes 221188
  85.2 7.7 %collective-permute-start.3 = (bf16[64,1024]{1,0:T(8,128)(2,1)S(1)}, bf16[64,1024]{1,0:T(8,128)(2,1)S(1)}, u32[]{:S(2)}, u32[]{:S(2)}) collective-permute-start(bf16[64,1024]{1,0:T(8,128)(2,1)S(1)} %shard_map.79), channel_id=1, source_target_pairs={{0,1},{1,2},{2,3},{3,0},{4,5},{5,6},{6,7},{7,4},{8,9},{9,10},{10,1... | collective-permute-start | bytes 393224 | tf_op jit(solution)/shard_map/ppermute | solution.py:728
  88.0 29.9 %collective-permute-start.8 = (f16[4,768,128]{2,1,0:T(8,128)(2,1)}, f16[4,768,128]{2,1,0:T(8,128)(2,1)S(1)}, u32[]{:S(2)}, u32[]{:S(2)}) collective-permute-start(f16[4,768,128]{2,1,0:T(8,128)(2,1)} %get-tuple-element.131), channel_id=1, source_target_pairs={{0,3},{1,0},{2,1},{3,2},{4,7},{5,4},{6,5},{7,6},{8,11},{9,8},{10,9... | collective-permute-start | bytes 2359304 | tf_op jit(solution)/shard_map/ppermute | solution.py:728
  88.1 62.8 %collective-permute-start.7 = (f16[4,768,128]{2,1,0:T(8,128)(2,1)}, f16[4,768,128]{2,1,0:T(8,128)(2,1)S(1)}, u32[]{:S(2)}, u32[]{:S(2)}) collective-permute-start(f16[4,768,128]{2,1,0:T(8,128)(2,1)} %get-tuple-element.132), channel_id=1, source_target_pairs={{0,2},{1,3},{2,0},{3,1},{4,6},{5,7},{6,4},{7,5},{8,10},{9,11},{10,... | collective-permute-start | bytes 2359304 | tf_op jit(solution)/shard_map/ppermute | solution.py:728
  89.2 61.8 %collective-permute-start.6 = (f16[4,768,128]{2,1,0:T(8,128)(2,1)}, f16[4,768,128]{2,1,0:T(8,128)(2,1)S(1)}, u32[]{:S(2)}, u32[]{:S(2)}) collective-permute-start(f16[4,768,128]{2,1,0:T(8,128)(2,1)} %get-tuple-element.133), channel_id=1, source_target_pairs={{0,1},{1,2},{2,3},{3,0},{4,5},{5,6},{6,7},{7,4},{8,9},{9,10},{10,1... | collective-permute-start | bytes 2359304 | tf_op jit(solution)/shard_map/ppermute | solution.py:728
  92.3 121.7 %collective-permute-start.9 = (f16[4,384,128]{2,1,0:T(8,128)(2,1)}, f16[4,384,128]{2,1,0:T(8,128)(2,1)}, u32[]{:S(2)}, u32[]{:S(2)}) collective-permute-start(f16[4,384,128]{2,1,0:T(8,128)(2,1)} %get-tuple-element.59), channel_id=1, source_target_pairs={{0,1},{1,2},{2,3},{3,0},{4,5},{5,6},{6,7},{7,4},{8,9},{9,10},{10,1... | collective-permute-start | bytes 1179656 | tf_op jit(solution)/shard_map/ppermute | solution.py:728
  92.9 121.8 %collective-permute-start.10 = (f16[4,384,128]{2,1,0:T(8,128)(2,1)}, f16[4,384,128]{2,1,0:T(8,128)(2,1)}, u32[]{:S(2)}, u32[]{:S(2)}) collective-permute-start(f16[4,384,128]{2,1,0:T(8,128)(2,1)} %get-tuple-element.60), channel_id=1, source_target_pairs={{0,2},{1,3},{2,0},{3,1},{4,6},{5,7},{6,4},{7,5},{8,10},{9,11},{10,... | collective-permute-start | bytes 1179656 | tf_op jit(solution)/shard_map/ppermute | solution.py:728
  114.5 2.0 copy-start.1
  117.8 96.8 %collective-permute-start.11 = (f16[4,384,128]{2,1,0:T(8,128)(2,1)}, f16[4,384,128]{2,1,0:T(8,128)(2,1)S(1)}, u32[]{:S(2)}, u32[]{:S(2)}) collective-permute-start(f16[4,384,128]{2,1,0:T(8,128)(2,1)} %get-tuple-element.61), channel_id=1, source_target_pairs={{0,3},{1,0},{2,1},{3,2},{4,7},{5,4},{6,5},{7,6},{8,11},{9,8},{10,9... | collective-permute-start | bytes 1179656 | tf_op jit(solution)/shard_map/ppermute | solution.py:728
  151.1 2.2 copy-start.2
  169.2 68.9 %collective-permute-start.20 = (f16[4,384,128]{2,1,0:T(8,128)(2,1)S(1)}, f16[4,384,128]{2,1,0:T(8,128)(2,1)S(1)}, u32[]{:S(2)}, u32[]{:S(2)}) collective-permute-start(f16[4,384,128]{2,1,0:T(8,128)(2,1)S(1)} %get-tuple-element.140), channel_id=1, source_target_pairs={{0,1},{1,2},{2,3},{3,0},{4,5},{5,6},{6,7},{7,4},{8,9},{9,10},{10,1... | collective-permute-start | bytes 1179656 | tf_op jit(solution)/shard_map/ppermute | solution.py:728
  198.3 40.8 %collective-permute-start.19 = (f16[4,384,128]{2,1,0:T(8,128)(2,1)S(1)}, f16[4,384,128]{2,1,0:T(8,128)(2,1)S(1)}, u32[]{:S(2)}, u32[]{:S(2)}) collective-permute-start(f16[4,384,128]{2,1,0:T(8,128)(2,1)S(1)} %get-tuple-element.141), channel_id=1, source_target_pairs={{0,2},{1,3},{2,0},{3,1},{4,6},{5,7},{6,4},{7,5},{8,10},{9,11},{10,... | collective-permute-start | bytes 1179656 | tf_op jit(solution)/shard_map/ppermute | solution.py:728
  214.0 26.0 %collective-permute-start.18 = (f16[4,384,128]{2,1,0:T(8,128)(2,1)S(1)}, f16[4,384,128]{2,1,0:T(8,128)(2,1)S(1)}, u32[]{:S(2)}, u32[]{:S(2)}) collective-permute-start(f16[4,384,128]{2,1,0:T(8,128)(2,1)S(1)} %get-tuple-element.142), channel_id=1, source_target_pairs={{0,3},{1,0},{2,1},{3,2},{4,7},{5,4},{6,5},{7,6},{8,11},{9,8},{10,9... | collective-permute-start | bytes 1179656 | tf_op jit(solution)/shard_map/ppermute | solution.py:728
  215.7 26.2 %slice-start.3 = ((s8[9437184]{0:T(1024)(128)(4,1)}), s8[4194304]{0:T(1024)(128)(4,1)S(1)}, s32[]{:S(2)}) async-start(s8[9437184]{0:T(1024)(128)(4,1)} %bitcast.71), calls=%async_computation.3 | async-start | bytes 8388608
  217.0 24.9 %slice-start.4 = ((s8[9437184]{0:T(1024)(128)(4,1)}), s8[4194304]{0:T(1024)(128)(4,1)S(1)}, s32[]{:S(2)}) async-start(s8[9437184]{0:T(1024)(128)(4,1)} %bitcast.71), calls=%async_computation.4 | async-start | bytes 8388608
  217.1 24.9 %slice-start.5 = ((s8[9437184]{0:T(1024)(128)(4,1)}), s8[1048576]{0:T(1024)(128)(4,1)S(1)}, s32[]{:S(2)}) async-start(s8[9437184]{0:T(1024)(128)(4,1)} %bitcast.71), calls=%async_computation.5 | async-start | bytes 2097152
  232.6 4.8 copy-start.5
  232.6 5.1 %copy-start.6 = (f32[12,384,128]{2,1,0:T(8,128)S(1)}, f32[12,384,128]{2,1,0:T(8,128)}, u32[]{:S(2)}) copy-start(f32[12,384,128]{2,1,0:T(8,128)} %get-tuple-element.86) | copy-start | bytes 7077892
  232.6 10.0 %slice-start = ((s8[9437184]{0:T(1024)(128)(4,1)}), s8[4194304]{0:T(1024)(128)(4,1)S(1)}, s32[]{:S(2)}) async-start(s8[9437184]{0:T(1024)(128)(4,1)} %bitcast.44), calls=%async_computation | async-start | bytes 8388608
  232.9 75.0 %collective-permute-start.14 = (f16[4,384,128]{2,1,0:T(8,128)(2,1)S(1)}, f16[4,384,128]{2,1,0:T(8,128)(2,1)S(1)}, u32[]{:S(2)}, u32[]{:S(2)}) collective-permute-start(f16[4,384,128]{2,1,0:T(8,128)(2,1)S(1)} %get-tuple-element.146), channel_id=1, source_target_pairs={{0,1},{1,2},{2,3},{3,0},{4,5},{5,6},{6,7},{7,4},{8,9},{9,10},{10,1... | collective-permute-start | bytes 1179656 | tf_op jit(solution)/shard_map/ppermute | solution.py:728
  236.3 71.6 %collective-permute-start.13 = (f16[4,384,128]{2,1,0:T(8,128)(2,1)S(1)}, f16[4,384,128]{2,1,0:T(8,128)(2,1)S(1)}, u32[]{:S(2)}, u32[]{:S(2)}) collective-permute-start(f16[4,384,128]{2,1,0:T(8,128)(2,1)S(1)} %get-tuple-element.147), channel_id=1, source_target_pairs={{0,2},{1,3},{2,0},{3,1},{4,6},{5,7},{6,4},{7,5},{8,10},{9,11},{10,... | collective-permute-start | bytes 1179656 | tf_op jit(solution)/shard_map/ppermute | solution.py:728
  237.5 5.2 %slice-start.1 = ((s8[9437184]{0:T(1024)(128)(4,1)}), s8[4194304]{0:T(1024)(128)(4,1)S(1)}, s32[]{:S(2)}) async-start(s8[9437184]{0:T(1024)(128)(4,1)} %bitcast.44), calls=%async_computation.1 | async-start | bytes 8388608
  238.1 24.7 %collective-permute-start.17 = (f16[4,384,128]{2,1,0:T(8,128)(2,1)S(1)}, f16[4,384,128]{2,1,0:T(8,128)(2,1)S(1)}, u32[]{:S(2)}, u32[]{:S(2)}) collective-permute-start(f16[4,384,128]{2,1,0:T(8,128)(2,1)S(1)} %get-tuple-element.143), channel_id=1, source_target_pairs={{0,1},{1,2},{2,3},{3,0},{4,5},{5,6},{6,7},{7,4},{8,9},{9,10},{10,1... | collective-permute-start | bytes 1179656 | tf_op jit(solution)/shard_map/ppermute | solution.py:728
  239.1 65.4 %collective-permute-start.16 = (f16[4,384,128]{2,1,0:T(8,128)(2,1)S(1)}, f16[4,384,128]{2,1,0:T(8,128)(2,1)S(1)}, u32[]{:S(2)}, u32[]{:S(2)}) collective-permute-start(f16[4,384,128]{2,1,0:T(8,128)(2,1)S(1)} %get-tuple-element.144), channel_id=1, source_target_pairs={{0,2},{1,3},{2,0},{3,1},{4,6},{5,7},{6,4},{7,5},{8,10},{9,11},{10,... | collective-permute-start | bytes 1179656 | tf_op jit(solution)/shard_map/ppermute | solution.py:728
  240.0 64.5 %collective-permute-start.15 = (f16[4,384,128]{2,1,0:T(8,128)(2,1)S(1)}, f16[4,384,128]{2,1,0:T(8,128)(2,1)S(1)}, u32[]{:S(2)}, u32[]{:S(2)}) collective-permute-start(f16[4,384,128]{2,1,0:T(8,128)(2,1)S(1)} %get-tuple-element.145), channel_id=1, source_target_pairs={{0,3},{1,0},{2,1},{3,2},{4,7},{5,4},{6,5},{7,6},{8,11},{9,8},{10,9... | collective-permute-start | bytes 1179656 | tf_op jit(solution)/shard_map/ppermute | solution.py:728
  242.0 1.2 slice-start.2
  262.7 45.2 %collective-permute-start.12 = (f16[4,384,128]{2,1,0:T(8,128)(2,1)S(1)}, f16[4,384,128]{2,1,0:T(8,128)(2,1)S(1)}, u32[]{:S(2)}, u32[]{:S(2)}) collective-permute-start(f16[4,384,128]{2,1,0:T(8,128)(2,1)S(1)} %get-tuple-element.148), channel_id=1, source_target_pairs={{0,3},{1,0},{2,1},{3,2},{4,7},{5,4},{6,5},{7,6},{8,11},{9,8},{10,9... | collective-permute-start | bytes 1179656 | tf_op jit(solution)/shard_map/ppermute | solution.py:728
  330.6 25.7 %copy-start.4 = (f32[12,384,128]{2,1,0:T(8,128)S(1)}, f32[12,384,128]{2,1,0:T(8,128)}, u32[]{:S(2)}) copy-start(f32[12,384,128]{2,1,0:T(8,128)} %get-tuple-element.88) | copy-start | bytes 7077892
  356.3 17.8 %collective-permute-start.23 = (bf16[64,1024]{1,0:T(8,128)(2,1)S(1)}, bf16[64,1024]{1,0:T(8,128)(2,1)S(1)}, u32[]{:S(2)}, u32[]{:S(2)}) collective-permute-start(bf16[64,1024]{1,0:T(8,128)(2,1)S(1)} %shard_map.90), channel_id=1, source_target_pairs={{0,3},{1,0},{2,1},{3,2},{4,7},{5,4},{6,5},{7,6},{8,11},{9,8},{10,9... | collective-permute-start | bytes 393224 | tf_op jit(solution)/shard_map/ppermute | solution.py:728
  356.7 35.3 %collective-permute-start.22 = (bf16[64,1024]{1,0:T(8,128)(2,1)S(1)}, bf16[64,1024]{1,0:T(8,128)(2,1)S(1)}, u32[]{:S(2)}, u32[]{:S(2)}) collective-permute-start(bf16[64,1024]{1,0:T(8,128)(2,1)S(1)} %shard_map.90), channel_id=1, source_target_pairs={{0,2},{1,3},{2,0},{3,1},{4,6},{5,7},{6,4},{7,5},{8,10},{9,11},{10,... | collective-permute-start | bytes 393224 | tf_op jit(solution)/shard_map/ppermute | solution.py:728
  356.7 35.4 %collective-permute-start.21 = (bf16[64,1024]{1,0:T(8,128)(2,1)S(1)}, bf16[64,1024]{1,0:T(8,128)(2,1)S(1)}, u32[]{:S(2)}, u32[]{:S(2)}) collective-permute-start(bf16[64,1024]{1,0:T(8,128)(2,1)S(1)} %shard_map.90), channel_id=1, source_target_pairs={{0,1},{1,2},{2,3},{3,0},{4,5},{5,6},{6,7},{7,4},{8,9},{9,10},{10,1... | collective-permute-start | bytes 393224 | tf_op jit(solution)/shard_map/ppermute | solution.py:728
  360.6 53.0 %collective-permute-start.30 = (f16[4,384,128]{2,1,0:T(8,128)(2,1)S(1)}, f16[4,384,128]{2,1,0:T(8,128)(2,1)S(1)}, u32[]{:S(2)}, u32[]{:S(2)}) collective-permute-start(f16[4,384,128]{2,1,0:T(8,128)(2,1)S(1)} %get-tuple-element.90), channel_id=1, source_target_pairs={{0,3},{1,0},{2,1},{3,2},{4,7},{5,4},{6,5},{7,6},{8,11},{9,8},{10,9... | collective-permute-start | bytes 1179656 | tf_op jit(solution)/shard_map/ppermute | solution.py:728
  361.1 55.6 %collective-permute-start.31 = (f16[4,384,128]{2,1,0:T(8,128)(2,1)S(1)}, f16[4,384,128]{2,1,0:T(8,128)(2,1)S(1)}, u32[]{:S(2)}, u32[]{:S(2)}) collective-permute-start(f16[4,384,128]{2,1,0:T(8,128)(2,1)S(1)} %get-tuple-element.91), channel_id=1, source_target_pairs={{0,2},{1,3},{2,0},{3,1},{4,6},{5,7},{6,4},{7,5},{8,10},{9,11},{10,... | collective-permute-start | bytes 1179656 | tf_op jit(solution)/shard_map/ppermute | solution.py:728
  374.1 42.7 %collective-permute-start.32 = (f16[4,384,128]{2,1,0:T(8,128)(2,1)S(1)}, f16[4,384,128]{2,1,0:T(8,128)(2,1)S(1)}, u32[]{:S(2)}, u32[]{:S(2)}) collective-permute-start(f16[4,384,128]{2,1,0:T(8,128)(2,1)S(1)} %get-tuple-element.92), channel_id=1, source_target_pairs={{0,1},{1,2},{2,3},{3,0},{4,5},{5,6},{6,7},{7,4},{8,9},{9,10},{10,1... | collective-permute-start | bytes 1179656 | tf_op jit(solution)/shard_map/ppermute | solution.py:728
  392.0 48.5 %copy-start.9 = (f32[4,384,128]{2,1,0:T(8,128)S(1)}, f32[4,384,128]{2,1,0:T(8,128)}, u32[]{:S(2)}) copy-start(f32[4,384,128]{2,1,0:T(8,128)} %get-tuple-element.89) | copy-start | bytes 2359300
  392.0 98.4 %collective-permute-start.26 = (f16[4,384,128]{2,1,0:T(8,128)(2,1)S(1)}, f16[4,384,128]{2,1,0:T(8,128)(2,1)S(1)}, u32[]{:S(2)}, u32[]{:S(2)}) collective-permute-start(f16[4,384,128]{2,1,0:T(8,128)(2,1)S(1)} %get-tuple-element.137), channel_id=1, source_target_pairs={{0,1},{1,2},{2,3},{3,0},{4,5},{5,6},{6,7},{7,4},{8,9},{9,10},{10,1... | collective-permute-start | bytes 1179656 | tf_op jit(solution)/shard_map/ppermute | solution.py:728
  392.1 98.2 %collective-permute-start.25 = (f16[4,384,128]{2,1,0:T(8,128)(2,1)S(1)}, f16[4,384,128]{2,1,0:T(8,128)(2,1)S(1)}, u32[]{:S(2)}, u32[]{:S(2)}) collective-permute-start(f16[4,384,128]{2,1,0:T(8,128)(2,1)S(1)} %get-tuple-element.138), channel_id=1, source_target_pairs={{0,2},{1,3},{2,0},{3,1},{4,6},{5,7},{6,4},{7,5},{8,10},{9,11},{10,... | collective-permute-start | bytes 1179656 | tf_op jit(solution)/shard_map/ppermute | solution.py:728
  413.6 44.5 %collective-permute-start.29 = (f16[4,384,128]{2,1,0:T(8,128)(2,1)S(1)}, f16[4,384,128]{2,1,0:T(8,128)(2,1)S(1)}, u32[]{:S(2)}, u32[]{:S(2)}) collective-permute-start(f16[4,384,128]{2,1,0:T(8,128)(2,1)S(1)} %get-tuple-element.134), channel_id=1, source_target_pairs={{0,1},{1,2},{2,3},{3,0},{4,5},{5,6},{6,7},{7,4},{8,9},{9,10},{10,1... | collective-permute-start | bytes 1179656 | tf_op jit(solution)/shard_map/ppermute | solution.py:728
  416.7 56.0 %collective-permute-start.28 = (f16[4,384,128]{2,1,0:T(8,128)(2,1)S(1)}, f16[4,384,128]{2,1,0:T(8,128)(2,1)S(1)}, u32[]{:S(2)}, u32[]{:S(2)}) collective-permute-start(f16[4,384,128]{2,1,0:T(8,128)(2,1)S(1)} %get-tuple-element.135), channel_id=1, source_target_pairs={{0,2},{1,3},{2,0},{3,1},{4,6},{5,7},{6,4},{7,5},{8,10},{9,11},{10,... | collective-permute-start | bytes 1179656 | tf_op jit(solution)/shard_map/ppermute | solution.py:728
  416.7 56.0 %collective-permute-start.27 = (f16[4,384,128]{2,1,0:T(8,128)(2,1)S(1)}, f16[4,384,128]{2,1,0:T(8,128)(2,1)S(1)}, u32[]{:S(2)}, u32[]{:S(2)}) collective-permute-start(f16[4,384,128]{2,1,0:T(8,128)(2,1)S(1)} %get-tuple-element.136), channel_id=1, source_target_pairs={{0,3},{1,0},{2,1},{3,2},{4,7},{5,4},{6,5},{7,6},{8,11},{9,8},{10,9... | collective-permute-start | bytes 1179656 | tf_op jit(solution)/shard_map/ppermute | solution.py:728
  440.9 31.8 %copy-start.7 = (f32[4,384,128]{2,1,0:T(8,128)S(1)}, f32[4,384,128]{2,1,0:T(8,128)}, u32[]{:S(2)}) copy-start(f32[4,384,128]{2,1,0:T(8,128)} %get-tuple-element.87) | copy-start | bytes 2359300
  458.1 32.3 %collective-permute-start.24 = (f16[4,384,128]{2,1,0:T(8,128)(2,1)S(1)}, f16[4,384,128]{2,1,0:T(8,128)(2,1)S(1)}, u32[]{:S(2)}, u32[]{:S(2)}) collective-permute-start(f16[4,384,128]{2,1,0:T(8,128)(2,1)S(1)} %get-tuple-element.139), channel_id=1, source_target_pairs={{0,3},{1,0},{2,1},{3,2},{4,7},{5,4},{6,5},{7,6},{8,11},{9,8},{10,9... | collective-permute-start | bytes 1179656 | tf_op jit(solution)/shard_map/ppermute | solution.py:728
  473.1 17.3 %copy-start.8 = (f32[4,384,128]{2,1,0:T(8,128)S(1)}, f32[4,384,128]{2,1,0:T(8,128)}, u32[]{:S(2)}) copy-start(f32[4,384,128]{2,1,0:T(8,128)} %get-tuple-element.85) | copy-start | bytes 2359300

commit v12 on v11

--- a/solution.py
+++ b/solution.py
@@ -29,7 +29,7 @@
 
 
 def wide_tile(pairs):
-    for blocks in (6, 4, 3, 2, 1):
+    for blocks in (9, 6, 4, 3, 2, 1):
         if pairs % (blocks * LANES) == 0:
             return blocks * LANES
     return None
@@ -282,7 +282,7 @@
             resident(kept),
         ],
         out_specs=pl.BlockSpec(kept.shape, lambda i: (0, 0)),
-        compiler_params=pltpu.CompilerParams(vmem_limit_bytes=18 << 20),
+        compiler_params=pltpu.CompilerParams(vmem_limit_bytes=24 << 20),
         cost_estimate=pl.CostEstimate(
             flops=4 * kept.size * pairs, bytes_accessed=2 * factors.size, transcendentals=0
         ),
@@ -838,9 +838,11 @@
         sources.append(added(us[n][0], inward[n], u_top, group))
         total = project(me, group[0], factors, sources[n], total)
 
+    last = max(chunks - 1, 1)
+    lots = [list(range(last))] + ([[last]] if last < chunks else [])
     halves, back = [], {}
-    for n in range(chunks):
-        halves.append(halved(vs[n][1], v_top))
+    for lot in lots:
+        halves.append(halved(jnp.concatenate([vs[k][1] for k in lot], axis=1), v_top))
 
     def returned(n):
         back[n] = passed(halves[n], True)
@@ -848,14 +850,15 @@
     halves[0], total = tie((halves[0], total))
     returned(0)
     near, _, blocks = ladder(total)
-    for n in range(1, chunks):
+    for n in range(1, len(lots)):
         returned(n)
     amplitudes = amplitude(me, factors, pair_weight, near, sources)
     gathered, _ = joined(blocks, near)
     outs = []
-    for k in range(chunks):
-        back[k], outs = tie((back[k], outs))
-        base = added(vs[k][0], back[k], v_top, calls[k])
+    for n, j, k in [(n, j, k) for n, lot in enumerate(lots) for j, k in enumerate(lot)]:
+        back[n], outs = tie((back[n], outs))
+        base = [m[:, j * size : (j + 1) * size] for m in back[n]]
+        base = added(vs[k][0], base, v_top, calls[k])
         outs = final(
             me,
             k,

time: 515 us -> 491 us (0.953)
  the two profiles are of different devices: /device:TPU:24 before, /device:TPU:0 now
where the time goes in v12:
time: 491 us; the launch traced here: 484 us
  Pallas kernels  269 us (55%)
  starting transfers between devices  94.3 us (19%)
  waiting for transfers between devices  77.8 us (16%)
  other arithmetic  21.3 us (4%)
  matrix products  12.6 us (3%)
  local copies, waits for them, and re-layouts  6.34 us (1%)
    ppermute x30, starting transfers between devices, shift(): lax.ppermute(x, 'freq', [(i, (i + by) % parts) for i in range(parts)])  94.3 us
    ppermute x30, waiting for transfers between devices, shift(): lax.ppermute(x, 'freq', [(i, (i + by) % parts) for i in range(parts)])  77.8 us
    pallas_call x4, Pallas kernels, gathered_over(): pl.pallas_call(functools.partial(gather_kernel, chips, parts), out_shape=...  61.4 us
    pallas_call x3, Pallas kernels, final(): pl.pallas_call(functools.partial(final_kernel, nf, parts, len(outs)), out...  51.6 us
    pallas_call x3, Pallas kernels, quarter_pass(): pl.pallas_call(functools.partial(quarter_kernel, nf, parts, sets), out_sh...  46.5 us
    pallas_call x2, Pallas kernels, summed(): pl.pallas_call(functools.partial(sum_kernel, chips), out_shape=jax.ShapeD...  39.2 us
    pallas_call x2, Pallas kernels, again(): pl.pallas_call(functools.partial(again_kernel, own), out_shape=jax.ShapeD...  23.9 us
    pallas_call x2, Pallas kernels, summed(): pl.pallas_call(functools.partial(reduce_kernel, chips), out_shape=jax.Sha...  22.5 us
  transfers between devices with their start and end apart: 30, of which 5 were waited for; matrix products, arithmetic and copies ran while one was open for 7% of the time, Pallas kernels for 51%

profile of v12, /device:TPU:0, one launch (start us, length us, event | category | flops | bytes accessed | tf_op | source)
XLA Modules:
  0.0 484.4 jit_solution(3588529048902009066)
XLA Ops:
  0.6 1.0 fusion.6
  1.6 5.1 %collective-permute-start.2 = (f16[2,4,4608]{2,1,0:T(4,128)(2,1)S(1)}, f16[2,4,4608]{2,1,0:T(4,128)(2,1)S(1)}, u32[]{:S(2)}, u32[]{:S(2)}) collective-permute-start(f16[2,4,4608]{2,1,0:T(4,128)(2,1)S(1)} %fusion.6), channel_id=1, source_target_pairs={{0,3},{1,0},{2,1},{3,2},{4,7},{5,4},{6,5},{7,6},{8,11},{9,8},{10,9... | collective-permute-start | bytes 221192 | tf_op jit(solution)/shard_map/ppermute | solution.py:728
  6.7 1.0 collective-permute-start
  7.7 11.6 %fusion = f32[4,128,1024]{2,1,0:T(8,128)S(1)} fusion(bf16[4608,1024]{1,0:T(8,128)(2,1)} %l_ref.23, f32[4,4608,128]{2,1,0:T(8,128)} %rest_0_.5), kind=kOutput, calls=%fused_computation | convolution fusion | flops 4834197504 | bytes 20971520 | tf_op jit(solution)/shard_map/pa,fpc->fca/dot_general | solution.py:770
  19.4 19.8 %shard_map.77 = bf16[4,2,64,1024]{3,2,1,0:T(8,128)(2,1)S(1)} custom-call(f32[4,2,64,1024]{3,2,1,0:T(8,128)S(1)} %bitcast.53), custom_call_target="tpu_custom_call" | custom-call | flops 20971520 | bytes 20971520 | tf_op jit(solution)/shard_map/pallas_call | solution.py:681
  39.2 12.0 %shard_map.78 = f32[512,1024]{1,0:T(8,128)S(1)} custom-call(bf16[4608,1024]{1,0:T(8,128)(2,1)S(1)} %copy-done, f32[4,4608]{1,0:T(4,128)S(1)} %copy-done.3, bf16[512,1024]{1,0:T(8,128)(2,1)S(1)} %bitcast.62, f32[512,1024]{1,0:T(8,128)S(1)} %bitcast.54), custom_call_target="tpu_custom_call" | custom-call | flops 9663676416 | bytes 9437184 | tf_op jit(solution)/shard_map/pallas_call | solution.py:274
  51.2 11.3 %shard_map.79 = bf16[64,1024]{1,0:T(8,128)(2,1)S(1)} custom-call(f32[4,2,64,1024]{3,2,1,0:T(8,128)S(1)} %bitcast.60), custom_call_target="tpu_custom_call" | custom-call | flops 10485760 | bytes 10485760 | tf_op jit(solution)/shard_map/pallas_call | solution.py:672
  62.5 2.9 collective-permute-start.5
  65.4 1.2 collective-permute-start.4
  67.5 2.7 multiply_convert_fusion.15
  70.2 4.0 multiply_convert_fusion
  74.5 0.6 reduce_max.18
  75.7 10.9 %shard_map.80 = (bf16[1,4,2,64,1024]{4,3,2,1,0:T(8,128)(2,1)S(1)}, f32[8,128]{1,0:T(8,128)S(1)}) custom-call(bf16[1,64,1024]{2,1,0:T(8,128)(2,1)S(1)} %bitcast.66), custom_call_target="tpu_custom_call" | custom-call | flops 20971520 | bytes 20971520 | tf_op jit(solution)/shard_map/pallas_call | solution.py:700
  86.8 3.9 collective-permute-start.8
  91.0 0.6 collective-permute-start.6
  91.7 3.0 collective-permute-start.9
  95.0 33.0 %collective-permute-start.10 = (f16[4,384,128]{2,1,0:T(8,128)(2,1)}, f16[4,384,128]{2,1,0:T(8,128)(2,1)}, u32[]{:S(2)}, u32[]{:S(2)}) collective-permute-start(f16[4,384,128]{2,1,0:T(8,128)(2,1)} %get-tuple-element.65), channel_id=1, source_target_pairs={{0,2},{1,3},{2,0},{3,1},{4,6},{5,7},{6,4},{7,5},{8,10},{9,11},{10,... | collective-permute-start | bytes 1179656 | tf_op jit(solution)/shard_map/ppermute | solution.py:728
  128.0 0.9 pad_maximum_fusion.x_ref
  128.9 19.3 %shard_map.81 = (bf16[4,4,2,64,1024]{4,3,2,1,0:T(8,128)(2,1)S(1)}, f32[8,128]{1,0:T(8,128)S(1)}) custom-call(bf16[3,64,1024]{2,1,0:T(8,128)(2,1)S(1)} %pad_maximum_fusion.x_ref, bf16[4,2,64,1024]{3,2,1,0:T(8,128)(2,1)S(1)} %bitcast.64), custom_call_target="tpu_custom_call" | custom-call | flops 62914560 | bytes 62914560 | tf_op jit(solution)/shard_map/pallas_call | solution.py:700
  148.2 2.0 copy-done.1
  150.2 0.6 reduce_sum.19
  151.5 0.5 collective-permute-start.11
  152.1 26.6 %collective-permute-done.7 = f16[4,768,128]{2,1,0:T(8,128)(2,1)S(1)} collective-permute-done((f16[4,768,128]{2,1,0:T(8,128)(2,1)}, f16[4,768,128]{2,1,0:T(8,128)(2,1)S(1)}, u32[]{:S(2)}, u32[]{:S(2)}) %collective-permute-start.7) | collective-permute-done | bytes 786464 | tf_op jit(solution)/shard_map/ppermute | solution.py:728
  178.9 2.2 copy-done.2
  181.1 15.4 %shard_map.82 = (f32[4,384,128]{2,1,0:T(8,128)S(1)}, f32[12,384,128]{2,1,0:T(8,128)S(1)}, f32[4,384,128]{2,1,0:T(8,128)}, f32[12,384,128]{2,1,0:T(8,128)}) custom-call(s32[1]{0:T(128)} %bitcast.me_ref, bf16[4608,1024]{1,0:T(8,128)(2,1)} %l_ref.23, f32[16,4608]{1,0:T(8,128)S(1)} %pad_maximum_fusion.2.k_ref, f32[16,4608]{1,0:T(8,128)S(1)} %pad_maximum_fusion.3.wt_ref, ...), custom_call_target="tpu_custom_call" | custom-call | flops 2415919104 | bytes 12582912 | tf_op jit(solution)/shard_map/pallas_call | solution.py:143
  196.8 1.2 multiply_convert_fusion.6
  198.3 15.5 %shard_map.83 = (f32[4,384,128]{2,1,0:T(8,128)S(1)}, f32[12,384,128]{2,1,0:T(8,128)S(1)}, f32[4,384,128]{2,1,0:T(8,128)}, f32[12,384,128]{2,1,0:T(8,128)}) custom-call(s32[1]{0:T(128)} %bitcast.me_ref, bf16[4608,1024]{1,0:T(8,128)(2,1)} %l_ref.23, f32[16,4608]{1,0:T(8,128)S(1)} %pad_maximum_fusion.2.k_ref, f32[16,4608]{1,0:T(8,128)S(1)} %pad_maximum_fusion.3.wt_ref, ...), custom_call_target="tpu_custom_call" | custom-call | flops 2415919104 | bytes 12582912 | tf_op jit(solution)/shard_map/pallas_call | solution.py:143
  213.8 1.6 constant_dynamic-update-slice_fusion.1
  215.4 1.2 multiply_convert_fusion.9
  216.6 3.5 collective-permute-start.18
  220.1 1.1 convert_multiply_fusion.2.rest_1_
  221.1 1.1 convert_multiply_fusion.1.rest_2_
  222.3 15.6 %shard_map.84 = (f32[4,384,128]{2,1,0:T(8,128)S(1)}, f32[12,384,128]{2,1,0:T(8,128)S(1)}, f32[4,384,128]{2,1,0:T(8,128)}, f32[12,384,128]{2,1,0:T(8,128)}) custom-call(s32[1]{0:T(128)} %bitcast.me_ref, bf16[4608,1024]{1,0:T(8,128)(2,1)} %l_ref.23, f32[16,4608]{1,0:T(8,128)S(1)} %pad_maximum_fusion.2.k_ref, f32[16,4608]{1,0:T(8,128)S(1)} %pad_maximum_fusion.3.wt_ref, ...), custom_call_target="tpu_custom_call" | custom-call | flops 2415919104 | bytes 12582912 | tf_op jit(solution)/shard_map/pallas_call | solution.py:143
  238.2 0.7 collective-permute-start.14
  238.8 1.5 collective-permute-start.13
  240.6 1.6 fusion.3
  242.3 2.4 collective-permute-start.17
  244.7 1.0 collective-permute-start.16
  245.7 1.5 collective-permute-start.15
  247.2 1.8 multiply_add_fusion.15
  249.3 3.1 shard_map.85.rest_4_
  252.4 16.8 %collective-permute-done.17 = f16[4,384,128]{2,1,0:T(8,128)(2,1)S(1)} collective-permute-done((f16[4,384,128]{2,1,0:T(8,128)(2,1)S(1)}, f16[4,384,128]{2,1,0:T(8,128)(2,1)S(1)}, u32[]{:S(2)}, u32[]{:S(2)}) %collective-permute-start.17) | collective-permute-done | bytes 393248 | tf_op jit(solution)/shard_map/ppermute | solution.py:728
  269.2 23.7 %collective-permute-done.16 = f16[4,384,128]{2,1,0:T(8,128)(2,1)S(1)} collective-permute-done((f16[4,384,128]{2,1,0:T(8,128)(2,1)S(1)}, f16[4,384,128]{2,1,0:T(8,128)(2,1)S(1)}, u32[]{:S(2)}, u32[]{:S(2)}) %collective-permute-start.16) | collective-permute-done | bytes 393248 | tf_op jit(solution)/shard_map/ppermute | solution.py:728
  292.9 0.4 multiply_add_fusion.12
  293.3 3.1 shard_map.86.rest_4_
  296.4 10.3 %collective-permute-done.12 = f16[4,384,128]{2,1,0:T(8,128)(2,1)S(1)} collective-permute-done((f16[4,384,128]{2,1,0:T(8,128)(2,1)S(1)}, f16[4,384,128]{2,1,0:T(8,128)(2,1)S(1)}, u32[]{:S(2)}, u32[]{:S(2)}) %collective-permute-start.12) | collective-permute-done | bytes 393248 | tf_op jit(solution)/shard_map/ppermute | solution.py:728
  307.1 3.1 shard_map.87.x_ref
  310.2 7.2 %collective-permute-start.27 = (f16[4,768,128]{2,1,0:T(8,128)(2,1)}, f16[4,768,128]{2,1,0:T(8,128)(2,1)S(1)}, u32[]{:S(2)}, u32[]{:S(2)}) collective-permute-start(f16[4,768,128]{2,1,0:T(8,128)(2,1)} %get-tuple-element.89), channel_id=1, source_target_pairs={{0,3},{1,0},{2,1},{3,2},{4,7},{5,4},{6,5},{7,6},{8,11},{9,8},{10,9... | collective-permute-start | bytes 2359304 | tf_op jit(solution)/shard_map/ppermute | solution.py:728
  317.3 0.6 collective-permute-start.29
  318.0 19.3 %shard_map.88 = bf16[4,2,64,1024]{3,2,1,0:T(8,128)(2,1)S(1)} custom-call(f32[4,2,64,1024]{3,2,1,0:T(8,128)S(1)} %bitcast.52), custom_call_target="tpu_custom_call" | custom-call | flops 20971520 | bytes 20971520 | tf_op jit(solution)/shard_map/pallas_call | solution.py:681
  337.3 11.9 %shard_map.89 = f32[512,1024]{1,0:T(8,128)S(1)} custom-call(bf16[4608,1024]{1,0:T(8,128)(2,1)S(1)} %bitcast.45, f32[4,4608]{1,0:T(4,128)S(1)} %copy-done.3, bf16[512,1024]{1,0:T(8,128)(2,1)S(1)} %bitcast.63, f32[512,1024]{1,0:T(8,128)S(1)} %shard_map.87.x_ref), custom_call_target="tpu_custom_call" | custom-call | flops 9663676416 | bytes 9437184 | tf_op jit(solution)/shard_map/pallas_call | solution.py:274
  349.3 11.3 %shard_map.90 = bf16[64,1024]{1,0:T(8,128)(2,1)S(1)} custom-call(f32[4,2,64,1024]{3,2,1,0:T(8,128)S(1)} %bitcast.61), custom_call_target="tpu_custom_call" | custom-call | flops 10485760 | bytes 10485760 | tf_op jit(solution)/shard_map/pallas_call | solution.py:672
  360.6 3.4 collective-permute-start.23
  364.3 1.2 collective-permute-start.22
  365.5 11.5 %shard_map.91 = (bf16[1,4,2,64,1024]{4,3,2,1,0:T(8,128)(2,1)S(1)}, f32[8,128]{1,0:T(8,128)}) custom-call(bf16[1,64,1024]{2,1,0:T(8,128)(2,1)S(1)} %bitcast.67), custom_call_target="tpu_custom_call" | custom-call | flops 20971520 | bytes 20971520 | tf_op jit(solution)/shard_map/pallas_call | solution.py:700
  377.0 15.8 %collective-permute-start.21 = (bf16[64,1024]{1,0:T(8,128)(2,1)S(1)}, bf16[64,1024]{1,0:T(8,128)(2,1)S(1)}, u32[]{:S(2)}, u32[]{:S(2)}) collective-permute-start(bf16[64,1024]{1,0:T(8,128)(2,1)S(1)} %shard_map.90), channel_id=1, source_target_pairs={{0,1},{1,2},{2,3},{3,0},{4,5},{5,6},{6,7},{7,4},{8,9},{9,10},{10,1... | collective-permute-start | bytes 393224 | tf_op jit(solution)/shard_map/ppermute | solution.py:728
  392.8 14.7 %shard_map.92 = f32[4,4608,128]{2,1,0:T(8,128)} custom-call(s32[1]{0:T(128)} %bitcast.me_ref, bf16[4608,1024]{1,0:T(8,128)(2,1)S(1)} %bitcast.45, f32[4,4608]{1,0:T(4,128)S(1)} %copy-done.3, bf16[512,1024]{1,0:T(8,128)(2,1)S(1)} %bitcast.55, f32[4,384,128]{2,1,0:T(8,128)S(1)} %get-tuple-element.127.rest_0_, f32[4,384,128]{2,1,0:T(8,128)S(1)} %get-tuple-element.126.rest_1_, ...), custom_call_target="tpu_custom_call" | custom-call | flops 4831838208 | bytes 18874368 | tf_op jit(solution)/shard_map/pallas_call | solution.py:362
  407.7 19.7 %shard_map.93 = (bf16[4,4,2,64,1024]{4,3,2,1,0:T(8,128)(2,1)S(1)}, f32[8,128]{1,0:T(8,128)}) custom-call(bf16[3,64,1024]{2,1,0:T(8,128)(2,1)S(1)} %pad_maximum_fusion.1.x_ref, bf16[4,2,64,1024]{3,2,1,0:T(8,128)(2,1)S(1)} %bitcast.56), custom_call_target="tpu_custom_call" | custom-call | flops 62914560 | bytes 62914560 | tf_op jit(solution)/shard_map/pallas_call | solution.py:700
  427.4 3.8 collective-permute-start.24
  431.2 0.4 multiply_add_fusion.6
  431.6 17.2 %shard_map.94.rest_4_ = f32[4,4608,128]{2,1,0:T(8,128)} custom-call(s32[1]{0:T(128)} %bitcast.me_ref, bf16[4608,1024]{1,0:T(8,128)(2,1)S(1)} %bitcast.45, f32[16,4608]{1,0:T(8,128)S(1)} %pad_maximum_fusion.2.k_ref, f32[16,4608]{1,0:T(8,128)S(1)} %pad_maximum_fusion.3.wt_ref, f32[64,16]{1,0:T(8,128)S(1)} %bitcast.68, bf16[2048,1024]{1,0:T(8,128)(2,1)S(1)} %bitcast.49, ...), custom_call_target="tpu_custom_call" | custom-call | flops 6442450944 | bytes 6291456 | tf_op jit(solution)/shard_map/pallas_call | solution.py:439
  449.3 17.2 %shard_map.95.rest_4_ = f32[4,4608,128]{2,1,0:T(8,128)} custom-call(s32[1]{0:T(128)} %bitcast.me_ref, bf16[4608,1024]{1,0:T(8,128)(2,1)S(1)} %bitcast.45, f32[16,4608]{1,0:T(8,128)S(1)} %pad_maximum_fusion.2.k_ref, f32[16,4608]{1,0:T(8,128)S(1)} %pad_maximum_fusion.3.wt_ref, f32[64,16]{1,0:T(8,128)S(1)} %bitcast.69, ...), custom_call_target="tpu_custom_call", output_to_operand_aliasing={{}: (10, {})} | custom-call | flops 6442450944 | bytes 6291456 | tf_op jit(solution)/shard_map/pallas_call | solution.py:439
  466.5 0.4 multiply_add_fusion
  466.9 17.2 %shard_map.96 = f32[4,4608,128]{2,1,0:T(8,128)} custom-call(s32[1]{0:T(128)} %bitcast.me_ref, bf16[4608,1024]{1,0:T(8,128)(2,1)S(1)} %bitcast.45, f32[16,4608]{1,0:T(8,128)S(1)} %pad_maximum_fusion.2.k_ref, f32[16,4608]{1,0:T(8,128)S(1)} %pad_maximum_fusion.3.wt_ref, f32[64,16]{1,0:T(8,128)S(1)} %bitcast.70, ...), custom_call_target="tpu_custom_call", output_to_operand_aliasing={{}: (10, {})} | custom-call | flops 6442450944 | bytes 6291456 | tf_op jit(solution)/shard_map/pallas_call | solution.py:439
  (117 shorter events, 4.8 us)
Async XLA Ops:
  1.6 85.1 %collective-permute-start.2 = (f16[2,4,4608]{2,1,0:T(4,128)(2,1)S(1)}, f16[2,4,4608]{2,1,0:T(4,128)(2,1)S(1)}, u32[]{:S(2)}, u32[]{:S(2)}) collective-permute-start(f16[2,4,4608]{2,1,0:T(4,128)(2,1)S(1)} %fusion.6), channel_id=1, source_target_pairs={{0,3},{1,0},{2,1},{3,2},{4,7},{5,4},{6,5},{7,6},{8,11},{9,8},{10,9... | collective-permute-start | bytes 221192 | tf_op jit(solution)/shard_map/ppermute | solution.py:728
  6.7 80.1 %collective-permute-start.1 = (f16[2,4,4608]{2,1,0:T(4,128)(2,1)S(1)}, f16[2,4,4608]{2,1,0:T(4,128)(2,1)S(1)}, u32[]{:S(2)}, u32[]{:S(2)}) collective-permute-start(f16[2,4,4608]{2,1,0:T(4,128)(2,1)S(1)} %fusion.6), channel_id=1, source_target_pairs={{0,2},{1,3},{2,0},{3,1},{4,6},{5,7},{6,4},{7,5},{8,10},{9,11},{10,... | collective-permute-start | bytes 221192 | tf_op jit(solution)/shard_map/ppermute | solution.py:728
  6.7 84.0 %collective-permute-start = (f16[2,4,4608]{2,1,0:T(4,128)(2,1)S(1)}, f16[2,4,4608]{2,1,0:T(4,128)(2,1)S(1)}, u32[]{:S(2)}, u32[]{:S(2)}) collective-permute-start(f16[2,4,4608]{2,1,0:T(4,128)(2,1)S(1)} %fusion.6), channel_id=1, source_target_pairs={{0,1},{1,2},{2,3},{3,0},{4,5},{5,6},{6,7},{7,4},{8,9},{9,10},{10,1... | collective-permute-start | bytes 221192 | tf_op jit(solution)/shard_map/ppermute | solution.py:728
  7.7 31.5 %copy-start = (bf16[4608,1024]{1,0:T(8,128)(2,1)S(1)}, bf16[4608,1024]{1,0:T(8,128)(2,1)}, u32[]{:S(2)}) copy-start(bf16[4608,1024]{1,0:T(8,128)(2,1)} %l_ref.23) | copy-start | bytes 28311556
  19.3 19.9 %copy-start.3 = (f32[4,4608]{1,0:T(4,128)S(1)}, f32[4,4608]{1,0:T(4,128)}, u32[]{:S(2)}) copy-start(f32[4,4608]{1,0:T(4,128)} %wt_ref.5) | copy-start | bytes 221188
  51.2 15.4 %copy-start.14 = (f32[16,16]{1,0:T(8,128)S(1)}, f32[16,16]{1,0:T(8,128)}, u32[]{:S(2)}) copy-start(f32[16,16]{1,0:T(8,128)} %param.10) | copy-start | bytes 3076
  51.2 15.8 %copy-start.15 = (f32[16,16]{1,0:T(8,128)S(1)}, f32[16,16]{1,0:T(8,128)}, u32[]{:S(2)}) copy-start(f32[16,16]{1,0:T(8,128)} %param.11) | copy-start | bytes 3076
  62.5 28.4 %collective-permute-start.5 = (bf16[64,1024]{1,0:T(8,128)(2,1)S(1)}, bf16[64,1024]{1,0:T(8,128)(2,1)S(1)}, u32[]{:S(2)}, u32[]{:S(2)}) collective-permute-start(bf16[64,1024]{1,0:T(8,128)(2,1)S(1)} %shard_map.79), channel_id=1, source_target_pairs={{0,3},{1,0},{2,1},{3,2},{4,7},{5,4},{6,5},{7,6},{8,11},{9,8},{10,9... | collective-permute-start | bytes 393224 | tf_op jit(solution)/shard_map/ppermute | solution.py:728
  65.4 26.3 %collective-permute-start.4 = (bf16[64,1024]{1,0:T(8,128)(2,1)S(1)}, bf16[64,1024]{1,0:T(8,128)(2,1)}, u32[]{:S(2)}, u32[]{:S(2)}) collective-permute-start(bf16[64,1024]{1,0:T(8,128)(2,1)S(1)} %shard_map.79), channel_id=1, source_target_pairs={{0,2},{1,3},{2,0},{3,1},{4,6},{5,7},{6,4},{7,5},{8,10},{9,11},{10,... | collective-permute-start | bytes 393224 | tf_op jit(solution)/shard_map/ppermute | solution.py:728
  74.3 17.4 %copy-start.13 = (f32[4,4608]{1,0:T(4,128)S(1)}, f32[4,4608]{1,0:T(4,128)}, u32[]{:S(2)}) copy-start(f32[4,4608]{1,0:T(4,128)} %param.9) | copy-start | bytes 221188
  86.7 8.3 %collective-permute-start.3 = (bf16[64,1024]{1,0:T(8,128)(2,1)S(1)}, bf16[64,1024]{1,0:T(8,128)(2,1)S(1)}, u32[]{:S(2)}, u32[]{:S(2)}) collective-permute-start(bf16[64,1024]{1,0:T(8,128)(2,1)S(1)} %shard_map.79), channel_id=1, source_target_pairs={{0,1},{1,2},{2,3},{3,0},{4,5},{5,6},{6,7},{7,4},{8,9},{9,10},{10,1... | collective-permute-start | bytes 393224 | tf_op jit(solution)/shard_map/ppermute | solution.py:728
  86.8 64.7 %collective-permute-start.8 = (f16[4,768,128]{2,1,0:T(8,128)(2,1)}, f16[4,768,128]{2,1,0:T(8,128)(2,1)S(1)}, u32[]{:S(2)}, u32[]{:S(2)}) collective-permute-start(f16[4,768,128]{2,1,0:T(8,128)(2,1)} %get-tuple-element.131), channel_id=1, source_target_pairs={{0,3},{1,0},{2,1},{3,2},{4,7},{5,4},{6,5},{7,6},{8,11},{9,8},{10,9... | collective-permute-start | bytes 2359304 | tf_op jit(solution)/shard_map/ppermute | solution.py:728
  90.8 88.0 %collective-permute-start.7 = (f16[4,768,128]{2,1,0:T(8,128)(2,1)}, f16[4,768,128]{2,1,0:T(8,128)(2,1)S(1)}, u32[]{:S(2)}, u32[]{:S(2)}) collective-permute-start(f16[4,768,128]{2,1,0:T(8,128)(2,1)} %get-tuple-element.132), channel_id=1, source_target_pairs={{0,2},{1,3},{2,0},{3,1},{4,6},{5,7},{6,4},{7,5},{8,10},{9,11},{10,... | collective-permute-start | bytes 2359304 | tf_op jit(solution)/shard_map/ppermute | solution.py:728
  91.0 87.9 %collective-permute-start.6 = (f16[4,768,128]{2,1,0:T(8,128)(2,1)}, f16[4,768,128]{2,1,0:T(8,128)(2,1)S(1)}, u32[]{:S(2)}, u32[]{:S(2)}) collective-permute-start(f16[4,768,128]{2,1,0:T(8,128)(2,1)} %get-tuple-element.133), channel_id=1, source_target_pairs={{0,1},{1,2},{2,3},{3,0},{4,5},{5,6},{6,7},{7,4},{8,9},{9,10},{10,1... | collective-permute-start | bytes 2359304 | tf_op jit(solution)/shard_map/ppermute | solution.py:728
  91.7 124.9 %collective-permute-start.9 = (f16[4,384,128]{2,1,0:T(8,128)(2,1)}, f16[4,384,128]{2,1,0:T(8,128)(2,1)}, u32[]{:S(2)}, u32[]{:S(2)}) collective-permute-start(f16[4,384,128]{2,1,0:T(8,128)(2,1)} %get-tuple-element.64), channel_id=1, source_target_pairs={{0,1},{1,2},{2,3},{3,0},{4,5},{5,6},{6,7},{7,4},{8,9},{9,10},{10,1... | collective-permute-start | bytes 1179656 | tf_op jit(solution)/shard_map/ppermute | solution.py:728
  95.0 125.1 %collective-permute-start.10 = (f16[4,384,128]{2,1,0:T(8,128)(2,1)}, f16[4,384,128]{2,1,0:T(8,128)(2,1)}, u32[]{:S(2)}, u32[]{:S(2)}) collective-permute-start(f16[4,384,128]{2,1,0:T(8,128)(2,1)} %get-tuple-element.65), channel_id=1, source_target_pairs={{0,2},{1,3},{2,0},{3,1},{4,6},{5,7},{6,4},{7,5},{8,10},{9,11},{10,... | collective-permute-start | bytes 1179656 | tf_op jit(solution)/shard_map/ppermute | solution.py:728
  148.2 2.0 copy-start.1
  151.5 68.5 %collective-permute-start.11 = (f16[4,384,128]{2,1,0:T(8,128)(2,1)}, f16[4,384,128]{2,1,0:T(8,128)(2,1)S(1)}, u32[]{:S(2)}, u32[]{:S(2)}) collective-permute-start(f16[4,384,128]{2,1,0:T(8,128)(2,1)} %get-tuple-element.66), channel_id=1, source_target_pairs={{0,3},{1,0},{2,1},{3,2},{4,7},{5,4},{6,5},{7,6},{8,11},{9,8},{10,9... | collective-permute-start | bytes 1179656 | tf_op jit(solution)/shard_map/ppermute | solution.py:728
  178.9 2.2 copy-start.2
  197.9 44.3 %collective-permute-start.20 = (f16[4,384,128]{2,1,0:T(8,128)(2,1)}, f16[4,384,128]{2,1,0:T(8,128)(2,1)}, u32[]{:S(2)}, u32[]{:S(2)}) collective-permute-start(f16[4,384,128]{2,1,0:T(8,128)(2,1)} %get-tuple-element.140), channel_id=1, source_target_pairs={{0,1},{1,2},{2,3},{3,0},{4,5},{5,6},{6,7},{7,4},{8,9},{9,10},{10,1... | collective-permute-start | bytes 1179656 | tf_op jit(solution)/shard_map/ppermute | solution.py:728
  198.0 15.9 %copy-start.5 = (f32[12,384,128]{2,1,0:T(8,128)S(1)}, f32[12,384,128]{2,1,0:T(8,128)}, u32[]{:S(2)}) copy-start(f32[12,384,128]{2,1,0:T(8,128)} %get-tuple-element.55) | copy-start | bytes 7077892
  198.0 46.7 %collective-permute-start.19 = (f16[4,384,128]{2,1,0:T(8,128)(2,1)}, f16[4,384,128]{2,1,0:T(8,128)(2,1)}, u32[]{:S(2)}, u32[]{:S(2)}) collective-permute-start(f16[4,384,128]{2,1,0:T(8,128)(2,1)} %get-tuple-element.141), channel_id=1, source_target_pairs={{0,2},{1,3},{2,0},{3,1},{4,6},{5,7},{6,4},{7,5},{8,10},{9,11},{10,... | collective-permute-start | bytes 1179656 | tf_op jit(solution)/shard_map/ppermute | solution.py:728
  216.6 29.1 %collective-permute-start.18 = (f16[4,384,128]{2,1,0:T(8,128)(2,1)}, f16[4,384,128]{2,1,0:T(8,128)(2,1)}, u32[]{:S(2)}, u32[]{:S(2)}) collective-permute-start(f16[4,384,128]{2,1,0:T(8,128)(2,1)} %get-tuple-element.142), channel_id=1, source_target_pairs={{0,3},{1,0},{2,1},{3,2},{4,7},{5,4},{6,5},{7,6},{8,11},{9,8},{10,9... | collective-permute-start | bytes 1179656 | tf_op jit(solution)/shard_map/ppermute | solution.py:728
  222.2 18.2 %slice-start.6 = ((s8[4718592]{0:T(1024)(128)(4,1)}), s8[4194304]{0:T(1024)(128)(4,1)S(1)}, s32[]{:S(2)}) async-start(s8[4718592]{0:T(1024)(128)(4,1)} %bitcast.73), calls=%async_computation.6 | async-start | bytes 8388608
  222.3 18.1 %slice-start.7 = ((s8[4718592]{0:T(1024)(128)(4,1)}), s8[524288]{0:T(1024)(128)(4,1)S(1)}, s32[]{:S(2)}) async-start(s8[4718592]{0:T(1024)(128)(4,1)} %bitcast.73), calls=%async_computation.7 | async-start | bytes 1048576
  222.3 24.8 %slice-start.3 = ((s8[9437184]{0:T(1024)(128)(4,1)}), s8[4194304]{0:T(1024)(128)(4,1)S(1)}, s32[]{:S(2)}) async-start(s8[9437184]{0:T(1024)(128)(4,1)} %bitcast.71), calls=%async_computation.3 | async-start | bytes 8388608
  222.3 24.8 %slice-start.4 = ((s8[9437184]{0:T(1024)(128)(4,1)}), s8[4194304]{0:T(1024)(128)(4,1)S(1)}, s32[]{:S(2)}) async-start(s8[9437184]{0:T(1024)(128)(4,1)} %bitcast.71), calls=%async_computation.4 | async-start | bytes 8388608
  237.9 2.5 copy-start.4
  237.9 9.3 %slice-start.5 = ((s8[9437184]{0:T(1024)(128)(4,1)}), s8[1048576]{0:T(1024)(128)(4,1)S(1)}, s32[]{:S(2)}) async-start(s8[9437184]{0:T(1024)(128)(4,1)} %bitcast.71), calls=%async_computation.5 | async-start | bytes 2097152
  238.2 58.2 %collective-permute-start.14 = (f16[4,384,128]{2,1,0:T(8,128)(2,1)S(1)}, f16[4,384,128]{2,1,0:T(8,128)(2,1)S(1)}, u32[]{:S(2)}, u32[]{:S(2)}) collective-permute-start(f16[4,384,128]{2,1,0:T(8,128)(2,1)S(1)} %get-tuple-element.146), channel_id=1, source_target_pairs={{0,1},{1,2},{2,3},{3,0},{4,5},{5,6},{6,7},{7,4},{8,9},{9,10},{10,1... | collective-permute-start | bytes 1179656 | tf_op jit(solution)/shard_map/ppermute | solution.py:728
  238.8 57.5 %collective-permute-start.13 = (f16[4,384,128]{2,1,0:T(8,128)(2,1)S(1)}, f16[4,384,128]{2,1,0:T(8,128)(2,1)S(1)}, u32[]{:S(2)}, u32[]{:S(2)}) collective-permute-start(f16[4,384,128]{2,1,0:T(8,128)(2,1)S(1)} %get-tuple-element.147), channel_id=1, source_target_pairs={{0,2},{1,3},{2,0},{3,1},{4,6},{5,7},{6,4},{7,5},{8,10},{9,11},{10,... | collective-permute-start | bytes 1179656 | tf_op jit(solution)/shard_map/ppermute | solution.py:728
  240.4 1.9 copy-start.12
  240.4 4.3 copy-start.11
  240.4 5.3 %copy-start.10 = (f16[4,384,128]{2,1,0:T(8,128)(2,1)S(1)}, f16[4,384,128]{2,1,0:T(8,128)(2,1)}, u32[]{:S(2)}) copy-start(f16[4,384,128]{2,1,0:T(8,128)(2,1)} %get-tuple-element.145) | copy-start | bytes 1179652
  240.6 8.6 %slice-start = ((s8[9437184]{0:T(1024)(128)(4,1)}), s8[4194304]{0:T(1024)(128)(4,1)S(1)}, s32[]{:S(2)}) async-start(s8[9437184]{0:T(1024)(128)(4,1)} %bitcast.44), calls=%async_computation | async-start | bytes 8388608
  240.6 8.6 %slice-start.1 = ((s8[9437184]{0:T(1024)(128)(4,1)}), s8[4194304]{0:T(1024)(128)(4,1)S(1)}, s32[]{:S(2)}) async-start(s8[9437184]{0:T(1024)(128)(4,1)} %bitcast.44), calls=%async_computation.1 | async-start | bytes 8388608
  242.3 26.9 %collective-permute-start.17 = (f16[4,384,128]{2,1,0:T(8,128)(2,1)S(1)}, f16[4,384,128]{2,1,0:T(8,128)(2,1)S(1)}, u32[]{:S(2)}, u32[]{:S(2)}) collective-permute-start(f16[4,384,128]{2,1,0:T(8,128)(2,1)S(1)} %copy-done.12), channel_id=1, source_target_pairs={{0,1},{1,2},{2,3},{3,0},{4,5},{5,6},{6,7},{7,4},{8,9},{9,10},{10,1... | collective-permute-start | bytes 1179656 | tf_op jit(solution)/shard_map/ppermute | solution.py:728
  244.7 48.2 %collective-permute-start.16 = (f16[4,384,128]{2,1,0:T(8,128)(2,1)S(1)}, f16[4,384,128]{2,1,0:T(8,128)(2,1)S(1)}, u32[]{:S(2)}, u32[]{:S(2)}) collective-permute-start(f16[4,384,128]{2,1,0:T(8,128)(2,1)S(1)} %copy-done.11), channel_id=1, source_target_pairs={{0,2},{1,3},{2,0},{3,1},{4,6},{5,7},{6,4},{7,5},{8,10},{9,11},{10,... | collective-permute-start | bytes 1179656 | tf_op jit(solution)/shard_map/ppermute | solution.py:728
  245.7 47.2 %collective-permute-start.15 = (f16[4,384,128]{2,1,0:T(8,128)(2,1)S(1)}, f16[4,384,128]{2,1,0:T(8,128)(2,1)S(1)}, u32[]{:S(2)}, u32[]{:S(2)}) collective-permute-start(f16[4,384,128]{2,1,0:T(8,128)(2,1)S(1)} %copy-done.10), channel_id=1, source_target_pairs={{0,3},{1,0},{2,1},{3,2},{4,7},{5,4},{6,5},{7,6},{8,11},{9,8},{10,9... | collective-permute-start | bytes 1179656 | tf_op jit(solution)/shard_map/ppermute | solution.py:728
  247.2 2.1 slice-start.2
  269.1 37.5 %collective-permute-start.12 = (f16[4,384,128]{2,1,0:T(8,128)(2,1)S(1)}, f16[4,384,128]{2,1,0:T(8,128)(2,1)S(1)}, u32[]{:S(2)}, u32[]{:S(2)}) collective-permute-start(f16[4,384,128]{2,1,0:T(8,128)(2,1)S(1)} %get-tuple-element.148), channel_id=1, source_target_pairs={{0,3},{1,0},{2,1},{3,2},{4,7},{5,4},{6,5},{7,6},{8,11},{9,8},{10,9... | collective-permute-start | bytes 1179656 | tf_op jit(solution)/shard_map/ppermute | solution.py:728
  310.2 117.2 %collective-permute-start.27 = (f16[4,768,128]{2,1,0:T(8,128)(2,1)}, f16[4,768,128]{2,1,0:T(8,128)(2,1)S(1)}, u32[]{:S(2)}, u32[]{:S(2)}) collective-permute-start(f16[4,768,128]{2,1,0:T(8,128)(2,1)} %get-tuple-element.89), channel_id=1, source_target_pairs={{0,3},{1,0},{2,1},{3,2},{4,7},{5,4},{6,5},{7,6},{8,11},{9,8},{10,9... | collective-permute-start | bytes 2359304 | tf_op jit(solution)/shard_map/ppermute | solution.py:728
  317.3 113.9 %collective-permute-start.28 = (f16[4,768,128]{2,1,0:T(8,128)(2,1)}, f16[4,768,128]{2,1,0:T(8,128)(2,1)S(1)}, u32[]{:S(2)}, u32[]{:S(2)}) collective-permute-start(f16[4,768,128]{2,1,0:T(8,128)(2,1)} %get-tuple-element.90), channel_id=1, source_target_pairs={{0,2},{1,3},{2,0},{3,1},{4,6},{5,7},{6,4},{7,5},{8,10},{9,11},{10,... | collective-permute-start | bytes 2359304 | tf_op jit(solution)/shard_map/ppermute | solution.py:728
  317.3 113.9 %collective-permute-start.29 = (f16[4,768,128]{2,1,0:T(8,128)(2,1)}, f16[4,768,128]{2,1,0:T(8,128)(2,1)S(1)}, u32[]{:S(2)}, u32[]{:S(2)}) collective-permute-start(f16[4,768,128]{2,1,0:T(8,128)(2,1)} %get-tuple-element.91), channel_id=1, source_target_pairs={{0,1},{1,2},{2,3},{3,0},{4,5},{5,6},{6,7},{7,4},{8,9},{9,10},{10,1... | collective-permute-start | bytes 2359304 | tf_op jit(solution)/shard_map/ppermute | solution.py:728
  337.3 26.7 %copy-start.6 = (f32[12,384,128]{2,1,0:T(8,128)S(1)}, f32[12,384,128]{2,1,0:T(8,128)}, u32[]{:S(2)}) copy-start(f32[12,384,128]{2,1,0:T(8,128)} %get-tuple-element.87) | copy-start | bytes 7077892
  360.6 16.4 %collective-permute-start.23 = (bf16[64,1024]{1,0:T(8,128)(2,1)S(1)}, bf16[64,1024]{1,0:T(8,128)(2,1)S(1)}, u32[]{:S(2)}, u32[]{:S(2)}) collective-permute-start(bf16[64,1024]{1,0:T(8,128)(2,1)S(1)} %shard_map.90), channel_id=1, source_target_pairs={{0,3},{1,0},{2,1},{3,2},{4,7},{5,4},{6,5},{7,6},{8,11},{9,8},{10,9... | collective-permute-start | bytes 393224 | tf_op jit(solution)/shard_map/ppermute | solution.py:728
  364.3 43.2 %collective-permute-start.22 = (bf16[64,1024]{1,0:T(8,128)(2,1)S(1)}, bf16[64,1024]{1,0:T(8,128)(2,1)S(1)}, u32[]{:S(2)}, u32[]{:S(2)}) collective-permute-start(bf16[64,1024]{1,0:T(8,128)(2,1)S(1)} %shard_map.90), channel_id=1, source_target_pairs={{0,2},{1,3},{2,0},{3,1},{4,6},{5,7},{6,4},{7,5},{8,10},{9,11},{10,... | collective-permute-start | bytes 393224 | tf_op jit(solution)/shard_map/ppermute | solution.py:728
  377.0 30.6 %collective-permute-start.21 = (bf16[64,1024]{1,0:T(8,128)(2,1)S(1)}, bf16[64,1024]{1,0:T(8,128)(2,1)S(1)}, u32[]{:S(2)}, u32[]{:S(2)}) collective-permute-start(bf16[64,1024]{1,0:T(8,128)(2,1)S(1)} %shard_map.90), channel_id=1, source_target_pairs={{0,1},{1,2},{2,3},{3,0},{4,5},{5,6},{6,7},{7,4},{8,9},{9,10},{10,1... | collective-permute-start | bytes 393224 | tf_op jit(solution)/shard_map/ppermute | solution.py:728
  407.5 23.7 %copy-start.7 = (f32[4,384,128]{2,1,0:T(8,128)S(1)}, f32[4,384,128]{2,1,0:T(8,128)}, u32[]{:S(2)}) copy-start(f32[4,384,128]{2,1,0:T(8,128)} %get-tuple-element.95) | copy-start | bytes 2359300
  407.5 59.0 %collective-permute-start.26 = (f16[4,384,128]{2,1,0:T(8,128)(2,1)S(1)}, f16[4,384,128]{2,1,0:T(8,128)(2,1)S(1)}, u32[]{:S(2)}, u32[]{:S(2)}) collective-permute-start(f16[4,384,128]{2,1,0:T(8,128)(2,1)S(1)} %get-tuple-element.137), channel_id=1, source_target_pairs={{0,1},{1,2},{2,3},{3,0},{4,5},{5,6},{6,7},{7,4},{8,9},{9,10},{10,1... | collective-permute-start | bytes 1179656 | tf_op jit(solution)/shard_map/ppermute | solution.py:728
  407.6 58.9 %collective-permute-start.25 = (f16[4,384,128]{2,1,0:T(8,128)(2,1)S(1)}, f16[4,384,128]{2,1,0:T(8,128)(2,1)S(1)}, u32[]{:S(2)}, u32[]{:S(2)}) collective-permute-start(f16[4,384,128]{2,1,0:T(8,128)(2,1)S(1)} %get-tuple-element.138), channel_id=1, source_target_pairs={{0,2},{1,3},{2,0},{3,1},{4,6},{5,7},{6,4},{7,5},{8,10},{9,11},{10,... | collective-permute-start | bytes 1179656 | tf_op jit(solution)/shard_map/ppermute | solution.py:728
  427.4 39.1 %collective-permute-start.24 = (f16[4,384,128]{2,1,0:T(8,128)(2,1)S(1)}, f16[4,384,128]{2,1,0:T(8,128)(2,1)S(1)}, u32[]{:S(2)}, u32[]{:S(2)}) collective-permute-start(f16[4,384,128]{2,1,0:T(8,128)(2,1)S(1)} %get-tuple-element.139), channel_id=1, source_target_pairs={{0,3},{1,0},{2,1},{3,2},{4,7},{5,4},{6,5},{7,6},{8,11},{9,8},{10,9... | collective-permute-start | bytes 1179656 | tf_op jit(solution)/shard_map/ppermute | solution.py:728
  431.6 17.2 %copy-start.8 = (f32[4,384,128]{2,1,0:T(8,128)S(1)}, f32[4,384,128]{2,1,0:T(8,128)}, u32[]{:S(2)}) copy-start(f32[4,384,128]{2,1,0:T(8,128)} %get-tuple-element.88) | copy-start | bytes 2359300
  449.3 17.3 %copy-start.9 = (f32[4,384,128]{2,1,0:T(8,128)S(1)}, f32[4,384,128]{2,1,0:T(8,128)}, u32[]{:S(2)}) copy-start(f32[4,384,128]{2,1,0:T(8,128)} %get-tuple-element.86) | copy-start | bytes 2359300
